TPU v7x, 128 devices: a whole 4x4x4 slice. The times are simulated.
128 devices in a mesh: req: 8 (over z, core), tok: 16 (over y, x).
Axes of the slice: x: 4, y: 4, z: 4, core: 2. Of those that a mesh axis runs over, the one named last changes fastest.
Arguments:
- draft_ids: int32 [32, 16], replicated, may hold values from 0 to 65535
- lengths: int32 [32], replicated, may hold values from 1 to 16384, as said below
- current_slot: int32 [32], replicated, may hold values from 0 to 31, as said below
- new_slot: int32 [32], replicated, may hold values from 0 to 31, as said below
- accepted: int32 [32], replicated, may hold values from 1 to 16, as said below
- embed_table: bfloat16 [65536, 3072], P(('req', 'tok')), may hold values from -6.5 to 6.5
- mixer_gain: float32 [3072], replicated, may hold values from 0.5 to 1.5
- query_weight: bfloat16 [3072, 768], replicated, may hold values from -0.3049512 to 0.3049512
- keyvalue_weight: bfloat16 [3072, 256], replicated, may hold values from -0.109375 to 0.109375
- key_cache: bfloat16 [32, 16384, 128], P('req', 'tok'), may hold values from -6 to 6
- value_cache: bfloat16 [32, 16384, 128], P('req', 'tok'), may hold values from -6 to 6
- attention_out: bfloat16 [768, 3072], P(None, 'tok'), may hold values from -0.21875 to 0.21875
- mamba_input: bfloat16 [3072, 2048], P(None, 'tok'), may hold values from -0.109375 to 0.109375
- mamba_gate: bfloat16 [3072, 2048], P(None, 'tok'), may hold values from -0.109375 to 0.109375
- state_proj: bfloat16 [3072, 512], replicated, may hold values from -0.02734375 to 0.02734375
- mamba_step: bfloat16 [3072, 16], P(None, 'tok'), may hold values from -0.109375 to 0.109375
- step_bias: float32 [16], P('tok'), may hold values from -4 to 0
- decay_log: float32 [16], P('tok'), may hold values from -2 to 1.5
- skip_gain: float32 [16], P('tok'), may hold values from 0.5 to 1.5
- states: float32 [32, 16, 128, 256], P('req', 'tok'), may hold values from -1.5 to 1.5
- mamba_out: bfloat16 [2048, 3072], P('tok'), may hold values from -0.125 to 0.125
- mlp_gain: float32 [3072], replicated, may hold values from 0.5 to 1.5
- gate_weight: bfloat16 [3072, 12288], P(None, ('req', 'tok')), may hold values from -0.109375 to 0.109375
- up_weight: bfloat16 [3072, 12288], P(None, ('req', 'tok')), may hold values from -0.109375 to 0.109375
- down_weight: bfloat16 [3072, 12288], P(None, ('req', 'tok')), may hold values from -0.0546875 to 0.0546875
Outputs:
- hidden_out: bfloat16 [512, 3072], P(('req', 'tok'))
- new_states: float32 [32, 16, 128, 256], P('req', 'tok')
Inputs may be any that keep to these rules, and one draw needn't show every extreme that they name: `lengths`: some request has exactly 16384 cached positions and some exactly one. `current_slot`: a permutation: each slot holds one request. `new_slot`: a permutation: each slot receives one request. `accepted`: some request accepts all 16 drafts and some exactly one.
All inputs are finite; a program needn't handle non-finite values.
Results may differ from a plain program's by a relative error of at most 0.02.
Values may be sent and summed in bfloat16 or wider, within the bound.
No kernel may reach another device: no remote copies, remote signals or barrier semaphores. Data moves between devices by JAX's collectives and lax.ppermute only.
A program may use at most 128 MiB of HBM per device.

v0:
```python
import jax
import jax.numpy as jnp
from jax import lax
from jax.sharding import PartitionSpec as P


def rms_rows(table_rows, norm_gain):
    values = table_rows.astype(jnp.float32)
    factor = lax.rsqrt(jnp.mean(values * values, axis=-1, keepdims=True) + 1e-05)
    return (values * factor * norm_gain).astype(jnp.bfloat16)


def inverse_of(mapping):
    places = jnp.arange(mapping.shape[0], dtype=jnp.int32)
    matches = mapping[None, :] == places[:, None]
    return jnp.sum(jnp.where(matches, places[None, :], 0), axis=1)


def recurrence(start_states, decay_rate, inputs, state_in, state_read, accept_count):

    def advance(state_pair, step_items):
        current, chosen = state_pair
        step_decay, step_input, step_in, step_read, step_index = step_items
        current = (
            step_decay[:, :, None, None] * current
            + step_input[..., None] * step_in[:, None, None, :]
        )
        readout = jnp.sum(current * step_read[:, None, None, :], axis=-1)
        chosen = jnp.where((accept_count == step_index + 1)[:, None, None, None], current, chosen)
        return ((current, chosen), readout)

    sequence = (
        jnp.swapaxes(decay_rate, 0, 1),
        jnp.swapaxes(inputs, 0, 1),
        jnp.swapaxes(state_in, 0, 1),
        jnp.swapaxes(state_read, 0, 1),
        jnp.arange(decay_rate.shape[1], dtype=jnp.int32),
    )
    (current, chosen), readouts = lax.scan(advance, (start_states, start_states), sequence)
    return (jnp.swapaxes(readouts, 0, 1), chosen)


def feed_units(block_rows, gate_cols, up_cols, down_cols):
    gate_part = jnp.dot(block_rows, gate_cols, preferred_element_type=jnp.float32)
    up_part = jnp.dot(block_rows, up_cols, preferred_element_type=jnp.float32)
    hidden = (jax.nn.silu(gate_part) * up_part).astype(jnp.bfloat16)
    return lax.dot_general(
        hidden, down_cols, (((1,), (1,)), ((), ())), preferred_element_type=jnp.float32
    )


def local(
    draft_ids,
    lengths,
    current_slot,
    new_slot,
    accepted,
    embed_table,
    mixer_gain,
    query_weight,
    keyvalue_weight,
    key_cache,
    value_cache,
    attention_out,
    mamba_input,
    mamba_gate,
    state_proj,
    mamba_step,
    step_bias,
    decay_log,
    skip_gain,
    states,
    mamba_out,
    mlp_gain,
    gate_weight,
    up_weight,
    down_weight,
):
    members = lax.axis_size("tok")
    group_index = lax.axis_index("req")
    member = lax.axis_index("tok")
    slots_dev, cache_dev, head_size = key_cache.shape
    draft_len = draft_ids.shape[1]
    group_tokens = slots_dev * draft_len
    vocab_dev = embed_table.shape[0]
    query_heads = query_weight.shape[1] // head_size
    heads_dev = step_bias.shape[0]
    mamba_head = mamba_input.shape[1] // heads_dev
    state_size = state_proj.shape[1] // 2
    slot_owner = inverse_of(current_slot)
    token_ids = jnp.take(draft_ids, slot_owner, axis=0).reshape(-1)
    vocab_start = (group_index * members + member) * vocab_dev
    wanted = token_ids - vocab_start
    inside = (wanted >= 0) & (wanted < vocab_dev)
    picked = jnp.take(embed_table, jnp.clip(wanted, 0, vocab_dev - 1), axis=0)
    embedded = lax.psum_scatter(
        jnp.where(inside[:, None], picked.astype(jnp.float32), 0.0),
        ("req", "tok"),
        scatter_dimension=0,
        tiled=True,
    ).astype(jnp.bfloat16)
    normed = rms_rows(embedded, mixer_gain)
    gathered = lax.all_gather(normed, "tok", axis=0, tiled=True)
    queries = jnp.dot(gathered, query_weight, preferred_element_type=jnp.float32).astype(
        jnp.bfloat16
    )
    queries = queries.reshape(slots_dev, draft_len, query_heads, head_size)
    keyvalue = jnp.dot(gathered, keyvalue_weight, preferred_element_type=jnp.float32).astype(
        jnp.bfloat16
    )
    keyvalue = keyvalue.reshape(slots_dev, draft_len, 2, head_size)
    local_owner = lax.dynamic_slice_in_dim(slot_owner, group_index * slots_dev, slots_dev)
    slot_length = jnp.take(lengths, local_owner)
    slot_accept = jnp.take(accepted, local_owner)
    score_scale = head_size ** (-0.5)
    positions = member * cache_dev + jnp.arange(cache_dev, dtype=jnp.int32)
    visible = (positions[None, :] < slot_length[:, None])[:, None, None, :]
    cache_scores = (
        jnp.einsum("sthd,spd->sthp", queries, key_cache, preferred_element_type=jnp.float32)
        * score_scale
    )
    local_max = jnp.max(jnp.where(visible, cache_scores, -1e30), axis=-1)
    cache_probs = jnp.where(visible, jnp.exp(cache_scores - local_max[..., None]), 0.0)
    local_total = jnp.sum(cache_probs, axis=-1)
    local_out = jnp.einsum(
        "sthp,spd->sthd",
        cache_probs.astype(jnp.bfloat16),
        value_cache,
        preferred_element_type=jnp.float32,
    )
    cache_max = lax.pmax(local_max, "tok")
    factor = jnp.exp(local_max - cache_max)
    cache_total, cache_out = (
        lax.psum((local_total * factor).astype(jnp.bfloat16), "tok").astype(jnp.float32),
        lax.psum((local_out * factor[..., None]).astype(jnp.bfloat16), "tok").astype(jnp.float32),
    )
    causal = (jnp.arange(draft_len)[None, :] <= jnp.arange(draft_len)[:, None])[None, :, None, :]
    draft_scores = (
        jnp.einsum("sthd,sud->sthu", queries, keyvalue[:, :, 0], preferred_element_type=jnp.float32)
        * score_scale
    )
    draft_max = jnp.max(jnp.where(causal, draft_scores, -1e30), axis=-1)
    joint_max = jnp.maximum(cache_max, draft_max)
    cache_factor = jnp.exp(cache_max - joint_max)
    draft_probs = jnp.where(causal, jnp.exp(draft_scores - joint_max[..., None]), 0.0)
    prob_total = cache_total * cache_factor + jnp.sum(draft_probs, axis=-1)
    summed = cache_out * cache_factor[..., None] + jnp.einsum(
        "sthu,sud->sthd",
        draft_probs.astype(jnp.bfloat16),
        keyvalue[:, :, 1],
        preferred_element_type=jnp.float32,
    )
    attended = (
        (summed / prob_total[..., None])
        .astype(jnp.bfloat16)
        .reshape(group_tokens, query_heads * head_size)
    )
    attn_proj = jnp.dot(attended, attention_out, preferred_element_type=jnp.float32)
    attn_rows = lax.all_to_all(
        attn_proj.astype(jnp.bfloat16), "tok", split_axis=0, concat_axis=1, tiled=True
    ).astype(attn_proj.dtype)
    mamba_x = jnp.dot(gathered, mamba_input, preferred_element_type=jnp.float32)
    mamba_x = mamba_x.reshape(slots_dev, draft_len, heads_dev, mamba_head)
    mamba_z = jnp.dot(gathered, mamba_gate, preferred_element_type=jnp.float32)
    mamba_z = mamba_z.reshape(slots_dev, draft_len, heads_dev, mamba_head)
    both_proj = jnp.dot(gathered, state_proj, preferred_element_type=jnp.float32)
    both_proj = both_proj.reshape(slots_dev, draft_len, 2, state_size)
    step_size = jax.nn.softplus(
        jnp.dot(gathered, mamba_step, preferred_element_type=jnp.float32) + step_bias
    ).reshape(slots_dev, draft_len, heads_dev)
    decay_rate = jnp.exp(-jnp.exp(decay_log) * step_size)
    readout, chosen = recurrence(
        states,
        decay_rate,
        step_size[..., None] * mamba_x,
        both_proj[:, :, 0],
        both_proj[:, :, 1],
        slot_accept,
    )
    readout = readout + skip_gain[None, None, :, None] * mamba_x
    gated = (
        (readout * jax.nn.silu(mamba_z))
        .astype(jnp.bfloat16)
        .reshape(group_tokens, heads_dev * mamba_head)
    )
    mamba_rows = lax.psum_scatter(
        jnp.dot(gated, mamba_out, preferred_element_type=jnp.float32).astype(jnp.bfloat16),
        "tok",
        scatter_dimension=0,
        tiled=True,
    ).astype(jnp.float32)
    mixed_rows = (embedded.astype(jnp.float32) + attn_rows + mamba_rows).astype(jnp.bfloat16)
    second = rms_rows(mixed_rows, mlp_gain)
    everything = lax.all_gather(second, ("req", "tok"), axis=0, tiled=True)
    mlp_rows = lax.psum_scatter(
        feed_units(everything, gate_weight, up_weight, down_weight),
        ("req", "tok"),
        scatter_dimension=0,
        tiled=True,
    )
    hidden_out = (mixed_rows.astype(jnp.float32) + mlp_rows).astype(jnp.bfloat16)
    every_state = lax.all_gather(chosen.astype(jnp.bfloat16), "req", axis=0, tiled=True).astype(
        chosen.dtype
    )
    incoming = inverse_of(new_slot)
    local_targets = lax.dynamic_slice_in_dim(incoming, group_index * slots_dev, slots_dev)
    sources = jnp.take(current_slot, local_targets)
    new_states = jnp.take(every_state, sources, axis=0)
    return (hidden_out, new_states)


def solution(mesh):
    return jax.shard_map(
        local,
        mesh=mesh,
        in_specs=(
            P(),
            P(),
            P(),
            P(),
            P(),
            P(("req", "tok"), None),
            P(),
            P(),
            P(),
            P("req", "tok", None),
            P("req", "tok", None),
            P(None, "tok"),
            P(None, "tok"),
            P(None, "tok"),
            P(),
            P(None, "tok"),
            P("tok"),
            P("tok"),
            P("tok"),
            P("req", "tok", None, None),
            P("tok", None),
            P(),
            P(None, ("req", "tok")),
            P(None, ("req", "tok")),
            P(None, ("req", "tok")),
        ),
        out_specs=(P(("req", "tok"), None), P("req", "tok", None, None)),
        check_vma=False,
    )
```

profile of v0, /device:TPU:0, one launch (start us, length us, event | category | flops | bytes accessed | tf_op | source)
XLA Modules:
  0.0 808.1 jit_solution(15467223869452533136)
XLA Ops:
  7.2 2.0 copy.142
  12.4 3.9 gather_fusion.1
  16.4 6.2 convert_select_fusion
  22.5 110.7 %all-reduce.11 = bf16[512,3072]{1,0:T(8,128)(2,1)} all-reduce(f32[512,3072]{1,0:T(8,128)} %convert_select_fusion), channel_id=2, replica_groups=mesh['req'=8,'tok'=16] {'req','tok'}, use_global_device_ids=true, to_apply=%region_1.2.clone | all-reduce | flops 1572864 | bytes 9437184
  134.8 23.9 %all-gather = bf16[16,4,3072]{2,1,0:T(4,128)(2,1)} all-gather(bf16[1,4,3072]{2,1,0:T(4,128)(2,1)S(1)} %fusion.44), channel_id=1, replica_groups=mesh['req'=8,'tok'=16] {'tok'}, dimensions={0}, use_global_device_ids=true | all-gather | bytes 417792 | tf_op jit(solution)/shard_map/all_gather | solution.py:103
  159.8 3.9 convolution_convert_fusion.1
  171.4 2.9 select_reduce_fusion
  174.4 72.1 %pmax.7 = f32[4,16,6]{1,2,0:T(8,128)} all-reduce(f32[4,16,6]{1,2,0:T(8,128)S(1)} %get-tuple-element.145), channel_id=1, replica_groups=mesh['req'=8,'tok'=16] {'tok'}, use_global_device_ids=true, to_apply=%region_4.6 | all-reduce | flops 384 | bytes 3072 | tf_op jit(solution)/shard_map/pmax | solution.py:131
  246.4 2.4 fusion.1
  248.8 2.4 convolution_convert_fusion.2
  254.1 3.2 fusion.54
  260.7 2.0 fusion.53
  274.9 165.3 %while.14 = (s32[]{:T(128)}, f32[4,1,128,256]{3,2,1,0:T(8,128)}, bf16[4,1,128,256]{3,2,1,0:T(8,128)(2,1)}, f32[16,4,1,128]{3,0,1,2:T(8,128)}, f32[16,4,1]{1,2,0:...) while((s32[]{:T(128)}, f32[4,1,128,256]{3,2,1,0:T(8,128)}, ...), condition=%wide.region_12.14_spmd, body=%wide.region_10.13_spmd.sunk | while | flops 785927 | bytes 2134257 | solution.py:39
  276.9 2.6 multiply_reduce_fusion.2
  287.3 2.6 multiply_reduce_fusion.2
  292.3 1.9 broadcast_select_fusion.4
  297.7 2.6 multiply_reduce_fusion.2
  308.0 2.6 multiply_reduce_fusion.2
  318.4 2.6 multiply_reduce_fusion.2
  328.7 2.6 multiply_reduce_fusion.2
  339.0 2.6 multiply_reduce_fusion.2
  344.0 1.9 broadcast_select_fusion.4
  349.3 2.6 multiply_reduce_fusion.2
  354.3 1.9 broadcast_select_fusion.4
  359.7 2.6 multiply_reduce_fusion.2
  369.9 2.6 multiply_reduce_fusion.2
  380.3 2.6 multiply_reduce_fusion.2
  390.7 2.6 multiply_reduce_fusion.2
  400.9 2.6 multiply_reduce_fusion.2
  411.3 2.6 multiply_reduce_fusion.2
  421.6 2.6 multiply_reduce_fusion.2
  431.9 2.6 multiply_reduce_fusion.2
  442.3 2.0 select_reduce_fusion.1
  445.0 2.2 convolution_convert_fusion
  448.0 2.8 fusion.5
  450.8 36.1 %psum.15 = bf16[4,16,6]{1,2,0:T(8,128)(2,1)S(1)} all-reduce(bf16[4,16,6]{1,2,0:T(8,128)(2,1)S(1)} %get-tuple-element.132), channel_id=1, replica_groups=mesh['req'=8,'tok'=16] {'tok'}, use_global_device_ids=true, to_apply=%region_8.10 | all-reduce | flops 384 | bytes 1536 | tf_op jit(solution)/shard_map/psum | solution.py:134
  488.5 42.4 %all-reduce.10.cloned.1.call-done = (bf16[4,16,6,128]{3,1,2,0:T(8,128)(2,1)}, bf16[64,3072]{1,0:T(8,128)(2,1)}) async-done(((bf16[4,16,6,128]{3,1,2,0:T(8,128)(2,1)}, bf16[64,3072]{1,0:T(8,128)(2,1)}), (bf16[4,16,6,128]{3,1,2,0:T(8,128)(2,1)}, bf16[64,3072]{1,0:T(8,128)(2,1)})) %all-reduce.10.cloned.1.call-update) | async-done | bytes 491536 | tf_op jit(solution)/shard_map/psum | solution.py:135
  533.0 4.3 all-to-all-start
  539.3 5.6 all-to-all-done
  548.4 62.7 %all-gather.7.cloned.1.call-done = bf16[128,4,3072]{2,1,0:T(4,128)(2,1)} async-done(((bf16[1,4,3072]{2,1,0:T(4,128)(2,1)}), bf16[128,4,3072]{2,1,0:T(4,128)(2,1)}) %all-gather.7.cloned.1.call-update) | async-done | bytes 3145744 | tf_op jit(solution)/shard_map/all_gather | solution.py:194
  611.1 6.0 reshape.403
  617.1 3.1 fusion.56
  620.2 7.0 fusion.7
  628.6 7.2 all-gather.5.cloned.1.call-done
  635.8 4.1 bitcast_convert_fusion
  639.8 3.6 gather_fusion.2
  643.4 1.9 fusion.15
  645.3 154.7 %all-reduce.8.cloned.1.call-done = f32[512,3072]{1,0:T(8,128)} async-done(((f32[512,3072]{1,0:T(8,128)}), f32[512,3072]{1,0:T(8,128)}) %all-reduce.8.cloned.1.call-update) | async-done | bytes 6291472
  (205 shorter events, 153.6 us)
Async XLA Ops:
  7.2 5.3 copy-start
  7.2 523.6 %all-reduce.10.cloned.1.call-start = ((), (), s32[]{:S(2)}) async-start(), calls=%async_computation.4 | async-start | bytes 983040 | tf_op jit(solution)/shard_map/psum | solution.py:135
  22.5 111.7 %copy-start.10 = (f32[3072]{0:T(1024)S(1)}, f32[3072]{0:T(1024)}, u32[]{:S(2)}) copy-start(f32[3072]{0:T(1024)} %param.35) | copy-start | bytes 36868
  134.2 0.6 copy-start.5
  158.7 6.7 copy-start.12
  158.7 8.6 %copy-start.1 = (s32[32]{0:T(128)S(1)}, s32[32]{0:T(128)}, u32[]{:S(2)}) copy-start(s32[32]{0:T(128)} %param.30) | copy-start | bytes 388
  159.8 8.6 %copy-start.2 = (s32[32]{0:T(128)S(1)}, s32[32]{0:T(128)}, u32[]{:S(2)}) copy-start(s32[32]{0:T(128)} %param.33) | copy-start | bytes 388
  170.8 0.6 copy-start.8
  441.6 46.3 %copy-start.7 = (f32[4,16,6]{1,2,0:T(8,128)S(1)}, f32[4,16,6]{1,2,0:T(8,128)}, u32[]{:S(2)}) copy-start(f32[4,16,6]{1,2,0:T(8,128)} %pmax.7) | copy-start | bytes 4612
  441.6 89.2 %copy-start.9 = (bf16[4,16,1,128]{3,2,1,0:T(2,128)(2,1)S(1)}, bf16[4,16,1,128]{3,2,1,0:T(2,128)(2,1)}, u32[]{:S(2)}) copy-start(bf16[4,16,1,128]{3,2,1,0:T(2,128)(2,1)} %get-tuple-element.140) | copy-start | bytes 49156
  445.0 87.1 %copy-start.4 = (bf16[768,192]{0,1:T(8,128)(2,1)S(1)}, bf16[768,192]{0,1:T(8,128)(2,1)}, u32[]{:S(2)}) copy-start(bf16[768,192]{0,1:T(8,128)(2,1)} %param.40) | copy-start | bytes 884740
  447.2 97.8 %copy-start.6 = (bf16[4,3072]{1,0:T(4,128)(2,1)S(1)}, bf16[4,3072]{1,0:T(4,128)(2,1)}, u32[]{:S(2)}) copy-start(bf16[4,3072]{1,0:T(4,128)(2,1)} %copy-done.5) | copy-start | bytes 73732
  533.0 11.9 %all-to-all-start = ((bf16[16,4,192]{2,1,0:T(4,128)(2,1)}), bf16[16,4,192]{2,1,0:T(4,128)(2,1)S(1)}, u32[]{:S(2)}, u32[]{:S(2)}) async-start(bf16[16,4,192]{2,1,0:T(4,128)(2,1)} %all_to_all.10), calls=%async_computation | async-start | bytes 65536 | tf_op jit(solution)/shard_map/all_to_all | solution.py:159
  537.3 73.8 %all-gather.7.cloned.1.call-start = ((), (), s32[]{:S(2)}) async-start(), calls=%async_computation.2 | async-start | bytes 3170304 | tf_op jit(solution)/shard_map/all_gather | solution.py:194
  547.4 88.3 %all-gather.5.cloned.1.call-start = ((), (), s32[]{:S(2)}) async-start(), calls=%async_computation.1 | async-start | bytes 2359296 | tf_op jit(solution)/shard_map/all_gather | solution.py:202
  548.2 251.9 %all-reduce.8.cloned.1.call-start = ((), (), s32[]{:S(2)}) async-start(), calls=%async_computation.3 | async-start | bytes 12582912
  627.2 0.7 copy-start.11
  627.2 0.7 copy-start.3
Sparse Core Ops, SparseCore 0:
  450.9 79.8 all-reduce.9
  547.6 63.5 all-gather.6
  613.0 22.7 all-gather.4
  641.2 158.7 all-reduce.7
where the time goes:
time: 814 us; the launch traced here: 808 us
  waiting for transfers between devices  273 us (34%)
  blocking collectives  243 us (30%)
  other arithmetic  113 us (14%)
  local copies, waits for them, and re-layouts  112 us (14%)
  matrix products  35.8 us (4%)
  between operations  16.7 us (2%)
  loops' own time  9.92 us (1%)
    unnamed x5, waiting for transfers between devices  155 us
    unnamed x1, blocking collectives  111 us
    pmax x1, blocking collectives, local(): cache_max = lax.pmax(local_max, 'tok')  72.1 us
    all_gather x1, waiting for transfers between devices, local(): everything = lax.all_gather(second, ('req', 'tok'), axis=0, tiled=True)  62.7 us
    psum x1, waiting for transfers between devices, local(): lax.psum((local_out * factor[..., None]).astype(jnp.bfloat16), 'tok')  42.4 us
    reduce_sum x16, other arithmetic, advance(): readout = jnp.sum(current * step_read[:, None, None, :], axis=-1)  41 us
    psum x1, blocking collectives, local(): lax.psum((local_total * factor).astype(jnp.bfloat16), 'tok')  36.1 us
    select_n x16, other arithmetic, advance(): jnp.where((accept_count == step_index + 1)[:, None, None, None], current,...  31 us
  transfers between devices with their start and end apart: 5, of which 5 were waited for; matrix products, arithmetic and copies ran while one was open for 4% of the time, Pallas kernels for 0%

commit v1 on v0

v1 whole, which is shorter than its diff:
```python
import functools

import jax
import jax.numpy as jnp
from jax import lax
from jax.experimental import pallas as pl
from jax.experimental.pallas import tpu as pltpu
from jax.sharding import PartitionSpec as P

BF = jnp.bfloat16
F32 = jnp.float32
NEG = -1e30
AUX = 128


def rms_rows(table_rows, norm_gain):
    values = table_rows.astype(F32)
    factor = lax.rsqrt(jnp.mean(values * values, axis=-1, keepdims=True) + 1e-05)
    return (values * factor * norm_gain).astype(BF)


def inverse_of(mapping):
    places = jnp.arange(mapping.shape[0], dtype=jnp.int32)
    matches = mapping[None, :] == places[:, None]
    return jnp.sum(jnp.where(matches, places[None, :], 0), axis=1)


def dot_nn(a, b, precision=None):
    return lax.dot_general(
        a, b, (((1,), (0,)), ((), ())), precision=precision, preferred_element_type=F32
    )


def dot_nt(a, b, precision=None):
    return lax.dot_general(
        a, b, (((1,), (1,)), ((), ())), precision=precision, preferred_element_type=F32
    )


def dot_tn(a, b, precision=None):
    return lax.dot_general(
        a, b, (((0,), (0,)), ((), ())), precision=precision, preferred_element_type=F32
    )


HI = lax.Precision.HIGHEST


def mixer_kernel(
    ints,
    reals,
    queries,
    keyvalue,
    keys,
    values,
    mamba_x,
    mamba_z,
    both,
    step,
    states,
    mamba_out,
    payload,
    chosen,
    *,
    heads,
):
    slot = pl.program_id(0)
    drafts = queries.shape[0]
    size = keys.shape[2]
    cache = keys.shape[1]
    length = ints[slot]
    member = ints[8]
    accept = ints[4 + slot]
    scale = size ** (-0.5)
    query = jnp.concatenate([queries[:, h * size : (h + 1) * size] for h in range(heads)], axis=0)
    rows = heads * drafts
    scores = dot_nt(query, keys[0]) * scale
    position = lax.broadcasted_iota(jnp.int32, (rows, cache), 1) + member * cache
    scores = jnp.where(position < length, scores, NEG)
    draft_scores = dot_nt(query, keyvalue[:, :size]) * scale
    token = lax.broadcasted_iota(jnp.int32, (heads, drafts, drafts), 1).reshape(rows, drafts)
    other = lax.broadcasted_iota(jnp.int32, (rows, drafts), 1)
    limit = jnp.where(member == 0, token, -1)
    draft_scores = jnp.where(other <= limit, draft_scores, NEG)
    top = jnp.maximum(
        jnp.max(scores, axis=-1, keepdims=True), jnp.max(draft_scores, axis=-1, keepdims=True)
    )
    probs = jnp.where(position < length, jnp.exp(scores - top), 0.0)
    draft_probs = jnp.where(other <= limit, jnp.exp(draft_scores - top), 0.0)
    total = jnp.sum(probs, axis=-1, keepdims=True) + jnp.sum(draft_probs, axis=-1, keepdims=True)
    summed = dot_nn(probs.astype(BF), values[0]) + dot_nn(
        draft_probs.astype(BF), keyvalue[:, size:]
    )
    for h in range(heads):
        payload[:, h * size : (h + 1) * size] = summed[h * drafts : (h + 1) * drafts].astype(BF)
    top_a = top.astype(BF).astype(F32)
    top_b = (top - top_a).astype(BF).astype(F32)
    top_c = top - top_a - top_b
    total_a = total.astype(BF).astype(F32)
    total_b = total - total_a
    lane = lax.broadcasted_iota(jnp.int32, (drafts, AUX), 1)
    aux = jnp.zeros((drafts, AUX), F32)
    for k, piece in enumerate((top_a, top_b, top_c, total_a, total_b)):
        for h in range(heads):
            part = piece[h * drafts : (h + 1) * drafts]
            aux = jnp.where(lane == k * heads + h, part, aux)
    payload[:, heads * size : heads * size + AUX] = aux.astype(BF)
    step_in = step[...] + reals[0]
    size_t = jnp.maximum(step_in, 0.0) + jnp.log1p(jnp.exp(-jnp.abs(step_in)))
    row = lax.broadcasted_iota(jnp.int32, (drafts, drafts), 0)
    col = lax.broadcasted_iota(jnp.int32, (drafts, drafts), 1)
    size_row = jnp.sum(jnp.where(row == col, size_t, 0.0), axis=0, keepdims=True)
    log_decay = -reals[1] * jnp.sum(
        jnp.where(col <= row, size_row, 0.0), axis=1, keepdims=True
    )
    log_row = jnp.sum(jnp.where(row == col, log_decay, 0.0), axis=0, keepdims=True)
    between = jnp.exp(jnp.where(col <= row, log_decay - log_row, NEG))
    state_size = both.shape[1] // 2
    state_in = both[:, :state_size]
    state_read = both[:, state_size:]
    x = mamba_x[...]
    inputs = size_t * x
    start = states[0, 0]
    weights = dot_nt(state_read, state_in, HI) * between
    readout = dot_nn(weights, inputs, HI) + jnp.exp(log_decay) * dot_nt(state_read, start, HI)
    readout = readout + reals[2] * x
    rows_in = lax.broadcasted_iota(jnp.int32, (drafts, 1), 0)
    last = jnp.sum(jnp.where(rows_in == accept - 1, log_decay, 0.0), axis=0, keepdims=True)
    remain = jnp.exp(jnp.where(rows_in < accept, last - log_decay, NEG))
    chosen[0, 0] = (jnp.exp(last) * start + dot_tn(remain * inputs, state_in, HI)).astype(BF)
    z = mamba_z[...]
    gated = (readout * (z / (1.0 + jnp.exp(-z)))).astype(BF)
    payload[:, heads * size + AUX :] = dot_nn(gated, mamba_out[...]).astype(BF)


def mixer(ints, reals, queries, keyvalue, keys, values, x, z, both, step, states, mamba_out):
    slots, cache, size = keys.shape
    tokens = queries.shape[0]
    drafts = tokens // slots
    heads = queries.shape[1] // size
    width = heads * size + AUX + mamba_out.shape[1]
    rows = lambda a: pl.BlockSpec((drafts, a.shape[1]), lambda s: (s, 0))
    smem = pl.BlockSpec(memory_space=pltpu.SMEM)
    return pl.pallas_call(
        functools.partial(mixer_kernel, heads=heads),
        grid=(slots,),
        in_specs=[
            smem,
            smem,
            rows(queries),
            rows(keyvalue),
            pl.BlockSpec((1, cache, size), lambda s: (s, 0, 0)),
            pl.BlockSpec((1, cache, size), lambda s: (s, 0, 0)),
            rows(x),
            rows(z),
            rows(both),
            rows(step),
            pl.BlockSpec((1, 1) + states.shape[2:], lambda s: (s, 0, 0, 0)),
            pl.BlockSpec(mamba_out.shape, lambda s: (0, 0)),
        ],
        out_specs=[
            pl.BlockSpec((drafts, width), lambda s: (s, 0)),
            pl.BlockSpec((1, 1) + states.shape[2:], lambda s: (s, 0, 0, 0)),
        ],
        out_shape=[
            jax.ShapeDtypeStruct((tokens, width), BF),
            jax.ShapeDtypeStruct(states.shape, BF),
        ],
        compiler_params=pltpu.CompilerParams(vmem_limit_bytes=40 << 20),
        name="mixer",
    )(ints, reals, queries, keyvalue, keys, values, x, z, both, step, states, mamba_out)


def join_kernel(parts, embedded, out_weight, gain, mixed, second, *, heads, size):
    aux = parts[:, :, heads * size : heads * size + AUX].astype(F32)
    pieces = []
    for h in range(heads):
        get = lambda k: aux[:, :, k * heads + h : k * heads + h + 1]
        top = get(0) + get(1) + get(2)
        total = get(3) + get(4)
        factor = jnp.exp(top - jnp.max(top, axis=0, keepdims=True))
        whole = jnp.sum(factor * total, axis=0)
        value = parts[:, :, h * size : (h + 1) * size].astype(F32)
        summed = jnp.sum(factor * value, axis=0)
        pieces.append((summed / whole).astype(BF))
    attended = jnp.concatenate(pieces, axis=1)
    attn = dot_nt(attended, out_weight[...])
    mamba = jnp.sum(parts[:, :, heads * size + AUX :].astype(F32), axis=0)
    rows = (embedded[...].astype(F32) + attn + mamba).astype(BF)
    mixed[...] = rows
    wide = rows.astype(F32)
    factor = lax.rsqrt(jnp.mean(wide * wide, axis=-1, keepdims=True) + 1e-05)
    normed = (wide * factor * gain[...]).astype(BF)
    for j in range(second.shape[0]):
        second[j] = normed


def join(parts, embedded, out_weight, gain, heads, size):
    vm = pl.BlockSpec(memory_space=pltpu.VMEM)
    return pl.pallas_call(
        functools.partial(join_kernel, heads=heads, size=size),
        in_specs=[vm] * 4,
        out_specs=[vm] * 2,
        out_shape=[
            jax.ShapeDtypeStruct(embedded.shape, BF),
            jax.ShapeDtypeStruct((parts.shape[0],) + embedded.shape, BF),
        ],
        compiler_params=pltpu.CompilerParams(vmem_limit_bytes=40 << 20),
        name="join",
    )(parts, embedded, out_weight, gain)


def pick_kernel(sources, states, out):
    out[...] = states[...].astype(F32)


def pick_states(sources, states, count):
    block = (1,) + states.shape[1:]
    zeros = (0,) * (len(block) - 1)
    return pl.pallas_call(
        pick_kernel,
        grid_spec=pltpu.PrefetchScalarGridSpec(
            num_scalar_prefetch=1,
            grid=(count,),
            in_specs=[pl.BlockSpec(block, lambda i, src: (src[i],) + zeros)],
            out_specs=pl.BlockSpec(block, lambda i, src: (i,) + zeros),
        ),
        out_shape=jax.ShapeDtypeStruct((count,) + states.shape[1:], F32),
        name="pick",
    )(sources, states)


def local(
    draft_ids,
    lengths,
    current_slot,
    new_slot,
    accepted,
    embed_table,
    mixer_gain,
    query_weight,
    keyvalue_weight,
    key_cache,
    value_cache,
    attention_out,
    mamba_input,
    mamba_gate,
    state_proj,
    mamba_step,
    step_bias,
    decay_log,
    skip_gain,
    states,
    mamba_out,
    mlp_gain,
    gate_weight,
    up_weight,
    down_weight,
):
    members = lax.axis_size("tok")
    groups = lax.axis_size("req")
    group_index = lax.axis_index("req")
    member = lax.axis_index("tok")
    slots_dev, cache_dev, head_size = key_cache.shape
    draft_len = draft_ids.shape[1]
    vocab_dev, width = embed_table.shape
    query_heads = query_weight.shape[1] // head_size
    own = slots_dev * draft_len // members

    out_all = lax.all_gather(attention_out.T, "tok", axis=0, tiled=True)
    gate_all = lax.all_gather(gate_weight.T, "req", axis=0, tiled=True)
    up_all = lax.all_gather(up_weight.T, "req", axis=0, tiled=True)
    down_all = lax.all_gather(down_weight.T, "req", axis=0, tiled=True)

    slot_owner = inverse_of(current_slot)
    token_ids = jnp.take(draft_ids, slot_owner, axis=0).reshape(-1)
    vocab_start = (group_index * members + member) * vocab_dev
    wanted = token_ids - vocab_start
    inside = (wanted >= 0) & (wanted < vocab_dev)
    picked = jnp.take(embed_table, jnp.clip(wanted, 0, vocab_dev - 1), axis=0)
    picked = jnp.where(inside[:, None], picked, jnp.zeros_like(picked))
    arrived = lax.all_to_all(
        picked.reshape(groups * members, own, width), ("req", "tok"), 0, 0, tiled=True
    )
    embedded = jnp.sum(arrived.astype(F32), axis=0).astype(BF)
    normed = rms_rows(embedded, mixer_gain)
    gathered = lax.all_to_all(
        jnp.broadcast_to(normed[None], (members, own, width)), "tok", 0, 0, tiled=True
    ).reshape(members * own, width)

    queries = jnp.dot(gathered, query_weight, preferred_element_type=F32).astype(BF)
    keyvalue = jnp.dot(gathered, keyvalue_weight, preferred_element_type=F32).astype(BF)
    x = jnp.dot(gathered, mamba_input, preferred_element_type=F32)
    z = jnp.dot(gathered, mamba_gate, preferred_element_type=F32)
    both = jnp.dot(gathered, state_proj, preferred_element_type=F32)
    step = jnp.dot(gathered, mamba_step, preferred_element_type=F32)

    local_owner = lax.dynamic_slice_in_dim(slot_owner, group_index * slots_dev, slots_dev)
    ints = jnp.concatenate(
        [jnp.take(lengths, local_owner), jnp.take(accepted, local_owner), member[None]]
    )
    reals = jnp.concatenate([step_bias, jnp.exp(decay_log), skip_gain])
    payload, chosen = mixer(
        ints,
        reals,
        queries,
        keyvalue,
        key_cache,
        value_cache,
        x,
        z,
        both,
        step,
        states,
        mamba_out,
    )
    every_state = lax.all_gather(chosen, "req", axis=0, tiled=True)
    parts = lax.all_to_all(
        payload.reshape(members, own, payload.shape[1]), "tok", 0, 0, tiled=True
    )
    mixed, second = join(parts, embedded, out_all, mlp_gain[None], query_heads, head_size)
    everything = lax.all_to_all(second, "tok", 0, 0, tiled=True).reshape(members * own, width)
    gate_part = dot_nt(everything, gate_all)
    up_part = dot_nt(everything, up_all)
    hidden = (jax.nn.silu(gate_part) * up_part).astype(BF)
    mlp_part = dot_nn(hidden, down_all).astype(BF)
    mlp_rows = lax.all_to_all(mlp_part.reshape(members, own, width), "tok", 0, 0, tiled=True)
    hidden_out = (
        mixed.astype(F32) + jnp.sum(mlp_rows.astype(F32), axis=0)
    ).astype(BF)

    incoming = inverse_of(new_slot)
    local_targets = lax.dynamic_slice_in_dim(incoming, group_index * slots_dev, slots_dev)
    sources = jnp.take(current_slot, local_targets)
    new_states = pick_states(sources, every_state, slots_dev)
    return (hidden_out, new_states)


def solution(mesh):
    return jax.shard_map(
        local,
        mesh=mesh,
        in_specs=(
            P(),
            P(),
            P(),
            P(),
            P(),
            P(("req", "tok"), None),
            P(),
            P(),
            P(),
            P("req", "tok", None),
            P("req", "tok", None),
            P(None, "tok"),
            P(None, "tok"),
            P(None, "tok"),
            P(),
            P(None, "tok"),
            P("tok"),
            P("tok"),
            P("tok"),
            P("req", "tok", None, None),
            P("tok", None),
            P(),
            P(None, ("req", "tok")),
            P(None, ("req", "tok")),
            P(None, ("req", "tok")),
        ),
        out_specs=(P(("req", "tok"), None), P("req", "tok", None, None)),
        check_vma=False,
    )
```

time: 814 us -> 245 us (0.30)
  blocking collectives: 243 us -> 14.7 us
  waiting for transfers between devices: 273 us -> 111 us
  other arithmetic: 113 us -> 12.8 us
  local copies, waits for them, and re-layouts: 112 us -> 27.5 us
  starting transfers between devices: 4.63 us -> 27.6 us
  matrix products: 35.8 us -> 22.2 us
  Pallas kernels: 0 us -> 10.3 us
  loops' own time: 9.92 us -> 0 us
    unnamed x5, waiting for transfers between devices: 155 us -> 2.6 us
    unnamed x1 -> x0, blocking collectives: 111 us -> none
    pmax x1 -> x0, blocking collectives: 72.1 us -> none  [local(): cache_max = lax.pmax(local_max, 'tok')]
    all_to_all x1 -> x4, waiting for transfers between devices: 5.57 us -> 74.6 us  [the longest x1 55.6 us: local(): lax.all_to_all(picked.reshape(groups * members, own, width), ('req', 'tok...]
    psum x1 -> x0, waiting for transfers between devices: 42.4 us -> none  [local(): lax.psum((local_out * factor[..., None]).astype(jnp.bfloat16), 'tok')]
    reduce_sum x18 -> x2, other arithmetic: 44.4 us -> 4.35 us  [the longest x1 3.18 us: local(): embedded = jnp.sum(arrived.astype(F32), axis=0).astype(BF)]
    psum x1 -> x0, blocking collectives: 36.1 us -> none  [local(): lax.psum((local_total * factor).astype(jnp.bfloat16), 'tok')]
    all_gather x2 -> x5, waiting for transfers between devices: 70 us -> 34 us  [the longest x1 25 us: local(): down_all = lax.all_gather(down_weight.T, 'req', axis=0, tiled=True)]
  transfers between devices with their start and end apart: 5 -> 9, of which waited for: 5 -> 5; matrix products, arithmetic and copies ran while one was open for 4% -> 23% of each run, Pallas kernels for 0% -> 4%
where the time goes in v1:
time: 245 us; the launch traced here: 242 us
  waiting for transfers between devices  111 us (45%)
  starting transfers between devices  27.6 us (11%)
  local copies, waits for them, and re-layouts  27.5 us (11%)
  matrix products  22.2 us (9%)
  between operations  16.1 us (7%)
  blocking collectives  14.7 us (6%)
  other arithmetic  12.8 us (5%)
  Pallas kernels  10.3 us (4%)
    all_to_all x1, waiting for transfers between devices, local(): lax.all_to_all(picked.reshape(groups * members, own, width), ('req', 'tok...  55.6 us
    all_gather x1, waiting for transfers between devices, local(): down_all = lax.all_gather(down_weight.T, 'req', axis=0, tiled=True)  25 us
    all_to_all x1, blocking collectives, local(): lax.all_to_all(payload.reshape(members, own, payload.shape[1]), 'tok', 0,...  14.7 us
    all_to_all x1, starting transfers between devices, local(): lax.all_to_all(picked.reshape(groups * members, own, width), ('req', 'tok...  11.6 us
    gather x2, local copies, waits for them, and re-layouts, local(): picked = jnp.take(embed_table, jnp.clip(wanted, 0, vocab_dev - 1), axis=0)  10 us
    all_to_all x1, waiting for transfers between devices, local(): lax.all_to_all(jnp.broadcast_to(normed[None], (members, own, width)), 'to...  9.87 us
    all_to_all x1, waiting for transfers between devices, local(): lax.all_to_all(second, 'tok', 0, 0, tiled=True)  9.1 us
    all_gather x1, waiting for transfers between devices, local(): every_state = lax.all_gather(chosen, 'req', axis=0, tiled=True)  9.01 us
  transfers between devices with their start and end apart: 9, of which 5 were waited for; matrix products, arithmetic and copies ran while one was open for 23% of the time, Pallas kernels for 4%

profile of v1, /device:TPU:0, one launch (start us, length us, event | category | flops | bytes accessed | tf_op | source)
XLA Modules:
  0.0 242.4 jit_solution(16996173540791446489)
XLA Ops:
  7.2 0.7 all-gather.6.cloned.1.call-update
  8.0 0.7 all-gather.8.cloned.1.call-update
  8.7 0.7 all-gather.10.cloned.1.call-update
  9.4 0.5 all-gather.12.cloned.1.call-update
  10.0 0.8 select_reduce_fusion.1
  10.8 0.8 copy.35
  11.5 0.6 gather_fusion
  13.0 3.8 %gather_fusion.1 = bf16[512,3072]{1,0:T(8,128)(2,1)} fusion(bf16[512,3072]{1,0:T(8,128)(2,1)S(1)} %copy-done, s32[1024]{0:T(1024)S(1)} %pad_clamp_fusion.1), kind=kCustom, calls=%fused_computation.4 | custom fusion | bytes 6293504 | tf_op jit(solution)/shard_map/jit(_take)/gather | solution.py:280
  16.8 6.2 %gather.18 = bf16[128,4,3072]{2,1,0:T(4,128)(2,1)} reshape(bf16[512,3072]{1,0:T(8,128)(2,1)} %gather_fusion.1) | data formatting | bytes 6291456 | tf_op jit(solution)/shard_map/jit(_take)/gather | solution.py:280
  23.0 5.6 %select_select_fusion = bf16[128,4,3072]{2,1,0:T(4,128)(2,1)} fusion(bf16[128,4,3072]{2,1,0:T(4,128)(2,1)} %gather.18, pred[128,4]{1,0:T(8,128)(4,1)S(1)} %copy.38, pred[128,4]{1,0:T(8,128)(4,1)S(1)} %copy.37), kind=kLoop, calls=%fused_computation.6 | loop fusion | flops 3145728 | bytes 6292480 | tf_op jit(solution)/shard_map/jit(_where)/select_n | solution.py:281
  28.6 11.6 %all-to-all-start = ((bf16[128,4,3072]{2,1,0:T(4,128)(2,1)}), bf16[128,4,3072]{2,1,0:T(4,128)(2,1)}, u32[]{:S(2)}, u32[]{:S(2)}) async-start(bf16[128,4,3072]{2,1,0:T(4,128)(2,1)} %select_select_fusion), calls=%async_computation | async-start | bytes 6291456 | tf_op jit(solution)/shard_map/all_to_all | solution.py:282
  40.3 0.6 gather_fusion.2
  41.0 0.6 gather_fusion.3
  43.6 55.6 %all-to-all-done = bf16[128,4,3072]{2,1,0:T(4,128)(2,1)} async-done(((bf16[128,4,3072]{2,1,0:T(4,128)(2,1)}), bf16[128,4,3072]{2,1,0:T(4,128)(2,1)}, u32[]{:S(2)}, u32[]{:S(2)}) %all-to-all-start) | async-done | bytes 3145760 | tf_op jit(solution)/shard_map/all_to_all | solution.py:282
  99.2 3.2 %reduce_sum.52.embedded = bf16[4,3072]{1,0:T(4,128)(2,1)S(1)} reduce(bf16[128,4,3072]{2,1,0:T(4,128)(2,1)} %all-to-all-done, bf16[]{:T(256)} %constant.68.clone.1), dimensions={0}, to_apply=%region_1.3 | reduce | flops 1560576 | bytes 3170306 | tf_op jit(solution)/shard_map/reduce_sum | solution.py:285
  102.4 0.1 fusion.7
  102.6 0.8 broadcast_in_dim.94
  103.5 4.6 %all-to-all-start.1 = ((bf16[16,4,3072]{2,1,0:T(4,128)(2,1)}), bf16[16,4,3072]{2,1,0:T(4,128)(2,1)}, u32[]{:S(2)}, u32[]{:S(2)}) async-start(bf16[16,4,3072]{2,1,0:T(4,128)(2,1)} %broadcast_in_dim.94), calls=%async_computation.1 | async-start | bytes 786432 | tf_op jit(solution)/shard_map/all_to_all | solution.py:287
  108.3 9.9 %all-to-all-done.1 = bf16[16,4,3072]{2,1,0:T(4,128)(2,1)} async-done(((bf16[16,4,3072]{2,1,0:T(4,128)(2,1)}), bf16[16,4,3072]{2,1,0:T(4,128)(2,1)}, u32[]{:S(2)}, u32[]{:S(2)}) %all-to-all-start.1) | async-done | bytes 393248 | tf_op jit(solution)/shard_map/all_to_all | solution.py:287
  118.2 1.8 reshape.160
  120.0 1.4 convolution_bitcast_fusion.step
  121.4 1.5 fusion.12.mamba_x
  123.0 1.5 fusion.13.mamba_z
  124.5 1.9 convolution_convert_fusion.2.keyvalue
  126.5 0.7 fusion.14.both
  127.2 3.4 %convolution_convert_fusion.1.queries = bf16[64,768]{1,0:T(8,128)(2,1)S(1)} fusion(bf16[64,3072]{1,0:T(8,128)(2,1)S(1)} %copy-done.13, bf16[3072,768]{1,0:T(8,128)(2,1)} %param.34), kind=kOutput, calls=%fused_computation.9 | convolution fusion | flops 302039040 | bytes 5210112 | tf_op jit(solution)/shard_map/dot_general | solution.py:291
  130.7 5.0 %mixer.1 = (bf16[64,3968]{1,0:T(8,128)(2,1)S(1)}, bf16[4,1,128,256]{3,2,1,0:T(8,128)(2,1)}) custom-call(s32[9]{0:T(128)S(1)} %pad_add_fusion.ints, f32[3]{0:T(128)S(1)} %pad_maximum_fusion.reals, bf16[64,768]{1,0:T(8,128)(2,1)S(1)} %convolution_convert_fusion.1.queries, bf16[64,256]{1,0:T(8,128)(2,1)S(1)} %convolution_convert_fusion.2.keyvalue, ...), custom_call_target="tpu_custom_call" | custom-call | tf_op jit(solution)/shard_map/mixer/pallas_call | solution.py:144
  135.7 0.8 copy-done.7
  136.5 2.0 reshape.162
  138.5 14.7 %all_to_all.25.parts = bf16[16,4,3968]{2,1,0:T(4,128)(2,1)} all-to-all(bf16[16,4,3968]{2,1,0:T(4,128)(2,1)} %reshape.162), channel_id=1, replica_groups=mesh['req'=8,'tok'=16] {'tok'}, dimensions={0} | all-to-all | bytes 1015808 | tf_op jit(solution)/shard_map/all_to_all | solution.py:318
  153.1 2.4 %copy-done.1 = bf16[3072,768]{1,0:T(8,128)(2,1)S(1)} copy-done((bf16[3072,768]{1,0:T(8,128)(2,1)S(1)}, bf16[3072,768]{1,0:T(8,128)(2,1)}, u32[]{:S(2)}) %copy-start.1) | copy-done | bytes 4718616
  155.6 1.1 copy-done.2
  156.7 1.6 join.1
  158.3 0.7 copy-done.8
  159.1 4.4 %all-to-all-start.3 = ((bf16[16,4,3072]{2,1,0:T(4,128)(2,1)}), bf16[16,4,3072]{2,1,0:T(4,128)(2,1)}, u32[]{:S(2)}, u32[]{:S(2)}) async-start(bf16[16,4,3072]{2,1,0:T(4,128)(2,1)} %copy-done.8), calls=%async_computation.3 | async-start | bytes 786432 | tf_op jit(solution)/shard_map/all_to_all | solution.py:322
  163.6 9.1 %all-to-all-done.3 = bf16[16,4,3072]{2,1,0:T(4,128)(2,1)} async-done(((bf16[16,4,3072]{2,1,0:T(4,128)(2,1)}), bf16[16,4,3072]{2,1,0:T(4,128)(2,1)}, u32[]{:S(2)}, u32[]{:S(2)}) %all-to-all-start.3) | async-done | bytes 393248 | tf_op jit(solution)/shard_map/all_to_all | solution.py:322
  172.7 1.8 reshape.163
  174.5 4.0 %fusion.15 = f32[64,768]{1,0:T(8,128)S(1)} fusion(bf16[64,3072]{1,0:T(8,128)(2,1)} %reshape.163, bf16[768,3072]{1,0:T(8,128)(2,1)} %all-gather.8.cloned.1.call-done), kind=kOutput, calls=%fused_computation.56 | convolution fusion | flops 301989888 | bytes 5308416 | tf_op jit(solution)/shard_map/dot_general | solution.py:35
  178.6 25.0 %all-gather.12.cloned.1.call-done = bf16[768,3072]{1,0:T(8,128)(2,1)} async-done(((bf16[96,3072]{1,0:T(8,128)(2,1)}), bf16[768,3072]{1,0:T(8,128)(2,1)}) %all-gather.12.cloned.1.call-update) | async-done | bytes 4718608 | tf_op jit(solution)/shard_map/all_gather | solution.py:273
  203.6 7.7 %convolution_convert_fusion = bf16[64,3072]{1,0:T(8,128)(2,1)} fusion(bf16[768,3072]{1,0:T(8,128)(2,1)} %all-gather.12.cloned.1.call-done, bf16[64,3072]{1,0:T(8,128)(2,1)} %reshape.163, bf16[768,3072]{1,0:T(8,128)(2,1)} %all-gather.10.cloned.1.call-done, f32[64,768]{1,0:T(8,128)S(1)} %fusion.15), kind=kOutput, calls=%fused_computation.5 | convolution fusion | flops 604471296 | bytes 10420224 | tf_op jit(solution)/shard_map/dot_general | solution.py:29
  211.3 1.9 reshape.164
  213.2 6.8 %all-to-all-start.4 = ((bf16[16,4,3072]{2,1,0:T(4,128)(2,1)}), bf16[16,4,3072]{2,1,0:T(4,128)(2,1)}, u32[]{:S(2)}, u32[]{:S(2)}) async-start(bf16[16,4,3072]{2,1,0:T(4,128)(2,1)} %reshape.164), calls=%async_computation.4 | async-start | bytes 786432 | tf_op jit(solution)/shard_map/all_to_all | solution.py:327
  220.2 0.6 gather_fusion.4
  220.8 0.6 and_select_fusion.sources
  221.4 9.0 %all-gather.14.cloned.1.call-done.states = bf16[32,1,128,256]{3,2,1,0:T(8,128)(2,1)} async-done(((bf16[4,1,128,256]{3,2,1,0:T(8,128)(2,1)}), bf16[32,1,128,256]{3,2,1,0:T(8,128)(2,1)}) %all-gather.14.cloned.1.call-update) | async-done | bytes 2097168 | tf_op jit(solution)/shard_map/all_gather | solution.py:317
  230.4 3.7 %pick.1 = f32[4,1,128,256]{3,2,1,0:T(8,128)} custom-call(s32[4]{0:T(128)} %and_select_fusion.sources, bf16[32,1,128,256]{3,2,1,0:T(8,128)(2,1)} %all-gather.14.cloned.1.call-done.states), custom_call_target="tpu_custom_call" | custom-call | tf_op jit(solution)/shard_map/pick/pallas_call | solution.py:220
  234.1 1.2 convert_reduce_fusion
  235.3 0.6 add_convert_fusion
  (66 shorter events, 1.8 us)
Async XLA Ops:
  7.2 5.8 %copy-start = (bf16[512,3072]{1,0:T(8,128)(2,1)S(1)}, bf16[512,3072]{1,0:T(8,128)(2,1)}, u32[]{:S(2)}) copy-start(bf16[512,3072]{1,0:T(8,128)(2,1)} %param.32) | copy-start | bytes 9437188
  7.2 146.0 %all-gather.6.cloned.1.call-start = ((), (), s32[]{:S(2)}) async-start(), calls=%async_computation.5 | async-start | bytes 5013504 | tf_op jit(solution)/shard_map/all_gather | solution.py:270
  7.9 166.6 %all-gather.8.cloned.1.call-start = ((), (), s32[]{:S(2)}) async-start(), calls=%async_computation.6 | async-start | bytes 5308416 | tf_op jit(solution)/shard_map/all_gather | solution.py:271
  8.7 169.9 %all-gather.10.cloned.1.call-start = ((), (), s32[]{:S(2)}) async-start(), calls=%async_computation.7 | async-start | bytes 5308416 | tf_op jit(solution)/shard_map/all_gather | solution.py:272
  9.4 194.2 %all-gather.12.cloned.1.call-start = ((), (), s32[]{:S(2)}) async-start(), calls=%async_computation.8 | async-start | bytes 5308416 | tf_op jit(solution)/shard_map/all_gather | solution.py:273
  28.6 11.7 %copy-start.10 = (s32[32]{0:T(128)S(1)}, s32[32]{0:T(128)}, u32[]{:S(2)}) copy-start(s32[32]{0:T(128)} %param.28) | copy-start | bytes 388
  28.6 12.4 %copy-start.11 = (s32[32]{0:T(128)S(1)}, s32[32]{0:T(128)}, u32[]{:S(2)}) copy-start(s32[32]{0:T(128)} %param.31) | copy-start | bytes 388
  28.6 70.6 %all-to-all-start = ((bf16[128,4,3072]{2,1,0:T(4,128)(2,1)}), bf16[128,4,3072]{2,1,0:T(4,128)(2,1)}, u32[]{:S(2)}, u32[]{:S(2)}) async-start(bf16[128,4,3072]{2,1,0:T(4,128)(2,1)} %select_select_fusion), calls=%async_computation | async-start | bytes 6291456 | tf_op jit(solution)/shard_map/all_to_all | solution.py:282
  40.2 62.3 %copy-start.15 = (f32[3072]{0:T(1024)S(1)}, f32[3072]{0:T(1024)}, u32[]{:S(2)}) copy-start(f32[3072]{0:T(1024)} %param.33) | copy-start | bytes 36868
  40.3 79.7 %copy-start.16 = (bf16[3072,1]{0,1:T(2,128)(2,1)S(1)}, bf16[3072,1]{0,1:T(2,128)(2,1)}, u32[]{:S(2)}) copy-start(bf16[3072,1]{0,1:T(2,128)(2,1)} %param.42) | copy-start | bytes 18436
  103.5 14.7 %all-to-all-start.1 = ((bf16[16,4,3072]{2,1,0:T(4,128)(2,1)}), bf16[16,4,3072]{2,1,0:T(4,128)(2,1)}, u32[]{:S(2)}, u32[]{:S(2)}) async-start(bf16[16,4,3072]{2,1,0:T(4,128)(2,1)} %broadcast_in_dim.94), calls=%async_computation.1 | async-start | bytes 786432 | tf_op jit(solution)/shard_map/all_to_all | solution.py:287
  108.0 122.4 %all-gather.14.cloned.1.call-start = ((), (), s32[]{:S(2)}) async-start(), calls=%async_computation.9 | async-start | bytes 2359296 | tf_op jit(solution)/shard_map/all_gather | solution.py:317
  120.0 6.4 %copy-start.13 = (bf16[64,3072]{1,0:T(8,128)(2,1)S(1)}, bf16[64,3072]{1,0:T(8,128)(2,1)}, u32[]{:S(2)}) copy-start(bf16[64,3072]{1,0:T(8,128)(2,1)} %reshape.160) | copy-start | bytes 1179652
  120.0 6.4 %copy-start.14 = (bf16[3072,512]{1,0:T(8,128)(2,1)S(1)}, bf16[3072,512]{1,0:T(8,128)(2,1)}, u32[]{:S(2)}) copy-start(bf16[3072,512]{1,0:T(8,128)(2,1)} %param.41) | copy-start | bytes 9437188
  127.2 3.5 %copy-start.3 = (bf16[4,1024,128]{2,1,0:T(8,128)(2,1)S(1)}, bf16[4,1024,128]{2,1,0:T(8,128)(2,1)}, u32[]{:S(2)}) copy-start(bf16[4,1024,128]{2,1,0:T(8,128)(2,1)} %keys.1) | copy-start | bytes 3145732
  127.2 3.5 %copy-start.4 = (bf16[4,1024,128]{2,1,0:T(8,128)(2,1)S(1)}, bf16[4,1024,128]{2,1,0:T(8,128)(2,1)}, u32[]{:S(2)}) copy-start(bf16[4,1024,128]{2,1,0:T(8,128)(2,1)} %values.1) | copy-start | bytes 3145732
  127.2 3.5 %copy-start.5 = (bf16[128,3072]{1,0:T(8,128)(2,1)S(1)}, bf16[128,3072]{1,0:T(8,128)(2,1)}, u32[]{:S(2)}) copy-start(bf16[128,3072]{1,0:T(8,128)(2,1)} %mamba_out.1) | copy-start | bytes 2359300
  127.2 3.5 %copy-start.6 = (f32[4,1,128,256]{3,2,1,0:T(8,128)S(1)}, f32[4,1,128,256]{3,2,1,0:T(8,128)}, u32[]{:S(2)}) copy-start(f32[4,1,128,256]{3,2,1,0:T(8,128)} %states.1) | copy-start | bytes 1572868
  130.7 22.4 %copy-start.9 = (f32[3072]{0:T(1024)S(1)}, f32[3072]{0:T(1024)}, u32[]{:S(2)}) copy-start(f32[3072]{0:T(1024)} %param.48) | copy-start | bytes 36868
  135.7 0.8 copy-start.7
  153.1 10.3 %copy-start.17 = (s32[32]{0:T(128)S(1)}, s32[32]{0:T(128)}, u32[]{:S(2)}) copy-start(s32[32]{0:T(128)} %param.30) | copy-start | bytes 388
  153.1 2.4 %copy-start.1 = (bf16[3072,768]{1,0:T(8,128)(2,1)S(1)}, bf16[3072,768]{1,0:T(8,128)(2,1)}, u32[]{:S(2)}) copy-start(bf16[3072,768]{1,0:T(8,128)(2,1)} %all-gather.6.cloned.1.call-done.out_weight) | copy-start | bytes 14155780
  155.6 1.1 copy-start.2
  158.3 0.7 copy-start.8
  159.1 13.6 %all-to-all-start.3 = ((bf16[16,4,3072]{2,1,0:T(4,128)(2,1)}), bf16[16,4,3072]{2,1,0:T(4,128)(2,1)}, u32[]{:S(2)}, u32[]{:S(2)}) async-start(bf16[16,4,3072]{2,1,0:T(4,128)(2,1)} %copy-done.8), calls=%async_computation.3 | async-start | bytes 786432 | tf_op jit(solution)/shard_map/all_to_all | solution.py:322
  178.5 41.6 %copy-start.12 = (s32[32]{0:T(128)S(1)}, s32[32]{0:T(128)}, u32[]{:S(2)}) copy-start(s32[32]{0:T(128)} %param.29) | copy-start | bytes 388
  213.2 20.9 %all-to-all-start.4 = ((bf16[16,4,3072]{2,1,0:T(4,128)(2,1)}), bf16[16,4,3072]{2,1,0:T(4,128)(2,1)}, u32[]{:S(2)}, u32[]{:S(2)}) async-start(bf16[16,4,3072]{2,1,0:T(4,128)(2,1)} %reshape.164), calls=%async_computation.4 | async-start | bytes 786432 | tf_op jit(solution)/shard_map/all_to_all | solution.py:327
Sparse Core Ops, SparseCore 0:
  10.1 84.3 all-gather.5
  96.2 35.3 all-gather.7
  133.2 34.3 all-gather.9
  169.2 34.3 all-gather.11
  205.1 25.2 all-gather.13

commit v2 on v1

v2 whole, which is shorter than its diff:
```python
import functools

import jax
import jax.numpy as jnp
from jax import lax
from jax.experimental import pallas as pl
from jax.experimental.pallas import tpu as pltpu
from jax.sharding import PartitionSpec as P

BF = jnp.bfloat16
F32 = jnp.float32
NEG = -1e30
AUX = 128
ROOM = 12


def inverse_of(mapping):
    places = jnp.arange(mapping.shape[0], dtype=jnp.int32)
    matches = mapping[None, :] == places[:, None]
    return jnp.sum(jnp.where(matches, places[None, :], 0), axis=1)


def dot_nn(a, b, precision=None):
    return lax.dot_general(
        a, b, (((1,), (0,)), ((), ())), precision=precision, preferred_element_type=F32
    )


def dot_nt(a, b, precision=None):
    return lax.dot_general(
        a, b, (((1,), (1,)), ((), ())), precision=precision, preferred_element_type=F32
    )


def dot_tn(a, b, precision=None):
    return lax.dot_general(
        a, b, (((0,), (0,)), ((), ())), precision=precision, preferred_element_type=F32
    )


HI = lax.Precision.HIGHEST


def cost(flops, moved, special=0):
    return pl.CostEstimate(flops=flops, bytes_accessed=moved, transcendentals=special)


def whole(count):
    return [pl.BlockSpec(memory_space=pltpu.VMEM)] * count


def scalars(count):
    return [pl.BlockSpec(memory_space=pltpu.SMEM)] * count


PARAMS = pltpu.CompilerParams(vmem_limit_bytes=48 << 20)


def fetch_kernel(ints, slots_row, draft_ids, table, payload, places, most, *, members):
    groups, room, width = payload.shape
    requests, drafts = draft_ids.shape
    vocab = table.shape[0]
    count = requests * drafts // groups
    slots = requests // groups
    group, member, base = ints[0], ints[1], ints[2]
    me = group * members + member
    sub = lax.broadcasted_iota(jnp.int32, (count, count), 0)
    lane = lax.broadcasted_iota(jnp.int32, (count, count), 1)
    ids = draft_ids[...]
    ids_hi = (ids // 256).astype(F32).astype(BF)
    ids_lo = (ids % 256).astype(F32).astype(BF)
    row_slot = lax.broadcasted_iota(jnp.int32, (count, requests), 0) // drafts
    token = lax.broadcasted_iota(jnp.int32, (count, drafts), 0) % drafts
    token_lane = lax.broadcasted_iota(jnp.int32, (count, drafts), 1)
    slot_iota = lax.broadcasted_iota(jnp.int32, (room, count), 0) + base
    local_iota = lax.broadcasted_iota(jnp.int32, (room, vocab), 1)
    hots = []
    own_place = jnp.zeros((count, 1), jnp.int32)
    peak = jnp.zeros((1, count), jnp.int32)
    for g in range(groups):
        pick = jnp.where(slots_row[...] == row_slot + g * slots, 1.0, 0.0).astype(BF)
        mixed_ids = dot_nn(pick, ids_hi) * 256.0 + dot_nn(pick, ids_lo)
        id_c = jnp.sum(
            jnp.where(token == token_lane, mixed_ids, 0.0), axis=1, keepdims=True
        ).astype(jnp.int32)
        id_r = jnp.sum(jnp.where(sub == lane, id_c, 0), axis=0, keepdims=True)
        same = id_c == id_r
        first_c = jnp.min(jnp.where(same, lane, count), axis=1, keepdims=True)
        first_r = jnp.min(jnp.where(same, sub, count), axis=0, keepdims=True)
        sub_c = sub[:, :1]
        lane_r = lane[:1, :]
        owner_c = id_c // vocab
        owner_r = id_r // vocab
        column_c = owner_c % members
        column_r = owner_r % members
        alike = column_c == column_r
        before_r = jnp.where(alike & (first_c == sub_c) & (sub < first_r), 1, 0)
        rank_r = jnp.sum(before_r, axis=0, keepdims=True)
        peak = jnp.maximum(peak, rank_r + 1)
        before_c = jnp.where(alike & (first_r == lane_r) & (lane < first_c), 1, 0)
        rank_c = jnp.sum(before_c, axis=1, keepdims=True)
        inside = (rank_c >= base) & (rank_c < base + room)
        place = jnp.where(inside, column_c * room + rank_c - base, -1)
        own_place = jnp.where(group == g, place, own_place)
        mine = (first_r == lane_r) & (owner_r == me)
        asked = jnp.where(mine & (rank_r == slot_iota), id_r % vocab + 1, 0)
        row = jnp.sum(asked, axis=1, keepdims=True) - 1
        hots.append(jnp.where(local_iota == row, 1.0, 0.0))
    hot = jnp.concatenate(hots, axis=0).astype(BF)
    rows = dot_nn(hot, table[...])
    for g in range(groups):
        payload[g] = rows[g * room : (g + 1) * room].astype(BF)
    places[...] = jnp.broadcast_to(own_place, places.shape)
    most[...] = jnp.broadcast_to(jnp.max(peak, axis=1, keepdims=True), most.shape)


def fetch(ints, slots_row, draft_ids, table, groups, members, room):
    count = draft_ids.size // groups
    width = table.shape[1]
    return pl.pallas_call(
        functools.partial(fetch_kernel, members=members),
        in_specs=scalars(1) + whole(3),
        out_specs=whole(3),
        out_shape=[
            jax.ShapeDtypeStruct((groups, room, width), BF),
            jax.ShapeDtypeStruct((count, AUX), jnp.int32),
            jax.ShapeDtypeStruct((8, AUX), jnp.int32),
        ],
        compiler_params=PARAMS,
        cost_estimate=cost(2 * groups * room * table.size, 2 * table.size),
        name="fetch",
    )(ints, slots_row, draft_ids, table)


def rows_of(arrived, places):
    peers, room, width = arrived.shape
    count = places.shape[0]
    slot = lax.broadcasted_iota(jnp.int32, (count, peers * room), 1)
    hot = jnp.where(slot == places[:, :1], 1.0, 0.0).astype(BF)
    slots = jnp.concatenate([arrived[j] for j in range(peers)], axis=0)
    return dot_nn(hot, slots)


def place_kernel(arrived, places, before, out):
    out[...] = (before[...].astype(F32) + rows_of(arrived, places)).astype(BF)


def place(arrived, places, before):
    return pl.pallas_call(
        place_kernel,
        in_specs=whole(3),
        out_specs=whole(1)[0],
        out_shape=jax.ShapeDtypeStruct(before.shape, BF),
        compiler_params=PARAMS,
        name="place",
    )(arrived, places, before)


def attend_kernel(
    ints,
    arrived,
    places,
    extra,
    gain,
    query_weight,
    keyvalue_weight,
    keys,
    values,
    payload,
    embedded,
    normed,
):
    slots, cache, size = keys.shape
    tokens = extra.shape[0]
    drafts = tokens // slots
    heads = query_weight.shape[1] // size
    own = payload.shape[1]
    rows_in = (rows_of(arrived, places) + extra[...].astype(F32)).astype(BF)
    embedded[...] = rows_in
    wide = rows_in.astype(F32)
    factor = lax.rsqrt(jnp.mean(wide * wide, axis=-1, keepdims=True) + 1e-05)
    normed[...] = (wide * factor * gain[...]).astype(BF)
    queries = dot_nn(normed[...], query_weight[...]).astype(BF)
    keyvalue = dot_nn(normed[...], keyvalue_weight[...]).astype(BF)
    member = ints[8]
    scale = size ** (-0.5)
    rows = heads * drafts
    position = lax.broadcasted_iota(jnp.int32, (rows, cache), 1) + member * cache
    token = lax.broadcasted_iota(jnp.int32, (rows, drafts), 0) % drafts
    other = lax.broadcasted_iota(jnp.int32, (rows, drafts), 1)
    seen = other <= jnp.where(member == 0, token, -1)
    lane = lax.broadcasted_iota(jnp.int32, (drafts, AUX), 1)
    for slot in range(slots):
        span = slice(slot * drafts, (slot + 1) * drafts)
        length = ints[slot]
        query = jnp.concatenate(
            [queries[span, h * size : (h + 1) * size] for h in range(heads)], axis=0
        )
        scores = dot_nt(query, keys[slot]) * scale
        scores = jnp.where(position < length, scores, NEG)
        draft_scores = dot_nt(query, keyvalue[span, :size]) * scale
        draft_scores = jnp.where(seen, draft_scores, NEG)
        top = jnp.maximum(
            jnp.max(scores, axis=-1, keepdims=True),
            jnp.max(draft_scores, axis=-1, keepdims=True),
        )
        probs = jnp.where(position < length, jnp.exp(scores - top), 0.0)
        draft_probs = jnp.where(seen, jnp.exp(draft_scores - top), 0.0)
        total = jnp.sum(probs, axis=-1, keepdims=True) + jnp.sum(
            draft_probs, axis=-1, keepdims=True
        )
        summed = dot_nn(probs.astype(BF), values[slot]) + dot_nn(
            draft_probs.astype(BF), keyvalue[span, size:]
        )
        top_a = top.astype(BF).astype(F32)
        top_b = (top - top_a).astype(BF).astype(F32)
        top_c = top - top_a - top_b
        total_a = total.astype(BF).astype(F32)
        total_b = total - total_a
        aux = jnp.zeros((drafts, AUX), F32)
        for k, piece in enumerate((top_a, top_b, top_c, total_a, total_b)):
            for h in range(heads):
                part = piece[h * drafts : (h + 1) * drafts]
                aux = jnp.where(lane == k * heads + h, part, aux)
        flat = jnp.concatenate(
            [summed[h * drafts : (h + 1) * drafts] for h in range(heads)] + [aux], axis=1
        ).astype(BF)
        for q in range(drafts // own):
            payload[slot * (drafts // own) + q] = flat[q * own : (q + 1) * own]


def attend(ints, arrived, places, extra, gain, query_weight, keyvalue_weight, keys, values):
    tokens, width = extra.shape
    members = arrived.shape[0]
    wide = query_weight.shape[1] + AUX
    return pl.pallas_call(
        attend_kernel,
        in_specs=scalars(1) + whole(8),
        out_specs=whole(3),
        out_shape=[
            jax.ShapeDtypeStruct((members, tokens // members, wide), BF),
            jax.ShapeDtypeStruct((tokens, width), BF),
            jax.ShapeDtypeStruct((tokens, width), BF),
        ],
        compiler_params=PARAMS,
        cost_estimate=cost(
            2 * tokens * query_weight.size * 2, 2 * (query_weight.size + keys.size * 2), keys.size
        ),
        name="attend",
    )(ints, arrived, places, extra, gain, query_weight, keyvalue_weight, keys, values)


def mamba_kernel(
    ints,
    reals,
    normed,
    input_weight,
    gate_weight,
    state_proj,
    step_row,
    states,
    mamba_out,
    blocks,
    chosen,
):
    slots = states.shape[0]
    tokens = normed.shape[0]
    drafts = tokens // slots
    rows = normed[...]
    x_all = dot_nn(rows, input_weight[...])
    z_all = dot_nn(rows, gate_weight[...])
    both = dot_nn(rows, state_proj[...])
    step_in = (
        jnp.sum(rows.astype(F32) * step_row[...].astype(F32), axis=1, keepdims=True) + reals[0]
    )
    sizes = jnp.maximum(step_in, 0.0) + jnp.log1p(jnp.exp(-jnp.abs(step_in)))
    state_size = both.shape[1] // 2
    row = lax.broadcasted_iota(jnp.int32, (drafts, drafts), 0)
    col = lax.broadcasted_iota(jnp.int32, (drafts, drafts), 1)
    rows_in = lax.broadcasted_iota(jnp.int32, (drafts, 1), 0)
    gated = []
    for slot in range(slots):
        span = slice(slot * drafts, (slot + 1) * drafts)
        accept = ints[4 + slot]
        size_t = sizes[span]
        size_row = jnp.sum(jnp.where(row == col, size_t, 0.0), axis=0, keepdims=True)
        log_decay = -reals[1] * jnp.sum(
            jnp.where(col <= row, size_row, 0.0), axis=1, keepdims=True
        )
        log_row = jnp.sum(jnp.where(row == col, log_decay, 0.0), axis=0, keepdims=True)
        between = jnp.exp(jnp.where(col <= row, log_decay - log_row, NEG))
        state_in = both[span, :state_size]
        state_read = both[span, state_size:]
        x = x_all[span]
        z = z_all[span]
        inputs = size_t * x
        start = states[slot, 0]
        weights = dot_nt(state_read, state_in, HI) * between
        readout = dot_nn(weights, inputs, HI) + jnp.exp(log_decay) * dot_nt(
            state_read, start, HI
        )
        readout = readout + reals[2] * x
        last = jnp.sum(jnp.where(rows_in == accept - 1, log_decay, 0.0), axis=0, keepdims=True)
        remain = jnp.exp(jnp.where(rows_in < accept, last - log_decay, NEG))
        chosen[slot, 0] = (
            jnp.exp(last) * start + dot_tn(remain * inputs, state_in, HI)
        ).astype(BF)
        gated.append((readout * (z / (1.0 + jnp.exp(-z)))).astype(BF))
    part = dot_nn(jnp.concatenate(gated, axis=0), mamba_out[...])
    share = blocks.shape[2]
    for j in range(blocks.shape[0]):
        blocks[j] = part[:, j * share : (j + 1) * share].astype(BF)


def mamba(ints, reals, normed, input_weight, gate_weight, state_proj, step_row, states, mamba_out, members):
    tokens = normed.shape[0]
    share = mamba_out.shape[1] // members
    return pl.pallas_call(
        mamba_kernel,
        in_specs=scalars(2) + whole(7),
        out_specs=whole(2),
        out_shape=[
            jax.ShapeDtypeStruct((members, tokens, share), BF),
            jax.ShapeDtypeStruct(states.shape, BF),
        ],
        compiler_params=PARAMS,
        cost_estimate=cost(2 * tokens * state_proj.size * 2, 4 * state_proj.size),
        name="mamba",
    )(ints, reals, normed, input_weight, gate_weight, state_proj, step_row, states, mamba_out)


def join_kernel(parts, blocks, payload, *, heads, size):
    peers, tokens, share = blocks.shape
    own = parts.shape[1]
    aux = parts[:, :, heads * size : heads * size + AUX].astype(F32)
    payload[:, :tokens, :] = blocks[...]
    for h in range(heads):
        get = lambda k: aux[:, :, k * heads + h : k * heads + h + 1]
        top = get(0) + get(1) + get(2)
        total = get(3) + get(4)
        factor = jnp.exp(top - jnp.max(top, axis=0, keepdims=True))
        norm = jnp.sum(factor * total, axis=0)
        value = parts[:, :, h * size : (h + 1) * size].astype(F32)
        summed = jnp.sum(factor * value, axis=0)
        piece = (summed / norm).astype(BF)
        for j in range(peers):
            payload[j, tokens + h * own : tokens + (h + 1) * own, :size] = piece


def join(parts, blocks, heads, size):
    members, tokens, share = blocks.shape
    own = parts.shape[1]
    return pl.pallas_call(
        functools.partial(join_kernel, heads=heads, size=size),
        in_specs=whole(2),
        out_specs=whole(1)[0],
        out_shape=jax.ShapeDtypeStruct((members, tokens + heads * own, share), BF),
        compiler_params=PARAMS,
        name="join",
    )(parts, blocks)


def project_kernel(parts, out_weight, spread, *, heads, size):
    peers, tokens, share = spread.shape
    own = (parts.shape[1] - tokens) // heads
    acc = jnp.sum(parts[:, :tokens, :].astype(F32), axis=0)
    for h in range(heads):
        attended = jnp.concatenate(
            [parts[j, tokens + h * own : tokens + (h + 1) * own, :size] for j in range(peers)],
            axis=0,
        )
        acc = acc + dot_nt(attended, out_weight[:, h * size : (h + 1) * size])
    out = acc.astype(BF)
    for j in range(peers):
        spread[j] = out


def project(parts, out_weight, tokens, heads, size):
    members, _, share = parts.shape
    return pl.pallas_call(
        functools.partial(project_kernel, heads=heads, size=size),
        in_specs=whole(2),
        out_specs=whole(1)[0],
        out_shape=jax.ShapeDtypeStruct((members, tokens, share), BF),
        compiler_params=PARAMS,
        name="project",
    )(parts, out_weight)


def feed_kernel(spread, embedded, gain, weights, out, mixed, second, acc):
    step = pl.program_id(0)
    peers, own, width = out.shape
    units = weights.shape[1] // 3

    @pl.when(step == 0)
    def _():
        added = jnp.concatenate([spread[j] for j in range(peers)], axis=1)
        rows = (embedded[...].astype(F32) + added.astype(F32)).astype(BF)
        mixed[...] = rows
        wide = rows.astype(F32)
        factor = lax.rsqrt(jnp.mean(wide * wide, axis=-1, keepdims=True) + 1e-05)
        second[...] = (wide * factor * gain[...]).astype(BF)
        acc[...] = jnp.zeros_like(acc)

    rows = second[...]
    gate = dot_nt(rows, weights[0, :units, :])
    up = dot_nt(rows, weights[0, units : 2 * units, :])
    hidden = (gate / (1.0 + jnp.exp(-gate)) * up).astype(BF)
    acc[...] += dot_nn(hidden, weights[0, 2 * units :, :])

    @pl.when(step == pl.num_programs(0) - 1)
    def _():
        for j in range(peers):
            out[j] = acc[j * own : (j + 1) * own, :].astype(BF)


def feed(spread, embedded, gain, weights):
    members, tokens, share = spread.shape
    width = embedded.shape[1]
    groups, packed, _ = weights.shape
    fixed = lambda a: pl.BlockSpec(a.shape, lambda g: (0,) * a.ndim)
    return pl.pallas_call(
        feed_kernel,
        grid=(groups,),
        in_specs=[
            fixed(spread),
            fixed(embedded),
            fixed(gain),
            pl.BlockSpec((1, packed, width), lambda g: (g, 0, 0)),
        ],
        out_specs=[
            pl.BlockSpec((members, tokens // members, width), lambda g: (0, 0, 0)),
            pl.BlockSpec((tokens, width), lambda g: (0, 0)),
        ],
        out_shape=[
            jax.ShapeDtypeStruct((members, tokens // members, width), BF),
            jax.ShapeDtypeStruct((tokens, width), BF),
        ],
        scratch_shapes=[pltpu.VMEM((tokens, width), BF), pltpu.VMEM((tokens, width), F32)],
        compiler_params=PARAMS,
        cost_estimate=cost(2 * tokens * weights.size, 2 * weights.size),
        name="feed",
    )(spread, embedded, gain, weights)


def pick_kernel(sources, states, out):
    out[...] = states[...].astype(F32)


def pick_states(sources, states, count):
    block = (1,) + states.shape[1:]
    zeros = (0,) * (len(block) - 1)
    return pl.pallas_call(
        pick_kernel,
        grid_spec=pltpu.PrefetchScalarGridSpec(
            num_scalar_prefetch=1,
            grid=(count,),
            in_specs=[pl.BlockSpec(block, lambda i, src: (src[i],) + zeros)],
            out_specs=pl.BlockSpec(block, lambda i, src: (i,) + zeros),
        ),
        out_shape=jax.ShapeDtypeStruct((count,) + states.shape[1:], F32),
        name="pick",
    )(sources, states)


def local(
    draft_ids,
    lengths,
    current_slot,
    new_slot,
    accepted,
    embed_table,
    mixer_gain,
    query_weight,
    keyvalue_weight,
    key_cache,
    value_cache,
    attention_out,
    mamba_input,
    mamba_gate,
    state_proj,
    mamba_step,
    step_bias,
    decay_log,
    skip_gain,
    states,
    mamba_out,
    mlp_gain,
    gate_weight,
    up_weight,
    down_weight,
):
    members = lax.axis_size("tok")
    groups = lax.axis_size("req")
    group_index = lax.axis_index("req")
    member = lax.axis_index("tok")
    slots_dev, cache_dev, head_size = key_cache.shape
    draft_len = draft_ids.shape[1]
    width = embed_table.shape[1]
    query_heads = query_weight.shape[1] // head_size
    own = slots_dev * draft_len // members

    packed = jnp.concatenate([gate_weight.T, up_weight.T, down_weight.T], axis=0)
    weights = lax.all_gather(packed, "req", axis=0, tiled=False)

    def exchange(base):
        where = jnp.stack([group_index, member, base]).astype(jnp.int32)
        payload, places, most = fetch(
            where, current_slot[None], draft_ids, embed_table, groups, members, ROOM
        )
        slots = lax.all_to_all(payload, "req", 0, 0, tiled=True)
        held = jnp.sum(slots.astype(F32), axis=0).astype(BF)
        spread = jnp.broadcast_to(held[None], (members,) + held.shape)
        return lax.all_to_all(spread, "tok", 0, 0, tiled=True), places, most[0, 0]

    arrived, places, most = exchange(jnp.int32(0))

    def more(carry):
        return carry[0] < most

    def round_of(carry):
        base, rows = carry
        later, spots, _ = exchange(base)
        return base + ROOM, place(later, spots, rows)

    _, extra = lax.while_loop(
        more, round_of, (jnp.int32(ROOM), jnp.zeros((members * own, width), BF))
    )

    slot_owner = inverse_of(current_slot)
    local_owner = lax.dynamic_slice_in_dim(slot_owner, group_index * slots_dev, slots_dev)
    ints = jnp.concatenate(
        [jnp.take(lengths, local_owner), jnp.take(accepted, local_owner), member[None]]
    )
    reals = jnp.concatenate([step_bias, jnp.exp(decay_log), skip_gain])
    payload, embedded, normed = attend(
        ints,
        arrived,
        places,
        extra,
        mixer_gain[None],
        query_weight,
        keyvalue_weight,
        key_cache,
        value_cache,
    )
    parts = lax.all_to_all(payload, "tok", 0, 0, tiled=True)
    blocks, chosen = mamba(
        ints,
        reals,
        normed,
        mamba_input,
        mamba_gate,
        state_proj,
        mamba_step.T,
        states,
        mamba_out,
        members,
    )
    every_state = lax.all_gather(chosen, "req", axis=0, tiled=True)
    joined = lax.all_to_all(join(parts, blocks, query_heads, head_size), "tok", 0, 0, tiled=True)
    spread = project(joined, attention_out.T, members * own, query_heads, head_size)
    added = lax.all_to_all(spread, "tok", 0, 0, tiled=True)
    mlp_part, mixed = feed(added, embedded, mlp_gain[None], weights)
    mlp_rows = lax.all_to_all(mlp_part, "tok", 0, 0, tiled=True)
    own_rows = lax.dynamic_slice_in_dim(mixed, member * own, own)
    hidden_out = (own_rows.astype(F32) + jnp.sum(mlp_rows.astype(F32), axis=0)).astype(BF)

    incoming = inverse_of(new_slot)
    local_targets = lax.dynamic_slice_in_dim(incoming, group_index * slots_dev, slots_dev)
    sources = jnp.take(current_slot, local_targets)
    new_states = pick_states(sources, every_state, slots_dev)
    return (hidden_out, new_states)


def solution(mesh):
    return jax.shard_map(
        local,
        mesh=mesh,
        in_specs=(
            P(),
            P(),
            P(),
            P(),
            P(),
            P(("req", "tok"), None),
            P(),
            P(),
            P(),
            P("req", "tok", None),
            P("req", "tok", None),
            P(None, "tok"),
            P(None, "tok"),
            P(None, "tok"),
            P(),
            P(None, "tok"),
            P("tok"),
            P("tok"),
            P("tok"),
            P("req", "tok", None, None),
            P("tok", None),
            P(),
            P(None, ("req", "tok")),
            P(None, ("req", "tok")),
            P(None, ("req", "tok")),
        ),
        out_specs=(P(("req", "tok"), None), P("req", "tok", None, None)),
        check_vma=False,
    )
```

time: 245 us -> 161 us (0.66)
  waiting for transfers between devices: 111 us -> 50.6 us
  matrix products: 22.2 us -> 0 us
  Pallas kernels: 10.3 us -> 32 us
  local copies, waits for them, and re-layouts: 27.5 us -> 8.64 us
  blocking collectives: 14.7 us -> 26.1 us
  starting transfers between devices: 27.6 us -> 20 us
  other arithmetic: 12.8 us -> 6.06 us
    all_gather x4 -> x1, waiting for transfers between devices: 25 us -> 0.01 us  [local(): weights = lax.all_gather(packed, 'req', axis=0, tiled=False)]
    all_to_all x4, waiting for transfers between devices: 74.6 us -> 50.5 us  [the longest x1 18.7 us: exchange(): slots = lax.all_to_all(payload, 'req', 0, 0, tiled=True)]
    pallas_call x1 -> x5, Pallas kernels: 5.01 us -> 28 us  [the longest x1 11.4 us: feed(): pl.pallas_call(feed_kernel, grid=(groups,), in_specs=[fixed(spread), fixe...]
    dot_general x8 -> x0, matrix products: 22.2 us -> none  [the longest x1 7.72 us: dot_nn(): lax.dot_general(a, b, (((1,), (0,)), ((), ())), precision=precision, pref...]
    all_to_all x1 -> x2, blocking collectives: 14.7 us -> 26.1 us  [the longest x1 14.6 us: local(): lax.all_to_all(join(parts, blocks, query_heads, head_size), 'tok', 0, 0,...]
    gather x5 -> x0, local copies, waits for them, and re-layouts: 10.8 us -> none  [the longest x2 10 us: local(): picked = jnp.take(embed_table, jnp.clip(wanted, 0, vocab_dev - 1), axis=0)]
    all_gather x1, waiting for transfers between devices: 9.01 us -> 0.01 us  [local(): every_state = lax.all_gather(chosen, 'req', axis=0, tiled=True)]
    reshape x4 -> x0, local copies, waits for them, and re-layouts: 7.53 us -> none  [the longest x1 1.95 us: local(): payload.reshape(members, own, payload.shape[1])]
  transfers between devices with their start and end apart: 9 -> 6, of which waited for: 5 -> 4; matrix products, arithmetic and copies ran while one was open for 23% -> 4% of each run, Pallas kernels for 4% -> 20%
where the time goes in v2:
time: 161 us; the launch traced here: 160 us
  waiting for transfers between devices  50.6 us (31%)
  Pallas kernels  32 us (20%)
  blocking collectives  26.1 us (16%)
  starting transfers between devices  20 us (12%)
  between operations  16.3 us (10%)
  local copies, waits for them, and re-layouts  8.64 us (5%)
  other arithmetic  6.06 us (4%)
    all_to_all x1, waiting for transfers between devices, exchange(): slots = lax.all_to_all(payload, 'req', 0, 0, tiled=True)  18.7 us
    all_to_all x1, waiting for transfers between devices, exchange(): return (lax.all_to_all(spread, 'tok', 0, 0, tiled=True), places, most[0, 0])  17.5 us
    all_to_all x1, blocking collectives, local(): lax.all_to_all(join(parts, blocks, query_heads, head_size), 'tok', 0, 0,...  14.6 us
    all_to_all x1, blocking collectives, local(): parts = lax.all_to_all(payload, 'tok', 0, 0, tiled=True)  11.5 us
    pallas_call x1, Pallas kernels, feed(): pl.pallas_call(feed_kernel, grid=(groups,), in_specs=[fixed(spread), fixe...  11.4 us
    all_to_all x1, waiting for transfers between devices, local(): added = lax.all_to_all(spread, 'tok', 0, 0, tiled=True)  9.98 us
    all_to_all x1, starting transfers between devices, exchange(): return (lax.all_to_all(spread, 'tok', 0, 0, tiled=True), places, most[0, 0])  7.41 us
    pallas_call x1, Pallas kernels, attend(): pl.pallas_call(attend_kernel, in_specs=scalars(1) + whole(8), out_specs=w...  6.01 us
  transfers between devices with their start and end apart: 6, of which 4 were waited for; matrix products, arithmetic and copies ran while one was open for 4% of the time, Pallas kernels for 20%

profile of v2, /device:TPU:0, one launch (start us, length us, event | category | flops | bytes accessed | tf_op | source)
XLA Modules:
  0.0 160.3 jit_solution(9100195214835243612)
XLA Ops:
  7.2 0.0 copy-start
  7.2 0.0 all-gather.6.cloned.1.call-start
  7.2 0.0 copy-start.17
  7.2 2.8 %pad_maximum_fusion = bf16[288,3072]{1,0:T(8,128)(2,1)} fusion(bf16[96,3072]{1,0:T(8,128)(2,1)} %bitcast.31, bf16[96,3072]{1,0:T(8,128)(2,1)} %bitcast.32, bf16[96,3072]{1,0:T(8,128)(2,1)} %bitcast.33), kind=kLoop, calls=%fused_computation.4 | loop fusion | flops 5308416 | bytes 3538944 | tf_op jit(solution)/shard_map/concatenate | solution.py:503
  10.0 0.0 all-gather.6.cloned.1.call-update
  10.1 0.1 copy.33.draft_ids
  10.1 0.1 pad_add_fusion.2.ints
  10.2 4.4 %fetch.5 = (bf16[8,12,3072]{2,1,0:T(8,128)(2,1)}, s32[64,128]{1,0:T(8,128)S(1)}, s32[8,128]{1,0:T(8,128)S(1)}) custom-call(s32[3]{0:T(128)S(1)} %pad_add_fusion.2.ints, s32[1,32]{1,0:T(1,128)S(1)} %bitcast.28, s32[32,16]{1,0:T(8,128)S(1)} %copy.33.draft_ids, bf16[512,3072]{1,0:T(8,128)(2,1)} %table.1), custom_call_target="tpu_custom_call" | custom-call | flops 301989888 | bytes 3145728 | tf_op jit(solution)/shard_map/fetch/pallas_call | solution.py:120
  14.6 0.6 copy-done.10
  15.2 5.4 %all-to-all-start.2 = ((bf16[8,12,3072]{2,1,0:T(8,128)(2,1)}), bf16[8,12,3072]{2,1,0:T(8,128)(2,1)S(1)}, u32[]{:S(2)}, u32[]{:S(2)}) async-start(bf16[8,12,3072]{2,1,0:T(8,128)(2,1)} %get-tuple-element.115), calls=%async_computation.2 | async-start | bytes 1572864 | tf_op jit(solution)/shard_map/all_to_all | solution.py:511
  20.6 0.5 slice.3
  21.1 18.7 %all-to-all-done.2 = bf16[8,12,3072]{2,1,0:T(8,128)(2,1)S(1)} async-done(((bf16[8,12,3072]{2,1,0:T(8,128)(2,1)}), bf16[8,12,3072]{2,1,0:T(8,128)(2,1)S(1)}, u32[]{:S(2)}, u32[]{:S(2)}) %all-to-all-start.2) | async-done | bytes 589856 | tf_op jit(solution)/shard_map/all_to_all | solution.py:511
  39.8 0.1 reduce_sum.52
  40.0 0.6 while.12
  40.6 1.4 broadcast_in_dim.64
  42.0 7.4 %all-to-all-start.3 = ((bf16[16,12,3072]{2,1,0:T(8,128)(2,1)}), bf16[16,12,3072]{2,1,0:T(8,128)(2,1)S(1)}, u32[]{:S(2)}, u32[]{:S(2)}) async-start(bf16[16,12,3072]{2,1,0:T(8,128)(2,1)} %broadcast_in_dim.64), calls=%async_computation.3 | async-start | bytes 3145728 | tf_op jit(solution)/shard_map/all_to_all | solution.py:514
  49.4 0.0 all-gather.4.cloned.1.call-start
  49.5 0.1 select_reduce_fusion.1
  49.6 0.1 compare_select_fusion.1
  49.7 0.6 gather_fusion
  50.3 0.6 gather_fusion.1
  52.9 0.1 broadcast_select_fusion.1
  53.0 0.6 pad_add_fusion.1.ints
  53.6 0.6 pad_maximum_fusion.1.reals
  54.2 17.5 %all-to-all-done.3.arrived = bf16[16,12,3072]{2,1,0:T(8,128)(2,1)S(1)} async-done(((bf16[16,12,3072]{2,1,0:T(8,128)(2,1)}), bf16[16,12,3072]{2,1,0:T(8,128)(2,1)S(1)}, u32[]{:S(2)}, u32[]{:S(2)}) %all-to-all-start.3) | async-done | bytes 1179680 | tf_op jit(solution)/shard_map/all_to_all | solution.py:514
  71.8 1.4 copy-done.2
  73.1 1.2 copy-done.3
  74.4 0.8 copy-done.11
  75.2 0.7 copy-done.15
  75.8 6.0 %attend.1 = (bf16[16,4,896]{2,1,0:T(4,128)(2,1)S(1)}, bf16[64,3072]{1,0:T(8,128)(2,1)S(1)}, bf16[64,3072]{1,0:T(8,128)(2,1)S(1)}) custom-call(s32[9]{0:T(128)S(1)} %copy-done.15, bf16[16,12,3072]{2,1,0:T(8,128)(2,1)S(1)} %all-to-all-done.3.arrived, s32[64,128]{1,0:T(8,128)S(1)} %copy-done.11, bf16[64,3072]{1,0:T(8,128)(2,1)} %copy-done.20, ...), custom_call_target="tpu_custom_call" | custom-call | flops 603979776 | bytes 6815744 | tf_op jit(solution)/shard_map/attend/pallas_call | solution.py:236
  81.9 5.1 %mamba.1 = (bf16[16,64,192]{2,1,0:T(8,128)(2,1)S(1)}, bf16[4,1,128,256]{3,2,1,0:T(8,128)(2,1)}) custom-call(s32[9]{0:T(128)S(1)} %copy-done.15, f32[3]{0:T(128)S(1)} %copy-done.16, bf16[64,3072]{1,0:T(8,128)(2,1)S(1)} %get-tuple-element.120.normed, bf16[3072,128]{1,0:T(8,128)(2,1)S(1)} %copy-done.4, bf16[3072,128]{1,0:T(8,128)(2,1)S(1)} %copy-done.5, ...), custom_call_target="tpu_custom_call" | custom-call | flops 402653184 | bytes 6291456 | tf_op jit(solution)/shard_map/mamba/pallas_call | solution.py:318
  87.0 0.0 all-gather.4.cloned.1.call-update
  87.0 11.5 %all_to_all.45.parts = bf16[16,4,896]{2,1,0:T(4,128)(2,1)S(1)} all-to-all(bf16[16,4,896]{2,1,0:T(4,128)(2,1)} %copy-done.9), channel_id=1, replica_groups=mesh['req'=8,'tok'=16] {'tok'}, dimensions={0} | all-to-all | bytes 229376 | tf_op jit(solution)/shard_map/all_to_all | solution.py:547
  98.6 0.3 join.1
  98.9 14.6 %all_to_all.46.parts = bf16[16,88,192]{2,1,0:T(8,128)(2,1)S(1)} all-to-all(bf16[16,88,192]{2,1,0:T(8,128)(2,1)S(1)} %join.1), channel_id=1, replica_groups=mesh['req'=8,'tok'=16] {'tok'}, dimensions={0} | all-to-all | bytes 1081344 | tf_op jit(solution)/shard_map/all_to_all | solution.py:561
  113.6 1.1 project.1
  114.7 3.6 %all-to-all-start.6 = ((bf16[16,64,192]{2,1,0:T(8,128)(2,1)}), bf16[16,64,192]{2,1,0:T(8,128)(2,1)S(1)}, u32[]{:S(2)}, u32[]{:S(2)}) async-start(bf16[16,64,192]{2,1,0:T(8,128)(2,1)} %project.1), calls=%async_computation.6 | async-start | bytes 1048576 | tf_op jit(solution)/shard_map/all_to_all | solution.py:563
  118.3 0.1 select_reduce_fusion
  118.4 10.0 %all-to-all-done.6.spread = bf16[16,64,192]{2,1,0:T(8,128)(2,1)S(1)} async-done(((bf16[16,64,192]{2,1,0:T(8,128)(2,1)}), bf16[16,64,192]{2,1,0:T(8,128)(2,1)S(1)}, u32[]{:S(2)}, u32[]{:S(2)}) %all-to-all-start.6) | async-done | bytes 393248 | tf_op jit(solution)/shard_map/all_to_all | solution.py:563
  128.4 11.4 %feed.1 = (bf16[16,4,3072]{2,1,0:T(4,128)(2,1)}, bf16[64,3072]{1,0:T(8,128)(2,1)S(1)}) custom-call(bf16[16,64,192]{2,1,0:T(8,128)(2,1)S(1)} %all-to-all-done.6.spread, bf16[64,3072]{1,0:T(8,128)(2,1)S(1)} %get-tuple-element.122.embedded, f32[1,3072]{1,0:T(1,128)S(1)} %bitcast.27, bf16[8,288,3072]{2,1,0:T(8,128)(2,1)} %bitcast.30), custom_call_target="tpu_custom_call" | custom-call | flops 905969664 | bytes 14155776 | tf_op jit(solution)/shard_map/feed/pallas_call | solution.py:422
  139.7 3.6 %all-to-all-start.7 = ((bf16[16,4,3072]{2,1,0:T(4,128)(2,1)}), bf16[16,4,3072]{2,1,0:T(4,128)(2,1)S(1)}, u32[]{:S(2)}, u32[]{:S(2)}) async-start(bf16[16,4,3072]{2,1,0:T(4,128)(2,1)} %get-tuple-element.124), calls=%async_computation.7 | async-start | bytes 786432 | tf_op jit(solution)/shard_map/all_to_all | solution.py:565
  143.3 0.1 compare_select_fusion
  143.4 0.6 gather_fusion.2
  144.0 0.6 and_select_fusion.sources
  144.6 3.7 %pick.1 = f32[4,1,128,256]{3,2,1,0:T(8,128)} custom-call(s32[4]{0:T(128)} %and_select_fusion.sources, bf16[32,1,128,256]{3,2,1,0:T(8,128)(2,1)} %all-gather.4.cloned.1.call-done.states), custom_call_target="tpu_custom_call" | custom-call | tf_op jit(solution)/shard_map/pick/pallas_call | solution.py:453
  148.3 4.3 %all-to-all-done.7 = bf16[16,4,3072]{2,1,0:T(4,128)(2,1)S(1)} async-done(((bf16[16,4,3072]{2,1,0:T(4,128)(2,1)}), bf16[16,4,3072]{2,1,0:T(4,128)(2,1)S(1)}, u32[]{:S(2)}, u32[]{:S(2)}) %all-to-all-start.7) | async-done | bytes 393248 | tf_op jit(solution)/shard_map/all_to_all | solution.py:565
  152.7 0.2 convert_reduce_fusion
  152.8 0.6 add_convert_fusion
  (44 shorter events, 0.1 us)
Async XLA Ops:
  7.2 42.5 %copy-start = (s32[32]{0:T(128)S(1)}, s32[32]{0:T(128)}, u32[]{:S(2)}) copy-start(s32[32]{0:T(128)} %param.30) | copy-start | bytes 388
  7.2 121.2 %all-gather.6.cloned.1.call-start = ((), (), s32[]{:S(2)}) async-start(), calls=%async_computation.9 | async-start | bytes 15925248 | tf_op jit(solution)/shard_map/all_gather | solution.py:504
  7.2 2.8 %copy-start.21 = (s32[32,16]{0,1:T(8,128)S(1)}, s32[32,16]{0,1:T(8,128)}, u32[]{:S(2)}) copy-start(s32[32,16]{0,1:T(8,128)} %param.29) | copy-start | bytes 6148
  7.2 3.0 %copy-start.17 = (s32[32]{0:T(128)S(1)}, s32[32]{0:T(128)}, u32[]{:S(2)}) copy-start(s32[32]{0:T(128)} %param.31) | copy-start | bytes 388
  14.6 0.6 copy-start.10
  15.2 24.6 %all-to-all-start.2 = ((bf16[8,12,3072]{2,1,0:T(8,128)(2,1)}), bf16[8,12,3072]{2,1,0:T(8,128)(2,1)S(1)}, u32[]{:S(2)}, u32[]{:S(2)}) async-start(bf16[8,12,3072]{2,1,0:T(8,128)(2,1)} %get-tuple-element.115), calls=%async_computation.2 | async-start | bytes 1572864 | tf_op jit(solution)/shard_map/all_to_all | solution.py:511
  40.6 1.4 copy-start.20
  42.0 8.3 %copy-start.19 = (s32[32]{0:T(128)S(1)}, s32[32]{0:T(128)}, u32[]{:S(2)}) copy-start(s32[32]{0:T(128)} %param.33) | copy-start | bytes 388
  42.0 29.8 %copy-start.1 = (bf16[3072,256]{1,0:T(8,128)(2,1)S(1)}, bf16[3072,256]{1,0:T(8,128)(2,1)}, u32[]{:S(2)}) copy-start(bf16[3072,256]{1,0:T(8,128)(2,1)} %keyvalue_weight.1) | copy-start | bytes 4718596
  42.0 29.8 %copy-start.12 = (f32[3072]{0:T(1024)S(1)}, f32[3072]{0:T(1024)}, u32[]{:S(2)}) copy-start(f32[3072]{0:T(1024)} %param.35) | copy-start | bytes 36868
  42.0 29.8 %all-to-all-start.3 = ((bf16[16,12,3072]{2,1,0:T(8,128)(2,1)}), bf16[16,12,3072]{2,1,0:T(8,128)(2,1)S(1)}, u32[]{:S(2)}, u32[]{:S(2)}) async-start(bf16[16,12,3072]{2,1,0:T(8,128)(2,1)} %broadcast_in_dim.64), calls=%async_computation.3 | async-start | bytes 3145728 | tf_op jit(solution)/shard_map/all_to_all | solution.py:514
  49.4 95.2 %all-gather.4.cloned.1.call-start = ((), (), s32[]{:S(2)}) async-start(), calls=%async_computation.8 | async-start | bytes 2359296 | tf_op jit(solution)/shard_map/all_gather | solution.py:560
  71.7 1.4 copy-start.2
  73.1 1.2 copy-start.3
  74.4 0.8 copy-start.11
  75.2 0.7 copy-start.15
  75.8 6.1 %copy-start.4 = (bf16[3072,128]{1,0:T(8,128)(2,1)S(1)}, bf16[3072,128]{1,0:T(8,128)(2,1)}, u32[]{:S(2)}) copy-start(bf16[3072,128]{1,0:T(8,128)(2,1)} %input_weight.1) | copy-start | bytes 2359300
  75.8 6.1 %copy-start.5 = (bf16[3072,128]{1,0:T(8,128)(2,1)S(1)}, bf16[3072,128]{1,0:T(8,128)(2,1)}, u32[]{:S(2)}) copy-start(bf16[3072,128]{1,0:T(8,128)(2,1)} %gate_weight.1) | copy-start | bytes 2359300
  75.8 6.1 %copy-start.6 = (bf16[128,3072]{1,0:T(8,128)(2,1)S(1)}, bf16[128,3072]{1,0:T(8,128)(2,1)}, u32[]{:S(2)}) copy-start(bf16[128,3072]{1,0:T(8,128)(2,1)} %mamba_out.1) | copy-start | bytes 2359300
  75.8 6.1 %copy-start.7 = (f32[4,1,128,256]{3,2,1,0:T(8,128)S(1)}, f32[4,1,128,256]{3,2,1,0:T(8,128)}, u32[]{:S(2)}) copy-start(f32[4,1,128,256]{3,2,1,0:T(8,128)} %states.1) | copy-start | bytes 1572868
  75.8 6.1 %copy-start.13 = (bf16[3072,1]{0,1:T(2,128)(2,1)S(1)}, bf16[3072,1]{0,1:T(2,128)(2,1)}, u32[]{:S(2)}) copy-start(bf16[3072,1]{0,1:T(2,128)(2,1)} %param.44) | copy-start | bytes 18436
  75.8 6.1 %copy-start.16 = (f32[3]{0:T(128)S(1)}, f32[3]{0:T(128)}, u32[]{:S(2)}) copy-start(f32[3]{0:T(128)} %pad_maximum_fusion.1.reals) | copy-start | bytes 40
  81.9 5.2 %copy-start.9 = (bf16[16,4,896]{2,1,0:T(4,128)(2,1)}, bf16[16,4,896]{2,1,0:T(4,128)(2,1)S(1)}, u32[]{:S(2)}) copy-start(bf16[16,4,896]{2,1,0:T(4,128)(2,1)S(1)} %get-tuple-element.119) | copy-start | bytes 344068
  87.0 26.5 %copy-start.8 = (bf16[768,192]{0,1:T(8,128)(2,1)S(1)}, bf16[768,192]{0,1:T(8,128)(2,1)}, u32[]{:S(2)}) copy-start(bf16[768,192]{0,1:T(8,128)(2,1)} %param.40) | copy-start | bytes 884740
  98.9 19.4 %copy-start.22 = (s32[32]{0:T(128)S(1)}, s32[32]{0:T(128)}, u32[]{:S(2)}) copy-start(s32[32]{0:T(128)} %param.32) | copy-start | bytes 388
  98.9 29.5 %copy-start.14 = (f32[3072]{0:T(1024)S(1)}, f32[3072]{0:T(1024)}, u32[]{:S(2)}) copy-start(f32[3072]{0:T(1024)} %param.50) | copy-start | bytes 36868
  114.7 13.7 %all-to-all-start.6 = ((bf16[16,64,192]{2,1,0:T(8,128)(2,1)}), bf16[16,64,192]{2,1,0:T(8,128)(2,1)S(1)}, u32[]{:S(2)}, u32[]{:S(2)}) async-start(bf16[16,64,192]{2,1,0:T(8,128)(2,1)} %project.1), calls=%async_computation.6 | async-start | bytes 1048576 | tf_op jit(solution)/shard_map/all_to_all | solution.py:563
  128.4 15.0 %copy-start.18 = (s32[32]{0:T(128)S(1)}, s32[32]{0:T(128)}, u32[]{:S(2)}) copy-start(s32[32]{0:T(128)} %param.31) | copy-start | bytes 388
  139.7 12.9 %all-to-all-start.7 = ((bf16[16,4,3072]{2,1,0:T(4,128)(2,1)}), bf16[16,4,3072]{2,1,0:T(4,128)(2,1)S(1)}, u32[]{:S(2)}, u32[]{:S(2)}) async-start(bf16[16,4,3072]{2,1,0:T(4,128)(2,1)} %get-tuple-element.124), calls=%async_computation.7 | async-start | bytes 786432 | tf_op jit(solution)/shard_map/all_to_all | solution.py:565
Sparse Core Ops, SparseCore 0:
  10.2 82.2 all-gather.5
  94.2 24.8 all-gather.3

commit v3 on v2

--- a/solution.py
+++ b/solution.py
@@ -11,7 +11,7 @@
 F32 = jnp.float32
 NEG = -1e30
 AUX = 128
-ROOM = 12
+ROOM = 16
 
 
 def inverse_of(mapping):
@@ -49,11 +49,15 @@
     return [pl.BlockSpec(memory_space=pltpu.VMEM)] * count
 
 
+def streamed(count):
+    return [pl.BlockSpec(memory_space=pltpu.HBM)] * count
+
+
 def scalars(count):
     return [pl.BlockSpec(memory_space=pltpu.SMEM)] * count
 
 
-PARAMS = pltpu.CompilerParams(vmem_limit_bytes=48 << 20)
+PARAMS = pltpu.CompilerParams(vmem_limit_bytes=16 << 20)
 
 
 def fetch_kernel(ints, slots_row, draft_ids, table, payload, places, most, *, members):
@@ -169,7 +173,21 @@
     payload,
     embedded,
     normed,
+    query_in,
+    keyvalue_in,
+    keys_in,
+    values_in,
+    sems,
 ):
+    moves = []
+    third = query_weight.shape[0] // 3
+    for k in range(3):
+        span = pl.ds(k * third, third)
+        moves.append((query_weight.at[span, :], query_in.at[span, :]))
+    moves += [(keyvalue_weight, keyvalue_in), (keys, keys_in), (values, values_in)]
+    copies = [pltpu.make_async_copy(a, b, sems.at[n]) for n, (a, b) in enumerate(moves)]
+    for copy in copies:
+        copy.start()
     slots, cache, size = keys.shape
     tokens = extra.shape[0]
     drafts = tokens // slots
@@ -179,9 +197,19 @@
     embedded[...] = rows_in
     wide = rows_in.astype(F32)
     factor = lax.rsqrt(jnp.mean(wide * wide, axis=-1, keepdims=True) + 1e-05)
-    normed[...] = (wide * factor * gain[...]).astype(BF)
-    queries = dot_nn(normed[...], query_weight[...]).astype(BF)
-    keyvalue = dot_nn(normed[...], keyvalue_weight[...]).astype(BF)
+    rows_norm = (wide * factor * gain[...]).astype(BF)
+    normed[...] = rows_norm
+    queries = None
+    for k in range(3):
+        copies[k].wait()
+        span = slice(k * third, (k + 1) * third)
+        part = dot_nn(rows_norm[:, span], query_in[span, :])
+        queries = part if queries is None else queries + part
+    queries = queries.astype(BF)
+    copies[3].wait()
+    keyvalue = dot_nn(rows_norm, keyvalue_in[...]).astype(BF)
+    copies[4].wait()
+    copies[5].wait()
     member = ints[8]
     scale = size ** (-0.5)
     rows = heads * drafts
@@ -196,7 +224,7 @@
         query = jnp.concatenate(
             [queries[span, h * size : (h + 1) * size] for h in range(heads)], axis=0
         )
-        scores = dot_nt(query, keys[slot]) * scale
+        scores = dot_nt(query, keys_in[slot]) * scale
         scores = jnp.where(position < length, scores, NEG)
         draft_scores = dot_nt(query, keyvalue[span, :size]) * scale
         draft_scores = jnp.where(seen, draft_scores, NEG)
@@ -209,7 +237,7 @@
         total = jnp.sum(probs, axis=-1, keepdims=True) + jnp.sum(
             draft_probs, axis=-1, keepdims=True
         )
-        summed = dot_nn(probs.astype(BF), values[slot]) + dot_nn(
+        summed = dot_nn(probs.astype(BF), values_in[slot]) + dot_nn(
             draft_probs.astype(BF), keyvalue[span, size:]
         )
         top_a = top.astype(BF).astype(F32)
@@ -235,19 +263,35 @@
     wide = query_weight.shape[1] + AUX
     return pl.pallas_call(
         attend_kernel,
-        in_specs=scalars(1) + whole(8),
+        in_specs=scalars(1) + whole(4) + streamed(4),
         out_specs=whole(3),
         out_shape=[
             jax.ShapeDtypeStruct((members, tokens // members, wide), BF),
             jax.ShapeDtypeStruct((tokens, width), BF),
             jax.ShapeDtypeStruct((tokens, width), BF),
         ],
-        compiler_params=PARAMS,
+        scratch_shapes=[
+            pltpu.VMEM(a.shape, a.dtype) for a in (query_weight, keyvalue_weight, keys, values)
+        ]
+        + [pltpu.SemaphoreType.DMA((6,))],
+        compiler_params=pltpu.CompilerParams(vmem_limit_bytes=28 << 20),
         cost_estimate=cost(
             2 * tokens * query_weight.size * 2, 2 * (query_weight.size + keys.size * 2), keys.size
         ),
         name="attend",
     )(ints, arrived, places, extra, gain, query_weight, keyvalue_weight, keys, values)
+
+
+def fold(block):
+    half = block.shape[0] // 2
+    rest = jnp.concatenate([block[:half, AUX:], block[half:, AUX:]], axis=1)
+    return jnp.concatenate([block[:, :AUX], rest], axis=0)
+
+
+def unfold(block, tokens):
+    half = AUX // 2
+    rest = jnp.concatenate([block[tokens:, :half], block[tokens:, half:]], axis=0)
+    return jnp.concatenate([block[:tokens], rest], axis=1)
 
 
 def mamba_kernel(
@@ -307,9 +351,9 @@
         ).astype(BF)
         gated.append((readout * (z / (1.0 + jnp.exp(-z)))).astype(BF))
     part = dot_nn(jnp.concatenate(gated, axis=0), mamba_out[...])
-    share = blocks.shape[2]
+    share = part.shape[1] // blocks.shape[0]
     for j in range(blocks.shape[0]):
-        blocks[j] = part[:, j * share : (j + 1) * share].astype(BF)
+        blocks[j] = fold(part[:, j * share : (j + 1) * share]).astype(BF)
 
 
 def mamba(ints, reals, normed, input_weight, gate_weight, state_proj, step_row, states, mamba_out, members):
@@ -320,17 +364,17 @@
         in_specs=scalars(2) + whole(7),
         out_specs=whole(2),
         out_shape=[
-            jax.ShapeDtypeStruct((members, tokens, share), BF),
+            jax.ShapeDtypeStruct((members, tokens * share // AUX, AUX), BF),
             jax.ShapeDtypeStruct(states.shape, BF),
         ],
         compiler_params=PARAMS,
-        cost_estimate=cost(2 * tokens * state_proj.size * 2, 4 * state_proj.size),
+        cost_estimate=cost(2 * tokens * state_proj.size * 2, 4 * state_proj.size, tokens * 4096),
         name="mamba",
     )(ints, reals, normed, input_weight, gate_weight, state_proj, step_row, states, mamba_out)
 
 
 def join_kernel(parts, blocks, payload, *, heads, size):
-    peers, tokens, share = blocks.shape
+    peers, tokens, _ = blocks.shape
     own = parts.shape[1]
     aux = parts[:, :, heads * size : heads * size + AUX].astype(F32)
     payload[:, :tokens, :] = blocks[...]
@@ -361,106 +405,124 @@
 
 
 def project_kernel(parts, out_weight, spread, *, heads, size):
-    peers, tokens, share = spread.shape
-    own = (parts.shape[1] - tokens) // heads
-    acc = jnp.sum(parts[:, :tokens, :].astype(F32), axis=0)
+    peers, packed, _ = spread.shape
+    own = (parts.shape[1] - packed) // heads
+    tokens = own * peers
+    acc = unfold(jnp.sum(parts[:, :packed, :].astype(F32), axis=0), tokens)
     for h in range(heads):
         attended = jnp.concatenate(
-            [parts[j, tokens + h * own : tokens + (h + 1) * own, :size] for j in range(peers)],
+            [parts[j, packed + h * own : packed + (h + 1) * own, :size] for j in range(peers)],
             axis=0,
         )
         acc = acc + dot_nt(attended, out_weight[:, h * size : (h + 1) * size])
-    out = acc.astype(BF)
+    out = fold(acc).astype(BF)
     for j in range(peers):
         spread[j] = out
 
 
-def project(parts, out_weight, tokens, heads, size):
-    members, _, share = parts.shape
+def project(parts, out_weight, packed, heads, size):
+    members = parts.shape[0]
     return pl.pallas_call(
         functools.partial(project_kernel, heads=heads, size=size),
         in_specs=whole(2),
         out_specs=whole(1)[0],
-        out_shape=jax.ShapeDtypeStruct((members, tokens, share), BF),
+        out_shape=jax.ShapeDtypeStruct((members, packed, AUX), BF),
         compiler_params=PARAMS,
         name="project",
     )(parts, out_weight)
 
 
-def feed_kernel(spread, embedded, gain, weights, out, mixed, second, acc):
-    step = pl.program_id(0)
+def feed_kernel(spread, embedded, gain, *refs, count):
+    weights = refs[:count]
+    out, mixed, gates, ups, downs, sems = refs[count:]
     peers, own, width = out.shape
-    units = weights.shape[1] // 3
-
-    @pl.when(step == 0)
-    def _():
-        added = jnp.concatenate([spread[j] for j in range(peers)], axis=1)
-        rows = (embedded[...].astype(F32) + added.astype(F32)).astype(BF)
-        mixed[...] = rows
-        wide = rows.astype(F32)
-        factor = lax.rsqrt(jnp.mean(wide * wide, axis=-1, keepdims=True) + 1e-05)
-        second[...] = (wide * factor * gain[...]).astype(BF)
-        acc[...] = jnp.zeros_like(acc)
-
-    rows = second[...]
-    gate = dot_nt(rows, weights[0, :units, :])
-    up = dot_nt(rows, weights[0, units : 2 * units, :])
-    hidden = (gate / (1.0 + jnp.exp(-gate)) * up).astype(BF)
-    acc[...] += dot_nn(hidden, weights[0, 2 * units :, :])
-
-    @pl.when(step == pl.num_programs(0) - 1)
-    def _():
-        for j in range(peers):
-            out[j] = acc[j * own : (j + 1) * own, :].astype(BF)
+    tokens = embedded.shape[0]
+    total = gates.shape[0]
+    pieces = []
+    begin = 0
+    units = min(w.shape[0] for w in weights) // 3
+    for w in weights:
+        for first in range(0, w.shape[0], 3 * units):
+            pieces.append((w, first, begin))
+            begin += units
+    copies = []
+    for n, (w, first, at) in enumerate(pieces):
+        trio = []
+        for k, to in enumerate((gates, ups, downs)):
+            copy = pltpu.make_async_copy(
+                w.at[pl.ds(first + k * units, units), :], to.at[pl.ds(at, units), :], sems.at[n, k]
+            )
+            copy.start()
+            trio.append(copy)
+        copies.append((at + units, trio))
+    added = jnp.concatenate([unfold(spread[j].astype(F32), tokens) for j in range(peers)], axis=1)
+    rows = (embedded[...].astype(F32) + added).astype(BF)
+    mixed[...] = rows
+    wide = rows.astype(F32)
+    factor = lax.rsqrt(jnp.mean(wide * wide, axis=-1, keepdims=True) + 1e-05)
+    second = (wide * factor * gain[...]).astype(BF)
+    chunk = 256
+    waited = 0
+    ready = 0
+    acc = None
+    for c in range(total // chunk):
+        while ready < (c + 1) * chunk:
+            ready, trio = copies[waited]
+            for copy in trio:
+                copy.wait()
+            waited += 1
+        span = slice(c * chunk, (c + 1) * chunk)
+        gate = dot_nt(second, gates[span, :])
+        up = dot_nt(second, ups[span, :])
+        hidden = (gate / (1.0 + jnp.exp(-gate)) * up).astype(BF)
+        part = dot_nn(hidden, downs[span, :])
+        acc = part if acc is None else acc + part
+    for j in range(peers):
+        out[j] = acc[j * own : (j + 1) * own, :].astype(BF)
 
 
 def feed(spread, embedded, gain, weights):
-    members, tokens, share = spread.shape
-    width = embedded.shape[1]
-    groups, packed, _ = weights.shape
-    fixed = lambda a: pl.BlockSpec(a.shape, lambda g: (0,) * a.ndim)
+    members = spread.shape[0]
+    tokens, width = embedded.shape
+    units = sum(w.shape[0] for w in weights) // 3
+    count = 3 * units // min(w.shape[0] for w in weights)
     return pl.pallas_call(
-        feed_kernel,
-        grid=(groups,),
-        in_specs=[
-            fixed(spread),
-            fixed(embedded),
-            fixed(gain),
-            pl.BlockSpec((1, packed, width), lambda g: (g, 0, 0)),
-        ],
-        out_specs=[
-            pl.BlockSpec((members, tokens // members, width), lambda g: (0, 0, 0)),
-            pl.BlockSpec((tokens, width), lambda g: (0, 0)),
-        ],
+        functools.partial(feed_kernel, count=len(weights)),
+        in_specs=whole(3) + streamed(len(weights)),
+        out_specs=whole(2),
         out_shape=[
             jax.ShapeDtypeStruct((members, tokens // members, width), BF),
             jax.ShapeDtypeStruct((tokens, width), BF),
         ],
-        scratch_shapes=[pltpu.VMEM((tokens, width), BF), pltpu.VMEM((tokens, width), F32)],
-        compiler_params=PARAMS,
-        cost_estimate=cost(2 * tokens * weights.size, 2 * weights.size),
+        scratch_shapes=[pltpu.VMEM((units, width), BF)] * 3
+        + [pltpu.SemaphoreType.DMA((count, 3))],
+        compiler_params=pltpu.CompilerParams(vmem_limit_bytes=36 << 20),
+        cost_estimate=cost(6 * tokens * units * width, 6 * units * width),
         name="feed",
-    )(spread, embedded, gain, weights)
-
-
-def pick_kernel(sources, states, out):
-    out[...] = states[...].astype(F32)
-
-
-def pick_states(sources, states, count):
-    block = (1,) + states.shape[1:]
-    zeros = (0,) * (len(block) - 1)
+    )(spread, embedded, gain, *weights)
+
+
+def pick_kernel(turns, rows, *refs):
+    held = refs[:-1]
+    out = refs[-1]
+    for i in range(out.shape[0]):
+        for n, ref in enumerate(held):
+
+            @pl.when(turns[i] == n)
+            def _():
+                out[i] = ref[rows[i]].astype(F32)
+
+
+def pick_states(turns, rows, held, count):
+    shape = (count,) + held[0].shape[1:]
     return pl.pallas_call(
         pick_kernel,
-        grid_spec=pltpu.PrefetchScalarGridSpec(
-            num_scalar_prefetch=1,
-            grid=(count,),
-            in_specs=[pl.BlockSpec(block, lambda i, src: (src[i],) + zeros)],
-            out_specs=pl.BlockSpec(block, lambda i, src: (i,) + zeros),
-        ),
-        out_shape=jax.ShapeDtypeStruct((count,) + states.shape[1:], F32),
+        in_specs=scalars(2) + whole(len(held)),
+        out_specs=whole(1)[0],
+        out_shape=jax.ShapeDtypeStruct(shape, F32),
+        compiler_params=PARAMS,
         name="pick",
-    )(sources, states)
+    )(turns, rows, *held)
 
 
 def local(
@@ -500,8 +562,16 @@
     query_heads = query_weight.shape[1] // head_size
     own = slots_dev * draft_len // members
 
-    packed = jnp.concatenate([gate_weight.T, up_weight.T, down_weight.T], axis=0)
-    weights = lax.all_gather(packed, "req", axis=0, tiled=False)
+    cores = 2
+    chips = groups // cores
+
+    def turn(value, by):
+        return lax.ppermute(
+            value, "req", [(g, (g + by * cores) % groups) for g in range(groups)]
+        )
+
+    def across(value):
+        return lax.ppermute(value, "req", [(g, g ^ 1) for g in range(groups)])
 
     def exchange(base):
         where = jnp.stack([group_index, member, base]).astype(jnp.int32)
@@ -509,19 +579,33 @@
             where, current_slot[None], draft_ids, embed_table, groups, members, ROOM
         )
         slots = lax.all_to_all(payload, "req", 0, 0, tiled=True)
+        return payload, slots, places, most[0, 0]
+
+    def spread_slots(slots):
         held = jnp.sum(slots.astype(F32), axis=0).astype(BF)
         spread = jnp.broadcast_to(held[None], (members,) + held.shape)
-        return lax.all_to_all(spread, "tok", 0, 0, tiled=True), places, most[0, 0]
-
-    arrived, places, most = exchange(jnp.int32(0))
+        return lax.all_to_all(spread, "tok", 0, 0, tiled=True)
+
+    sent, slots, places, most = exchange(jnp.int32(0))
+
+    half = gate_weight.shape[1] // 2
+    *trio, _ = lax.optimization_barrier((gate_weight.T, up_weight.T, down_weight.T, sent))
+    low = jnp.concatenate([w[:half] for w in trio], axis=0)
+    high = jnp.concatenate([w[half:] for w in trio], axis=0)
+    own_weights = jnp.concatenate([low, high], axis=0)
+    own_weights, slots = lax.optimization_barrier((own_weights, slots))
+    arrived = spread_slots(slots)
+    from_below = turn(own_weights, 1)
+    from_above = turn(own_weights, -1)
+    weights = [own_weights, from_below, from_above]
 
     def more(carry):
         return carry[0] < most
 
     def round_of(carry):
         base, rows = carry
-        later, spots, _ = exchange(base)
-        return base + ROOM, place(later, spots, rows)
+        _, later, spots, _ = exchange(base)
+        return base + ROOM, place(spread_slots(later), spots, rows)
 
     _, extra = lax.while_loop(
         more, round_of, (jnp.int32(ROOM), jnp.zeros((members * own, width), BF))
@@ -557,9 +641,15 @@
         mamba_out,
         members,
     )
-    every_state = lax.all_gather(chosen, "req", axis=0, tiled=True)
+    from_below, from_above, parts, chosen = lax.optimization_barrier(
+        (from_below, from_above, parts, chosen)
+    )
+    far = [turn(from_below[: 3 * half], 1), turn(from_above[3 * half :], -1)]
+    weights += [across(w) for w in weights]
     joined = lax.all_to_all(join(parts, blocks, query_heads, head_size), "tok", 0, 0, tiled=True)
-    spread = project(joined, attention_out.T, members * own, query_heads, head_size)
+    *far, joined = lax.optimization_barrier((*far, joined))
+    weights += far + [across(w) for w in far]
+    spread = project(joined, attention_out.T, blocks.shape[1], query_heads, head_size)
     added = lax.all_to_all(spread, "tok", 0, 0, tiled=True)
     mlp_part, mixed = feed(added, embedded, mlp_gain[None], weights)
     mlp_rows = lax.all_to_all(mlp_part, "tok", 0, 0, tiled=True)
@@ -569,7 +659,14 @@
     incoming = inverse_of(new_slot)
     local_targets = lax.dynamic_slice_in_dim(incoming, group_index * slots_dev, slots_dev)
     sources = jnp.take(current_slot, local_targets)
-    new_states = pick_states(sources, every_state, slots_dev)
+    chosen = chosen[:, 0]
+    pair = jnp.concatenate([chosen, across(chosen)], axis=0)
+    held = [pair] + [turn(pair, by) for by in range(1, chips)]
+    source_group = sources // slots_dev
+    turns = (group_index // cores - source_group // cores) % chips
+    other_core = (source_group % cores) != (group_index % cores)
+    rows = sources % slots_dev + jnp.where(other_core, slots_dev, 0)
+    new_states = pick_states(turns, rows, held, slots_dev)[:, None]
     return (hidden_out, new_states)
 
 

time: 161 us -> 165 us (1.025)
  starting transfers between devices: 20 us -> 46.2 us
  blocking collectives: 26.1 us -> 0 us
  local copies, waits for them, and re-layouts: 8.64 us -> 33.3 us
  between operations: 16.3 us -> 2.92 us
  Pallas kernels: 32 us -> 24.9 us
  other arithmetic: 6.06 us -> 3.68 us
    all_to_all x2 -> x0, blocking collectives: 26.1 us -> none  [the longest x1 14.6 us: local(): lax.all_to_all(join(parts, blocks, query_heads, head_size), 'tok', 0, 0,...]
    unnamed x47 -> x76, local copies, waits for them, and re-layouts: 4.82 us -> 24.2 us
    ppermute x0 -> x13, waiting for transfers between devices: none -> 13.6 us  [the longest x7 13.6 us: turn(): lax.ppermute(value, 'req', [(g, (g + by * cores) % groups) for g in range...]
    ppermute x0 -> x13, starting transfers between devices: none -> 12.6 us  [the longest x7 11.5 us: turn(): lax.ppermute(value, 'req', [(g, (g + by * cores) % groups) for g in range...]
    all_to_all x1 -> x3, starting transfers between devices: 7.41 us -> 17.8 us  [the longest x1 7.18 us: spread_slots(): return lax.all_to_all(spread, 'tok', 0, 0, tiled=True)]
    all_to_all x1, waiting for transfers between devices: 18.7 us -> 11.1 us  [exchange(): slots = lax.all_to_all(payload, 'req', 0, 0, tiled=True)]
    pallas_call x3, Pallas kernels: 21.1 us -> 15 us  [the longest x1 7.18 us: feed(): pl.pallas_call(functools.partial(feed_kernel, count=len(weights)), in_spe...]
    all_to_all x1, waiting for transfers between devices: 9.98 us -> 4.19 us  [local(): added = lax.all_to_all(spread, 'tok', 0, 0, tiled=True)]
  transfers between devices with their start and end apart: 6 -> 19, of which waited for: 4 -> 7; matrix products, arithmetic and copies ran while one was open for 4% -> 6% of each run, Pallas kernels for 20% -> 13%
where the time goes in v3:
time: 165 us; the launch traced here: 163 us
  waiting for transfers between devices  51.4 us (31%)
  starting transfers between devices  46.2 us (28%)
  local copies, waits for them, and re-layouts  33.3 us (20%)
  Pallas kernels  24.9 us (15%)
  other arithmetic  3.68 us (2%)
  between operations  2.92 us (2%)
    unnamed x76, local copies, waits for them, and re-layouts  24.2 us
    all_to_all x1, waiting for transfers between devices, spread_slots(): return lax.all_to_all(spread, 'tok', 0, 0, tiled=True)  17.5 us
    ppermute x7, waiting for transfers between devices, turn(): lax.ppermute(value, 'req', [(g, (g + by * cores) % groups) for g in range...  13.6 us
    ppermute x7, starting transfers between devices, turn(): lax.ppermute(value, 'req', [(g, (g + by * cores) % groups) for g in range...  11.5 us
    all_to_all x1, waiting for transfers between devices, exchange(): slots = lax.all_to_all(payload, 'req', 0, 0, tiled=True)  11.1 us
    all_to_all x1, starting transfers between devices, spread_slots(): return lax.all_to_all(spread, 'tok', 0, 0, tiled=True)  7.18 us
    pallas_call x1, Pallas kernels, feed(): pl.pallas_call(functools.partial(feed_kernel, count=len(weights)), in_spe...  7.18 us
    all_to_all x1, starting transfers between devices, local(): lax.all_to_all(join(parts, blocks, query_heads, head_size), 'tok', 0, 0,...  7.14 us
  transfers between devices with their start and end apart: 19, of which 7 were waited for; matrix products, arithmetic and copies ran while one was open for 6% of the time, Pallas kernels for 13%

profile of v3, /device:TPU:0, one launch (start us, length us, event | category | flops | bytes accessed | tf_op | source)
XLA Modules:
  0.0 163.1 jit_solution(13149947789145987023)
XLA Ops:
  0.7 0.8 copy.33.draft_ids
  1.6 4.4 %fetch.5 = (bf16[8,16,3072]{2,1,0:T(8,128)(2,1)}, s32[64,128]{1,0:T(8,128)S(1)}, s32[8,128]{1,0:T(8,128)S(1)}) custom-call(s32[3]{0:T(128)S(1)} %pad_add_fusion.1.ints, s32[1,32]{1,0:T(1,128)} %bitcast.33, s32[32,16]{1,0:T(8,128)S(1)} %copy.33.draft_ids, bf16[512,3072]{1,0:T(8,128)(2,1)} %table.1), custom_call_target="tpu_custom_call" | custom-call | flops 402653184 | bytes 3145728 | tf_op jit(solution)/shard_map/fetch/pallas_call | solution.py:124
  6.6 0.7 slice_dynamic-update-slice_fusion.5
  7.3 0.8 slice_dynamic-update-slice_fusion.4
  8.1 0.8 slice_dynamic-update-slice_fusion.3
  8.9 0.8 slice_dynamic-update-slice_fusion.2
  9.6 5.5 %all-to-all-start.2 = ((bf16[8,16,3072]{2,1,0:T(8,128)(2,1)}), bf16[8,16,3072]{2,1,0:T(8,128)(2,1)S(1)}, u32[]{:S(2)}, u32[]{:S(2)}) async-start(bf16[8,16,3072]{2,1,0:T(8,128)(2,1)} %get-tuple-element.127), calls=%async_computation.2 | async-start | bytes 1572864 | tf_op jit(solution)/shard_map/all_to_all | solution.py:581
  15.1 0.8 slice_dynamic-update-slice_fusion.1
  16.5 0.7 slice_dynamic-update-slice_fusion.refs_0_
  17.2 11.1 %all-to-all-done.2 = bf16[8,16,3072]{2,1,0:T(8,128)(2,1)S(1)} async-done(((bf16[8,16,3072]{2,1,0:T(8,128)(2,1)}), bf16[8,16,3072]{2,1,0:T(8,128)(2,1)S(1)}, u32[]{:S(2)}, u32[]{:S(2)}) %all-to-all-start.2) | async-done | bytes 786464 | tf_op jit(solution)/shard_map/all_to_all | solution.py:581
  28.9 2.7 %collective-permute-start.1 = (bf16[288,3072]{1,0:T(8,128)(2,1)}, bf16[288,3072]{1,0:T(8,128)(2,1)}, u32[]{:S(2)}, u32[]{:S(2)}) collective-permute-start(bf16[288,3072]{1,0:T(8,128)(2,1)} %slice_dynamic-update-slice_fusion.refs_0_), channel_id=1, source_target_pairs={{0,96},{16,112},{32,0},{48,16},{64,32},{80,48},{96,64},{112,80},{1... | collective-permute-start | bytes 5308424 | tf_op jit(solution)/shard_map/ppermute | solution.py:569
  32.4 1.4 broadcast_in_dim.68
  33.8 7.2 %all-to-all-start.3 = ((bf16[16,16,3072]{2,1,0:T(8,128)(2,1)}), bf16[16,16,3072]{2,1,0:T(8,128)(2,1)S(1)}, u32[]{:S(2)}, u32[]{:S(2)}) async-start(bf16[16,16,3072]{2,1,0:T(8,128)(2,1)} %broadcast_in_dim.68), calls=%async_computation.3 | async-start | bytes 3145728 | tf_op jit(solution)/shard_map/all_to_all | solution.py:587
  46.4 17.5 %all-to-all-done.3.arrived = bf16[16,16,3072]{2,1,0:T(8,128)(2,1)S(1)} async-done(((bf16[16,16,3072]{2,1,0:T(8,128)(2,1)}), bf16[16,16,3072]{2,1,0:T(8,128)(2,1)S(1)}, u32[]{:S(2)}, u32[]{:S(2)}) %all-to-all-start.3) | async-done | bytes 1572896 | tf_op jit(solution)/shard_map/all_to_all | solution.py:587
  63.9 2.3 %copy-done.1 = bf16[3072,768]{1,0:T(8,128)(2,1)S(1)} copy-done((bf16[3072,768]{1,0:T(8,128)(2,1)S(1)}, bf16[3072,768]{1,0:T(8,128)(2,1)}, u32[]{:S(2)}) %copy-start.1) | copy-done | bytes 4718616
  66.3 1.2 copy-done.4
  67.5 1.2 copy-done.5
  68.7 0.8 copy-done.18
  70.1 5.7 %attend.1 = (bf16[16,4,896]{2,1,0:T(4,128)(2,1)S(1)}, bf16[64,3072]{1,0:T(8,128)(2,1)S(1)}, bf16[64,3072]{1,0:T(8,128)(2,1)S(1)}) custom-call(s32[9]{0:T(128)S(1)} %copy-done.22, bf16[16,16,3072]{2,1,0:T(8,128)(2,1)S(1)} %all-to-all-done.3.arrived, s32[64,128]{1,0:T(8,128)S(1)} %copy-done.18, bf16[64,3072]{1,0:T(8,128)(2,1)} %copy-done.28, ...), custom_call_target="tpu_custom_call" | custom-call | flops 603979776 | bytes 6815744 | tf_op jit(solution)/shard_map/attend/pallas_call | solution.py:264
  75.8 0.7 copy-done.11
  77.2 3.5 %all-to-all-start.4 = ((bf16[16,4,896]{2,1,0:T(4,128)(2,1)}), bf16[16,4,896]{2,1,0:T(4,128)(2,1)S(1)}, u32[]{:S(2)}, u32[]{:S(2)}) async-start(bf16[16,4,896]{2,1,0:T(4,128)(2,1)} %copy-done.16), calls=%async_computation.4 | async-start | bytes 229376 | tf_op jit(solution)/shard_map/all_to_all | solution.py:631
  80.8 1.9 %copy-done.2 = bf16[3072,512]{1,0:T(8,128)(2,1)S(1)} copy-done((bf16[3072,512]{1,0:T(8,128)(2,1)S(1)}, bf16[3072,512]{1,0:T(8,128)(2,1)}, u32[]{:S(2)}) %copy-start.2) | copy-done | bytes 3145752
  82.7 1.1 copy-done.6
  83.8 1.1 copy-done.7
  84.9 1.1 copy-done.8
  86.1 1.0 copy-done.9
  88.4 3.2 %mamba.1 = (bf16[16,96,128]{2,1,0:T(8,128)(2,1)S(1)}, bf16[4,1,128,256]{3,2,1,0:T(8,128)(2,1)S(1)}) custom-call(s32[9]{0:T(128)S(1)} %copy-done.23, f32[3]{0:T(128)S(1)} %pad_maximum_fusion.1.reals, bf16[64,3072]{1,0:T(8,128)(2,1)S(1)} %get-tuple-element.137.normed, bf16[3072,128]{1,0:T(8,128)(2,1)S(1)} %copy-done.6, bf16[3072,128]{1,0:T(8,128)(2,1)S(1)} %copy-done.7, ...), custom_call_target="tpu_custom_call" | custom-call | flops 402653184 | bytes 6291456 | tf_op jit(solution)/shard_map/mamba/pallas_call | solution.py:362
  92.4 2.1 %slice.34 = bf16[144,3072]{1,0:T(8,128)(2,1)} slice(bf16[288,3072]{1,0:T(8,128)(2,1)} %collective-permute-done.refs_1_), slice={[0:144], [0:3072]} | slice | bytes 1769472 | tf_op jit(solution)/shard_map/slice | solution.py:647
  94.6 2.2 %slice.35 = bf16[144,3072]{1,0:T(8,128)(2,1)} slice(bf16[288,3072]{1,0:T(8,128)(2,1)} %collective-permute-done.1.refs_2_), slice={[144:288], [0:3072]} | slice | bytes 1769472 | tf_op jit(solution)/shard_map/slice | solution.py:647
  96.8 3.1 %collective-permute-start.3 = (bf16[144,3072]{1,0:T(8,128)(2,1)}, bf16[144,3072]{1,0:T(8,128)(2,1)}, u32[]{:S(2)}, u32[]{:S(2)}) collective-permute-start(bf16[144,3072]{1,0:T(8,128)(2,1)} %slice.35), channel_id=1, source_target_pairs={{0,96},{16,112},{32,0},{48,16},{64,32},{80,48},{96,64},{112,80},{1... | collective-permute-start | bytes 2654216 | tf_op jit(solution)/shard_map/ppermute | solution.py:569
  100.4 1.1 join.1
  101.5 7.1 %all-to-all-start.5 = ((bf16[16,120,128]{2,1,0:T(8,128)(2,1)}), bf16[16,120,128]{2,1,0:T(8,128)(2,1)S(1)}, u32[]{:S(2)}, u32[]{:S(2)}) async-start(bf16[16,120,128]{2,1,0:T(8,128)(2,1)} %join.1), calls=%async_computation.5 | async-start | bytes 983040 | tf_op jit(solution)/shard_map/all_to_all | solution.py:649
  108.7 8.3 %collective-permute-done.2.refs_6_ = bf16[144,3072]{1,0:T(8,128)(2,1)} collective-permute-done((bf16[144,3072]{1,0:T(8,128)(2,1)}, bf16[144,3072]{1,0:T(8,128)(2,1)}, u32[]{:S(2)}, u32[]{:S(2)}) %collective-permute-start.2) | collective-permute-done | bytes 884768 | tf_op jit(solution)/shard_map/ppermute | solution.py:569
  117.0 3.3 %all-to-all-done.5.parts = bf16[16,120,128]{2,1,0:T(8,128)(2,1)S(1)} async-done(((bf16[16,120,128]{2,1,0:T(8,128)(2,1)}), bf16[16,120,128]{2,1,0:T(8,128)(2,1)S(1)}, u32[]{:S(2)}, u32[]{:S(2)}) %all-to-all-start.5) | async-done | bytes 491552 | tf_op jit(solution)/shard_map/all_to_all | solution.py:649
  120.8 1.1 project.1
  121.9 6.7 %all-to-all-start.6 = ((bf16[16,96,128]{2,1,0:T(8,128)(2,1)}), bf16[16,96,128]{2,1,0:T(8,128)(2,1)S(1)}, u32[]{:S(2)}, u32[]{:S(2)}) async-start(bf16[16,96,128]{2,1,0:T(8,128)(2,1)} %project.1), calls=%async_computation.6 | async-start | bytes 786432 | tf_op jit(solution)/shard_map/all_to_all | solution.py:653
  128.6 0.8 gather_fusion.2
  129.6 5.1 %collective-permute-start.11 = (bf16[8,128,256]{2,1,0:T(8,128)(2,1)S(1)}, bf16[8,128,256]{2,1,0:T(8,128)(2,1)}, u32[]{:S(2)}, u32[]{:S(2)}) collective-permute-start(bf16[8,128,256]{2,1,0:T(8,128)(2,1)S(1)} %pad_maximum_fusion.refs_0_), channel_id=1, source_target_pairs={{0,64},{16,80},{32,96},{48,112},{64,0},{80,16},{96,32},{112,48},{1... | collective-permute-start | bytes 1572872 | tf_op jit(solution)/shard_map/ppermute | solution.py:569
  134.7 4.2 %all-to-all-done.6.spread = bf16[16,96,128]{2,1,0:T(8,128)(2,1)S(1)} async-done(((bf16[16,96,128]{2,1,0:T(8,128)(2,1)}), bf16[16,96,128]{2,1,0:T(8,128)(2,1)S(1)}, u32[]{:S(2)}, u32[]{:S(2)}) %all-to-all-start.6) | async-done | bytes 393248 | tf_op jit(solution)/shard_map/all_to_all | solution.py:653
  138.9 1.0 copy-done.12
  139.9 7.2 %feed.1 = (bf16[16,4,3072]{2,1,0:T(4,128)(2,1)S(1)}, bf16[64,3072]{1,0:T(8,128)(2,1)S(1)}) custom-call(bf16[16,96,128]{2,1,0:T(8,128)(2,1)S(1)} %all-to-all-done.6.spread, bf16[64,3072]{1,0:T(8,128)(2,1)S(1)} %copy-done.12, f32[1,3072]{1,0:T(1,128)S(1)} %bitcast.32, bf16[288,3072]{1,0:T(8,128)(2,1)} %slice_dynamic-update-slice_fusion.refs_0_, ...), custom_call_target="tpu_custom_call" | custom-call | flops 905969664 | bytes 14155776 | tf_op jit(solution)/shard_map/feed/pallas_call | solution.py:489
  147.1 0.8 copy-done.10
  147.9 0.8 copy-done.24
  148.6 3.6 %all-to-all-start.7 = ((bf16[16,4,3072]{2,1,0:T(4,128)(2,1)}), bf16[16,4,3072]{2,1,0:T(4,128)(2,1)S(1)}, u32[]{:S(2)}, u32[]{:S(2)}) async-start(bf16[16,4,3072]{2,1,0:T(4,128)(2,1)} %copy-done.10), calls=%async_computation.7 | async-start | bytes 786432 | tf_op jit(solution)/shard_map/all_to_all | solution.py:655
  152.3 5.3 %collective-permute-done.11.refs_2_ = bf16[8,128,256]{2,1,0:T(8,128)(2,1)} collective-permute-done((bf16[8,128,256]{2,1,0:T(8,128)(2,1)S(1)}, bf16[8,128,256]{2,1,0:T(8,128)(2,1)}, u32[]{:S(2)}, u32[]{:S(2)}) %collective-permute-start.11) | collective-permute-done | bytes 524320 | tf_op jit(solution)/shard_map/ppermute | solution.py:569
  157.6 2.2 %pick.1 = f32[4,128,256]{2,1,0:T(8,128)} custom-call(s32[4]{0:T(128)S(1)} %and_select_fusion.3.turns, s32[4]{0:T(128)S(1)} %get-tuple-element.196.rows, bf16[8,128,256]{2,1,0:T(8,128)(2,1)S(1)} %pad_maximum_fusion.refs_0_, bf16[8,128,256]{2,1,0:T(8,128)(2,1)S(1)} %collective-permute-done.10.refs_1_, bf16[8,128,256]{2,1,0:T(8,128)(2,1)} %collective-permute-done.11.refs_2_, ...), custom_call_target="tpu_custom_call" | custom-call | tf_op jit(solution)/shard_map/pick/pallas_call | solution.py:518
  159.8 1.8 %all-to-all-done.7 = bf16[16,4,3072]{2,1,0:T(4,128)(2,1)S(1)} async-done(((bf16[16,4,3072]{2,1,0:T(4,128)(2,1)}), bf16[16,4,3072]{2,1,0:T(4,128)(2,1)S(1)}, u32[]{:S(2)}, u32[]{:S(2)}) %all-to-all-start.7) | async-done | bytes 393248 | tf_op jit(solution)/shard_map/all_to_all | solution.py:655
  161.7 1.4 add_convert_fusion
  (98 shorter events, 11.1 us)
Async XLA Ops:
  0.6 41.9 %copy-start = (s32[32]{0:T(128)S(1)}, s32[32]{0:T(128)}, u32[]{:S(2)}) copy-start(s32[32]{0:T(128)} %param.30) | copy-start | bytes 388
  0.6 6.0 %copy-start.29 = (bf16[3072,96]{0,1:T(8,128)(2,1)S(1)}, bf16[3072,96]{0,1:T(8,128)(2,1)}, u32[]{:S(2)}) copy-start(bf16[3072,96]{0,1:T(8,128)(2,1)} %param.51) | copy-start | bytes 1769476
  1.6 5.8 %copy-start.30 = (bf16[3072,96]{0,1:T(8,128)(2,1)S(1)}, bf16[3072,96]{0,1:T(8,128)(2,1)}, u32[]{:S(2)}) copy-start(bf16[3072,96]{0,1:T(8,128)(2,1)} %param.52) | copy-start | bytes 1769476
  1.6 6.5 %copy-start.31 = (bf16[3072,96]{0,1:T(8,128)(2,1)S(1)}, bf16[3072,96]{0,1:T(8,128)(2,1)}, u32[]{:S(2)}) copy-start(bf16[3072,96]{0,1:T(8,128)(2,1)} %param.53) | copy-start | bytes 1769476
  9.6 22.1 %copy-start.25 = (s32[32]{0:T(128)S(1)}, s32[32]{0:T(128)}, u32[]{:S(2)}) copy-start(s32[32]{0:T(128)} %param.31) | copy-start | bytes 388
  9.6 18.7 %all-to-all-start.2 = ((bf16[8,16,3072]{2,1,0:T(8,128)(2,1)}), bf16[8,16,3072]{2,1,0:T(8,128)(2,1)S(1)}, u32[]{:S(2)}, u32[]{:S(2)}) async-start(bf16[8,16,3072]{2,1,0:T(8,128)(2,1)} %get-tuple-element.127), calls=%async_computation.2 | async-start | bytes 1572864 | tf_op jit(solution)/shard_map/all_to_all | solution.py:581
  28.3 64.1 %collective-permute-start = (bf16[288,3072]{1,0:T(8,128)(2,1)}, bf16[288,3072]{1,0:T(8,128)(2,1)}, u32[]{:S(2)}, u32[]{:S(2)}) collective-permute-start(bf16[288,3072]{1,0:T(8,128)(2,1)} %slice_dynamic-update-slice_fusion.refs_0_), channel_id=1, source_target_pairs={{0,32},{16,48},{32,64},{48,80},{64,96},{80,112},{96,0},{112,16},{1... | collective-permute-start | bytes 5308424 | tf_op jit(solution)/shard_map/ppermute | solution.py:569
  28.9 63.5 %collective-permute-start.1 = (bf16[288,3072]{1,0:T(8,128)(2,1)}, bf16[288,3072]{1,0:T(8,128)(2,1)}, u32[]{:S(2)}, u32[]{:S(2)}) collective-permute-start(bf16[288,3072]{1,0:T(8,128)(2,1)} %slice_dynamic-update-slice_fusion.refs_0_), channel_id=1, source_target_pairs={{0,96},{16,112},{32,0},{48,16},{64,32},{80,48},{96,64},{112,80},{1... | collective-permute-start | bytes 5308424 | tf_op jit(solution)/shard_map/ppermute | solution.py:569
  32.4 1.4 copy-start.28
  33.8 7.2 %copy-start.34 = (s32[32]{0:T(128)S(1)}, s32[32]{0:T(128)}, u32[]{:S(2)}) copy-start(s32[32]{0:T(128)} %param.32) | copy-start | bytes 388
  33.8 9.4 %copy-start.27 = (s32[32]{0:T(128)S(1)}, s32[32]{0:T(128)}, u32[]{:S(2)}) copy-start(s32[32]{0:T(128)} %param.33) | copy-start | bytes 388
  33.8 30.1 %copy-start.3 = (bf16[3072,256]{1,0:T(8,128)(2,1)S(1)}, bf16[3072,256]{1,0:T(8,128)(2,1)}, u32[]{:S(2)}) copy-start(bf16[3072,256]{1,0:T(8,128)(2,1)} %keyvalue_weight.1) | copy-start | bytes 4718596
  33.8 30.1 %copy-start.19 = (f32[3072]{0:T(1024)S(1)}, f32[3072]{0:T(1024)}, u32[]{:S(2)}) copy-start(f32[3072]{0:T(1024)} %param.35) | copy-start | bytes 36868
  33.8 30.1 %all-to-all-start.3 = ((bf16[16,16,3072]{2,1,0:T(8,128)(2,1)}), bf16[16,16,3072]{2,1,0:T(8,128)(2,1)S(1)}, u32[]{:S(2)}, u32[]{:S(2)}) async-start(bf16[16,16,3072]{2,1,0:T(8,128)(2,1)} %broadcast_in_dim.68), calls=%async_computation.3 | async-start | bytes 3145728 | tf_op jit(solution)/shard_map/all_to_all | solution.py:587
  63.9 2.3 %copy-start.1 = (bf16[3072,768]{1,0:T(8,128)(2,1)S(1)}, bf16[3072,768]{1,0:T(8,128)(2,1)}, u32[]{:S(2)}) copy-start(bf16[3072,768]{1,0:T(8,128)(2,1)} %query_weight.1) | copy-start | bytes 14155780
  66.3 1.2 copy-start.4
  67.5 1.2 copy-start.5
  68.7 0.8 copy-start.18
  75.8 0.8 copy-start.11
  77.2 15.2 %all-to-all-start.4 = ((bf16[16,4,896]{2,1,0:T(4,128)(2,1)}), bf16[16,4,896]{2,1,0:T(4,128)(2,1)S(1)}, u32[]{:S(2)}, u32[]{:S(2)}) async-start(bf16[16,4,896]{2,1,0:T(4,128)(2,1)} %copy-done.16), calls=%async_computation.4 | async-start | bytes 229376 | tf_op jit(solution)/shard_map/all_to_all | solution.py:631
  80.8 1.9 %copy-start.2 = (bf16[3072,512]{1,0:T(8,128)(2,1)S(1)}, bf16[3072,512]{1,0:T(8,128)(2,1)}, u32[]{:S(2)}) copy-start(bf16[3072,512]{1,0:T(8,128)(2,1)} %state_proj.1) | copy-start | bytes 9437188
  82.7 1.1 copy-start.6
  83.8 1.1 copy-start.7
  84.9 1.1 copy-start.8
  86.1 1.0 copy-start.9
  91.6 0.7 copy-start.14
  94.5 22.5 %copy-start.15 = (bf16[4,1,128,256]{3,2,1,0:T(8,128)(2,1)S(1)}, bf16[4,1,128,256]{3,2,1,0:T(8,128)(2,1)}, u32[]{:S(2)}) copy-start(bf16[4,1,128,256]{3,2,1,0:T(8,128)(2,1)} %copy-done.14) | copy-start | bytes 786436
  94.5 26.3 %copy-start.13 = (bf16[768,192]{0,1:T(8,128)(2,1)S(1)}, bf16[768,192]{0,1:T(8,128)(2,1)}, u32[]{:S(2)}) copy-start(bf16[768,192]{0,1:T(8,128)(2,1)} %param.40) | copy-start | bytes 884740
  94.5 22.5 %collective-permute-start.2 = (bf16[144,3072]{1,0:T(8,128)(2,1)}, bf16[144,3072]{1,0:T(8,128)(2,1)}, u32[]{:S(2)}, u32[]{:S(2)}) collective-permute-start(bf16[144,3072]{1,0:T(8,128)(2,1)} %slice.34), channel_id=1, source_target_pairs={{0,32},{16,48},{32,64},{48,80},{64,96},{80,112},{96,0},{112,16},{1... | collective-permute-start | bytes 2654216 | tf_op jit(solution)/shard_map/ppermute | solution.py:569
  94.5 34.9 %collective-permute-start.4 = (bf16[288,3072]{1,0:T(8,128)(2,1)}, bf16[288,3072]{1,0:T(8,128)(2,1)S(1)}, u32[]{:S(2)}, u32[]{:S(2)}) collective-permute-start(bf16[288,3072]{1,0:T(8,128)(2,1)} %slice_dynamic-update-slice_fusion.refs_0_), channel_id=1, source_target_pairs={{0,16},{16,0},{32,48},{48,32},{64,80},{80,64},{96,112},{112,96},{1... | collective-permute-start | bytes 5308424 | tf_op jit(solution)/shard_map/ppermute | solution.py:574
  96.8 23.4 %collective-permute-start.3 = (bf16[144,3072]{1,0:T(8,128)(2,1)}, bf16[144,3072]{1,0:T(8,128)(2,1)}, u32[]{:S(2)}, u32[]{:S(2)}) collective-permute-start(bf16[144,3072]{1,0:T(8,128)(2,1)} %slice.35), channel_id=1, source_target_pairs={{0,96},{16,112},{32,0},{48,16},{64,32},{80,48},{96,64},{112,80},{1... | collective-permute-start | bytes 2654216 | tf_op jit(solution)/shard_map/ppermute | solution.py:569
  99.9 29.6 %collective-permute-start.5 = (bf16[288,3072]{1,0:T(8,128)(2,1)}, bf16[288,3072]{1,0:T(8,128)(2,1)}, u32[]{:S(2)}, u32[]{:S(2)}) collective-permute-start(bf16[288,3072]{1,0:T(8,128)(2,1)} %collective-permute-done.refs_1_), channel_id=1, source_target_pairs={{0,16},{16,0},{32,48},{48,32},{64,80},{80,64},{96,112},{112,96},{1... | collective-permute-start | bytes 5308424 | tf_op jit(solution)/shard_map/ppermute | solution.py:574
  100.2 34.6 %collective-permute-start.6 = (bf16[288,3072]{1,0:T(8,128)(2,1)}, bf16[288,3072]{1,0:T(8,128)(2,1)}, u32[]{:S(2)}, u32[]{:S(2)}) collective-permute-start(bf16[288,3072]{1,0:T(8,128)(2,1)} %collective-permute-done.1.refs_2_), channel_id=1, source_target_pairs={{0,16},{16,0},{32,48},{48,32},{64,80},{80,64},{96,112},{112,96},{1... | collective-permute-start | bytes 5308424 | tf_op jit(solution)/shard_map/ppermute | solution.py:574
  100.4 28.2 %copy-start.26 = (s32[32]{0:T(128)S(1)}, s32[32]{0:T(128)}, u32[]{:S(2)}) copy-start(s32[32]{0:T(128)} %param.31) | copy-start | bytes 388
  101.5 18.7 %all-to-all-start.5 = ((bf16[16,120,128]{2,1,0:T(8,128)(2,1)}), bf16[16,120,128]{2,1,0:T(8,128)(2,1)S(1)}, u32[]{:S(2)}, u32[]{:S(2)}) async-start(bf16[16,120,128]{2,1,0:T(8,128)(2,1)} %join.1), calls=%async_computation.5 | async-start | bytes 983040 | tf_op jit(solution)/shard_map/all_to_all | solution.py:649
  117.0 3.3 %collective-permute-start.9 = (bf16[4,128,256]{2,1,0:T(8,128)(2,1)S(1)}, bf16[4,128,256]{2,1,0:T(8,128)(2,1)S(1)}, u32[]{:S(2)}, u32[]{:S(2)}) collective-permute-start(bf16[4,128,256]{2,1,0:T(8,128)(2,1)S(1)} %bitcast.28), channel_id=1, source_target_pairs={{0,16},{16,0},{32,48},{48,32},{64,80},{80,64},{96,112},{112,96},{1... | collective-permute-start | bytes 786440 | tf_op jit(solution)/shard_map/ppermute | solution.py:574
  120.3 18.6 %collective-permute-start.7 = (bf16[144,3072]{1,0:T(8,128)(2,1)}, bf16[144,3072]{1,0:T(8,128)(2,1)}, u32[]{:S(2)}, u32[]{:S(2)}) collective-permute-start(bf16[144,3072]{1,0:T(8,128)(2,1)} %collective-permute-done.2.refs_6_), channel_id=1, source_target_pairs={{0,16},{16,0},{32,48},{48,32},{64,80},{80,64},{96,112},{112,96},{1... | collective-permute-start | bytes 2654216 | tf_op jit(solution)/shard_map/ppermute | solution.py:574
  120.3 18.6 %collective-permute-start.8 = (bf16[144,3072]{1,0:T(8,128)(2,1)}, bf16[144,3072]{1,0:T(8,128)(2,1)}, u32[]{:S(2)}, u32[]{:S(2)}) collective-permute-start(bf16[144,3072]{1,0:T(8,128)(2,1)} %collective-permute-done.3.refs_7_), channel_id=1, source_target_pairs={{0,16},{16,0},{32,48},{48,32},{64,80},{80,64},{96,112},{112,96},{1... | collective-permute-start | bytes 2654216 | tf_op jit(solution)/shard_map/ppermute | solution.py:574
  120.8 18.1 %copy-start.21 = (f32[3072]{0:T(1024)S(1)}, f32[3072]{0:T(1024)}, u32[]{:S(2)}) copy-start(f32[3072]{0:T(1024)} %param.50) | copy-start | bytes 36868
  121.9 17.0 %all-to-all-start.6 = ((bf16[16,96,128]{2,1,0:T(8,128)(2,1)}), bf16[16,96,128]{2,1,0:T(8,128)(2,1)S(1)}, u32[]{:S(2)}, u32[]{:S(2)}) async-start(bf16[16,96,128]{2,1,0:T(8,128)(2,1)} %project.1), calls=%async_computation.6 | async-start | bytes 786432 | tf_op jit(solution)/shard_map/all_to_all | solution.py:653
  129.5 22.8 %collective-permute-start.10 = (bf16[8,128,256]{2,1,0:T(8,128)(2,1)S(1)}, bf16[8,128,256]{2,1,0:T(8,128)(2,1)S(1)}, u32[]{:S(2)}, u32[]{:S(2)}) collective-permute-start(bf16[8,128,256]{2,1,0:T(8,128)(2,1)S(1)} %pad_maximum_fusion.refs_0_), channel_id=1, source_target_pairs={{0,32},{16,48},{32,64},{48,80},{64,96},{80,112},{96,0},{112,16},{1... | collective-permute-start | bytes 1572872 | tf_op jit(solution)/shard_map/ppermute | solution.py:569
  129.6 28.0 %collective-permute-start.11 = (bf16[8,128,256]{2,1,0:T(8,128)(2,1)S(1)}, bf16[8,128,256]{2,1,0:T(8,128)(2,1)}, u32[]{:S(2)}, u32[]{:S(2)}) collective-permute-start(bf16[8,128,256]{2,1,0:T(8,128)(2,1)S(1)} %pad_maximum_fusion.refs_0_), channel_id=1, source_target_pairs={{0,64},{16,80},{32,96},{48,112},{64,0},{80,16},{96,32},{112,48},{1... | collective-permute-start | bytes 1572872 | tf_op jit(solution)/shard_map/ppermute | solution.py:569
  134.7 22.9 %collective-permute-start.12 = (bf16[8,128,256]{2,1,0:T(8,128)(2,1)S(1)}, bf16[8,128,256]{2,1,0:T(8,128)(2,1)}, u32[]{:S(2)}, u32[]{:S(2)}) collective-permute-start(bf16[8,128,256]{2,1,0:T(8,128)(2,1)S(1)} %pad_maximum_fusion.refs_0_), channel_id=1, source_target_pairs={{0,96},{16,112},{32,0},{48,16},{64,32},{80,48},{96,64},{112,80},{1... | collective-permute-start | bytes 1572872 | tf_op jit(solution)/shard_map/ppermute | solution.py:569
  138.9 1.0 copy-start.12
  139.9 12.3 %copy-start.33 = (s32[32]{0:T(128)S(1)}, s32[32]{0:T(128)}, u32[]{:S(2)}) copy-start(s32[32]{0:T(128)} %copy-done.32) | copy-start | bytes 388
  147.1 0.8 copy-start.10
  147.9 0.8 copy-start.24
  148.6 12.9 %all-to-all-start.7 = ((bf16[16,4,3072]{2,1,0:T(4,128)(2,1)}), bf16[16,4,3072]{2,1,0:T(4,128)(2,1)S(1)}, u32[]{:S(2)}, u32[]{:S(2)}) async-start(bf16[16,4,3072]{2,1,0:T(4,128)(2,1)} %copy-done.10), calls=%async_computation.7 | async-start | bytes 786432 | tf_op jit(solution)/shard_map/all_to_all | solution.py:655
  (6 other events, 3.7 us)

commit v4 on v3

--- a/solution.py
+++ b/solution.py
@@ -45,8 +45,8 @@
     return pl.CostEstimate(flops=flops, bytes_accessed=moved, transcendentals=special)
 
 
-def whole(count):
-    return [pl.BlockSpec(memory_space=pltpu.VMEM)] * count
+def whole(shapes):
+    return [pl.BlockSpec(a.shape, lambda i, n=len(a.shape): (0,) * n) for a in shapes]
 
 
 def streamed(count):
@@ -57,10 +57,14 @@
     return [pl.BlockSpec(memory_space=pltpu.SMEM)] * count
 
 
-PARAMS = pltpu.CompilerParams(vmem_limit_bytes=16 << 20)
-
-
-def fetch_kernel(ints, slots_row, draft_ids, table, payload, places, most, *, members):
+PARAMS = pltpu.CompilerParams(vmem_limit_bytes=60 << 20)
+
+
+def fetch_kernel(
+    ints, slots_row, draft_ids, table_far, payload, places, most, table, sem, *, members
+):
+    load = pltpu.make_async_copy(table_far, table, sem)
+    load.start()
     groups, room, width = payload.shape
     requests, drafts = draft_ids.shape
     vocab = table.shape[0]
@@ -111,6 +115,7 @@
         row = jnp.sum(asked, axis=1, keepdims=True) - 1
         hots.append(jnp.where(local_iota == row, 1.0, 0.0))
     hot = jnp.concatenate(hots, axis=0).astype(BF)
+    load.wait()
     rows = dot_nn(hot, table[...])
     for g in range(groups):
         payload[g] = rows[g * room : (g + 1) * room].astype(BF)
@@ -121,15 +126,18 @@
 def fetch(ints, slots_row, draft_ids, table, groups, members, room):
     count = draft_ids.size // groups
     width = table.shape[1]
+    outs = [
+        jax.ShapeDtypeStruct((groups, room, width), BF),
+        jax.ShapeDtypeStruct((count, AUX), jnp.int32),
+        jax.ShapeDtypeStruct((8, AUX), jnp.int32),
+    ]
     return pl.pallas_call(
         functools.partial(fetch_kernel, members=members),
-        in_specs=scalars(1) + whole(3),
-        out_specs=whole(3),
-        out_shape=[
-            jax.ShapeDtypeStruct((groups, room, width), BF),
-            jax.ShapeDtypeStruct((count, AUX), jnp.int32),
-            jax.ShapeDtypeStruct((8, AUX), jnp.int32),
-        ],
+        grid=(1,),
+        in_specs=scalars(1) + whole([slots_row, draft_ids]) + streamed(1),
+        out_specs=whole(outs),
+        out_shape=outs,
+        scratch_shapes=[pltpu.VMEM(table.shape, table.dtype), pltpu.SemaphoreType.DMA],
         compiler_params=PARAMS,
         cost_estimate=cost(2 * groups * room * table.size, 2 * table.size),
         name="fetch",
@@ -152,8 +160,9 @@
 def place(arrived, places, before):
     return pl.pallas_call(
         place_kernel,
-        in_specs=whole(3),
-        out_specs=whole(1)[0],
+        grid=(1,),
+        in_specs=whole([arrived, places, before]),
+        out_specs=whole([before])[0],
         out_shape=jax.ShapeDtypeStruct(before.shape, BF),
         compiler_params=PARAMS,
         name="place",
@@ -173,13 +182,14 @@
     payload,
     embedded,
     normed,
+    arrived_in,
     query_in,
     keyvalue_in,
     keys_in,
     values_in,
     sems,
 ):
-    moves = []
+    moves = [(arrived, arrived_in)]
     third = query_weight.shape[0] // 3
     for k in range(3):
         span = pl.ds(k * third, third)
@@ -193,7 +203,8 @@
     drafts = tokens // slots
     heads = query_weight.shape[1] // size
     own = payload.shape[1]
-    rows_in = (rows_of(arrived, places) + extra[...].astype(F32)).astype(BF)
+    copies[0].wait()
+    rows_in = (rows_of(arrived_in, places) + extra[...].astype(F32)).astype(BF)
     embedded[...] = rows_in
     wide = rows_in.astype(F32)
     factor = lax.rsqrt(jnp.mean(wide * wide, axis=-1, keepdims=True) + 1e-05)
@@ -201,15 +212,15 @@
     normed[...] = rows_norm
     queries = None
     for k in range(3):
-        copies[k].wait()
+        copies[k + 1].wait()
         span = slice(k * third, (k + 1) * third)
         part = dot_nn(rows_norm[:, span], query_in[span, :])
         queries = part if queries is None else queries + part
     queries = queries.astype(BF)
-    copies[3].wait()
+    copies[4].wait()
     keyvalue = dot_nn(rows_norm, keyvalue_in[...]).astype(BF)
-    copies[4].wait()
     copies[5].wait()
+    copies[6].wait()
     member = ints[8]
     scale = size ** (-0.5)
     rows = heads * drafts
@@ -261,20 +272,21 @@
     tokens, width = extra.shape
     members = arrived.shape[0]
     wide = query_weight.shape[1] + AUX
+    far = (arrived, query_weight, keyvalue_weight, keys, values)
+    outs = [
+        jax.ShapeDtypeStruct((members, tokens // members, wide), BF),
+        jax.ShapeDtypeStruct((tokens, width), BF),
+        jax.ShapeDtypeStruct((tokens, width), BF),
+    ]
     return pl.pallas_call(
         attend_kernel,
-        in_specs=scalars(1) + whole(4) + streamed(4),
-        out_specs=whole(3),
-        out_shape=[
-            jax.ShapeDtypeStruct((members, tokens // members, wide), BF),
-            jax.ShapeDtypeStruct((tokens, width), BF),
-            jax.ShapeDtypeStruct((tokens, width), BF),
-        ],
-        scratch_shapes=[
-            pltpu.VMEM(a.shape, a.dtype) for a in (query_weight, keyvalue_weight, keys, values)
-        ]
-        + [pltpu.SemaphoreType.DMA((6,))],
-        compiler_params=pltpu.CompilerParams(vmem_limit_bytes=28 << 20),
+        grid=(1,),
+        in_specs=scalars(1) + streamed(1) + whole([places, extra, gain]) + streamed(4),
+        out_specs=whole(outs),
+        out_shape=outs,
+        scratch_shapes=[pltpu.VMEM(a.shape, a.dtype) for a in far]
+        + [pltpu.SemaphoreType.DMA((7,))],
+        compiler_params=PARAMS,
         cost_estimate=cost(
             2 * tokens * query_weight.size * 2, 2 * (query_weight.size + keys.size * 2), keys.size
         ),
@@ -306,18 +318,38 @@
     mamba_out,
     blocks,
     chosen,
+    proj_in,
+    input_in,
+    gate_in,
+    states_in,
+    out_in,
+    sems,
 ):
+    moves = (
+        (state_proj, proj_in),
+        (input_weight, input_in),
+        (gate_weight, gate_in),
+        (states, states_in),
+        (mamba_out, out_in),
+    )
+    copies = [pltpu.make_async_copy(a, b, sems.at[n]) for n, (a, b) in enumerate(moves)]
+    for copy in copies:
+        copy.start()
     slots = states.shape[0]
     tokens = normed.shape[0]
     drafts = tokens // slots
     rows = normed[...]
-    x_all = dot_nn(rows, input_weight[...])
-    z_all = dot_nn(rows, gate_weight[...])
-    both = dot_nn(rows, state_proj[...])
     step_in = (
         jnp.sum(rows.astype(F32) * step_row[...].astype(F32), axis=1, keepdims=True) + reals[0]
     )
     sizes = jnp.maximum(step_in, 0.0) + jnp.log1p(jnp.exp(-jnp.abs(step_in)))
+    copies[0].wait()
+    both = dot_nn(rows, proj_in[...])
+    copies[1].wait()
+    x_all = dot_nn(rows, input_in[...])
+    copies[2].wait()
+    z_all = dot_nn(rows, gate_in[...])
+    copies[3].wait()
     state_size = both.shape[1] // 2
     row = lax.broadcasted_iota(jnp.int32, (drafts, drafts), 0)
     col = lax.broadcasted_iota(jnp.int32, (drafts, drafts), 1)
@@ -338,7 +370,7 @@
         x = x_all[span]
         z = z_all[span]
         inputs = size_t * x
-        start = states[slot, 0]
+        start = states_in[slot, 0]
         weights = dot_nt(state_read, state_in, HI) * between
         readout = dot_nn(weights, inputs, HI) + jnp.exp(log_decay) * dot_nt(
             state_read, start, HI
@@ -350,7 +382,8 @@
             jnp.exp(last) * start + dot_tn(remain * inputs, state_in, HI)
         ).astype(BF)
         gated.append((readout * (z / (1.0 + jnp.exp(-z)))).astype(BF))
-    part = dot_nn(jnp.concatenate(gated, axis=0), mamba_out[...])
+    copies[4].wait()
+    part = dot_nn(jnp.concatenate(gated, axis=0), out_in[...])
     share = part.shape[1] // blocks.shape[0]
     for j in range(blocks.shape[0]):
         blocks[j] = fold(part[:, j * share : (j + 1) * share]).astype(BF)
@@ -359,14 +392,23 @@
 def mamba(ints, reals, normed, input_weight, gate_weight, state_proj, step_row, states, mamba_out, members):
     tokens = normed.shape[0]
     share = mamba_out.shape[1] // members
+    outs = [
+        jax.ShapeDtypeStruct((members, tokens * share // AUX, AUX), BF),
+        jax.ShapeDtypeStruct(states.shape, BF),
+    ]
+    far = (state_proj, input_weight, gate_weight, states, mamba_out)
     return pl.pallas_call(
         mamba_kernel,
-        in_specs=scalars(2) + whole(7),
-        out_specs=whole(2),
-        out_shape=[
-            jax.ShapeDtypeStruct((members, tokens * share // AUX, AUX), BF),
-            jax.ShapeDtypeStruct(states.shape, BF),
-        ],
+        grid=(1,),
+        in_specs=scalars(2)
+        + whole([normed])
+        + streamed(3)
+        + whole([step_row])
+        + streamed(2),
+        out_specs=whole(outs),
+        out_shape=outs,
+        scratch_shapes=[pltpu.VMEM(a.shape, a.dtype) for a in far]
+        + [pltpu.SemaphoreType.DMA((5,))],
         compiler_params=PARAMS,
         cost_estimate=cost(2 * tokens * state_proj.size * 2, 4 * state_proj.size, tokens * 4096),
         name="mamba",
@@ -394,11 +436,13 @@
 def join(parts, blocks, heads, size):
     members, tokens, share = blocks.shape
     own = parts.shape[1]
+    out = jax.ShapeDtypeStruct((members, tokens + heads * own, share), BF)
     return pl.pallas_call(
         functools.partial(join_kernel, heads=heads, size=size),
-        in_specs=whole(2),
-        out_specs=whole(1)[0],
-        out_shape=jax.ShapeDtypeStruct((members, tokens + heads * own, share), BF),
+        grid=(1,),
+        in_specs=whole([parts, blocks]),
+        out_specs=whole([out])[0],
+        out_shape=out,
         compiler_params=PARAMS,
         name="join",
     )(parts, blocks)
@@ -422,11 +466,13 @@
 
 def project(parts, out_weight, packed, heads, size):
     members = parts.shape[0]
+    out = jax.ShapeDtypeStruct((members, packed, AUX), BF)
     return pl.pallas_call(
         functools.partial(project_kernel, heads=heads, size=size),
-        in_specs=whole(2),
-        out_specs=whole(1)[0],
-        out_shape=jax.ShapeDtypeStruct((members, packed, AUX), BF),
+        grid=(1,),
+        in_specs=whole([parts, out_weight]),
+        out_specs=whole([out])[0],
+        out_shape=out,
         compiler_params=PARAMS,
         name="project",
     )(parts, out_weight)
@@ -486,20 +532,53 @@
     tokens, width = embedded.shape
     units = sum(w.shape[0] for w in weights) // 3
     count = 3 * units // min(w.shape[0] for w in weights)
+    outs = [
+        jax.ShapeDtypeStruct((members, tokens // members, width), BF),
+        jax.ShapeDtypeStruct((tokens, width), BF),
+    ]
     return pl.pallas_call(
         functools.partial(feed_kernel, count=len(weights)),
-        in_specs=whole(3) + streamed(len(weights)),
-        out_specs=whole(2),
-        out_shape=[
-            jax.ShapeDtypeStruct((members, tokens // members, width), BF),
-            jax.ShapeDtypeStruct((tokens, width), BF),
-        ],
+        grid=(1,),
+        in_specs=whole([spread, embedded, gain]) + streamed(len(weights)),
+        out_specs=whole(outs),
+        out_shape=outs,
         scratch_shapes=[pltpu.VMEM((units, width), BF)] * 3
         + [pltpu.SemaphoreType.DMA((count, 3))],
-        compiler_params=pltpu.CompilerParams(vmem_limit_bytes=36 << 20),
+        compiler_params=PARAMS,
         cost_estimate=cost(6 * tokens * units * width, 6 * units * width),
         name="feed",
     )(spread, embedded, gain, *weights)
+
+
+def pack_kernel(gate, up, down, ready, low, high, sems):
+    half = low.shape[0] // 3
+    copies = []
+    for k, part in enumerate((gate, up, down)):
+        for h, out in enumerate((low, high)):
+            copy = pltpu.make_async_copy(
+                part.at[pl.ds(h * half, half), :],
+                out.at[pl.ds(k * half, half), :],
+                sems.at[k, h],
+            )
+            copy.start()
+            copies.append(copy)
+    for copy in copies:
+        copy.wait()
+
+
+def pack(gate, up, down, ready):
+    units, width = gate.shape
+    out = jax.ShapeDtypeStruct((3 * units // 2, width), gate.dtype)
+    return pl.pallas_call(
+        pack_kernel,
+        in_specs=streamed(4),
+        out_specs=streamed(2),
+        out_shape=[out, out],
+        scratch_shapes=[pltpu.SemaphoreType.DMA((3, 2))],
+        compiler_params=PARAMS,
+        cost_estimate=cost(0, 1024),
+        name="pack",
+    )(gate, up, down, ready)
 
 
 def pick_kernel(turns, rows, *refs):
@@ -515,11 +594,13 @@
 
 def pick_states(turns, rows, held, count):
     shape = (count,) + held[0].shape[1:]
+    out = jax.ShapeDtypeStruct(shape, F32)
     return pl.pallas_call(
         pick_kernel,
-        in_specs=scalars(2) + whole(len(held)),
-        out_specs=whole(1)[0],
-        out_shape=jax.ShapeDtypeStruct(shape, F32),
+        grid=(1,),
+        in_specs=scalars(2) + whole(held),
+        out_specs=whole([out])[0],
+        out_shape=out,
         compiler_params=PARAMS,
         name="pick",
     )(turns, rows, *held)
@@ -588,16 +669,10 @@
 
     sent, slots, places, most = exchange(jnp.int32(0))
 
-    half = gate_weight.shape[1] // 2
-    *trio, _ = lax.optimization_barrier((gate_weight.T, up_weight.T, down_weight.T, sent))
-    low = jnp.concatenate([w[:half] for w in trio], axis=0)
-    high = jnp.concatenate([w[half:] for w in trio], axis=0)
-    own_weights = jnp.concatenate([low, high], axis=0)
-    own_weights, slots = lax.optimization_barrier((own_weights, slots))
+    low, high = pack(gate_weight.T, up_weight.T, down_weight.T, sent)
+    low, high, _ = lax.optimization_barrier((low, high, slots))
     arrived = spread_slots(slots)
-    from_below = turn(own_weights, 1)
-    from_above = turn(own_weights, -1)
-    weights = [own_weights, from_below, from_above]
+    near = [turn(low, 1), turn(high, -1), turn(high, 1), turn(low, -1)]
 
     def more(carry):
         return carry[0] < most
@@ -641,15 +716,14 @@
         mamba_out,
         members,
     )
-    from_below, from_above, parts, chosen = lax.optimization_barrier(
-        (from_below, from_above, parts, chosen)
-    )
-    far = [turn(from_below[: 3 * half], 1), turn(from_above[3 * half :], -1)]
+    *near, chosen, _ = lax.optimization_barrier((*near, chosen, parts))
+    far = [turn(near[0], 1), turn(near[1], -1)]
+    weights = [low, high] + near
     weights += [across(w) for w in weights]
     joined = lax.all_to_all(join(parts, blocks, query_heads, head_size), "tok", 0, 0, tiled=True)
-    *far, joined = lax.optimization_barrier((*far, joined))
+    spread = project(joined, attention_out.T, blocks.shape[1], query_heads, head_size)
+    *far, _ = lax.optimization_barrier((*far, spread))
     weights += far + [across(w) for w in far]
-    spread = project(joined, attention_out.T, blocks.shape[1], query_heads, head_size)
     added = lax.all_to_all(spread, "tok", 0, 0, tiled=True)
     mlp_part, mixed = feed(added, embedded, mlp_gain[None], weights)
     mlp_rows = lax.all_to_all(mlp_part, "tok", 0, 0, tiled=True)

time: 165 us -> 200 us (1.21)
  Pallas kernels: 24.9 us -> 88.8 us
  local copies, waits for them, and re-layouts: 33.3 us -> 8.09 us
  waiting for transfers between devices: 51.4 us -> 43.6 us
  starting transfers between devices: 46.2 us -> 49.2 us
    pallas_call x6 -> x7, Pallas kernels: 23.8 us -> 86.6 us  [the longest x1 54.8 us: pack(): pl.pallas_call(pack_kernel, in_specs=streamed(4), out_specs=streamed(2),...]
    unnamed x76 -> x31, local copies, waits for them, and re-layouts: 24.2 us -> 3.54 us
    all_to_all x1, waiting for transfers between devices: 17.5 us -> 0.01 us  [spread_slots(): return lax.all_to_all(spread, 'tok', 0, 0, tiled=True)]
    ppermute x7 -> x9, waiting for transfers between devices: 13.6 us -> 19 us  [turn(): lax.ppermute(value, 'req', [(g, (g + by * cores) % groups) for g in range...]
    slice x2 -> x0, local copies, waits for them, and re-layouts: 4.36 us -> none  [local(): far = [turn(from_below[:3 * half], 1), turn(from_above[3 * half:], -1)]]
    all_to_all x1, starting transfers between devices: 3.51 us -> 7.23 us  [local(): parts = lax.all_to_all(payload, 'tok', 0, 0, tiled=True)]
    all_to_all x1, starting transfers between devices: 6.69 us -> 3.74 us  [local(): added = lax.all_to_all(spread, 'tok', 0, 0, tiled=True)]
    all_to_all x1, waiting for transfers between devices: 4.19 us -> 6.34 us  [local(): added = lax.all_to_all(spread, 'tok', 0, 0, tiled=True)]
  transfers between devices with their start and end apart: 19 -> 24, of which waited for: 7 -> 8; matrix products, arithmetic and copies ran while one was open for 6% -> 3% of each run, Pallas kernels for 13% -> 43%
where the time goes in v4:
time: 200 us; the launch traced here: 199 us
  Pallas kernels  88.8 us (44%)
  starting transfers between devices  49.2 us (25%)
  waiting for transfers between devices  43.6 us (22%)
  local copies, waits for them, and re-layouts  8.09 us (4%)
  other arithmetic  5.22 us (3%)
  between operations  2.92 us (1%)
    pallas_call x1, Pallas kernels, pack(): pl.pallas_call(pack_kernel, in_specs=streamed(4), out_specs=streamed(2),...  54.8 us
    ppermute x9, waiting for transfers between devices, turn(): lax.ppermute(value, 'req', [(g, (g + by * cores) % groups) for g in range...  19 us
    ppermute x9, starting transfers between devices, turn(): lax.ppermute(value, 'req', [(g, (g + by * cores) % groups) for g in range...  13.4 us
    all_to_all x1, waiting for transfers between devices, exchange(): slots = lax.all_to_all(payload, 'req', 0, 0, tiled=True)  11.9 us
    pallas_call x1, Pallas kernels, feed(): pl.pallas_call(functools.partial(feed_kernel, count=len(weights)), grid=(...  9.14 us
    all_to_all x1, starting transfers between devices, local(): parts = lax.all_to_all(payload, 'tok', 0, 0, tiled=True)  7.23 us
    pallas_call x1, Pallas kernels, attend(): pl.pallas_call(attend_kernel, grid=(1,), in_specs=scalars(1) + streamed(1...  7.15 us
    all_to_all x1, starting transfers between devices, local(): lax.all_to_all(join(parts, blocks, query_heads, head_size), 'tok', 0, 0,...  7.06 us
  transfers between devices with their start and end apart: 24, of which 8 were waited for; matrix products, arithmetic and copies ran while one was open for 3% of the time, Pallas kernels for 43%

profile of v4, /device:TPU:0, one launch (start us, length us, event | category | flops | bytes accessed | tf_op | source)
XLA Modules:
  0.0 198.5 jit_solution(3889838849863731785)
XLA Ops:
  0.7 0.8 copy.33.draft_ids
  1.4 0.6 pad_add_fusion.2.ints
  2.0 4.0 %fetch.5 = (bf16[8,16,3072]{2,1,0:T(8,128)(2,1)}, s32[64,128]{1,0:T(8,128)}, s32[8,128]{1,0:T(8,128)}) custom-call(s32[3]{0:T(128)} %pad_add_fusion.2.ints, s32[1,32]{1,0:T(1,128)} %bitcast.27, s32[32,16]{1,0:T(8,128)S(1)} %copy.33.draft_ids, bf16[512,3072]{1,0:T(8,128)(2,1)} %table_far.1), custom_call_target="tpu_custom_call" | custom-call | flops 402653184 | bytes 3145728 | tf_op jit(solution)/shard_map/fetch/pallas_call | solution.py:134
  6.1 5.4 %all-to-all-start.2 = ((bf16[8,16,3072]{2,1,0:T(8,128)(2,1)}), bf16[8,16,3072]{2,1,0:T(8,128)(2,1)S(1)}, u32[]{:S(2)}, u32[]{:S(2)}) async-start(bf16[8,16,3072]{2,1,0:T(8,128)(2,1)} %get-tuple-element.126.ready), calls=%async_computation.2 | async-start | bytes 1572864 | tf_op jit(solution)/shard_map/all_to_all | solution.py:662
  11.5 1.3 slice.3
  12.7 11.9 %all-to-all-done.2 = bf16[8,16,3072]{2,1,0:T(8,128)(2,1)S(1)} async-done(((bf16[8,16,3072]{2,1,0:T(8,128)(2,1)}), bf16[8,16,3072]{2,1,0:T(8,128)(2,1)S(1)}, u32[]{:S(2)}, u32[]{:S(2)}) %all-to-all-start.2) | async-done | bytes 786464 | tf_op jit(solution)/shard_map/all_to_all | solution.py:662
  24.8 0.7 while.12
  25.5 1.3 broadcast_in_dim.71
  26.8 7.0 %all-to-all-start.3 = ((bf16[16,16,3072]{2,1,0:T(8,128)(2,1)}), bf16[16,16,3072]{2,1,0:T(8,128)(2,1)S(1)}, u32[]{:S(2)}, u32[]{:S(2)}) async-start(bf16[16,16,3072]{2,1,0:T(8,128)(2,1)} %broadcast_in_dim.71), calls=%async_computation.3 | async-start | bytes 3145728 | tf_op jit(solution)/shard_map/all_to_all | solution.py:668
  33.9 54.8 %pack.1 = (bf16[144,3072]{1,0:T(8,128)(2,1)}, bf16[144,3072]{1,0:T(8,128)(2,1)}) custom-call(bf16[96,3072]{1,0:T(8,128)(2,1)} %bitcast.29, bf16[96,3072]{1,0:T(8,128)(2,1)} %bitcast.30, bf16[96,3072]{1,0:T(8,128)(2,1)} %bitcast.31, bf16[8,16,3072]{2,1,0:T(8,128)(2,1)} %get-tuple-element.126.ready), custom_call_target="tpu_custom_call" | custom-call | bytes 1024 | tf_op jit(solution)/shard_map/pack/pallas_call | solution.py:572
  88.6 0.6 collective-permute-start
  89.3 2.7 %collective-permute-start.1 = (bf16[144,3072]{1,0:T(8,128)(2,1)}, bf16[144,3072]{1,0:T(8,128)(2,1)}, u32[]{:S(2)}, u32[]{:S(2)}) collective-permute-start(bf16[144,3072]{1,0:T(8,128)(2,1)} %get-tuple-element.137.refs_1_), channel_id=1, source_target_pairs={{0,96},{16,112},{32,0},{48,16},{64,32},{80,48},{96,64},{112,80},{1... | collective-permute-start | bytes 2654216 | tf_op jit(solution)/shard_map/ppermute | solution.py:650
  92.0 3.2 %collective-permute-start.3 = (bf16[144,3072]{1,0:T(8,128)(2,1)}, bf16[144,3072]{1,0:T(8,128)(2,1)}, u32[]{:S(2)}, u32[]{:S(2)}) collective-permute-start(bf16[144,3072]{1,0:T(8,128)(2,1)} %get-tuple-element.136.refs_0_), channel_id=1, source_target_pairs={{0,96},{16,112},{32,0},{48,16},{64,32},{80,48},{96,64},{112,80},{1... | collective-permute-start | bytes 2654216 | tf_op jit(solution)/shard_map/ppermute | solution.py:650
  95.4 0.6 gather_fusion
  96.0 0.6 gather_fusion.1
  98.7 0.6 pad_add_fusion.1.ints
  99.3 1.1 copy-done.4
  100.5 7.2 %attend.1 = (bf16[16,4,896]{2,1,0:T(4,128)(2,1)}, bf16[64,3072]{1,0:T(8,128)(2,1)}, bf16[64,3072]{1,0:T(8,128)(2,1)}) custom-call(s32[9]{0:T(128)} %pad_add_fusion.1.ints, bf16[16,16,3072]{2,1,0:T(8,128)(2,1)} %copy-done.4, s32[64,128]{1,0:T(8,128)} %get-tuple-element.127.places, bf16[64,3072]{1,0:T(8,128)(2,1)S(1)} %get-tuple-element.129.extra, ...), custom_call_target="tpu_custom_call" | custom-call | flops 603979776 | bytes 6815744 | tf_op jit(solution)/shard_map/attend/pallas_call | solution.py:281
  107.6 7.2 %all-to-all-start.4 = ((bf16[16,4,896]{2,1,0:T(4,128)(2,1)}), bf16[16,4,896]{2,1,0:T(4,128)(2,1)S(1)}, u32[]{:S(2)}, u32[]{:S(2)}) async-start(bf16[16,4,896]{2,1,0:T(4,128)(2,1)} %get-tuple-element.130), calls=%async_computation.4 | async-start | bytes 229376 | tf_op jit(solution)/shard_map/all_to_all | solution.py:706
  114.9 0.6 pad_maximum_fusion.1.reals
  115.5 6.8 %mamba.1 = (bf16[16,96,128]{2,1,0:T(8,128)(2,1)}, bf16[4,1,128,256]{3,2,1,0:T(8,128)(2,1)}) custom-call(s32[9]{0:T(128)} %pad_add_fusion.1.ints, f32[3]{0:T(128)} %pad_maximum_fusion.1.reals, bf16[64,3072]{1,0:T(8,128)(2,1)} %get-tuple-element.131.normed, bf16[3072,128]{1,0:T(8,128)(2,1)} %input_weight.1, bf16[3072,128]{1,0:T(8,128)(2,1)} %gate_weight.1, ...), custom_call_target="tpu_custom_call" | custom-call | flops 402653184 | bytes 6291456 | tf_op jit(solution)/shard_map/mamba/pallas_call | solution.py:400
  122.3 7.8 %collective-permute-done.2.refs_4_ = bf16[144,3072]{1,0:T(8,128)(2,1)} collective-permute-done((bf16[144,3072]{1,0:T(8,128)(2,1)}, bf16[144,3072]{1,0:T(8,128)(2,1)}, u32[]{:S(2)}, u32[]{:S(2)}) %collective-permute-start.2) | collective-permute-done | bytes 884768 | tf_op jit(solution)/shard_map/ppermute | solution.py:650
  130.1 0.3 collective-permute-start.10
  130.4 3.2 %collective-permute-start.11 = (bf16[144,3072]{1,0:T(8,128)(2,1)}, bf16[144,3072]{1,0:T(8,128)(2,1)}, u32[]{:S(2)}, u32[]{:S(2)}) collective-permute-start(bf16[144,3072]{1,0:T(8,128)(2,1)} %collective-permute-done.1.refs_3_), channel_id=1, source_target_pairs={{0,96},{16,112},{32,0},{48,16},{64,32},{80,48},{96,64},{112,80},{1... | collective-permute-start | bytes 2654216 | tf_op jit(solution)/shard_map/ppermute | solution.py:650
  133.6 0.5 collective-permute-start.5
  134.2 2.2 %join.1 = bf16[16,120,128]{2,1,0:T(8,128)(2,1)} custom-call(bf16[16,4,896]{2,1,0:T(4,128)(2,1)} %copy-done.13, bf16[16,96,128]{2,1,0:T(8,128)(2,1)} %get-tuple-element.132.blocks), custom_call_target="tpu_custom_call" | custom-call | tf_op jit(solution)/shard_map/join/pallas_call | solution.py:440
  136.4 7.1 %all-to-all-start.5 = ((bf16[16,120,128]{2,1,0:T(8,128)(2,1)}), bf16[16,120,128]{2,1,0:T(8,128)(2,1)S(1)}, u32[]{:S(2)}, u32[]{:S(2)}) async-start(bf16[16,120,128]{2,1,0:T(8,128)(2,1)} %join.1), calls=%async_computation.5 | async-start | bytes 983040 | tf_op jit(solution)/shard_map/all_to_all | solution.py:723
  143.4 8.4 %collective-permute-done.10.refs_12_ = bf16[144,3072]{1,0:T(8,128)(2,1)} collective-permute-done((bf16[144,3072]{1,0:T(8,128)(2,1)}, bf16[144,3072]{1,0:T(8,128)(2,1)}, u32[]{:S(2)}, u32[]{:S(2)}) %collective-permute-start.10) | collective-permute-done | bytes 884768 | tf_op jit(solution)/shard_map/ppermute | solution.py:650
  151.9 3.3 %all-to-all-done.5.parts = bf16[16,120,128]{2,1,0:T(8,128)(2,1)S(1)} async-done(((bf16[16,120,128]{2,1,0:T(8,128)(2,1)}), bf16[16,120,128]{2,1,0:T(8,128)(2,1)S(1)}, u32[]{:S(2)}, u32[]{:S(2)}) %all-to-all-start.5) | async-done | bytes 491552 | tf_op jit(solution)/shard_map/all_to_all | solution.py:723
  155.2 0.8 copy-done.6
  156.0 2.3 %project.1 = bf16[16,96,128]{2,1,0:T(8,128)(2,1)} custom-call(bf16[16,120,128]{2,1,0:T(8,128)(2,1)} %copy-done.6, bf16[192,768]{1,0:T(8,128)(2,1)} %bitcast.33), custom_call_target="tpu_custom_call" | custom-call | tf_op jit(solution)/shard_map/project/pallas_call | solution.py:470
  158.3 0.5 collective-permute-start.8
  158.9 0.4 collective-permute-start.12
  159.4 3.7 %all-to-all-start.6 = ((bf16[16,96,128]{2,1,0:T(8,128)(2,1)}), bf16[16,96,128]{2,1,0:T(8,128)(2,1)S(1)}, u32[]{:S(2)}, u32[]{:S(2)}) async-start(bf16[16,96,128]{2,1,0:T(8,128)(2,1)} %project.1), calls=%async_computation.6 | async-start | bytes 786432 | tf_op jit(solution)/shard_map/all_to_all | solution.py:727
  163.4 0.6 gather_fusion.2
  164.2 2.7 %collective-permute-start.16 = (bf16[8,128,256]{2,1,0:T(8,128)(2,1)S(1)}, bf16[8,128,256]{2,1,0:T(8,128)(2,1)}, u32[]{:S(2)}, u32[]{:S(2)}) collective-permute-start(bf16[8,128,256]{2,1,0:T(8,128)(2,1)S(1)} %pad_maximum_fusion.refs_0_), channel_id=1, source_target_pairs={{0,64},{16,80},{32,96},{48,112},{64,0},{80,16},{96,32},{112,48},{1... | collective-permute-start | bytes 1572872 | tf_op jit(solution)/shard_map/ppermute | solution.py:650
  166.9 0.6 collective-permute-start.17
  167.5 6.3 %all-to-all-done.6.spread = bf16[16,96,128]{2,1,0:T(8,128)(2,1)S(1)} async-done(((bf16[16,96,128]{2,1,0:T(8,128)(2,1)}), bf16[16,96,128]{2,1,0:T(8,128)(2,1)S(1)}, u32[]{:S(2)}, u32[]{:S(2)}) %all-to-all-start.6) | async-done | bytes 393248 | tf_op jit(solution)/shard_map/all_to_all | solution.py:727
  173.9 0.7 copy-done.7
  174.6 9.1 %feed.1 = (bf16[16,4,3072]{2,1,0:T(4,128)(2,1)}, bf16[64,3072]{1,0:T(8,128)(2,1)}) custom-call(bf16[16,96,128]{2,1,0:T(8,128)(2,1)} %copy-done.7, bf16[64,3072]{1,0:T(8,128)(2,1)} %get-tuple-element.133.embedded, f32[1,3072]{1,0:T(1,128)} %bitcast.38, bf16[144,3072]{1,0:T(8,128)(2,1)} %get-tuple-element.136.refs_0_, ...), custom_call_target="tpu_custom_call" | custom-call | flops 905969664 | bytes 14155776 | tf_op jit(solution)/shard_map/feed/pallas_call | solution.py:539
  183.8 3.6 %all-to-all-start.7 = ((bf16[16,4,3072]{2,1,0:T(4,128)(2,1)}), bf16[16,4,3072]{2,1,0:T(4,128)(2,1)S(1)}, u32[]{:S(2)}, u32[]{:S(2)}) async-start(bf16[16,4,3072]{2,1,0:T(4,128)(2,1)} %get-tuple-element.146), calls=%async_computation.7 | async-start | bytes 786432 | tf_op jit(solution)/shard_map/all_to_all | solution.py:729
  187.4 0.6 fusion
  188.0 0.6 and_select_fusion.3.turns
  188.6 2.1 %collective-permute-done.15.refs_1_ = bf16[8,128,256]{2,1,0:T(8,128)(2,1)S(1)} collective-permute-done((bf16[8,128,256]{2,1,0:T(8,128)(2,1)S(1)}, bf16[8,128,256]{2,1,0:T(8,128)(2,1)S(1)}, u32[]{:S(2)}, u32[]{:S(2)}) %collective-permute-start.15) | collective-permute-done | bytes 524320 | tf_op jit(solution)/shard_map/ppermute | solution.py:650
  190.7 0.7 collective-permute-done.17.refs_3_
  191.5 2.5 %pick.1 = f32[4,128,256]{2,1,0:T(8,128)} custom-call(s32[4]{0:T(128)} %and_select_fusion.3.turns, s32[4]{0:T(128)} %get-tuple-element.194.rows, bf16[8,128,256]{2,1,0:T(8,128)(2,1)} %copy-done.5, bf16[8,128,256]{2,1,0:T(8,128)(2,1)} %copy-done.12, bf16[8,128,256]{2,1,0:T(8,128)(2,1)} %collective-permute-done.16.refs_2_, ...), custom_call_target="tpu_custom_call" | custom-call | tf_op jit(solution)/shard_map/pick/pallas_call | solution.py:598
  194.0 3.0 %all-to-all-done.7 = bf16[16,4,3072]{2,1,0:T(4,128)(2,1)S(1)} async-done(((bf16[16,4,3072]{2,1,0:T(4,128)(2,1)}), bf16[16,4,3072]{2,1,0:T(4,128)(2,1)S(1)}, u32[]{:S(2)}, u32[]{:S(2)}) %all-to-all-start.7) | async-done | bytes 393248 | tf_op jit(solution)/shard_map/all_to_all | solution.py:729
  197.1 1.4 add_convert_fusion
  (62 shorter events, 1.4 us)
Async XLA Ops:
  0.6 94.8 %copy-start = (s32[32]{0:T(128)S(1)}, s32[32]{0:T(128)}, u32[]{:S(2)}) copy-start(s32[32]{0:T(128)} %param.30) | copy-start | bytes 388
  6.0 18.7 %copy-start.1 = (s32[32]{0:T(128)S(1)}, s32[32]{0:T(128)}, u32[]{:S(2)}) copy-start(s32[32]{0:T(128)} %param.31) | copy-start | bytes 388
  6.1 18.6 %all-to-all-start.2 = ((bf16[8,16,3072]{2,1,0:T(8,128)(2,1)}), bf16[8,16,3072]{2,1,0:T(8,128)(2,1)S(1)}, u32[]{:S(2)}, u32[]{:S(2)}) async-start(bf16[8,16,3072]{2,1,0:T(8,128)(2,1)} %get-tuple-element.126.ready), calls=%async_computation.2 | async-start | bytes 1572864 | tf_op jit(solution)/shard_map/all_to_all | solution.py:662
  26.8 72.5 %all-to-all-start.3 = ((bf16[16,16,3072]{2,1,0:T(8,128)(2,1)}), bf16[16,16,3072]{2,1,0:T(8,128)(2,1)S(1)}, u32[]{:S(2)}, u32[]{:S(2)}) async-start(bf16[16,16,3072]{2,1,0:T(8,128)(2,1)} %broadcast_in_dim.71), calls=%async_computation.3 | async-start | bytes 3145728 | tf_op jit(solution)/shard_map/all_to_all | solution.py:668
  33.9 62.2 %copy-start.2 = (s32[32]{0:T(128)S(1)}, s32[32]{0:T(128)}, u32[]{:S(2)}) copy-start(s32[32]{0:T(128)} %param.33) | copy-start | bytes 388
  88.6 33.7 %collective-permute-start = (bf16[144,3072]{1,0:T(8,128)(2,1)}, bf16[144,3072]{1,0:T(8,128)(2,1)}, u32[]{:S(2)}, u32[]{:S(2)}) collective-permute-start(bf16[144,3072]{1,0:T(8,128)(2,1)} %get-tuple-element.136.refs_0_), channel_id=1, source_target_pairs={{0,32},{16,48},{32,64},{48,80},{64,96},{80,112},{96,0},{112,16},{1... | collective-permute-start | bytes 2654216 | tf_op jit(solution)/shard_map/ppermute | solution.py:650
  89.3 33.1 %collective-permute-start.1 = (bf16[144,3072]{1,0:T(8,128)(2,1)}, bf16[144,3072]{1,0:T(8,128)(2,1)}, u32[]{:S(2)}, u32[]{:S(2)}) collective-permute-start(bf16[144,3072]{1,0:T(8,128)(2,1)} %get-tuple-element.137.refs_1_), channel_id=1, source_target_pairs={{0,96},{16,112},{32,0},{48,16},{64,32},{80,48},{96,64},{112,80},{1... | collective-permute-start | bytes 2654216 | tf_op jit(solution)/shard_map/ppermute | solution.py:650
  91.9 38.2 %collective-permute-start.2 = (bf16[144,3072]{1,0:T(8,128)(2,1)}, bf16[144,3072]{1,0:T(8,128)(2,1)}, u32[]{:S(2)}, u32[]{:S(2)}) collective-permute-start(bf16[144,3072]{1,0:T(8,128)(2,1)} %get-tuple-element.137.refs_1_), channel_id=1, source_target_pairs={{0,32},{16,48},{32,64},{48,80},{64,96},{80,112},{96,0},{112,16},{1... | collective-permute-start | bytes 2654216 | tf_op jit(solution)/shard_map/ppermute | solution.py:650
  92.0 38.2 %collective-permute-start.3 = (bf16[144,3072]{1,0:T(8,128)(2,1)}, bf16[144,3072]{1,0:T(8,128)(2,1)}, u32[]{:S(2)}, u32[]{:S(2)}) collective-permute-start(bf16[144,3072]{1,0:T(8,128)(2,1)} %get-tuple-element.136.refs_0_), channel_id=1, source_target_pairs={{0,96},{16,112},{32,0},{48,16},{64,32},{80,48},{96,64},{112,80},{1... | collective-permute-start | bytes 2654216 | tf_op jit(solution)/shard_map/ppermute | solution.py:650
  99.3 1.1 copy-start.4
  107.6 22.5 %all-to-all-start.4 = ((bf16[16,4,896]{2,1,0:T(4,128)(2,1)}), bf16[16,4,896]{2,1,0:T(4,128)(2,1)S(1)}, u32[]{:S(2)}, u32[]{:S(2)}) async-start(bf16[16,4,896]{2,1,0:T(4,128)(2,1)} %get-tuple-element.130), calls=%async_computation.4 | async-start | bytes 229376 | tf_op jit(solution)/shard_map/all_to_all | solution.py:706
  115.5 18.1 %copy-start.8 = (bf16[144,3072]{1,0:T(8,128)(2,1)S(1)}, bf16[144,3072]{1,0:T(8,128)(2,1)}, u32[]{:S(2)}) copy-start(bf16[144,3072]{1,0:T(8,128)(2,1)} %get-tuple-element.136.refs_0_) | copy-start | bytes 2654212
  115.5 18.1 %copy-start.9 = (bf16[144,3072]{1,0:T(8,128)(2,1)S(1)}, bf16[144,3072]{1,0:T(8,128)(2,1)}, u32[]{:S(2)}) copy-start(bf16[144,3072]{1,0:T(8,128)(2,1)} %get-tuple-element.137.refs_1_) | copy-start | bytes 2654212
  122.3 29.6 %copy-start.14 = (bf16[4,1,128,256]{3,2,1,0:T(8,128)(2,1)S(1)}, bf16[4,1,128,256]{3,2,1,0:T(8,128)(2,1)}, u32[]{:S(2)}) copy-start(bf16[4,1,128,256]{3,2,1,0:T(8,128)(2,1)} %get-tuple-element.147) | copy-start | bytes 786436
  130.1 4.1 %copy-start.13 = (bf16[16,4,896]{2,1,0:T(4,128)(2,1)}, bf16[16,4,896]{2,1,0:T(4,128)(2,1)S(1)}, u32[]{:S(2)}) copy-start(bf16[16,4,896]{2,1,0:T(4,128)(2,1)S(1)} %all-to-all-done.4.parts) | copy-start | bytes 344068
  130.1 21.8 %collective-permute-start.10 = (bf16[144,3072]{1,0:T(8,128)(2,1)}, bf16[144,3072]{1,0:T(8,128)(2,1)}, u32[]{:S(2)}, u32[]{:S(2)}) collective-permute-start(bf16[144,3072]{1,0:T(8,128)(2,1)} %collective-permute-done.refs_2_), channel_id=1, source_target_pairs={{0,32},{16,48},{32,64},{48,80},{64,96},{80,112},{96,0},{112,16},{1... | collective-permute-start | bytes 2654216 | tf_op jit(solution)/shard_map/ppermute | solution.py:650
  130.4 27.9 %collective-permute-start.11 = (bf16[144,3072]{1,0:T(8,128)(2,1)}, bf16[144,3072]{1,0:T(8,128)(2,1)}, u32[]{:S(2)}, u32[]{:S(2)}) collective-permute-start(bf16[144,3072]{1,0:T(8,128)(2,1)} %collective-permute-done.1.refs_3_), channel_id=1, source_target_pairs={{0,96},{16,112},{32,0},{48,16},{64,32},{80,48},{96,64},{112,80},{1... | collective-permute-start | bytes 2654216 | tf_op jit(solution)/shard_map/ppermute | solution.py:650
  133.6 24.7 %collective-permute-start.4 = (bf16[144,3072]{1,0:T(8,128)(2,1)S(1)}, bf16[144,3072]{1,0:T(8,128)(2,1)}, u32[]{:S(2)}, u32[]{:S(2)}) collective-permute-start(bf16[144,3072]{1,0:T(8,128)(2,1)S(1)} %copy-done.8), channel_id=1, source_target_pairs={{0,16},{16,0},{32,48},{48,32},{64,80},{80,64},{96,112},{112,96},{1... | collective-permute-start | bytes 2654216 | tf_op jit(solution)/shard_map/ppermute | solution.py:655
  133.6 25.2 %collective-permute-start.5 = (bf16[144,3072]{1,0:T(8,128)(2,1)S(1)}, bf16[144,3072]{1,0:T(8,128)(2,1)}, u32[]{:S(2)}, u32[]{:S(2)}) collective-permute-start(bf16[144,3072]{1,0:T(8,128)(2,1)S(1)} %copy-done.9), channel_id=1, source_target_pairs={{0,16},{16,0},{32,48},{48,32},{64,80},{80,64},{96,112},{112,96},{1... | collective-permute-start | bytes 2654216 | tf_op jit(solution)/shard_map/ppermute | solution.py:655
  134.1 25.2 %collective-permute-start.6 = (bf16[144,3072]{1,0:T(8,128)(2,1)}, bf16[144,3072]{1,0:T(8,128)(2,1)}, u32[]{:S(2)}, u32[]{:S(2)}) collective-permute-start(bf16[144,3072]{1,0:T(8,128)(2,1)} %collective-permute-done.refs_2_), channel_id=1, source_target_pairs={{0,16},{16,0},{32,48},{48,32},{64,80},{80,64},{96,112},{112,96},{1... | collective-permute-start | bytes 2654216 | tf_op jit(solution)/shard_map/ppermute | solution.py:655
  136.4 26.8 %copy-start.15 = (s32[32]{0:T(128)S(1)}, s32[32]{0:T(128)}, u32[]{:S(2)}) copy-start(s32[32]{0:T(128)} %param.32) | copy-start | bytes 388
  136.4 18.9 %all-to-all-start.5 = ((bf16[16,120,128]{2,1,0:T(8,128)(2,1)}), bf16[16,120,128]{2,1,0:T(8,128)(2,1)S(1)}, u32[]{:S(2)}, u32[]{:S(2)}) async-start(bf16[16,120,128]{2,1,0:T(8,128)(2,1)} %join.1), calls=%async_computation.5 | async-start | bytes 983040 | tf_op jit(solution)/shard_map/all_to_all | solution.py:723
  151.9 7.0 %collective-permute-start.14 = (bf16[4,128,256]{2,1,0:T(8,128)(2,1)S(1)}, bf16[4,128,256]{2,1,0:T(8,128)(2,1)S(1)}, u32[]{:S(2)}, u32[]{:S(2)}) collective-permute-start(bf16[4,128,256]{2,1,0:T(8,128)(2,1)S(1)} %bitcast.34), channel_id=1, source_target_pairs={{0,16},{16,0},{32,48},{48,32},{64,80},{80,64},{96,112},{112,96},{1... | collective-permute-start | bytes 786440 | tf_op jit(solution)/shard_map/ppermute | solution.py:655
  155.2 0.8 copy-start.6
  158.3 5.8 %collective-permute-start.7 = (bf16[144,3072]{1,0:T(8,128)(2,1)}, bf16[144,3072]{1,0:T(8,128)(2,1)}, u32[]{:S(2)}, u32[]{:S(2)}) collective-permute-start(bf16[144,3072]{1,0:T(8,128)(2,1)} %collective-permute-done.1.refs_3_), channel_id=1, source_target_pairs={{0,16},{16,0},{32,48},{48,32},{64,80},{80,64},{96,112},{112,96},{1... | collective-permute-start | bytes 2654216 | tf_op jit(solution)/shard_map/ppermute | solution.py:655
  158.3 5.9 %collective-permute-start.8 = (bf16[144,3072]{1,0:T(8,128)(2,1)}, bf16[144,3072]{1,0:T(8,128)(2,1)S(1)}, u32[]{:S(2)}, u32[]{:S(2)}) collective-permute-start(bf16[144,3072]{1,0:T(8,128)(2,1)} %collective-permute-done.2.refs_4_), channel_id=1, source_target_pairs={{0,16},{16,0},{32,48},{48,32},{64,80},{80,64},{96,112},{112,96},{1... | collective-permute-start | bytes 2654216 | tf_op jit(solution)/shard_map/ppermute | solution.py:655
  158.8 8.1 %collective-permute-start.9 = (bf16[144,3072]{1,0:T(8,128)(2,1)}, bf16[144,3072]{1,0:T(8,128)(2,1)S(1)}, u32[]{:S(2)}, u32[]{:S(2)}) collective-permute-start(bf16[144,3072]{1,0:T(8,128)(2,1)} %collective-permute-done.3.refs_5_), channel_id=1, source_target_pairs={{0,16},{16,0},{32,48},{48,32},{64,80},{80,64},{96,112},{112,96},{1... | collective-permute-start | bytes 2654216 | tf_op jit(solution)/shard_map/ppermute | solution.py:655
  158.9 15.0 %collective-permute-start.12 = (bf16[144,3072]{1,0:T(8,128)(2,1)}, bf16[144,3072]{1,0:T(8,128)(2,1)}, u32[]{:S(2)}, u32[]{:S(2)}) collective-permute-start(bf16[144,3072]{1,0:T(8,128)(2,1)} %collective-permute-done.10.refs_12_), channel_id=1, source_target_pairs={{0,16},{16,0},{32,48},{48,32},{64,80},{80,64},{96,112},{112,96},{1... | collective-permute-start | bytes 2654216 | tf_op jit(solution)/shard_map/ppermute | solution.py:655
  159.3 14.6 %collective-permute-start.13 = (bf16[144,3072]{1,0:T(8,128)(2,1)}, bf16[144,3072]{1,0:T(8,128)(2,1)}, u32[]{:S(2)}, u32[]{:S(2)}) collective-permute-start(bf16[144,3072]{1,0:T(8,128)(2,1)} %collective-permute-done.11.refs_13_), channel_id=1, source_target_pairs={{0,16},{16,0},{32,48},{48,32},{64,80},{80,64},{96,112},{112,96},{1... | collective-permute-start | bytes 2654216 | tf_op jit(solution)/shard_map/ppermute | solution.py:655
  159.4 14.5 %all-to-all-start.6 = ((bf16[16,96,128]{2,1,0:T(8,128)(2,1)}), bf16[16,96,128]{2,1,0:T(8,128)(2,1)S(1)}, u32[]{:S(2)}, u32[]{:S(2)}) async-start(bf16[16,96,128]{2,1,0:T(8,128)(2,1)} %project.1), calls=%async_computation.6 | async-start | bytes 786432 | tf_op jit(solution)/shard_map/all_to_all | solution.py:727
  164.1 19.7 %copy-start.5 = (bf16[8,128,256]{2,1,0:T(8,128)(2,1)}, bf16[8,128,256]{2,1,0:T(8,128)(2,1)S(1)}, u32[]{:S(2)}) copy-start(bf16[8,128,256]{2,1,0:T(8,128)(2,1)S(1)} %pad_maximum_fusion.refs_0_) | copy-start | bytes 1572868
  164.1 26.6 %collective-permute-start.15 = (bf16[8,128,256]{2,1,0:T(8,128)(2,1)S(1)}, bf16[8,128,256]{2,1,0:T(8,128)(2,1)S(1)}, u32[]{:S(2)}, u32[]{:S(2)}) collective-permute-start(bf16[8,128,256]{2,1,0:T(8,128)(2,1)S(1)} %pad_maximum_fusion.refs_0_), channel_id=1, source_target_pairs={{0,32},{16,48},{32,64},{48,80},{64,96},{80,112},{96,0},{112,16},{1... | collective-permute-start | bytes 1572872 | tf_op jit(solution)/shard_map/ppermute | solution.py:650
  164.2 9.7 %copy-start.10 = (bf16[144,3072]{1,0:T(8,128)(2,1)}, bf16[144,3072]{1,0:T(8,128)(2,1)S(1)}, u32[]{:S(2)}) copy-start(bf16[144,3072]{1,0:T(8,128)(2,1)S(1)} %collective-permute-done.8.refs_10_) | copy-start | bytes 2654212
  164.2 26.5 %collective-permute-start.16 = (bf16[8,128,256]{2,1,0:T(8,128)(2,1)S(1)}, bf16[8,128,256]{2,1,0:T(8,128)(2,1)}, u32[]{:S(2)}, u32[]{:S(2)}) collective-permute-start(bf16[8,128,256]{2,1,0:T(8,128)(2,1)S(1)} %pad_maximum_fusion.refs_0_), channel_id=1, source_target_pairs={{0,64},{16,80},{32,96},{48,112},{64,0},{80,16},{96,32},{112,48},{1... | collective-permute-start | bytes 1572872 | tf_op jit(solution)/shard_map/ppermute | solution.py:650
  166.9 7.0 %copy-start.11 = (bf16[144,3072]{1,0:T(8,128)(2,1)}, bf16[144,3072]{1,0:T(8,128)(2,1)S(1)}, u32[]{:S(2)}) copy-start(bf16[144,3072]{1,0:T(8,128)(2,1)S(1)} %collective-permute-done.9.refs_11_) | copy-start | bytes 2654212
  166.9 24.5 %collective-permute-start.17 = (bf16[8,128,256]{2,1,0:T(8,128)(2,1)S(1)}, bf16[8,128,256]{2,1,0:T(8,128)(2,1)}, u32[]{:S(2)}, u32[]{:S(2)}) collective-permute-start(bf16[8,128,256]{2,1,0:T(8,128)(2,1)S(1)} %pad_maximum_fusion.refs_0_), channel_id=1, source_target_pairs={{0,96},{16,112},{32,0},{48,16},{64,32},{80,48},{96,64},{112,80},{1... | collective-permute-start | bytes 1572872 | tf_op jit(solution)/shard_map/ppermute | solution.py:650
  173.9 0.7 copy-start.7
  183.8 13.2 %all-to-all-start.7 = ((bf16[16,4,3072]{2,1,0:T(4,128)(2,1)}), bf16[16,4,3072]{2,1,0:T(4,128)(2,1)S(1)}, u32[]{:S(2)}, u32[]{:S(2)}) async-start(bf16[16,4,3072]{2,1,0:T(4,128)(2,1)} %get-tuple-element.146), calls=%async_computation.7 | async-start | bytes 786432 | tf_op jit(solution)/shard_map/all_to_all | solution.py:729
  190.7 0.8 copy-start.12

commit v5 on v4

--- a/solution.py
+++ b/solution.py
@@ -182,14 +182,13 @@
     payload,
     embedded,
     normed,
-    arrived_in,
     query_in,
     keyvalue_in,
     keys_in,
     values_in,
     sems,
 ):
-    moves = [(arrived, arrived_in)]
+    moves = []
     third = query_weight.shape[0] // 3
     for k in range(3):
         span = pl.ds(k * third, third)
@@ -203,8 +202,7 @@
     drafts = tokens // slots
     heads = query_weight.shape[1] // size
     own = payload.shape[1]
-    copies[0].wait()
-    rows_in = (rows_of(arrived_in, places) + extra[...].astype(F32)).astype(BF)
+    rows_in = (rows_of(arrived, places) + extra[...].astype(F32)).astype(BF)
     embedded[...] = rows_in
     wide = rows_in.astype(F32)
     factor = lax.rsqrt(jnp.mean(wide * wide, axis=-1, keepdims=True) + 1e-05)
@@ -212,15 +210,15 @@
     normed[...] = rows_norm
     queries = None
     for k in range(3):
-        copies[k + 1].wait()
+        copies[k].wait()
         span = slice(k * third, (k + 1) * third)
         part = dot_nn(rows_norm[:, span], query_in[span, :])
         queries = part if queries is None else queries + part
     queries = queries.astype(BF)
+    copies[3].wait()
+    keyvalue = dot_nn(rows_norm, keyvalue_in[...]).astype(BF)
     copies[4].wait()
-    keyvalue = dot_nn(rows_norm, keyvalue_in[...]).astype(BF)
     copies[5].wait()
-    copies[6].wait()
     member = ints[8]
     scale = size ** (-0.5)
     rows = heads * drafts
@@ -272,7 +270,7 @@
     tokens, width = extra.shape
     members = arrived.shape[0]
     wide = query_weight.shape[1] + AUX
-    far = (arrived, query_weight, keyvalue_weight, keys, values)
+    far = (query_weight, keyvalue_weight, keys, values)
     outs = [
         jax.ShapeDtypeStruct((members, tokens // members, wide), BF),
         jax.ShapeDtypeStruct((tokens, width), BF),
@@ -281,11 +279,11 @@
     return pl.pallas_call(
         attend_kernel,
         grid=(1,),
-        in_specs=scalars(1) + streamed(1) + whole([places, extra, gain]) + streamed(4),
+        in_specs=scalars(1) + whole([arrived, places, extra, gain]) + streamed(4),
         out_specs=whole(outs),
         out_shape=outs,
         scratch_shapes=[pltpu.VMEM(a.shape, a.dtype) for a in far]
-        + [pltpu.SemaphoreType.DMA((7,))],
+        + [pltpu.SemaphoreType.DMA((6,))],
         compiler_params=PARAMS,
         cost_estimate=cost(
             2 * tokens * query_weight.size * 2, 2 * (query_weight.size + keys.size * 2), keys.size
@@ -550,20 +548,11 @@
     )(spread, embedded, gain, *weights)
 
 
-def pack_kernel(gate, up, down, ready, low, high, sems):
+def pack_kernel(gate, up, down, ready, low, high):
     half = low.shape[0] // 3
-    copies = []
     for k, part in enumerate((gate, up, down)):
-        for h, out in enumerate((low, high)):
-            copy = pltpu.make_async_copy(
-                part.at[pl.ds(h * half, half), :],
-                out.at[pl.ds(k * half, half), :],
-                sems.at[k, h],
-            )
-            copy.start()
-            copies.append(copy)
-    for copy in copies:
-        copy.wait()
+        low[k * half : (k + 1) * half] = part[:half]
+        high[k * half : (k + 1) * half] = part[half:]
 
 
 def pack(gate, up, down, ready):
@@ -571,10 +560,10 @@
     out = jax.ShapeDtypeStruct((3 * units // 2, width), gate.dtype)
     return pl.pallas_call(
         pack_kernel,
-        in_specs=streamed(4),
-        out_specs=streamed(2),
+        grid=(1,),
+        in_specs=whole([gate, up, down]) + streamed(1),
+        out_specs=whole([out, out]),
         out_shape=[out, out],
-        scratch_shapes=[pltpu.SemaphoreType.DMA((3, 2))],
         compiler_params=PARAMS,
         cost_estimate=cost(0, 1024),
         name="pack",
@@ -670,7 +659,7 @@
     sent, slots, places, most = exchange(jnp.int32(0))
 
     low, high = pack(gate_weight.T, up_weight.T, down_weight.T, sent)
-    low, high, _ = lax.optimization_barrier((low, high, slots))
+    low, high, slots = lax.optimization_barrier((low, high, slots))
     arrived = spread_slots(slots)
     near = [turn(low, 1), turn(high, -1), turn(high, 1), turn(low, -1)]
 
@@ -727,7 +716,7 @@
     added = lax.all_to_all(spread, "tok", 0, 0, tiled=True)
     mlp_part, mixed = feed(added, embedded, mlp_gain[None], weights)
     mlp_rows = lax.all_to_all(mlp_part, "tok", 0, 0, tiled=True)
-    own_rows = lax.dynamic_slice_in_dim(mixed, member * own, own)
+    own_rows = lax.optimization_barrier(lax.dynamic_slice_in_dim(mixed, member * own, own))
     hidden_out = (own_rows.astype(F32) + jnp.sum(mlp_rows.astype(F32), axis=0)).astype(BF)
 
     incoming = inverse_of(new_slot)

time: 200 us -> 148 us (0.74)
  Pallas kernels: 88.8 us -> 37.4 us
    pallas_call x2, Pallas kernels: 61.9 us -> 10.5 us  [the longest x1 7.77 us: attend(): pl.pallas_call(attend_kernel, grid=(1,), in_specs=scalars(1) + whole([arr...]
    all_to_all x1, waiting for transfers between devices: 0.01 us -> 13.4 us  [spread_slots(): return lax.all_to_all(spread, 'tok', 0, 0, tiled=True)]
    ppermute x9, waiting for transfers between devices: 19 us -> 14.6 us  [turn(): lax.ppermute(value, 'req', [(g, (g + by * cores) % groups) for g in range...]
    all_to_all x1, starting transfers between devices: 7.23 us -> 3.52 us  [local(): parts = lax.all_to_all(payload, 'tok', 0, 0, tiled=True)]
    all_to_all x1, waiting for transfers between devices: 11.9 us -> 9.16 us  [exchange(): slots = lax.all_to_all(payload, 'req', 0, 0, tiled=True)]
    all_to_all x1, starting transfers between devices: 3.74 us -> 6.36 us  [local(): added = lax.all_to_all(spread, 'tok', 0, 0, tiled=True)]
    all_to_all x1, waiting for transfers between devices: 3.34 us -> 0.8 us  [local(): lax.all_to_all(join(parts, blocks, query_heads, head_size), 'tok', 0, 0,...]
    all_to_all x1, waiting for transfers between devices: 6.34 us -> 3.96 us  [local(): added = lax.all_to_all(spread, 'tok', 0, 0, tiled=True)]
  transfers between devices with their start and end apart: 24 -> 24, of which waited for: 8 -> 7; matrix products, arithmetic and copies ran while one was open for 3% -> 5% of each run, Pallas kernels for 43% -> 23%
where the time goes in v5:
time: 148 us; the launch traced here: 147 us
  starting transfers between devices  49.3 us (33%)
  waiting for transfers between devices  42.9 us (29%)
  Pallas kernels  37.4 us (25%)
  local copies, waits for them, and re-layouts  8.89 us (6%)
  other arithmetic  5.28 us (4%)
  between operations  2.96 us (2%)
    ppermute x9, waiting for transfers between devices, turn(): lax.ppermute(value, 'req', [(g, (g + by * cores) % groups) for g in range...  14.6 us
    ppermute x9, starting transfers between devices, turn(): lax.ppermute(value, 'req', [(g, (g + by * cores) % groups) for g in range...  13.9 us
    all_to_all x1, waiting for transfers between devices, spread_slots(): return lax.all_to_all(spread, 'tok', 0, 0, tiled=True)  13.4 us
    all_to_all x1, waiting for transfers between devices, exchange(): slots = lax.all_to_all(payload, 'req', 0, 0, tiled=True)  9.16 us
    pallas_call x1, Pallas kernels, feed(): pl.pallas_call(functools.partial(feed_kernel, count=len(weights)), grid=(...  9.15 us
    pallas_call x1, Pallas kernels, attend(): pl.pallas_call(attend_kernel, grid=(1,), in_specs=scalars(1) + whole([arr...  7.77 us
    all_to_all x1, starting transfers between devices, spread_slots(): return lax.all_to_all(spread, 'tok', 0, 0, tiled=True)  7.17 us
    all_to_all x1, starting transfers between devices, local(): lax.all_to_all(join(parts, blocks, query_heads, head_size), 'tok', 0, 0,...  7.15 us
  transfers between devices with their start and end apart: 24, of which 7 were waited for; matrix products, arithmetic and copies ran while one was open for 5% of the time, Pallas kernels for 23%

profile of v5, /device:TPU:0, one launch (start us, length us, event | category | flops | bytes accessed | tf_op | source)
XLA Modules:
  0.0 147.3 jit_solution(4504740687521913282)
XLA Ops:
  0.7 0.8 copy.33.draft_ids
  1.4 0.6 pad_add_fusion.2.ints
  2.0 4.0 %fetch.5 = (bf16[8,16,3072]{2,1,0:T(8,128)(2,1)}, s32[64,128]{1,0:T(8,128)}, s32[8,128]{1,0:T(8,128)}) custom-call(s32[3]{0:T(128)} %pad_add_fusion.2.ints, s32[1,32]{1,0:T(1,128)} %bitcast.27, s32[32,16]{1,0:T(8,128)S(1)} %copy.33.draft_ids, bf16[512,3072]{1,0:T(8,128)(2,1)} %table_far.1), custom_call_target="tpu_custom_call" | custom-call | flops 402653184 | bytes 3145728 | tf_op jit(solution)/shard_map/fetch/pallas_call | solution.py:134
  6.1 5.4 %all-to-all-start.2 = ((bf16[8,16,3072]{2,1,0:T(8,128)(2,1)}), bf16[8,16,3072]{2,1,0:T(8,128)(2,1)S(1)}, u32[]{:S(2)}, u32[]{:S(2)}) async-start(bf16[8,16,3072]{2,1,0:T(8,128)(2,1)} %get-tuple-element.127.ready), calls=%async_computation.2 | async-start | bytes 1572864 | tf_op jit(solution)/shard_map/all_to_all | solution.py:651
  11.5 1.2 slice.3
  12.7 2.8 %pack.1 = (bf16[144,3072]{1,0:T(8,128)(2,1)}, bf16[144,3072]{1,0:T(8,128)(2,1)}) custom-call(bf16[96,3072]{1,0:T(8,128)(2,1)} %bitcast.29, bf16[96,3072]{1,0:T(8,128)(2,1)} %bitcast.30, bf16[96,3072]{1,0:T(8,128)(2,1)} %bitcast.31, bf16[8,16,3072]{2,1,0:T(8,128)(2,1)} %get-tuple-element.127.ready), custom_call_target="tpu_custom_call" | custom-call | bytes 1024 | tf_op jit(solution)/shard_map/pack/pallas_call | solution.py:561
  15.5 9.2 %all-to-all-done.2 = bf16[8,16,3072]{2,1,0:T(8,128)(2,1)S(1)} async-done(((bf16[8,16,3072]{2,1,0:T(8,128)(2,1)}), bf16[8,16,3072]{2,1,0:T(8,128)(2,1)S(1)}, u32[]{:S(2)}, u32[]{:S(2)}) %all-to-all-start.2) | async-done | bytes 786464 | tf_op jit(solution)/shard_map/all_to_all | solution.py:651
  24.8 0.6 while.12
  25.4 1.3 broadcast_in_dim.71
  26.7 7.2 %all-to-all-start.3 = ((bf16[16,16,3072]{2,1,0:T(8,128)(2,1)}), bf16[16,16,3072]{2,1,0:T(8,128)(2,1)S(1)}, u32[]{:S(2)}, u32[]{:S(2)}) async-start(bf16[16,16,3072]{2,1,0:T(8,128)(2,1)} %broadcast_in_dim.71), calls=%async_computation.3 | async-start | bytes 3145728 | tf_op jit(solution)/shard_map/all_to_all | solution.py:657
  33.9 0.6 collective-permute-start
  34.6 2.7 %collective-permute-start.1 = (bf16[144,3072]{1,0:T(8,128)(2,1)}, bf16[144,3072]{1,0:T(8,128)(2,1)}, u32[]{:S(2)}, u32[]{:S(2)}) collective-permute-start(bf16[144,3072]{1,0:T(8,128)(2,1)} %get-tuple-element.139.refs_1_), channel_id=1, source_target_pairs={{0,96},{16,112},{32,0},{48,16},{64,32},{80,48},{96,64},{112,80},{1... | collective-permute-start | bytes 2654216 | tf_op jit(solution)/shard_map/ppermute | solution.py:639
  37.2 3.2 %collective-permute-start.3 = (bf16[144,3072]{1,0:T(8,128)(2,1)S(1)}, bf16[144,3072]{1,0:T(8,128)(2,1)}, u32[]{:S(2)}, u32[]{:S(2)}) collective-permute-start(bf16[144,3072]{1,0:T(8,128)(2,1)S(1)} %copy-done.8), channel_id=1, source_target_pairs={{0,96},{16,112},{32,0},{48,16},{64,32},{80,48},{96,64},{112,80},{1... | collective-permute-start | bytes 2654216 | tf_op jit(solution)/shard_map/ppermute | solution.py:639
  40.7 0.6 gather_fusion
  41.3 0.6 gather_fusion.1
  44.0 0.6 pad_add_fusion.1.ints
  44.6 13.4 %all-to-all-done.3.arrived = bf16[16,16,3072]{2,1,0:T(8,128)(2,1)S(1)} async-done(((bf16[16,16,3072]{2,1,0:T(8,128)(2,1)}), bf16[16,16,3072]{2,1,0:T(8,128)(2,1)S(1)}, u32[]{:S(2)}, u32[]{:S(2)}) %all-to-all-start.3) | async-done | bytes 1572896 | tf_op jit(solution)/shard_map/all_to_all | solution.py:657
  58.1 1.2 copy-done.4
  59.3 7.8 %attend.1 = (bf16[16,4,896]{2,1,0:T(4,128)(2,1)}, bf16[64,3072]{1,0:T(8,128)(2,1)}, bf16[64,3072]{1,0:T(8,128)(2,1)}) custom-call(s32[9]{0:T(128)} %pad_add_fusion.1.ints, bf16[16,16,3072]{2,1,0:T(8,128)(2,1)} %copy-done.4, s32[64,128]{1,0:T(8,128)} %get-tuple-element.131.places, bf16[64,3072]{1,0:T(8,128)(2,1)S(1)} %get-tuple-element.133.extra, ...), custom_call_target="tpu_custom_call" | custom-call | flops 603979776 | bytes 6815744 | tf_op jit(solution)/shard_map/attend/pallas_call | solution.py:279
  67.1 3.5 %all-to-all-start.4 = ((bf16[16,4,896]{2,1,0:T(4,128)(2,1)}), bf16[16,4,896]{2,1,0:T(4,128)(2,1)S(1)}, u32[]{:S(2)}, u32[]{:S(2)}) async-start(bf16[16,4,896]{2,1,0:T(4,128)(2,1)} %get-tuple-element.134), calls=%async_computation.4 | async-start | bytes 229376 | tf_op jit(solution)/shard_map/all_to_all | solution.py:695
  70.6 0.6 pad_maximum_fusion.1.reals
  71.2 6.8 %mamba.1 = (bf16[16,96,128]{2,1,0:T(8,128)(2,1)}, bf16[4,1,128,256]{3,2,1,0:T(8,128)(2,1)}) custom-call(s32[9]{0:T(128)} %pad_add_fusion.1.ints, f32[3]{0:T(128)} %pad_maximum_fusion.1.reals, bf16[64,3072]{1,0:T(8,128)(2,1)} %get-tuple-element.135.normed, bf16[3072,128]{1,0:T(8,128)(2,1)} %input_weight.1, bf16[3072,128]{1,0:T(8,128)(2,1)} %gate_weight.1, ...), custom_call_target="tpu_custom_call" | custom-call | flops 402653184 | bytes 6291456 | tf_op jit(solution)/shard_map/mamba/pallas_call | solution.py:398
  78.0 0.6 collective-permute-start.5
  78.6 0.6 collective-permute-start.10
  79.3 2.7 %collective-permute-start.11 = (bf16[144,3072]{1,0:T(8,128)(2,1)}, bf16[144,3072]{1,0:T(8,128)(2,1)}, u32[]{:S(2)}, u32[]{:S(2)}) collective-permute-start(bf16[144,3072]{1,0:T(8,128)(2,1)} %collective-permute-done.1.refs_3_), channel_id=1, source_target_pairs={{0,96},{16,112},{32,0},{48,16},{64,32},{80,48},{96,64},{112,80},{1... | collective-permute-start | bytes 2654216 | tf_op jit(solution)/shard_map/ppermute | solution.py:639
  82.0 2.2 %join.1 = bf16[16,120,128]{2,1,0:T(8,128)(2,1)} custom-call(bf16[16,4,896]{2,1,0:T(4,128)(2,1)} %copy-done.13, bf16[16,96,128]{2,1,0:T(8,128)(2,1)} %get-tuple-element.136.blocks), custom_call_target="tpu_custom_call" | custom-call | tf_op jit(solution)/shard_map/join/pallas_call | solution.py:438
  84.1 7.2 %all-to-all-start.5 = ((bf16[16,120,128]{2,1,0:T(8,128)(2,1)}), bf16[16,120,128]{2,1,0:T(8,128)(2,1)S(1)}, u32[]{:S(2)}, u32[]{:S(2)}) async-start(bf16[16,120,128]{2,1,0:T(8,128)(2,1)} %join.1), calls=%async_computation.5 | async-start | bytes 983040 | tf_op jit(solution)/shard_map/all_to_all | solution.py:712
  91.9 9.9 %collective-permute-done.10.refs_12_ = bf16[144,3072]{1,0:T(8,128)(2,1)} collective-permute-done((bf16[144,3072]{1,0:T(8,128)(2,1)}, bf16[144,3072]{1,0:T(8,128)(2,1)}, u32[]{:S(2)}, u32[]{:S(2)}) %collective-permute-start.10) | collective-permute-done | bytes 884768 | tf_op jit(solution)/shard_map/ppermute | solution.py:639
  101.8 0.5 collective-permute-start.9
  102.3 0.8 all-to-all-done.5.parts
  103.1 0.8 copy-done.6
  103.9 2.3 %project.1 = bf16[16,96,128]{2,1,0:T(8,128)(2,1)} custom-call(bf16[16,120,128]{2,1,0:T(8,128)(2,1)} %copy-done.6, bf16[192,768]{1,0:T(8,128)(2,1)} %bitcast.33), custom_call_target="tpu_custom_call" | custom-call | tf_op jit(solution)/shard_map/project/pallas_call | solution.py:468
  106.2 0.5 collective-permute-start.13
  106.9 6.4 %all-to-all-start.6 = ((bf16[16,96,128]{2,1,0:T(8,128)(2,1)}), bf16[16,96,128]{2,1,0:T(8,128)(2,1)S(1)}, u32[]{:S(2)}, u32[]{:S(2)}) async-start(bf16[16,96,128]{2,1,0:T(8,128)(2,1)} %project.1), calls=%async_computation.6 | async-start | bytes 786432 | tf_op jit(solution)/shard_map/all_to_all | solution.py:716
  113.3 0.6 gather_fusion.2
  114.0 1.0 pad_maximum_fusion.refs_0_
  115.1 4.0 %collective-permute-start.16 = (bf16[8,128,256]{2,1,0:T(8,128)(2,1)S(1)}, bf16[8,128,256]{2,1,0:T(8,128)(2,1)}, u32[]{:S(2)}, u32[]{:S(2)}) collective-permute-start(bf16[8,128,256]{2,1,0:T(8,128)(2,1)S(1)} %pad_maximum_fusion.refs_0_), channel_id=1, source_target_pairs={{0,64},{16,80},{32,96},{48,112},{64,0},{80,16},{96,32},{112,48},{1... | collective-permute-start | bytes 1572872 | tf_op jit(solution)/shard_map/ppermute | solution.py:639
  119.1 0.6 fusion
  119.7 4.0 %all-to-all-done.6.spread = bf16[16,96,128]{2,1,0:T(8,128)(2,1)S(1)} async-done(((bf16[16,96,128]{2,1,0:T(8,128)(2,1)}), bf16[16,96,128]{2,1,0:T(8,128)(2,1)S(1)}, u32[]{:S(2)}, u32[]{:S(2)}) %all-to-all-start.6) | async-done | bytes 393248 | tf_op jit(solution)/shard_map/all_to_all | solution.py:716
  123.7 0.7 copy-done.7
  124.4 9.2 %feed.1 = (bf16[16,4,3072]{2,1,0:T(4,128)(2,1)}, bf16[64,3072]{1,0:T(8,128)(2,1)}) custom-call(bf16[16,96,128]{2,1,0:T(8,128)(2,1)} %copy-done.7, bf16[64,3072]{1,0:T(8,128)(2,1)} %get-tuple-element.137.embedded, f32[1,3072]{1,0:T(1,128)} %bitcast.38, bf16[144,3072]{1,0:T(8,128)(2,1)} %get-tuple-element.138.refs_0_, ...), custom_call_target="tpu_custom_call" | custom-call | flops 905969664 | bytes 14155776 | tf_op jit(solution)/shard_map/feed/pallas_call | solution.py:537
  133.6 3.6 %all-to-all-start.7 = ((bf16[16,4,3072]{2,1,0:T(4,128)(2,1)}), bf16[16,4,3072]{2,1,0:T(4,128)(2,1)S(1)}, u32[]{:S(2)}, u32[]{:S(2)}) async-start(bf16[16,4,3072]{2,1,0:T(4,128)(2,1)} %get-tuple-element.148), calls=%async_computation.7 | async-start | bytes 786432 | tf_op jit(solution)/shard_map/all_to_all | solution.py:718
  137.1 0.5 and_select_fusion.3.turns
  137.6 4.7 %collective-permute-done.16.refs_2_ = bf16[8,128,256]{2,1,0:T(8,128)(2,1)} collective-permute-done((bf16[8,128,256]{2,1,0:T(8,128)(2,1)S(1)}, bf16[8,128,256]{2,1,0:T(8,128)(2,1)}, u32[]{:S(2)}, u32[]{:S(2)}) %collective-permute-start.16) | collective-permute-done | bytes 524320 | tf_op jit(solution)/shard_map/ppermute | solution.py:639
  142.4 2.5 %pick.1 = f32[4,128,256]{2,1,0:T(8,128)} custom-call(s32[4]{0:T(128)} %and_select_fusion.3.turns, s32[4]{0:T(128)} %get-tuple-element.196.rows, bf16[8,128,256]{2,1,0:T(8,128)(2,1)} %copy-done.5, bf16[8,128,256]{2,1,0:T(8,128)(2,1)} %copy-done.12, bf16[8,128,256]{2,1,0:T(8,128)(2,1)} %collective-permute-done.16.refs_2_, ...), custom_call_target="tpu_custom_call" | custom-call | tf_op jit(solution)/shard_map/pick/pallas_call | solution.py:587
  144.8 0.8 constant_dynamic-slice_fusion
  145.7 0.9 all-to-all-done.7
  146.7 0.6 add_convert_fusion
  (67 shorter events, 1.6 us)
Async XLA Ops:
  0.6 40.0 %copy-start = (s32[32]{0:T(128)S(1)}, s32[32]{0:T(128)}, u32[]{:S(2)}) copy-start(s32[32]{0:T(128)} %param.30) | copy-start | bytes 388
  6.1 18.6 %all-to-all-start.2 = ((bf16[8,16,3072]{2,1,0:T(8,128)(2,1)}), bf16[8,16,3072]{2,1,0:T(8,128)(2,1)S(1)}, u32[]{:S(2)}, u32[]{:S(2)}) async-start(bf16[8,16,3072]{2,1,0:T(8,128)(2,1)} %get-tuple-element.127.ready), calls=%async_computation.2 | async-start | bytes 1572864 | tf_op jit(solution)/shard_map/all_to_all | solution.py:651
  12.7 12.1 %copy-start.1 = (s32[32]{0:T(128)S(1)}, s32[32]{0:T(128)}, u32[]{:S(2)}) copy-start(s32[32]{0:T(128)} %param.31) | copy-start | bytes 388
  26.7 7.2 %copy-start.8 = (bf16[144,3072]{1,0:T(8,128)(2,1)S(1)}, bf16[144,3072]{1,0:T(8,128)(2,1)}, u32[]{:S(2)}) copy-start(bf16[144,3072]{1,0:T(8,128)(2,1)} %get-tuple-element.138.refs_0_) | copy-start | bytes 2654212
  26.7 14.6 %copy-start.2 = (s32[32]{0:T(128)S(1)}, s32[32]{0:T(128)}, u32[]{:S(2)}) copy-start(s32[32]{0:T(128)} %param.33) | copy-start | bytes 388
  26.7 31.3 %all-to-all-start.3 = ((bf16[16,16,3072]{2,1,0:T(8,128)(2,1)}), bf16[16,16,3072]{2,1,0:T(8,128)(2,1)S(1)}, u32[]{:S(2)}, u32[]{:S(2)}) async-start(bf16[16,16,3072]{2,1,0:T(8,128)(2,1)} %broadcast_in_dim.71), calls=%async_computation.3 | async-start | bytes 3145728 | tf_op jit(solution)/shard_map/all_to_all | solution.py:657
  33.9 44.1 %collective-permute-start = (bf16[144,3072]{1,0:T(8,128)(2,1)S(1)}, bf16[144,3072]{1,0:T(8,128)(2,1)}, u32[]{:S(2)}, u32[]{:S(2)}) collective-permute-start(bf16[144,3072]{1,0:T(8,128)(2,1)S(1)} %copy-done.8), channel_id=1, source_target_pairs={{0,32},{16,48},{32,64},{48,80},{64,96},{80,112},{96,0},{112,16},{1... | collective-permute-start | bytes 2654216 | tf_op jit(solution)/shard_map/ppermute | solution.py:639
  34.6 44.0 %collective-permute-start.1 = (bf16[144,3072]{1,0:T(8,128)(2,1)}, bf16[144,3072]{1,0:T(8,128)(2,1)}, u32[]{:S(2)}, u32[]{:S(2)}) collective-permute-start(bf16[144,3072]{1,0:T(8,128)(2,1)} %get-tuple-element.139.refs_1_), channel_id=1, source_target_pairs={{0,96},{16,112},{32,0},{48,16},{64,32},{80,48},{96,64},{112,80},{1... | collective-permute-start | bytes 2654216 | tf_op jit(solution)/shard_map/ppermute | solution.py:639
  37.2 41.4 %collective-permute-start.2 = (bf16[144,3072]{1,0:T(8,128)(2,1)}, bf16[144,3072]{1,0:T(8,128)(2,1)}, u32[]{:S(2)}, u32[]{:S(2)}) collective-permute-start(bf16[144,3072]{1,0:T(8,128)(2,1)} %get-tuple-element.139.refs_1_), channel_id=1, source_target_pairs={{0,32},{16,48},{32,64},{48,80},{64,96},{80,112},{96,0},{112,16},{1... | collective-permute-start | bytes 2654216 | tf_op jit(solution)/shard_map/ppermute | solution.py:639
  37.2 41.4 %collective-permute-start.3 = (bf16[144,3072]{1,0:T(8,128)(2,1)S(1)}, bf16[144,3072]{1,0:T(8,128)(2,1)}, u32[]{:S(2)}, u32[]{:S(2)}) collective-permute-start(bf16[144,3072]{1,0:T(8,128)(2,1)S(1)} %copy-done.8), channel_id=1, source_target_pairs={{0,96},{16,112},{32,0},{48,16},{64,32},{80,48},{96,64},{112,80},{1... | collective-permute-start | bytes 2654216 | tf_op jit(solution)/shard_map/ppermute | solution.py:639
  58.1 1.2 copy-start.4
  67.1 11.5 %all-to-all-start.4 = ((bf16[16,4,896]{2,1,0:T(4,128)(2,1)}), bf16[16,4,896]{2,1,0:T(4,128)(2,1)S(1)}, u32[]{:S(2)}, u32[]{:S(2)}) async-start(bf16[16,4,896]{2,1,0:T(4,128)(2,1)} %get-tuple-element.134), calls=%async_computation.4 | async-start | bytes 229376 | tf_op jit(solution)/shard_map/all_to_all | solution.py:695
  71.2 20.1 %collective-permute-start.4 = (bf16[144,3072]{1,0:T(8,128)(2,1)S(1)}, bf16[144,3072]{1,0:T(8,128)(2,1)S(1)}, u32[]{:S(2)}, u32[]{:S(2)}) collective-permute-start(bf16[144,3072]{1,0:T(8,128)(2,1)S(1)} %copy-done.8), channel_id=1, source_target_pairs={{0,16},{16,0},{32,48},{48,32},{64,80},{80,64},{96,112},{112,96},{1... | collective-permute-start | bytes 2654216 | tf_op jit(solution)/shard_map/ppermute | solution.py:644
  71.2 6.8 %copy-start.9 = (bf16[144,3072]{1,0:T(8,128)(2,1)S(1)}, bf16[144,3072]{1,0:T(8,128)(2,1)}, u32[]{:S(2)}) copy-start(bf16[144,3072]{1,0:T(8,128)(2,1)} %get-tuple-element.139.refs_1_) | copy-start | bytes 2654212
  78.0 13.3 %copy-start.14 = (bf16[4,1,128,256]{3,2,1,0:T(8,128)(2,1)S(1)}, bf16[4,1,128,256]{3,2,1,0:T(8,128)(2,1)}, u32[]{:S(2)}) copy-start(bf16[4,1,128,256]{3,2,1,0:T(8,128)(2,1)} %get-tuple-element.149) | copy-start | bytes 786436
  78.0 13.6 %collective-permute-start.5 = (bf16[144,3072]{1,0:T(8,128)(2,1)S(1)}, bf16[144,3072]{1,0:T(8,128)(2,1)}, u32[]{:S(2)}, u32[]{:S(2)}) collective-permute-start(bf16[144,3072]{1,0:T(8,128)(2,1)S(1)} %copy-done.9), channel_id=1, source_target_pairs={{0,16},{16,0},{32,48},{48,32},{64,80},{80,64},{96,112},{112,96},{1... | collective-permute-start | bytes 2654216 | tf_op jit(solution)/shard_map/ppermute | solution.py:644
  78.6 3.3 %copy-start.13 = (bf16[16,4,896]{2,1,0:T(4,128)(2,1)}, bf16[16,4,896]{2,1,0:T(4,128)(2,1)S(1)}, u32[]{:S(2)}) copy-start(bf16[16,4,896]{2,1,0:T(4,128)(2,1)S(1)} %all-to-all-done.4.parts) | copy-start | bytes 344068
  78.6 23.2 %collective-permute-start.10 = (bf16[144,3072]{1,0:T(8,128)(2,1)}, bf16[144,3072]{1,0:T(8,128)(2,1)}, u32[]{:S(2)}, u32[]{:S(2)}) collective-permute-start(bf16[144,3072]{1,0:T(8,128)(2,1)} %collective-permute-done.refs_2_), channel_id=1, source_target_pairs={{0,32},{16,48},{32,64},{48,80},{64,96},{80,112},{96,0},{112,16},{1... | collective-permute-start | bytes 2654216 | tf_op jit(solution)/shard_map/ppermute | solution.py:639
  79.3 22.6 %collective-permute-start.11 = (bf16[144,3072]{1,0:T(8,128)(2,1)}, bf16[144,3072]{1,0:T(8,128)(2,1)}, u32[]{:S(2)}, u32[]{:S(2)}) collective-permute-start(bf16[144,3072]{1,0:T(8,128)(2,1)} %collective-permute-done.1.refs_3_), channel_id=1, source_target_pairs={{0,96},{16,112},{32,0},{48,16},{64,32},{80,48},{96,64},{112,80},{1... | collective-permute-start | bytes 2654216 | tf_op jit(solution)/shard_map/ppermute | solution.py:639
  82.0 24.3 %collective-permute-start.6 = (bf16[144,3072]{1,0:T(8,128)(2,1)}, bf16[144,3072]{1,0:T(8,128)(2,1)}, u32[]{:S(2)}, u32[]{:S(2)}) collective-permute-start(bf16[144,3072]{1,0:T(8,128)(2,1)} %collective-permute-done.refs_2_), channel_id=1, source_target_pairs={{0,16},{16,0},{32,48},{48,32},{64,80},{80,64},{96,112},{112,96},{1... | collective-permute-start | bytes 2654216 | tf_op jit(solution)/shard_map/ppermute | solution.py:644
  82.0 24.8 %copy-start.17 = (s32[32]{0:T(128)S(1)}, s32[32]{0:T(128)}, u32[]{:S(2)}) copy-start(s32[32]{0:T(128)} %param.32) | copy-start | bytes 388
  84.1 19.0 %all-to-all-start.5 = ((bf16[16,120,128]{2,1,0:T(8,128)(2,1)}), bf16[16,120,128]{2,1,0:T(8,128)(2,1)S(1)}, u32[]{:S(2)}, u32[]{:S(2)}) async-start(bf16[16,120,128]{2,1,0:T(8,128)(2,1)} %join.1), calls=%async_computation.5 | async-start | bytes 983040 | tf_op jit(solution)/shard_map/all_to_all | solution.py:712
  91.3 32.3 %copy-start.10 = (bf16[144,3072]{1,0:T(8,128)(2,1)}, bf16[144,3072]{1,0:T(8,128)(2,1)S(1)}, u32[]{:S(2)}) copy-start(bf16[144,3072]{1,0:T(8,128)(2,1)S(1)} %collective-permute-done.4.refs_6_) | copy-start | bytes 2654212
  91.3 22.6 %copy-start.15 = (bf16[4,1,128,256]{3,2,1,0:T(8,128)(2,1)S(1)}, bf16[4,1,128,256]{3,2,1,0:T(8,128)(2,1)}, u32[]{:S(2)}) copy-start(bf16[4,1,128,256]{3,2,1,0:T(8,128)(2,1)} %get-tuple-element.149) | copy-start | bytes 786436
  91.3 14.9 %collective-permute-start.14 = (bf16[4,128,256]{2,1,0:T(8,128)(2,1)S(1)}, bf16[4,128,256]{2,1,0:T(8,128)(2,1)S(1)}, u32[]{:S(2)}, u32[]{:S(2)}) collective-permute-start(bf16[4,128,256]{2,1,0:T(8,128)(2,1)S(1)} %bitcast.34), channel_id=1, source_target_pairs={{0,16},{16,0},{32,48},{48,32},{64,80},{80,64},{96,112},{112,96},{1... | collective-permute-start | bytes 786440 | tf_op jit(solution)/shard_map/ppermute | solution.py:644
  91.6 23.3 %collective-permute-start.7 = (bf16[144,3072]{1,0:T(8,128)(2,1)}, bf16[144,3072]{1,0:T(8,128)(2,1)S(1)}, u32[]{:S(2)}, u32[]{:S(2)}) collective-permute-start(bf16[144,3072]{1,0:T(8,128)(2,1)} %collective-permute-done.1.refs_3_), channel_id=1, source_target_pairs={{0,16},{16,0},{32,48},{48,32},{64,80},{80,64},{96,112},{112,96},{1... | collective-permute-start | bytes 2654216 | tf_op jit(solution)/shard_map/ppermute | solution.py:644
  101.8 13.2 %collective-permute-start.8 = (bf16[144,3072]{1,0:T(8,128)(2,1)}, bf16[144,3072]{1,0:T(8,128)(2,1)}, u32[]{:S(2)}, u32[]{:S(2)}) collective-permute-start(bf16[144,3072]{1,0:T(8,128)(2,1)} %collective-permute-done.2.refs_4_), channel_id=1, source_target_pairs={{0,16},{16,0},{32,48},{48,32},{64,80},{80,64},{96,112},{112,96},{1... | collective-permute-start | bytes 2654216 | tf_op jit(solution)/shard_map/ppermute | solution.py:644
  101.8 17.2 %collective-permute-start.9 = (bf16[144,3072]{1,0:T(8,128)(2,1)}, bf16[144,3072]{1,0:T(8,128)(2,1)}, u32[]{:S(2)}, u32[]{:S(2)}) collective-permute-start(bf16[144,3072]{1,0:T(8,128)(2,1)} %collective-permute-done.3.refs_5_), channel_id=1, source_target_pairs={{0,16},{16,0},{32,48},{48,32},{64,80},{80,64},{96,112},{112,96},{1... | collective-permute-start | bytes 2654216 | tf_op jit(solution)/shard_map/ppermute | solution.py:644
  103.1 0.8 copy-start.6
  106.2 0.7 copy-start.16
  106.2 17.4 %collective-permute-start.12 = (bf16[144,3072]{1,0:T(8,128)(2,1)}, bf16[144,3072]{1,0:T(8,128)(2,1)}, u32[]{:S(2)}, u32[]{:S(2)}) collective-permute-start(bf16[144,3072]{1,0:T(8,128)(2,1)} %collective-permute-done.10.refs_12_), channel_id=1, source_target_pairs={{0,16},{16,0},{32,48},{48,32},{64,80},{80,64},{96,112},{112,96},{1... | collective-permute-start | bytes 2654216 | tf_op jit(solution)/shard_map/ppermute | solution.py:644
  106.2 17.4 %collective-permute-start.13 = (bf16[144,3072]{1,0:T(8,128)(2,1)}, bf16[144,3072]{1,0:T(8,128)(2,1)}, u32[]{:S(2)}, u32[]{:S(2)}) collective-permute-start(bf16[144,3072]{1,0:T(8,128)(2,1)} %collective-permute-done.11.refs_13_), channel_id=1, source_target_pairs={{0,16},{16,0},{32,48},{48,32},{64,80},{80,64},{96,112},{112,96},{1... | collective-permute-start | bytes 2654216 | tf_op jit(solution)/shard_map/ppermute | solution.py:644
  106.9 16.7 %all-to-all-start.6 = ((bf16[16,96,128]{2,1,0:T(8,128)(2,1)}), bf16[16,96,128]{2,1,0:T(8,128)(2,1)S(1)}, u32[]{:S(2)}, u32[]{:S(2)}) async-start(bf16[16,96,128]{2,1,0:T(8,128)(2,1)} %project.1), calls=%async_computation.6 | async-start | bytes 786432 | tf_op jit(solution)/shard_map/all_to_all | solution.py:716
  115.0 18.6 %copy-start.5 = (bf16[8,128,256]{2,1,0:T(8,128)(2,1)}, bf16[8,128,256]{2,1,0:T(8,128)(2,1)S(1)}, u32[]{:S(2)}) copy-start(bf16[8,128,256]{2,1,0:T(8,128)(2,1)S(1)} %pad_maximum_fusion.refs_0_) | copy-start | bytes 1572868
  115.0 8.7 %copy-start.11 = (bf16[144,3072]{1,0:T(8,128)(2,1)}, bf16[144,3072]{1,0:T(8,128)(2,1)S(1)}, u32[]{:S(2)}) copy-start(bf16[144,3072]{1,0:T(8,128)(2,1)S(1)} %collective-permute-done.7.refs_9_) | copy-start | bytes 2654212
  115.0 22.7 %collective-permute-start.15 = (bf16[8,128,256]{2,1,0:T(8,128)(2,1)S(1)}, bf16[8,128,256]{2,1,0:T(8,128)(2,1)S(1)}, u32[]{:S(2)}, u32[]{:S(2)}) collective-permute-start(bf16[8,128,256]{2,1,0:T(8,128)(2,1)S(1)} %pad_maximum_fusion.refs_0_), channel_id=1, source_target_pairs={{0,32},{16,48},{32,64},{48,80},{64,96},{80,112},{96,0},{112,16},{1... | collective-permute-start | bytes 1572872 | tf_op jit(solution)/shard_map/ppermute | solution.py:639
  115.1 27.3 %collective-permute-start.16 = (bf16[8,128,256]{2,1,0:T(8,128)(2,1)S(1)}, bf16[8,128,256]{2,1,0:T(8,128)(2,1)}, u32[]{:S(2)}, u32[]{:S(2)}) collective-permute-start(bf16[8,128,256]{2,1,0:T(8,128)(2,1)S(1)} %pad_maximum_fusion.refs_0_), channel_id=1, source_target_pairs={{0,64},{16,80},{32,96},{48,112},{64,0},{80,16},{96,32},{112,48},{1... | collective-permute-start | bytes 1572872 | tf_op jit(solution)/shard_map/ppermute | solution.py:639
  119.1 23.3 %collective-permute-start.17 = (bf16[8,128,256]{2,1,0:T(8,128)(2,1)S(1)}, bf16[8,128,256]{2,1,0:T(8,128)(2,1)}, u32[]{:S(2)}, u32[]{:S(2)}) collective-permute-start(bf16[8,128,256]{2,1,0:T(8,128)(2,1)S(1)} %pad_maximum_fusion.refs_0_), channel_id=1, source_target_pairs={{0,96},{16,112},{32,0},{48,16},{64,32},{80,48},{96,64},{112,80},{1... | collective-permute-start | bytes 1572872 | tf_op jit(solution)/shard_map/ppermute | solution.py:639
  123.6 0.7 copy-start.7
  133.6 13.0 %all-to-all-start.7 = ((bf16[16,4,3072]{2,1,0:T(4,128)(2,1)}), bf16[16,4,3072]{2,1,0:T(4,128)(2,1)S(1)}, u32[]{:S(2)}, u32[]{:S(2)}) async-start(bf16[16,4,3072]{2,1,0:T(4,128)(2,1)} %get-tuple-element.148), calls=%async_computation.7 | async-start | bytes 786432 | tf_op jit(solution)/shard_map/all_to_all | solution.py:718
  137.6 4.7 %copy-start.12 = (bf16[8,128,256]{2,1,0:T(8,128)(2,1)}, bf16[8,128,256]{2,1,0:T(8,128)(2,1)S(1)}, u32[]{:S(2)}) copy-start(bf16[8,128,256]{2,1,0:T(8,128)(2,1)S(1)} %collective-permute-done.15.refs_1_) | copy-start | bytes 1572868

commit v6 on v5

--- a/solution.py
+++ b/solution.py
@@ -11,7 +11,6 @@
 F32 = jnp.float32
 NEG = -1e30
 AUX = 128
-ROOM = 16
 
 
 def inverse_of(mapping):
@@ -49,6 +48,10 @@
     return [pl.BlockSpec(a.shape, lambda i, n=len(a.shape): (0,) * n) for a in shapes]
 
 
+def near(count):
+    return [pl.BlockSpec(memory_space=pltpu.VMEM)] * count
+
+
 def streamed(count):
     return [pl.BlockSpec(memory_space=pltpu.HBM)] * count
 
@@ -58,36 +61,42 @@
 
 
 PARAMS = pltpu.CompilerParams(vmem_limit_bytes=60 << 20)
+SMALL = pltpu.CompilerParams(vmem_limit_bytes=8 << 20)
 
 
 def fetch_kernel(
-    ints, slots_row, draft_ids, table_far, payload, places, most, table, sem, *, members
+    turn, slots_row, ids_cols, table_far, payload, places, origin, most, table, sem, *, groups, members
 ):
     load = pltpu.make_async_copy(table_far, table, sem)
     load.start()
-    groups, room, width = payload.shape
-    requests, drafts = draft_ids.shape
+    drafts, requests = ids_cols.shape
     vocab = table.shape[0]
     count = requests * drafts // groups
     slots = requests // groups
-    group, member, base = ints[0], ints[1], ints[2]
+    group = lax.axis_index("req")
+    member = lax.axis_index("tok")
     me = group * members + member
+    now = turn[0]
     sub = lax.broadcasted_iota(jnp.int32, (count, count), 0)
     lane = lax.broadcasted_iota(jnp.int32, (count, count), 1)
-    ids = draft_ids[...]
+    sub_c = sub[:, :1]
+    lane_r = lane[:1, :]
+    ids = ids_cols[...]
     ids_hi = (ids // 256).astype(F32).astype(BF)
     ids_lo = (ids % 256).astype(F32).astype(BF)
     row_slot = lax.broadcasted_iota(jnp.int32, (count, requests), 0) // drafts
     token = lax.broadcasted_iota(jnp.int32, (count, drafts), 0) % drafts
     token_lane = lax.broadcasted_iota(jnp.int32, (count, drafts), 1)
-    slot_iota = lax.broadcasted_iota(jnp.int32, (room, count), 0) + base
-    local_iota = lax.broadcasted_iota(jnp.int32, (room, vocab), 1)
+    column = lax.broadcasted_iota(jnp.int32, (members, count), 0)
+    local_iota = lax.broadcasted_iota(jnp.int32, (members, vocab), 1)
+    own = count // members
     hots = []
     own_place = jnp.zeros((count, 1), jnp.int32)
+    own_from = [jnp.zeros((1, count), jnp.int32)] * own
     peak = jnp.zeros((1, count), jnp.int32)
     for g in range(groups):
         pick = jnp.where(slots_row[...] == row_slot + g * slots, 1.0, 0.0).astype(BF)
-        mixed_ids = dot_nn(pick, ids_hi) * 256.0 + dot_nn(pick, ids_lo)
+        mixed_ids = dot_nt(pick, ids_hi) * 256.0 + dot_nt(pick, ids_lo)
         id_c = jnp.sum(
             jnp.where(token == token_lane, mixed_ids, 0.0), axis=1, keepdims=True
         ).astype(jnp.int32)
@@ -95,62 +104,88 @@
         same = id_c == id_r
         first_c = jnp.min(jnp.where(same, lane, count), axis=1, keepdims=True)
         first_r = jnp.min(jnp.where(same, sub, count), axis=0, keepdims=True)
-        sub_c = sub[:, :1]
-        lane_r = lane[:1, :]
         owner_c = id_c // vocab
         owner_r = id_r // vocab
-        column_c = owner_c % members
-        column_r = owner_r % members
-        alike = column_c == column_r
-        before_r = jnp.where(alike & (first_c == sub_c) & (sub < first_r), 1, 0)
-        rank_r = jnp.sum(before_r, axis=0, keepdims=True)
-        peak = jnp.maximum(peak, rank_r + 1)
-        before_c = jnp.where(alike & (first_r == lane_r) & (lane < first_c), 1, 0)
-        rank_c = jnp.sum(before_c, axis=1, keepdims=True)
-        inside = (rank_c >= base) & (rank_c < base + room)
-        place = jnp.where(inside, column_c * room + rank_c - base, -1)
-        own_place = jnp.where(group == g, place, own_place)
-        mine = (first_r == lane_r) & (owner_r == me)
-        asked = jnp.where(mine & (rank_r == slot_iota), id_r % vocab + 1, 0)
-        row = jnp.sum(asked, axis=1, keepdims=True) - 1
+        alike = owner_c == owner_r
+        before_r = (first_c == sub_c) & alike & (sub < first_r)
+        less_r = (first_c == sub_c) & (owner_c < owner_r)
+        nth_r = jnp.sum(jnp.where(before_r, 1, 0), axis=0, keepdims=True)
+        rank_r = nth_r + jnp.sum(jnp.where(less_r, 1, 0), axis=0, keepdims=True)
+        peak = jnp.maximum(peak, nth_r // members + 1)
+        before_c = (first_r == lane_r) & alike & (lane < first_c)
+        less_c = (first_r == lane_r) & (owner_r < owner_c)
+        nth_c = jnp.sum(jnp.where(before_c, 1, 0), axis=1, keepdims=True)
+        rank_c = nth_c + jnp.sum(jnp.where(less_c, 1, 0), axis=1, keepdims=True)
+        spot = (rank_c % members) * own + rank_c // members
+        spot = jnp.where(nth_c // members == now, spot, -1)
+        own_place = jnp.where(group == g, spot, own_place)
+        sent_r = (first_r == lane_r) & (nth_r // members == now)
+        asked = sent_r & (owner_r == me) & (rank_r % members == column)
+        row = jnp.sum(jnp.where(asked, id_r % vocab + 1, 0), axis=1, keepdims=True) - 1
         hots.append(jnp.where(local_iota == row, 1.0, 0.0))
+        for k in range(own):
+            here = sent_r & (rank_r == k * members + member) & (group == g)
+            own_from[k] = own_from[k] + jnp.where(here, owner_r + 1, 0)
+    places[...] = jnp.broadcast_to(own_place, places.shape)
+    for k in range(own):
+        origin[k] = jnp.sum(own_from[k]) - 1
+    most[0] = jnp.max(peak)
     hot = jnp.concatenate(hots, axis=0).astype(BF)
     load.wait()
-    rows = dot_nn(hot, table[...])
-    for g in range(groups):
-        payload[g] = rows[g * room : (g + 1) * room].astype(BF)
-    places[...] = jnp.broadcast_to(own_place, places.shape)
-    most[...] = jnp.broadcast_to(jnp.max(peak, axis=1, keepdims=True), most.shape)
-
-
-def fetch(ints, slots_row, draft_ids, table, groups, members, room):
-    count = draft_ids.size // groups
-    width = table.shape[1]
+    payload[...] = dot_nn(hot, table[...]).reshape(payload.shape).astype(BF)
+
+
+def fetch(turn, slots_row, ids_cols, table, groups, members):
+    count = ids_cols.size // groups
     outs = [
-        jax.ShapeDtypeStruct((groups, room, width), BF),
+        jax.ShapeDtypeStruct((groups * members, table.shape[1] // AUX, AUX), BF),
         jax.ShapeDtypeStruct((count, AUX), jnp.int32),
-        jax.ShapeDtypeStruct((8, AUX), jnp.int32),
+        jax.ShapeDtypeStruct((count // members,), jnp.int32),
+        jax.ShapeDtypeStruct((1,), jnp.int32),
     ]
     return pl.pallas_call(
-        functools.partial(fetch_kernel, members=members),
+        functools.partial(fetch_kernel, groups=groups, members=members),
         grid=(1,),
-        in_specs=scalars(1) + whole([slots_row, draft_ids]) + streamed(1),
-        out_specs=whole(outs),
+        in_specs=scalars(1) + whole([slots_row, ids_cols]) + streamed(1),
+        out_specs=whole(outs[:2]) + scalars(2),
         out_shape=outs,
         scratch_shapes=[pltpu.VMEM(table.shape, table.dtype), pltpu.SemaphoreType.DMA],
         compiler_params=PARAMS,
-        cost_estimate=cost(2 * groups * room * table.size, 2 * table.size),
+        cost_estimate=cost(2 * groups * members * table.size, 2 * table.size),
         name="fetch",
-    )(ints, slots_row, draft_ids, table)
+    )(turn, slots_row, ids_cols, table)
+
+
+def hand_kernel(origin, came, spread):
+    peers, own, lines = spread.shape[0], origin.shape[0], came.shape[1]
+    for k in range(own):
+        source = origin[k]
+        row = came[jnp.maximum(source, 0)]
+        row = jnp.where(source >= 0, row.astype(F32), 0.0).astype(BF)
+        for j in range(peers):
+            spread[j, k * lines : (k + 1) * lines, :] = row
+
+
+def hand(origin, came, members):
+    own = origin.shape[0]
+    out = jax.ShapeDtypeStruct((members, own * came.shape[1], AUX), BF)
+    return pl.pallas_call(
+        hand_kernel,
+        in_specs=scalars(1) + near(1),
+        out_specs=near(1)[0],
+        out_shape=out,
+        compiler_params=SMALL,
+        name="hand",
+    )(origin, came)
 
 
 def rows_of(arrived, places):
-    peers, room, width = arrived.shape
     count = places.shape[0]
-    slot = lax.broadcasted_iota(jnp.int32, (count, peers * room), 1)
+    width = arrived.size // count
+    slot = lax.broadcasted_iota(jnp.int32, (count, count), 1)
     hot = jnp.where(slot == places[:, :1], 1.0, 0.0).astype(BF)
-    slots = jnp.concatenate([arrived[j] for j in range(peers)], axis=0)
-    return dot_nn(hot, slots)
+    lines = arrived[...].astype(F32).reshape(count, width // AUX, AUX)
+    return dot_nn(hot, lines.reshape(count, width).astype(BF))
 
 
 def place_kernel(arrived, places, before, out):
@@ -279,7 +314,7 @@
     return pl.pallas_call(
         attend_kernel,
         grid=(1,),
-        in_specs=scalars(1) + whole([arrived, places, extra, gain]) + streamed(4),
+        in_specs=scalars(1) + near(1) + whole([places, extra, gain]) + streamed(4),
         out_specs=whole(outs),
         out_shape=outs,
         scratch_shapes=[pltpu.VMEM(a.shape, a.dtype) for a in far]
@@ -438,7 +473,7 @@
     return pl.pallas_call(
         functools.partial(join_kernel, heads=heads, size=size),
         grid=(1,),
-        in_specs=whole([parts, blocks]),
+        in_specs=near(1) + whole([blocks]),
         out_specs=whole([out])[0],
         out_shape=out,
         compiler_params=PARAMS,
@@ -468,7 +503,7 @@
     return pl.pallas_call(
         functools.partial(project_kernel, heads=heads, size=size),
         grid=(1,),
-        in_specs=whole([parts, out_weight]),
+        in_specs=near(1) + whole([out_weight]),
         out_specs=whole([out])[0],
         out_shape=out,
         compiler_params=PARAMS,
@@ -537,7 +572,7 @@
     return pl.pallas_call(
         functools.partial(feed_kernel, count=len(weights)),
         grid=(1,),
-        in_specs=whole([spread, embedded, gain]) + streamed(len(weights)),
+        in_specs=near(1) + whole([embedded, gain]) + streamed(len(weights)),
         out_specs=whole(outs),
         out_shape=outs,
         scratch_shapes=[pltpu.VMEM((units, width), BF)] * 3
@@ -643,36 +678,34 @@
     def across(value):
         return lax.ppermute(value, "req", [(g, g ^ 1) for g in range(groups)])
 
-    def exchange(base):
-        where = jnp.stack([group_index, member, base]).astype(jnp.int32)
-        payload, places, most = fetch(
-            where, current_slot[None], draft_ids, embed_table, groups, members, ROOM
+    def exchange(turn):
+        sent, places, origin, most = fetch(
+            turn, current_slot[None], draft_ids.T, embed_table, groups, members
         )
-        slots = lax.all_to_all(payload, "req", 0, 0, tiled=True)
-        return payload, slots, places, most[0, 0]
-
-    def spread_slots(slots):
-        held = jnp.sum(slots.astype(F32), axis=0).astype(BF)
-        spread = jnp.broadcast_to(held[None], (members,) + held.shape)
-        return lax.all_to_all(spread, "tok", 0, 0, tiled=True)
-
-    sent, slots, places, most = exchange(jnp.int32(0))
-
-    low, high = pack(gate_weight.T, up_weight.T, down_weight.T, sent)
-    low, high, slots = lax.optimization_barrier((low, high, slots))
-    arrived = spread_slots(slots)
-    near = [turn(low, 1), turn(high, -1), turn(high, 1), turn(low, -1)]
+        came = lax.all_to_all(sent, ("req", "tok"), 0, 0, tiled=True)
+        return came, places, origin, most
+
+    def plane(rows):
+        return lax.all_to_all(rows, "tok", 0, 0, tiled=True)
+
+    came, places, origin, most = exchange(jnp.zeros((1,), jnp.int32))
+
+    low, high = pack(gate_weight.T, up_weight.T, down_weight.T, places)
+    low, high, came = lax.optimization_barrier((low, high, came))
+    handed = hand(origin, came, members)
+    arrived = plane(handed)
+    near_a = [turn(low, 1), turn(high, -1)]
 
     def more(carry):
-        return carry[0] < most
+        return carry[0][0] < most[0]
 
     def round_of(carry):
-        base, rows = carry
-        _, later, spots, _ = exchange(base)
-        return base + ROOM, place(spread_slots(later), spots, rows)
+        at, rows = carry
+        later, spots, froms, _ = exchange(at)
+        return at + 1, place(plane(hand(froms, later, members)), spots, rows)
 
     _, extra = lax.while_loop(
-        more, round_of, (jnp.int32(ROOM), jnp.zeros((members * own, width), BF))
+        more, round_of, (jnp.ones((1,), jnp.int32), jnp.zeros((members * own, width), BF))
     )
 
     slot_owner = inverse_of(current_slot)
@@ -705,9 +738,9 @@
         mamba_out,
         members,
     )
-    *near, chosen, _ = lax.optimization_barrier((*near, chosen, parts))
-    far = [turn(near[0], 1), turn(near[1], -1)]
-    weights = [low, high] + near
+    *near_a, chosen, _ = lax.optimization_barrier((*near_a, chosen, parts))
+    weights = [low, high] + near_a
+    far = [turn(near_a[0], 1), turn(near_a[1], -1), turn(high, 1), turn(low, -1)]
     weights += [across(w) for w in weights]
     joined = lax.all_to_all(join(parts, blocks, query_heads, head_size), "tok", 0, 0, tiled=True)
     spread = project(joined, attention_out.T, blocks.shape[1], query_heads, head_size)

time: 148 us -> 141 us (0.953)
  starting transfers between devices: 49.3 us -> 42.8 us
  local copies, waits for them, and re-layouts: 8.89 us -> 5.13 us
  waiting for transfers between devices: 42.9 us -> 46 us
  other arithmetic: 5.28 us -> 3.68 us
    all_to_all x2, waiting for transfers between devices: 22.6 us -> 18.8 us  [the longest x1 13.4 us: exchange(): came = lax.all_to_all(sent, ('req', 'tok'), 0, 0, tiled=True)]
    all_to_all x1, starting transfers between devices: 7.15 us -> 4.14 us  [local(): lax.all_to_all(join(parts, blocks, query_heads, head_size), 'tok', 0, 0,...]
    all_to_all x1, starting transfers between devices: 6.36 us -> 3.56 us  [local(): added = lax.all_to_all(spread, 'tok', 0, 0, tiled=True)]
    ppermute x9, waiting for transfers between devices: 14.6 us -> 17.3 us  [turn(): lax.ppermute(value, 'req', [(g, (g + by * cores) % groups) for g in range...]
    ppermute x9, starting transfers between devices: 13.9 us -> 11.4 us  [turn(): lax.ppermute(value, 'req', [(g, (g + by * cores) % groups) for g in range...]
    all_to_all x1, waiting for transfers between devices: 3.96 us -> 6.18 us  [local(): added = lax.all_to_all(spread, 'tok', 0, 0, tiled=True)]
    all_to_all x2, starting transfers between devices: 12.6 us -> 14.7 us  [the longest x1 11.1 us: exchange(): came = lax.all_to_all(sent, ('req', 'tok'), 0, 0, tiled=True)]
    all_to_all x1, waiting for transfers between devices: 0.89 us -> 2.55 us  [local(): mlp_rows = lax.all_to_all(mlp_part, 'tok', 0, 0, tiled=True)]
  transfers between devices with their start and end apart: 24 -> 24, of which waited for: 7 -> 11; matrix products, arithmetic and copies ran while one was open for 5% -> 4% of each run, Pallas kernels for 23% -> 25%
where the time goes in v6:
time: 141 us; the launch traced here: 140 us
  waiting for transfers between devices  46 us (33%)
  starting transfers between devices  42.8 us (30%)
  Pallas kernels  38.5 us (27%)
  local copies, waits for them, and re-layouts  5.13 us (4%)
  other arithmetic  3.68 us (3%)
  between operations  2.94 us (2%)
    ppermute x9, waiting for transfers between devices, turn(): lax.ppermute(value, 'req', [(g, (g + by * cores) % groups) for g in range...  17.3 us
    all_to_all x1, waiting for transfers between devices, exchange(): came = lax.all_to_all(sent, ('req', 'tok'), 0, 0, tiled=True)  13.4 us
    ppermute x9, starting transfers between devices, turn(): lax.ppermute(value, 'req', [(g, (g + by * cores) % groups) for g in range...  11.4 us
    all_to_all x1, starting transfers between devices, exchange(): came = lax.all_to_all(sent, ('req', 'tok'), 0, 0, tiled=True)  11.1 us
    pallas_call x1, Pallas kernels, feed(): pl.pallas_call(functools.partial(feed_kernel, count=len(weights)), grid=(...  9.12 us
    pallas_call x1, Pallas kernels, attend(): pl.pallas_call(attend_kernel, grid=(1,), in_specs=scalars(1) + near(1) +...  7.28 us
    pallas_call x1, Pallas kernels, mamba(): pl.pallas_call(mamba_kernel, grid=(1,), in_specs=scalars(2) + whole([norm...  6.82 us
    all_to_all x1, waiting for transfers between devices, local(): added = lax.all_to_all(spread, 'tok', 0, 0, tiled=True)  6.18 us
  transfers between devices with their start and end apart: 24, of which 11 were waited for; matrix products, arithmetic and copies ran while one was open for 4% of the time, Pallas kernels for 25%

profile of v6, /device:TPU:0, one launch (start us, length us, event | category | flops | bytes accessed | tf_op | source)
XLA Modules:
  0.0 139.6 jit_solution(2024805540759355805)
XLA Ops:
  0.7 4.3 %fetch.2 = (bf16[128,24,128]{2,1,0:T(8,128)(2,1)}, s32[64,128]{1,0:T(8,128)}, s32[4]{0:T(128)}, s32[1]{0:T(128)}) custom-call(s32[1]{0:T(128)} %constant.90.clone.1.turn, s32[1,32]{1,0:T(1,128)} %bitcast.20, s32[16,32]{1,0:T(8,128)} %bitcast.26, bf16[512,3072]{1,0:T(8,128)(2,1)} %table_far.1), custom_call_target="tpu_custom_call" | custom-call | flops 402653184 | bytes 3145728 | tf_op jit(solution)/shard_map/fetch/pallas_call | solution.py:146
  5.0 11.1 %all-to-all-start.2 = ((bf16[128,24,128]{2,1,0:T(8,128)(2,1)}), bf16[128,24,128]{2,1,0:T(8,128)(2,1)S(1)}, u32[]{:S(2)}, u32[]{:S(2)}) async-start(bf16[128,24,128]{2,1,0:T(8,128)(2,1)} %get-tuple-element.66), calls=%async_computation.2 | async-start | bytes 1572864 | tf_op jit(solution)/shard_map/all_to_all | solution.py:685
  16.1 2.8 %pack.1 = (bf16[144,3072]{1,0:T(8,128)(2,1)}, bf16[144,3072]{1,0:T(8,128)(2,1)}) custom-call(bf16[96,3072]{1,0:T(8,128)(2,1)} %bitcast.22, bf16[96,3072]{1,0:T(8,128)(2,1)} %bitcast.23, bf16[96,3072]{1,0:T(8,128)(2,1)} %bitcast.24, s32[64,128]{1,0:T(8,128)} %get-tuple-element.63.ready.places), custom_call_target="tpu_custom_call" | custom-call | bytes 1024 | tf_op jit(solution)/shard_map/pack/pallas_call | solution.py:596
  19.0 13.4 %all-to-all-done.2.came = bf16[128,24,128]{2,1,0:T(8,128)(2,1)S(1)} async-done(((bf16[128,24,128]{2,1,0:T(8,128)(2,1)}), bf16[128,24,128]{2,1,0:T(8,128)(2,1)S(1)}, u32[]{:S(2)}, u32[]{:S(2)}) %all-to-all-start.2) | async-done | bytes 786464 | tf_op jit(solution)/shard_map/all_to_all | solution.py:685
  32.5 0.9 collective-permute-start.1
  33.4 1.1 collective-permute-start.8
  34.5 0.8 collective-permute-start
  35.4 2.4 %collective-permute-start.9 = (bf16[144,3072]{1,0:T(8,128)(2,1)}, bf16[144,3072]{1,0:T(8,128)(2,1)}, u32[]{:S(2)}, u32[]{:S(2)}) collective-permute-start(bf16[144,3072]{1,0:T(8,128)(2,1)} %get-tuple-element.74.refs_0_), channel_id=1, source_target_pairs={{0,96},{16,112},{32,0},{48,16},{64,32},{80,48},{96,64},{112,80},{1... | collective-permute-start | bytes 2654216 | tf_op jit(solution)/shard_map/ppermute | solution.py:674
  37.8 1.3 hand.2
  39.2 0.6 while.10
  39.8 3.6 %all-to-all-start.3 = ((bf16[16,96,128]{2,1,0:T(8,128)(2,1)}), bf16[16,96,128]{2,1,0:T(8,128)(2,1)S(1)}, u32[]{:S(2)}, u32[]{:S(2)}) async-start(bf16[16,96,128]{2,1,0:T(8,128)(2,1)} %hand.2), calls=%async_computation.3 | async-start | bytes 786432 | tf_op jit(solution)/shard_map/all_to_all | solution.py:689
  43.4 0.6 gather_fusion
  44.0 0.6 gather_fusion.1
  46.7 0.6 pad_add_fusion.ints
  47.3 5.4 %all-to-all-done.3.arrived = bf16[16,96,128]{2,1,0:T(8,128)(2,1)S(1)} async-done(((bf16[16,96,128]{2,1,0:T(8,128)(2,1)}), bf16[16,96,128]{2,1,0:T(8,128)(2,1)S(1)}, u32[]{:S(2)}, u32[]{:S(2)}) %all-to-all-start.3) | async-done | bytes 393248 | tf_op jit(solution)/shard_map/all_to_all | solution.py:689
  52.7 0.7 copy-done.8
  53.4 7.3 %attend.1 = (bf16[16,4,896]{2,1,0:T(4,128)(2,1)}, bf16[64,3072]{1,0:T(8,128)(2,1)}, bf16[64,3072]{1,0:T(8,128)(2,1)}) custom-call(s32[9]{0:T(128)} %pad_add_fusion.ints, bf16[16,96,128]{2,1,0:T(8,128)(2,1)} %copy-done.8, s32[64,128]{1,0:T(8,128)} %get-tuple-element.63.ready.places, bf16[64,3072]{1,0:T(8,128)(2,1)S(1)} %get-tuple-element.69.extra, ...), custom_call_target="tpu_custom_call" | custom-call | flops 603979776 | bytes 6815744 | tf_op jit(solution)/shard_map/attend/pallas_call | solution.py:314
  60.7 3.7 %all-to-all-start.4 = ((bf16[16,4,896]{2,1,0:T(4,128)(2,1)}), bf16[16,4,896]{2,1,0:T(4,128)(2,1)S(1)}, u32[]{:S(2)}, u32[]{:S(2)}) async-start(bf16[16,4,896]{2,1,0:T(4,128)(2,1)} %get-tuple-element.70), calls=%async_computation.4 | async-start | bytes 229376 | tf_op jit(solution)/shard_map/all_to_all | solution.py:728
  64.4 0.6 pad_maximum_fusion.1.reals
  65.0 6.8 %mamba.1 = (bf16[16,96,128]{2,1,0:T(8,128)(2,1)}, bf16[4,1,128,256]{3,2,1,0:T(8,128)(2,1)}) custom-call(s32[9]{0:T(128)} %pad_add_fusion.ints, f32[3]{0:T(128)} %pad_maximum_fusion.1.reals, bf16[64,3072]{1,0:T(8,128)(2,1)} %get-tuple-element.71.normed, bf16[3072,128]{1,0:T(8,128)(2,1)} %input_weight.1, bf16[3072,128]{1,0:T(8,128)(2,1)} %gate_weight.1, ...), custom_call_target="tpu_custom_call" | custom-call | flops 402653184 | bytes 6291456 | tf_op jit(solution)/shard_map/mamba/pallas_call | solution.py:433
  72.1 2.7 %collective-permute-done.refs_2_ = bf16[144,3072]{1,0:T(8,128)(2,1)} collective-permute-done((bf16[144,3072]{1,0:T(8,128)(2,1)}, bf16[144,3072]{1,0:T(8,128)(2,1)}, u32[]{:S(2)}, u32[]{:S(2)}) %collective-permute-start) | collective-permute-done | bytes 884768 | tf_op jit(solution)/shard_map/ppermute | solution.py:674
  74.8 3.2 %collective-permute-start.7 = (bf16[144,3072]{1,0:T(8,128)(2,1)}, bf16[144,3072]{1,0:T(8,128)(2,1)}, u32[]{:S(2)}, u32[]{:S(2)}) collective-permute-start(bf16[144,3072]{1,0:T(8,128)(2,1)} %collective-permute-done.1.refs_3_), channel_id=1, source_target_pairs={{0,96},{16,112},{32,0},{48,16},{64,32},{80,48},{96,64},{112,80},{1... | collective-permute-start | bytes 2654216 | tf_op jit(solution)/shard_map/ppermute | solution.py:674
  78.1 0.5 collective-permute-start.3
  78.7 2.2 %join.1 = bf16[16,120,128]{2,1,0:T(8,128)(2,1)} custom-call(bf16[16,4,896]{2,1,0:T(4,128)(2,1)} %copy-done.15, bf16[16,96,128]{2,1,0:T(8,128)(2,1)} %get-tuple-element.72.blocks), custom_call_target="tpu_custom_call" | custom-call | tf_op jit(solution)/shard_map/join/pallas_call | solution.py:473
  80.8 4.1 %all-to-all-start.5 = ((bf16[16,120,128]{2,1,0:T(8,128)(2,1)}), bf16[16,120,128]{2,1,0:T(8,128)(2,1)S(1)}, u32[]{:S(2)}, u32[]{:S(2)}) async-start(bf16[16,120,128]{2,1,0:T(8,128)(2,1)} %join.1), calls=%async_computation.5 | async-start | bytes 983040 | tf_op jit(solution)/shard_map/all_to_all | solution.py:745
  85.0 11.4 %collective-permute-done.6.refs_8_ = bf16[144,3072]{1,0:T(8,128)(2,1)} collective-permute-done((bf16[144,3072]{1,0:T(8,128)(2,1)}, bf16[144,3072]{1,0:T(8,128)(2,1)}, u32[]{:S(2)}, u32[]{:S(2)}) %collective-permute-start.6) | collective-permute-done | bytes 884768 | tf_op jit(solution)/shard_map/ppermute | solution.py:674
  96.4 0.4 all-to-all-done.5.parts
  96.8 0.8 copy-done.7
  97.5 2.2 %project.1 = bf16[16,96,128]{2,1,0:T(8,128)(2,1)} custom-call(bf16[16,120,128]{2,1,0:T(8,128)(2,1)} %copy-done.7, bf16[192,768]{1,0:T(8,128)(2,1)} %bitcast.28), custom_call_target="tpu_custom_call" | custom-call | tf_op jit(solution)/shard_map/project/pallas_call | solution.py:503
  99.9 0.4 collective-permute-start.10
  100.5 0.4 collective-permute-start.12
  101.2 3.6 %all-to-all-start.6 = ((bf16[16,96,128]{2,1,0:T(8,128)(2,1)}), bf16[16,96,128]{2,1,0:T(8,128)(2,1)S(1)}, u32[]{:S(2)}, u32[]{:S(2)}) async-start(bf16[16,96,128]{2,1,0:T(8,128)(2,1)} %project.1), calls=%async_computation.6 | async-start | bytes 786432 | tf_op jit(solution)/shard_map/all_to_all | solution.py:749
  104.8 0.6 gather_fusion.2
  105.6 1.4 collective-permute-start.16
  107.0 0.5 collective-permute-done.11.refs_13_
  107.5 1.4 collective-permute-start.17
  108.9 0.6 fusion
  109.5 6.2 %all-to-all-done.6.spread = bf16[16,96,128]{2,1,0:T(8,128)(2,1)S(1)} async-done(((bf16[16,96,128]{2,1,0:T(8,128)(2,1)}), bf16[16,96,128]{2,1,0:T(8,128)(2,1)S(1)}, u32[]{:S(2)}, u32[]{:S(2)}) %all-to-all-start.6) | async-done | bytes 393248 | tf_op jit(solution)/shard_map/all_to_all | solution.py:749
  115.7 0.7 copy-done.9
  116.4 9.1 %feed.1 = (bf16[16,4,3072]{2,1,0:T(4,128)(2,1)}, bf16[64,3072]{1,0:T(8,128)(2,1)}) custom-call(bf16[16,96,128]{2,1,0:T(8,128)(2,1)} %copy-done.9, bf16[64,3072]{1,0:T(8,128)(2,1)} %get-tuple-element.73.embedded, f32[1,3072]{1,0:T(1,128)} %bitcast.33, bf16[144,3072]{1,0:T(8,128)(2,1)} %get-tuple-element.74.refs_0_, ...), custom_call_target="tpu_custom_call" | custom-call | flops 905969664 | bytes 14155776 | tf_op jit(solution)/shard_map/feed/pallas_call | solution.py:572
  125.5 3.6 %all-to-all-start.7 = ((bf16[16,4,3072]{2,1,0:T(4,128)(2,1)}), bf16[16,4,3072]{2,1,0:T(4,128)(2,1)S(1)}, u32[]{:S(2)}, u32[]{:S(2)}) async-start(bf16[16,4,3072]{2,1,0:T(4,128)(2,1)} %get-tuple-element.84), calls=%async_computation.7 | async-start | bytes 786432 | tf_op jit(solution)/shard_map/all_to_all | solution.py:751
  129.1 0.6 and_select_fusion.3.turns
  129.7 2.5 %collective-permute-done.15.refs_1_ = bf16[8,128,256]{2,1,0:T(8,128)(2,1)S(1)} collective-permute-done((bf16[8,128,256]{2,1,0:T(8,128)(2,1)S(1)}, bf16[8,128,256]{2,1,0:T(8,128)(2,1)S(1)}, u32[]{:S(2)}, u32[]{:S(2)}) %collective-permute-start.15) | collective-permute-done | bytes 524320 | tf_op jit(solution)/shard_map/ppermute | solution.py:674
  132.2 0.7 collective-permute-done.17.refs_3_
  133.0 2.5 %pick.1 = f32[4,128,256]{2,1,0:T(8,128)} custom-call(s32[4]{0:T(128)} %and_select_fusion.3.turns, s32[4]{0:T(128)} %get-tuple-element.104.rows, bf16[8,128,256]{2,1,0:T(8,128)(2,1)} %copy-done.6, bf16[8,128,256]{2,1,0:T(8,128)(2,1)} %copy-done.14, bf16[8,128,256]{2,1,0:T(8,128)(2,1)} %collective-permute-done.16.refs_2_, ...), custom_call_target="tpu_custom_call" | custom-call | tf_op jit(solution)/shard_map/pick/pallas_call | solution.py:622
  135.5 0.8 constant_dynamic-slice_fusion
  136.3 2.6 %all-to-all-done.7 = bf16[16,4,3072]{2,1,0:T(4,128)(2,1)S(1)} async-done(((bf16[16,4,3072]{2,1,0:T(4,128)(2,1)}), bf16[16,4,3072]{2,1,0:T(4,128)(2,1)S(1)}, u32[]{:S(2)}, u32[]{:S(2)}) %all-to-all-start.7) | async-done | bytes 393248 | tf_op jit(solution)/shard_map/all_to_all | solution.py:751
  139.0 0.6 add_convert_fusion
  (63 shorter events, 1.7 us)
Async XLA Ops:
  0.6 42.7 %copy-start = (s32[32]{0:T(128)S(1)}, s32[32]{0:T(128)}, u32[]{:S(2)}) copy-start(s32[32]{0:T(128)} %param.30) | copy-start | bytes 388
  0.6 18.3 %copy-start.3 = (s32[32]{0:T(128)S(1)}, s32[32]{0:T(128)}, u32[]{:S(2)}) copy-start(s32[32]{0:T(128)} %param.31) | copy-start | bytes 388
  5.0 32.9 %copy-start.2 = (s32[4]{0:T(128)S(1)}, s32[4]{0:T(128)}, u32[]{:S(2)}) copy-start(s32[4]{0:T(128)} %get-tuple-element.62.origin) | copy-start | bytes 52
  5.0 34.2 %copy-start.16 = (s32[32,16]{0,1:T(8,128)S(1)}, s32[32,16]{0,1:T(8,128)}, u32[]{:S(2)}) copy-start(s32[32,16]{0,1:T(8,128)} %param.29) | copy-start | bytes 6148
  5.0 27.5 %all-to-all-start.2 = ((bf16[128,24,128]{2,1,0:T(8,128)(2,1)}), bf16[128,24,128]{2,1,0:T(8,128)(2,1)S(1)}, u32[]{:S(2)}, u32[]{:S(2)}) async-start(bf16[128,24,128]{2,1,0:T(8,128)(2,1)} %get-tuple-element.66), calls=%async_computation.2 | async-start | bytes 1572864 | tf_op jit(solution)/shard_map/all_to_all | solution.py:685
  32.5 42.4 %collective-permute-start.1 = (bf16[144,3072]{1,0:T(8,128)(2,1)}, bf16[144,3072]{1,0:T(8,128)(2,1)}, u32[]{:S(2)}, u32[]{:S(2)}) collective-permute-start(bf16[144,3072]{1,0:T(8,128)(2,1)} %get-tuple-element.75.refs_1_), channel_id=1, source_target_pairs={{0,96},{16,112},{32,0},{48,16},{64,32},{80,48},{96,64},{112,80},{1... | collective-permute-start | bytes 2654216 | tf_op jit(solution)/shard_map/ppermute | solution.py:674
  33.4 44.7 %collective-permute-start.8 = (bf16[144,3072]{1,0:T(8,128)(2,1)}, bf16[144,3072]{1,0:T(8,128)(2,1)}, u32[]{:S(2)}, u32[]{:S(2)}) collective-permute-start(bf16[144,3072]{1,0:T(8,128)(2,1)} %get-tuple-element.75.refs_1_), channel_id=1, source_target_pairs={{0,32},{16,48},{32,64},{48,80},{64,96},{80,112},{96,0},{112,16},{1... | collective-permute-start | bytes 2654216 | tf_op jit(solution)/shard_map/ppermute | solution.py:674
  34.5 40.3 %collective-permute-start = (bf16[144,3072]{1,0:T(8,128)(2,1)}, bf16[144,3072]{1,0:T(8,128)(2,1)}, u32[]{:S(2)}, u32[]{:S(2)}) collective-permute-start(bf16[144,3072]{1,0:T(8,128)(2,1)} %get-tuple-element.74.refs_0_), channel_id=1, source_target_pairs={{0,32},{16,48},{32,64},{48,80},{64,96},{80,112},{96,0},{112,16},{1... | collective-permute-start | bytes 2654216 | tf_op jit(solution)/shard_map/ppermute | solution.py:674
  35.4 43.2 %collective-permute-start.9 = (bf16[144,3072]{1,0:T(8,128)(2,1)}, bf16[144,3072]{1,0:T(8,128)(2,1)}, u32[]{:S(2)}, u32[]{:S(2)}) collective-permute-start(bf16[144,3072]{1,0:T(8,128)(2,1)} %get-tuple-element.74.refs_0_), channel_id=1, source_target_pairs={{0,96},{16,112},{32,0},{48,16},{64,32},{80,48},{96,64},{112,80},{1... | collective-permute-start | bytes 2654216 | tf_op jit(solution)/shard_map/ppermute | solution.py:674
  39.2 4.8 %copy-start.4 = (s32[32]{0:T(128)S(1)}, s32[32]{0:T(128)}, u32[]{:S(2)}) copy-start(s32[32]{0:T(128)} %param.33) | copy-start | bytes 388
  39.8 12.9 %all-to-all-start.3 = ((bf16[16,96,128]{2,1,0:T(8,128)(2,1)}), bf16[16,96,128]{2,1,0:T(8,128)(2,1)S(1)}, u32[]{:S(2)}, u32[]{:S(2)}) async-start(bf16[16,96,128]{2,1,0:T(8,128)(2,1)} %hand.2), calls=%async_computation.3 | async-start | bytes 786432 | tf_op jit(solution)/shard_map/all_to_all | solution.py:689
  52.7 0.7 copy-start.8
  60.7 11.4 %all-to-all-start.4 = ((bf16[16,4,896]{2,1,0:T(4,128)(2,1)}), bf16[16,4,896]{2,1,0:T(4,128)(2,1)S(1)}, u32[]{:S(2)}, u32[]{:S(2)}) async-start(bf16[16,4,896]{2,1,0:T(4,128)(2,1)} %get-tuple-element.70), calls=%async_computation.4 | async-start | bytes 229376 | tf_op jit(solution)/shard_map/all_to_all | solution.py:728
  65.0 13.0 %copy-start.10 = (bf16[144,3072]{1,0:T(8,128)(2,1)S(1)}, bf16[144,3072]{1,0:T(8,128)(2,1)}, u32[]{:S(2)}) copy-start(bf16[144,3072]{1,0:T(8,128)(2,1)} %get-tuple-element.74.refs_0_) | copy-start | bytes 2654212
  65.0 13.0 %copy-start.11 = (bf16[144,3072]{1,0:T(8,128)(2,1)S(1)}, bf16[144,3072]{1,0:T(8,128)(2,1)}, u32[]{:S(2)}) copy-start(bf16[144,3072]{1,0:T(8,128)(2,1)} %get-tuple-element.75.refs_1_) | copy-start | bytes 2654212
  71.9 29.1 %copy-start.18 = (s32[32]{0:T(128)S(1)}, s32[32]{0:T(128)}, u32[]{:S(2)}) copy-start(s32[32]{0:T(128)} %param.32) | copy-start | bytes 388
  71.9 33.5 %copy-start.17 = (bf16[4,1,128,256]{3,2,1,0:T(8,128)(2,1)S(1)}, bf16[4,1,128,256]{3,2,1,0:T(8,128)(2,1)}, u32[]{:S(2)}) copy-start(bf16[4,1,128,256]{3,2,1,0:T(8,128)(2,1)} %get-tuple-element.85) | copy-start | bytes 786436
  72.1 6.6 %copy-start.15 = (bf16[16,4,896]{2,1,0:T(4,128)(2,1)}, bf16[16,4,896]{2,1,0:T(4,128)(2,1)S(1)}, u32[]{:S(2)}) copy-start(bf16[16,4,896]{2,1,0:T(4,128)(2,1)S(1)} %all-to-all-done.4.parts) | copy-start | bytes 344068
  74.8 21.6 %collective-permute-start.6 = (bf16[144,3072]{1,0:T(8,128)(2,1)}, bf16[144,3072]{1,0:T(8,128)(2,1)}, u32[]{:S(2)}, u32[]{:S(2)}) collective-permute-start(bf16[144,3072]{1,0:T(8,128)(2,1)} %collective-permute-done.refs_2_), channel_id=1, source_target_pairs={{0,32},{16,48},{32,64},{48,80},{64,96},{80,112},{96,0},{112,16},{1... | collective-permute-start | bytes 2654216 | tf_op jit(solution)/shard_map/ppermute | solution.py:674
  74.8 25.0 %collective-permute-start.7 = (bf16[144,3072]{1,0:T(8,128)(2,1)}, bf16[144,3072]{1,0:T(8,128)(2,1)}, u32[]{:S(2)}, u32[]{:S(2)}) collective-permute-start(bf16[144,3072]{1,0:T(8,128)(2,1)} %collective-permute-done.1.refs_3_), channel_id=1, source_target_pairs={{0,96},{16,112},{32,0},{48,16},{64,32},{80,48},{96,64},{112,80},{1... | collective-permute-start | bytes 2654216 | tf_op jit(solution)/shard_map/ppermute | solution.py:674
  78.1 21.9 %collective-permute-start.2 = (bf16[144,3072]{1,0:T(8,128)(2,1)S(1)}, bf16[144,3072]{1,0:T(8,128)(2,1)}, u32[]{:S(2)}, u32[]{:S(2)}) collective-permute-start(bf16[144,3072]{1,0:T(8,128)(2,1)S(1)} %copy-done.10), channel_id=1, source_target_pairs={{0,16},{16,0},{32,48},{48,32},{64,80},{80,64},{96,112},{112,96},{1... | collective-permute-start | bytes 2654216 | tf_op jit(solution)/shard_map/ppermute | solution.py:679
  78.1 22.2 %collective-permute-start.3 = (bf16[144,3072]{1,0:T(8,128)(2,1)S(1)}, bf16[144,3072]{1,0:T(8,128)(2,1)}, u32[]{:S(2)}, u32[]{:S(2)}) collective-permute-start(bf16[144,3072]{1,0:T(8,128)(2,1)S(1)} %copy-done.11), channel_id=1, source_target_pairs={{0,16},{16,0},{32,48},{48,32},{64,80},{80,64},{96,112},{112,96},{1... | collective-permute-start | bytes 2654216 | tf_op jit(solution)/shard_map/ppermute | solution.py:679
  78.6 22.2 %collective-permute-start.4 = (bf16[144,3072]{1,0:T(8,128)(2,1)}, bf16[144,3072]{1,0:T(8,128)(2,1)}, u32[]{:S(2)}, u32[]{:S(2)}) collective-permute-start(bf16[144,3072]{1,0:T(8,128)(2,1)} %collective-permute-done.refs_2_), channel_id=1, source_target_pairs={{0,16},{16,0},{32,48},{48,32},{64,80},{80,64},{96,112},{112,96},{1... | collective-permute-start | bytes 2654216 | tf_op jit(solution)/shard_map/ppermute | solution.py:679
  80.8 15.9 %all-to-all-start.5 = ((bf16[16,120,128]{2,1,0:T(8,128)(2,1)}), bf16[16,120,128]{2,1,0:T(8,128)(2,1)S(1)}, u32[]{:S(2)}, u32[]{:S(2)}) async-start(bf16[16,120,128]{2,1,0:T(8,128)(2,1)} %join.1), calls=%async_computation.5 | async-start | bytes 983040 | tf_op jit(solution)/shard_map/all_to_all | solution.py:745
  96.4 4.1 %collective-permute-start.14 = (bf16[4,128,256]{2,1,0:T(8,128)(2,1)}, bf16[4,128,256]{2,1,0:T(8,128)(2,1)S(1)}, u32[]{:S(2)}, u32[]{:S(2)}) collective-permute-start(bf16[4,128,256]{2,1,0:T(8,128)(2,1)} %bitcast.29), channel_id=1, source_target_pairs={{0,16},{16,0},{32,48},{48,32},{64,80},{80,64},{96,112},{112,96},{1... | collective-permute-start | bytes 786440 | tf_op jit(solution)/shard_map/ppermute | solution.py:679
  96.8 0.8 copy-start.7
  99.8 5.7 %collective-permute-start.5 = (bf16[144,3072]{1,0:T(8,128)(2,1)}, bf16[144,3072]{1,0:T(8,128)(2,1)}, u32[]{:S(2)}, u32[]{:S(2)}) collective-permute-start(bf16[144,3072]{1,0:T(8,128)(2,1)} %collective-permute-done.1.refs_3_), channel_id=1, source_target_pairs={{0,16},{16,0},{32,48},{48,32},{64,80},{80,64},{96,112},{112,96},{1... | collective-permute-start | bytes 2654216 | tf_op jit(solution)/shard_map/ppermute | solution.py:679
  99.9 5.6 %collective-permute-start.10 = (bf16[144,3072]{1,0:T(8,128)(2,1)}, bf16[144,3072]{1,0:T(8,128)(2,1)S(1)}, u32[]{:S(2)}, u32[]{:S(2)}) collective-permute-start(bf16[144,3072]{1,0:T(8,128)(2,1)} %collective-permute-done.6.refs_8_), channel_id=1, source_target_pairs={{0,16},{16,0},{32,48},{48,32},{64,80},{80,64},{96,112},{112,96},{1... | collective-permute-start | bytes 2654216 | tf_op jit(solution)/shard_map/ppermute | solution.py:679
  100.3 7.2 %collective-permute-start.11 = (bf16[144,3072]{1,0:T(8,128)(2,1)}, bf16[144,3072]{1,0:T(8,128)(2,1)S(1)}, u32[]{:S(2)}, u32[]{:S(2)}) collective-permute-start(bf16[144,3072]{1,0:T(8,128)(2,1)} %collective-permute-done.7.refs_9_), channel_id=1, source_target_pairs={{0,16},{16,0},{32,48},{48,32},{64,80},{80,64},{96,112},{112,96},{1... | collective-permute-start | bytes 2654216 | tf_op jit(solution)/shard_map/ppermute | solution.py:679
  100.5 15.2 %collective-permute-start.12 = (bf16[144,3072]{1,0:T(8,128)(2,1)}, bf16[144,3072]{1,0:T(8,128)(2,1)}, u32[]{:S(2)}, u32[]{:S(2)}) collective-permute-start(bf16[144,3072]{1,0:T(8,128)(2,1)} %collective-permute-done.8.refs_10_), channel_id=1, source_target_pairs={{0,16},{16,0},{32,48},{48,32},{64,80},{80,64},{96,112},{112,96},{1... | collective-permute-start | bytes 2654216 | tf_op jit(solution)/shard_map/ppermute | solution.py:679
  100.8 14.8 %collective-permute-start.13 = (bf16[144,3072]{1,0:T(8,128)(2,1)}, bf16[144,3072]{1,0:T(8,128)(2,1)}, u32[]{:S(2)}, u32[]{:S(2)}) collective-permute-start(bf16[144,3072]{1,0:T(8,128)(2,1)} %collective-permute-done.9.refs_11_), channel_id=1, source_target_pairs={{0,16},{16,0},{32,48},{48,32},{64,80},{80,64},{96,112},{112,96},{1... | collective-permute-start | bytes 2654216 | tf_op jit(solution)/shard_map/ppermute | solution.py:679
  101.2 14.5 %all-to-all-start.6 = ((bf16[16,96,128]{2,1,0:T(8,128)(2,1)}), bf16[16,96,128]{2,1,0:T(8,128)(2,1)S(1)}, u32[]{:S(2)}, u32[]{:S(2)}) async-start(bf16[16,96,128]{2,1,0:T(8,128)(2,1)} %project.1), calls=%async_computation.6 | async-start | bytes 786432 | tf_op jit(solution)/shard_map/all_to_all | solution.py:749
  105.4 20.1 %copy-start.6 = (bf16[8,128,256]{2,1,0:T(8,128)(2,1)}, bf16[8,128,256]{2,1,0:T(8,128)(2,1)S(1)}, u32[]{:S(2)}) copy-start(bf16[8,128,256]{2,1,0:T(8,128)(2,1)S(1)} %pad_maximum_fusion.refs_0_) | copy-start | bytes 1572868
  105.5 26.7 %collective-permute-start.15 = (bf16[8,128,256]{2,1,0:T(8,128)(2,1)S(1)}, bf16[8,128,256]{2,1,0:T(8,128)(2,1)S(1)}, u32[]{:S(2)}, u32[]{:S(2)}) collective-permute-start(bf16[8,128,256]{2,1,0:T(8,128)(2,1)S(1)} %pad_maximum_fusion.refs_0_), channel_id=1, source_target_pairs={{0,32},{16,48},{32,64},{48,80},{64,96},{80,112},{96,0},{112,16},{1... | collective-permute-start | bytes 1572872 | tf_op jit(solution)/shard_map/ppermute | solution.py:674
  105.6 10.1 %copy-start.12 = (bf16[144,3072]{1,0:T(8,128)(2,1)}, bf16[144,3072]{1,0:T(8,128)(2,1)S(1)}, u32[]{:S(2)}) copy-start(bf16[144,3072]{1,0:T(8,128)(2,1)S(1)} %collective-permute-done.10.refs_12_) | copy-start | bytes 2654212
  105.6 26.6 %collective-permute-start.16 = (bf16[8,128,256]{2,1,0:T(8,128)(2,1)S(1)}, bf16[8,128,256]{2,1,0:T(8,128)(2,1)}, u32[]{:S(2)}, u32[]{:S(2)}) collective-permute-start(bf16[8,128,256]{2,1,0:T(8,128)(2,1)S(1)} %pad_maximum_fusion.refs_0_), channel_id=1, source_target_pairs={{0,64},{16,80},{32,96},{48,112},{64,0},{80,16},{96,32},{112,48},{1... | collective-permute-start | bytes 1572872 | tf_op jit(solution)/shard_map/ppermute | solution.py:674
  107.5 8.2 %copy-start.13 = (bf16[144,3072]{1,0:T(8,128)(2,1)}, bf16[144,3072]{1,0:T(8,128)(2,1)S(1)}, u32[]{:S(2)}) copy-start(bf16[144,3072]{1,0:T(8,128)(2,1)S(1)} %collective-permute-done.11.refs_13_) | copy-start | bytes 2654212
  107.5 25.4 %collective-permute-start.17 = (bf16[8,128,256]{2,1,0:T(8,128)(2,1)S(1)}, bf16[8,128,256]{2,1,0:T(8,128)(2,1)}, u32[]{:S(2)}, u32[]{:S(2)}) collective-permute-start(bf16[8,128,256]{2,1,0:T(8,128)(2,1)S(1)} %pad_maximum_fusion.refs_0_), channel_id=1, source_target_pairs={{0,96},{16,112},{32,0},{48,16},{64,32},{80,48},{96,64},{112,80},{1... | collective-permute-start | bytes 1572872 | tf_op jit(solution)/shard_map/ppermute | solution.py:674
  115.6 0.7 copy-start.9
  125.5 13.3 %all-to-all-start.7 = ((bf16[16,4,3072]{2,1,0:T(4,128)(2,1)}), bf16[16,4,3072]{2,1,0:T(4,128)(2,1)S(1)}, u32[]{:S(2)}, u32[]{:S(2)}) async-start(bf16[16,4,3072]{2,1,0:T(4,128)(2,1)} %get-tuple-element.84), calls=%async_computation.7 | async-start | bytes 786432 | tf_op jit(solution)/shard_map/all_to_all | solution.py:751
  132.2 0.8 copy-start.14

commit v7 on v6

--- a/solution.py
+++ b/solution.py
@@ -42,6 +42,10 @@
 
 def cost(flops, moved, special=0):
     return pl.CostEstimate(flops=flops, bytes_accessed=moved, transcendentals=special)
+
+
+def lasting(microseconds):
+    return cost(int(microseconds * 1e9), 1024)
 
 
 def whole(shapes):
@@ -175,6 +179,7 @@
         out_specs=near(1)[0],
         out_shape=out,
         compiler_params=SMALL,
+        cost_estimate=lasting(10),
         name="hand",
     )(origin, came)
 
@@ -320,9 +325,7 @@
         scratch_shapes=[pltpu.VMEM(a.shape, a.dtype) for a in far]
         + [pltpu.SemaphoreType.DMA((6,))],
         compiler_params=PARAMS,
-        cost_estimate=cost(
-            2 * tokens * query_weight.size * 2, 2 * (query_weight.size + keys.size * 2), keys.size
-        ),
+        cost_estimate=lasting(20),
         name="attend",
     )(ints, arrived, places, extra, gain, query_weight, keyvalue_weight, keys, values)
 
@@ -419,14 +422,28 @@
     part = dot_nn(jnp.concatenate(gated, axis=0), out_in[...])
     share = part.shape[1] // blocks.shape[0]
     for j in range(blocks.shape[0]):
-        blocks[j] = fold(part[:, j * share : (j + 1) * share]).astype(BF)
-
-
-def mamba(ints, reals, normed, input_weight, gate_weight, state_proj, step_row, states, mamba_out, members):
+        block = fold(part[:, j * share : (j + 1) * share]).astype(BF)
+        blocks[j, : block.shape[0]] = block
+        blocks[j, block.shape[0] :] = jnp.zeros_like(blocks[j, block.shape[0] :])
+
+
+def mamba(
+    ints,
+    reals,
+    normed,
+    input_weight,
+    gate_weight,
+    state_proj,
+    step_row,
+    states,
+    mamba_out,
+    members,
+    room,
+):
     tokens = normed.shape[0]
     share = mamba_out.shape[1] // members
     outs = [
-        jax.ShapeDtypeStruct((members, tokens * share // AUX, AUX), BF),
+        jax.ShapeDtypeStruct((members, tokens * share // AUX + room, AUX), BF),
         jax.ShapeDtypeStruct(states.shape, BF),
     ]
     far = (state_proj, input_weight, gate_weight, states, mamba_out)
@@ -443,16 +460,15 @@
         scratch_shapes=[pltpu.VMEM(a.shape, a.dtype) for a in far]
         + [pltpu.SemaphoreType.DMA((5,))],
         compiler_params=PARAMS,
-        cost_estimate=cost(2 * tokens * state_proj.size * 2, 4 * state_proj.size, tokens * 4096),
+        cost_estimate=lasting(8),
         name="mamba",
     )(ints, reals, normed, input_weight, gate_weight, state_proj, step_row, states, mamba_out)
 
 
-def join_kernel(parts, blocks, payload, *, heads, size):
-    peers, tokens, _ = blocks.shape
-    own = parts.shape[1]
+def join_kernel(parts, blocks, payload, piece, sem, *, heads, size):
+    peers, own, _ = parts.shape
+    rows = heads * own
     aux = parts[:, :, heads * size : heads * size + AUX].astype(F32)
-    payload[:, :tokens, :] = blocks[...]
     for h in range(heads):
         get = lambda k: aux[:, :, k * heads + h : k * heads + h + 1]
         top = get(0) + get(1) + get(2)
@@ -461,22 +477,33 @@
         norm = jnp.sum(factor * total, axis=0)
         value = parts[:, :, h * size : (h + 1) * size].astype(F32)
         summed = jnp.sum(factor * value, axis=0)
-        piece = (summed / norm).astype(BF)
-        for j in range(peers):
-            payload[j, tokens + h * own : tokens + (h + 1) * own, :size] = piece
+        piece[h * own : (h + 1) * own, :] = (summed / norm).astype(BF)
+    first = payload.shape[1] - rows
+    copies = [
+        pltpu.make_async_copy(piece, payload.at[j, pl.ds(first, rows), :], sem.at[j])
+        for j in range(peers)
+    ]
+    for copy in copies:
+        copy.start()
+    for copy in copies:
+        copy.wait()
 
 
 def join(parts, blocks, heads, size):
-    members, tokens, share = blocks.shape
-    own = parts.shape[1]
-    out = jax.ShapeDtypeStruct((members, tokens + heads * own, share), BF)
+    peers, own, _ = parts.shape
     return pl.pallas_call(
         functools.partial(join_kernel, heads=heads, size=size),
         grid=(1,),
-        in_specs=near(1) + whole([blocks]),
-        out_specs=whole([out])[0],
-        out_shape=out,
-        compiler_params=PARAMS,
+        in_specs=near(1) + streamed(1),
+        out_specs=streamed(1)[0],
+        out_shape=jax.ShapeDtypeStruct(blocks.shape, BF),
+        input_output_aliases={1: 0},
+        scratch_shapes=[
+            pltpu.VMEM((heads * own, size), BF),
+            pltpu.SemaphoreType.DMA((peers,)),
+        ],
+        compiler_params=PARAMS,
+        cost_estimate=lasting(20),
         name="join",
     )(parts, blocks)
 
@@ -507,102 +534,157 @@
         out_specs=whole([out])[0],
         out_shape=out,
         compiler_params=PARAMS,
+        cost_estimate=lasting(20),
         name="project",
     )(parts, out_weight)
 
 
-def feed_kernel(spread, embedded, gain, *refs, count):
-    weights = refs[:count]
-    out, mixed, gates, ups, downs, sems = refs[count:]
-    peers, own, width = out.shape
-    tokens = embedded.shape[0]
-    total = gates.shape[0]
-    pieces = []
+def load_units(weights, gates, ups, downs, sems, units):
+    copies = []
     begin = 0
-    units = min(w.shape[0] for w in weights) // 3
     for w in weights:
         for first in range(0, w.shape[0], 3 * units):
-            pieces.append((w, first, begin))
+            trio = []
+            for k, to in enumerate((gates, ups, downs)):
+                copy = pltpu.make_async_copy(
+                    w.at[pl.ds(first + k * units, units), :],
+                    to.at[pl.ds(begin, units), :],
+                    sems.at[len(copies), k],
+                )
+                copy.start()
+                trio.append(copy)
             begin += units
-    copies = []
-    for n, (w, first, at) in enumerate(pieces):
-        trio = []
-        for k, to in enumerate((gates, ups, downs)):
-            copy = pltpu.make_async_copy(
-                w.at[pl.ds(first + k * units, units), :], to.at[pl.ds(at, units), :], sems.at[n, k]
-            )
-            copy.start()
-            trio.append(copy)
-        copies.append((at + units, trio))
+            copies.append((begin, trio))
+    return copies
+
+
+def use_units(second, copies, gates, ups, downs, acc, chunk=192):
+    ready = 0
+    waiting = list(copies)
+    for first in range(0, gates.shape[0], chunk):
+        while ready < first + chunk:
+            ready, trio = waiting.pop(0)
+            for copy in trio:
+                copy.wait()
+        span = slice(first, first + chunk)
+        gate = dot_nt(second, gates[span, :])
+        up = dot_nt(second, ups[span, :])
+        hidden = (gate / (1.0 + jnp.exp(-gate)) * up).astype(BF)
+        part = dot_nn(hidden, downs[span, :])
+        acc = part if acc is None else acc + part
+    return acc
+
+
+def feed_kernel(spread, embedded, gain, *refs, count, units):
+    weights = refs[:count]
+    acc, second, mixed, gates, ups, downs, sems = refs[count:]
+    copies = load_units(weights, gates, ups, downs, sems, units)
+    tokens = embedded.shape[0]
+    peers = spread.shape[0]
     added = jnp.concatenate([unfold(spread[j].astype(F32), tokens) for j in range(peers)], axis=1)
     rows = (embedded[...].astype(F32) + added).astype(BF)
     mixed[...] = rows
     wide = rows.astype(F32)
     factor = lax.rsqrt(jnp.mean(wide * wide, axis=-1, keepdims=True) + 1e-05)
-    second = (wide * factor * gain[...]).astype(BF)
-    chunk = 256
-    waited = 0
-    ready = 0
-    acc = None
-    for c in range(total // chunk):
-        while ready < (c + 1) * chunk:
-            ready, trio = copies[waited]
-            for copy in trio:
-                copy.wait()
-            waited += 1
-        span = slice(c * chunk, (c + 1) * chunk)
-        gate = dot_nt(second, gates[span, :])
-        up = dot_nt(second, ups[span, :])
-        hidden = (gate / (1.0 + jnp.exp(-gate)) * up).astype(BF)
-        part = dot_nn(hidden, downs[span, :])
-        acc = part if acc is None else acc + part
+    rows_norm = (wide * factor * gain[...]).astype(BF)
+    second[...] = rows_norm
+    acc[...] = use_units(rows_norm, copies, gates, ups, downs, None)
+
+
+def rest_kernel(so_far, second, *refs, count, units):
+    weights = refs[:count]
+    out, gates, ups, downs, sems = refs[count:]
+    copies = load_units(weights, gates, ups, downs, sems, units)
+    peers, own, _ = out.shape
+    acc = use_units(second[...], copies, gates, ups, downs, so_far[...])
     for j in range(peers):
         out[j] = acc[j * own : (j + 1) * own, :].astype(BF)
 
 
-def feed(spread, embedded, gain, weights):
-    members = spread.shape[0]
-    tokens, width = embedded.shape
-    units = sum(w.shape[0] for w in weights) // 3
-    count = 3 * units // min(w.shape[0] for w in weights)
+def unit_scratch(weights, units):
+    width = weights[0].shape[1]
+    rows = sum(w.shape[0] for w in weights)
+    count = rows // (3 * units)
+    return [pltpu.VMEM((rows // 3, width), BF)] * 3 + [pltpu.SemaphoreType.DMA((count, 3))]
+
+
+def feed(spread, embedded, gain, weights, units):
     outs = [
-        jax.ShapeDtypeStruct((members, tokens // members, width), BF),
-        jax.ShapeDtypeStruct((tokens, width), BF),
+        jax.ShapeDtypeStruct(embedded.shape, F32),
+        jax.ShapeDtypeStruct(embedded.shape, BF),
+        jax.ShapeDtypeStruct(embedded.shape, BF),
     ]
     return pl.pallas_call(
-        functools.partial(feed_kernel, count=len(weights)),
+        functools.partial(feed_kernel, count=len(weights), units=units),
         grid=(1,),
         in_specs=near(1) + whole([embedded, gain]) + streamed(len(weights)),
         out_specs=whole(outs),
         out_shape=outs,
-        scratch_shapes=[pltpu.VMEM((units, width), BF)] * 3
-        + [pltpu.SemaphoreType.DMA((count, 3))],
-        compiler_params=PARAMS,
-        cost_estimate=cost(6 * tokens * units * width, 6 * units * width),
+        scratch_shapes=unit_scratch(weights, units),
+        compiler_params=PARAMS,
+        cost_estimate=lasting(20),
         name="feed",
     )(spread, embedded, gain, *weights)
 
 
-def pack_kernel(gate, up, down, ready, low, high):
-    half = low.shape[0] // 3
-    for k, part in enumerate((gate, up, down)):
-        low[k * half : (k + 1) * half] = part[:half]
-        high[k * half : (k + 1) * half] = part[half:]
+def feed_rest(acc, second, weights, units, members):
+    tokens, width = acc.shape
+    out = jax.ShapeDtypeStruct((members, tokens // members, width), BF)
+    return pl.pallas_call(
+        functools.partial(rest_kernel, count=len(weights), units=units),
+        grid=(1,),
+        in_specs=whole([acc, second]) + streamed(len(weights)),
+        out_specs=whole([out])[0],
+        out_shape=out,
+        scratch_shapes=unit_scratch(weights, units),
+        compiler_params=PARAMS,
+        cost_estimate=lasting(4),
+        name="feed_rest",
+    )(acc, second, *weights)
+
+
+def pack_kernel(gate, up, down, ready, out):
+    half = gate.shape[0] // 2
+    for h in range(2):
+        for k, part in enumerate((gate, up, down)):
+            at = (3 * h + k) * half
+            out[at : at + half] = part[h * half : (h + 1) * half]
 
 
 def pack(gate, up, down, ready):
     units, width = gate.shape
-    out = jax.ShapeDtypeStruct((3 * units // 2, width), gate.dtype)
+    out = jax.ShapeDtypeStruct((3 * units, width), gate.dtype)
     return pl.pallas_call(
         pack_kernel,
         grid=(1,),
         in_specs=whole([gate, up, down]) + streamed(1),
-        out_specs=whole([out, out]),
-        out_shape=[out, out],
+        out_specs=whole([out])[0],
+        out_shape=out,
         compiler_params=PARAMS,
         cost_estimate=cost(0, 1024),
         name="pack",
     )(gate, up, down, ready)
+
+
+def split_kernel(below, above, beside, ready, low, high):
+    low[...] = below[...]
+    high[...] = above[...]
+
+
+def split(below, above, beside, ready):
+    rows, width = below.shape
+    out = jax.ShapeDtypeStruct((rows // 2, width), below.dtype)
+    block = lambda n: pl.BlockSpec(out.shape, lambda i: (n, 0))
+    return pl.pallas_call(
+        split_kernel,
+        grid=(1,),
+        in_specs=[block(0), block(1)] + streamed(2),
+        out_specs=[block(0), block(0)],
+        out_shape=[out, out],
+        compiler_params=PARAMS,
+        cost_estimate=cost(0, 1024),
+        name="split",
+    )(below, above, beside, ready)
 
 
 def pick_kernel(turns, rows, *refs):
@@ -690,11 +772,9 @@
 
     came, places, origin, most = exchange(jnp.zeros((1,), jnp.int32))
 
-    low, high = pack(gate_weight.T, up_weight.T, down_weight.T, places)
-    low, high, came = lax.optimization_barrier((low, high, came))
-    handed = hand(origin, came, members)
-    arrived = plane(handed)
-    near_a = [turn(low, 1), turn(high, -1)]
+    block = pack(gate_weight.T, up_weight.T, down_weight.T, places)
+    below, above = turn(block, 1), turn(block, -1)
+    arrived = plane(hand(origin, came, members))
 
     def more(carry):
         return carry[0][0] < most[0]
@@ -726,6 +806,10 @@
         value_cache,
     )
     parts = lax.all_to_all(payload, "tok", 0, 0, tiled=True)
+    beside = across(block)
+    low, high = split(below, above, beside, payload)
+    far = [turn(low, 1), turn(high, -1)]
+    weights = [block, beside, below, above]
     blocks, chosen = mamba(
         ints,
         reals,
@@ -737,17 +821,21 @@
         states,
         mamba_out,
         members,
-    )
-    *near_a, chosen, _ = lax.optimization_barrier((*near_a, chosen, parts))
-    weights = [low, high] + near_a
-    far = [turn(near_a[0], 1), turn(near_a[1], -1), turn(high, 1), turn(low, -1)]
-    weights += [across(w) for w in weights]
-    joined = lax.all_to_all(join(parts, blocks, query_heads, head_size), "tok", 0, 0, tiled=True)
-    spread = project(joined, attention_out.T, blocks.shape[1], query_heads, head_size)
+        query_heads * own,
+    )
+    blocks, *_ = lax.optimization_barrier((blocks, low, high))
+    joint = join(parts, blocks, query_heads, head_size)
+    joined = lax.all_to_all(joint, "tok", 0, 0, tiled=True)
+    below, above, chosen, _ = lax.optimization_barrier((below, above, chosen, joint))
+    weights += [across(below), across(above)]
+    folded = members * own * (width // members) // AUX
+    spread = project(joined, attention_out.T, folded, query_heads, head_size)
     *far, _ = lax.optimization_barrier((*far, spread))
-    weights += far + [across(w) for w in far]
+    half = gate_weight.shape[1] // 2
+    last = far + [across(w) for w in far]
     added = lax.all_to_all(spread, "tok", 0, 0, tiled=True)
-    mlp_part, mixed = feed(added, embedded, mlp_gain[None], weights)
+    acc, second, mixed = feed(added, embedded, mlp_gain[None], weights, half)
+    mlp_part = feed_rest(acc, second, last, half, members)
     mlp_rows = lax.all_to_all(mlp_part, "tok", 0, 0, tiled=True)
     own_rows = lax.optimization_barrier(lax.dynamic_slice_in_dim(mixed, member * own, own))
     hidden_out = (own_rows.astype(F32) + jnp.sum(mlp_rows.astype(F32), axis=0)).astype(BF)

time: 141 us -> 149 us (1.057)
  waiting for transfers between devices: 46 us -> 39.1 us
  Pallas kernels: 38.5 us -> 44.9 us
  starting transfers between devices: 42.8 us -> 48.3 us
  local copies, waits for them, and re-layouts: 5.13 us -> 8.38 us
    pallas_call x1 -> x3, Pallas kernels: 9.12 us -> 15.8 us  [the longest x1 7.87 us: feed(): pl.pallas_call(functools.partial(feed_kernel, count=len(weights), units=u...]
    all_to_all x1, waiting for transfers between devices: 13.4 us -> 6.8 us  [exchange(): came = lax.all_to_all(sent, ('req', 'tok'), 0, 0, tiled=True)]
    all_to_all x1, waiting for transfers between devices: 6.18 us -> 0.01 us  [local(): added = lax.all_to_all(spread, 'tok', 0, 0, tiled=True)]
    all_to_all x1, waiting for transfers between devices: 0.37 us -> 6.47 us  [local(): joined = lax.all_to_all(joint, 'tok', 0, 0, tiled=True)]
    ppermute x9 -> x7, waiting for transfers between devices: 17.3 us -> 11.4 us  [turn(): lax.ppermute(value, 'req', [(g, (g + by * cores) % groups) for g in range...]
    all_to_all x1, waiting for transfers between devices: 5.37 us -> 8.92 us  [plane(): return lax.all_to_all(rows, 'tok', 0, 0, tiled=True)]
    all_to_all x1, starting transfers between devices: 3.56 us -> 7.06 us  [local(): mlp_rows = lax.all_to_all(mlp_part, 'tok', 0, 0, tiled=True)]
    unnamed x34, local copies, waits for them, and re-layouts: 2.37 us -> 5.61 us
  transfers between devices with their start and end apart: 24 -> 19, of which waited for: 11 -> 7; matrix products, arithmetic and copies ran while one was open for 4% -> 4% of each run, Pallas kernels for 25% -> 26%
where the time goes in v7:
time: 149 us; the launch traced here: 148 us
  starting transfers between devices  48.3 us (32%)
  Pallas kernels  44.9 us (30%)
  waiting for transfers between devices  39.1 us (26%)
  local copies, waits for them, and re-layouts  8.38 us (6%)
  other arithmetic  3.64 us (2%)
  between operations  2.92 us (2%)
    ppermute x7, waiting for transfers between devices, turn(): lax.ppermute(value, 'req', [(g, (g + by * cores) % groups) for g in range...  11.4 us
    all_to_all x1, starting transfers between devices, exchange(): came = lax.all_to_all(sent, ('req', 'tok'), 0, 0, tiled=True)  11.2 us
    ppermute x7, starting transfers between devices, turn(): lax.ppermute(value, 'req', [(g, (g + by * cores) % groups) for g in range...  11.1 us
    all_to_all x1, waiting for transfers between devices, plane(): return lax.all_to_all(rows, 'tok', 0, 0, tiled=True)  8.92 us
    pallas_call x1, Pallas kernels, feed(): pl.pallas_call(functools.partial(feed_kernel, count=len(weights), units=u...  7.87 us
    pallas_call x1, Pallas kernels, attend(): pl.pallas_call(attend_kernel, grid=(1,), in_specs=scalars(1) + near(1) +...  7.28 us
    all_to_all x1, starting transfers between devices, local(): mlp_rows = lax.all_to_all(mlp_part, 'tok', 0, 0, tiled=True)  7.06 us
    all_to_all x1, waiting for transfers between devices, exchange(): came = lax.all_to_all(sent, ('req', 'tok'), 0, 0, tiled=True)  6.8 us
  transfers between devices with their start and end apart: 19, of which 7 were waited for; matrix products, arithmetic and copies ran while one was open for 4% of the time, Pallas kernels for 26%

profile of v7, /device:TPU:0, one launch (start us, length us, event | category | flops | bytes accessed | tf_op | source)
XLA Modules:
  0.0 147.9 jit_solution(13069885906804538625)
XLA Ops:
  0.6 4.3 %fetch.2 = (bf16[128,24,128]{2,1,0:T(8,128)(2,1)}, s32[64,128]{1,0:T(8,128)}, s32[4]{0:T(128)}, s32[1]{0:T(128)}) custom-call(s32[1]{0:T(128)} %constant.90.clone.1.turn, s32[1,32]{1,0:T(1,128)} %bitcast.20, s32[16,32]{1,0:T(8,128)} %bitcast.26, bf16[512,3072]{1,0:T(8,128)(2,1)} %table_far.1), custom_call_target="tpu_custom_call" | custom-call | flops 402653184 | bytes 3145728 | tf_op jit(solution)/shard_map/fetch/pallas_call | solution.py:150
  4.9 11.2 %all-to-all-start.2 = ((bf16[128,24,128]{2,1,0:T(8,128)(2,1)}), bf16[128,24,128]{2,1,0:T(8,128)(2,1)S(1)}, u32[]{:S(2)}, u32[]{:S(2)}) async-start(bf16[128,24,128]{2,1,0:T(8,128)(2,1)} %get-tuple-element.60), calls=%async_computation.2 | async-start | bytes 1572864 | tf_op jit(solution)/shard_map/all_to_all | solution.py:767
  16.1 2.8 %pack.1.refs_0_ = bf16[288,3072]{1,0:T(8,128)(2,1)} custom-call(bf16[96,3072]{1,0:T(8,128)(2,1)} %bitcast.22, bf16[96,3072]{1,0:T(8,128)(2,1)} %bitcast.23, bf16[96,3072]{1,0:T(8,128)(2,1)} %bitcast.24, s32[64,128]{1,0:T(8,128)} %get-tuple-element.61.places.ready), custom_call_target="tpu_custom_call" | custom-call | bytes 1024 | tf_op jit(solution)/shard_map/pack/pallas_call | solution.py:657
  18.9 1.1 collective-permute-start
  20.0 2.2 %collective-permute-start.1 = (bf16[288,3072]{1,0:T(8,128)(2,1)}, bf16[288,3072]{1,0:T(8,128)(2,1)}, u32[]{:S(2)}, u32[]{:S(2)}) collective-permute-start(bf16[288,3072]{1,0:T(8,128)(2,1)} %pack.1.refs_0_), channel_id=1, source_target_pairs={{0,96},{16,112},{32,0},{48,16},{64,32},{80,48},{96,64},{112,80},{1... | collective-permute-start | bytes 5308424 | tf_op jit(solution)/shard_map/ppermute | solution.py:756
  22.4 0.6 gather_fusion
  23.0 0.6 gather_fusion.1
  25.6 6.8 %all-to-all-done.2.came = bf16[128,24,128]{2,1,0:T(8,128)(2,1)S(1)} async-done(((bf16[128,24,128]{2,1,0:T(8,128)(2,1)}), bf16[128,24,128]{2,1,0:T(8,128)(2,1)S(1)}, u32[]{:S(2)}, u32[]{:S(2)}) %all-to-all-start.2) | async-done | bytes 786464 | tf_op jit(solution)/shard_map/all_to_all | solution.py:767
  32.4 1.3 hand.2
  33.8 0.6 while.10
  34.5 3.6 %all-to-all-start.3 = ((bf16[16,96,128]{2,1,0:T(8,128)(2,1)}), bf16[16,96,128]{2,1,0:T(8,128)(2,1)S(1)}, u32[]{:S(2)}, u32[]{:S(2)}) async-start(bf16[16,96,128]{2,1,0:T(8,128)(2,1)} %hand.2), calls=%async_computation.3 | async-start | bytes 786432 | tf_op jit(solution)/shard_map/all_to_all | solution.py:771
  38.1 0.6 pad_add_fusion.ints
  38.7 0.6 pad_maximum_fusion.1.reals
  39.3 8.9 %all-to-all-done.3.arrived = bf16[16,96,128]{2,1,0:T(8,128)(2,1)S(1)} async-done(((bf16[16,96,128]{2,1,0:T(8,128)(2,1)}), bf16[16,96,128]{2,1,0:T(8,128)(2,1)S(1)}, u32[]{:S(2)}, u32[]{:S(2)}) %all-to-all-start.3) | async-done | bytes 393248 | tf_op jit(solution)/shard_map/all_to_all | solution.py:771
  48.2 0.7 copy-done.12
  48.9 7.3 %attend.1 = (bf16[16,4,896]{2,1,0:T(4,128)(2,1)}, bf16[64,3072]{1,0:T(8,128)(2,1)}, bf16[64,3072]{1,0:T(8,128)(2,1)}) custom-call(s32[9]{0:T(128)} %pad_add_fusion.ints, bf16[16,96,128]{2,1,0:T(8,128)(2,1)} %copy-done.12, s32[64,128]{1,0:T(8,128)} %get-tuple-element.61.places.ready, bf16[64,3072]{1,0:T(8,128)(2,1)S(1)} %get-tuple-element.63.extra, ...), custom_call_target="tpu_custom_call" | custom-call | flops 20000000000 | bytes 1024 | tf_op jit(solution)/shard_map/attend/pallas_call | solution.py:319
  56.2 3.7 %all-to-all-start.4 = ((bf16[16,4,896]{2,1,0:T(4,128)(2,1)}), bf16[16,4,896]{2,1,0:T(4,128)(2,1)S(1)}, u32[]{:S(2)}, u32[]{:S(2)}) async-start(bf16[16,4,896]{2,1,0:T(4,128)(2,1)} %get-tuple-element.64.ready), calls=%async_computation.4 | async-start | bytes 229376 | tf_op jit(solution)/shard_map/all_to_all | solution.py:808
  59.9 6.7 %mamba.1 = (bf16[16,120,128]{2,1,0:T(8,128)(2,1)}, bf16[4,1,128,256]{3,2,1,0:T(8,128)(2,1)}) custom-call(s32[9]{0:T(128)} %pad_add_fusion.ints, f32[3]{0:T(128)} %pad_maximum_fusion.1.reals, bf16[64,3072]{1,0:T(8,128)(2,1)} %get-tuple-element.65.normed, bf16[3072,128]{1,0:T(8,128)(2,1)} %input_weight.1, bf16[3072,128]{1,0:T(8,128)(2,1)} %gate_weight.1, ...), custom_call_target="tpu_custom_call" | custom-call | flops 8000000000 | bytes 1024 | tf_op jit(solution)/shard_map/mamba/pallas_call | solution.py:450
  66.7 0.5 collective-permute-done.below.refs_2_
  67.2 1.2 copy-done.7
  68.4 2.7 %split.1 = (bf16[144,3072]{1,0:T(8,128)(2,1)}, bf16[144,3072]{1,0:T(8,128)(2,1)}) custom-call(bf16[288,3072]{1,0:T(8,128)(2,1)} %copy-done.7, bf16[288,3072]{1,0:T(8,128)(2,1)} %collective-permute-done.1.above.refs_3_, bf16[288,3072]{1,0:T(8,128)(2,1)} %collective-permute-done.2.beside.refs_1_, bf16[16,4,896]{2,1,0:T(4,128)(2,1)} %get-tuple-element.64.ready), custom_call_target="tpu_custom_call" | custom-call | bytes 1024 | tf_op jit(solution)/shard_map/split/pallas_call | solution.py:678
  71.1 0.6 copy-done.15
  71.8 2.0 %join.1 = bf16[16,120,128]{2,1,0:T(8,128)(2,1)} custom-call(bf16[16,4,896]{2,1,0:T(4,128)(2,1)} %copy-done.15, bf16[16,120,128]{2,1,0:T(8,128)(2,1)} %get-tuple-element.69.blocks), custom_call_target="tpu_custom_call", output_to_operand_aliasing={{}: (1, {})} | custom-call | flops 20000000000 | bytes 1024 | tf_op jit(solution)/shard_map/join/pallas_call | solution.py:494
  73.8 6.5 %all-to-all-start.5 = ((bf16[16,120,128]{2,1,0:T(8,128)(2,1)}), bf16[16,120,128]{2,1,0:T(8,128)(2,1)S(1)}, u32[]{:S(2)}, u32[]{:S(2)}) async-start(bf16[16,120,128]{2,1,0:T(8,128)(2,1)} %join.1), calls=%async_computation.5 | async-start | bytes 983040 | tf_op jit(solution)/shard_map/all_to_all | solution.py:828
  80.5 0.8 collective-permute-start.5
  81.3 2.4 %collective-permute-start.6 = (bf16[144,3072]{1,0:T(8,128)(2,1)}, bf16[144,3072]{1,0:T(8,128)(2,1)}, u32[]{:S(2)}, u32[]{:S(2)}) collective-permute-start(bf16[144,3072]{1,0:T(8,128)(2,1)} %get-tuple-element.68), channel_id=1, source_target_pairs={{0,96},{16,112},{32,0},{48,16},{64,32},{80,48},{96,64},{112,80},{1... | collective-permute-start | bytes 2654216 | tf_op jit(solution)/shard_map/ppermute | solution.py:756
  83.7 0.5 collective-permute-start.4
  84.3 6.5 %all-to-all-done.5.parts = bf16[16,120,128]{2,1,0:T(8,128)(2,1)S(1)} async-done(((bf16[16,120,128]{2,1,0:T(8,128)(2,1)}), bf16[16,120,128]{2,1,0:T(8,128)(2,1)S(1)}, u32[]{:S(2)}, u32[]{:S(2)}) %all-to-all-start.5) | async-done | bytes 491552 | tf_op jit(solution)/shard_map/all_to_all | solution.py:828
  90.7 0.8 copy-done.11
  91.5 2.2 %project.1 = bf16[16,96,128]{2,1,0:T(8,128)(2,1)} custom-call(bf16[16,120,128]{2,1,0:T(8,128)(2,1)} %copy-done.11, bf16[192,768]{1,0:T(8,128)(2,1)} %bitcast.30), custom_call_target="tpu_custom_call" | custom-call | flops 20000000000 | bytes 1024 | tf_op jit(solution)/shard_map/project/pallas_call | solution.py:530
  93.7 4.2 %all-to-all-start.6 = ((bf16[16,96,128]{2,1,0:T(8,128)(2,1)}), bf16[16,96,128]{2,1,0:T(8,128)(2,1)}, u32[]{:S(2)}, u32[]{:S(2)}) async-start(bf16[16,96,128]{2,1,0:T(8,128)(2,1)} %project.1), calls=%async_computation.6 | async-start | bytes 786432 | tf_op jit(solution)/shard_map/all_to_all | solution.py:836
  98.0 0.6 gather_fusion.2
  98.6 0.6 fusion
  99.3 0.4 collective-permute-start.10
  99.7 3.7 %collective-permute-done.5.refs_0_ = bf16[144,3072]{1,0:T(8,128)(2,1)} collective-permute-done((bf16[144,3072]{1,0:T(8,128)(2,1)}, bf16[144,3072]{1,0:T(8,128)(2,1)}, u32[]{:S(2)}, u32[]{:S(2)}) %collective-permute-start.5) | collective-permute-done | bytes 884768 | tf_op jit(solution)/shard_map/ppermute | solution.py:756
  103.4 7.2 %collective-permute-done.6.refs_1_ = bf16[144,3072]{1,0:T(8,128)(2,1)} collective-permute-done((bf16[144,3072]{1,0:T(8,128)(2,1)}, bf16[144,3072]{1,0:T(8,128)(2,1)}, u32[]{:S(2)}, u32[]{:S(2)}) %collective-permute-start.6) | collective-permute-done | bytes 884768 | tf_op jit(solution)/shard_map/ppermute | solution.py:756
  110.6 4.2 %collective-permute-start.12 = (bf16[8,128,256]{2,1,0:T(8,128)(2,1)S(1)}, bf16[8,128,256]{2,1,0:T(8,128)(2,1)}, u32[]{:S(2)}, u32[]{:S(2)}) collective-permute-start(bf16[8,128,256]{2,1,0:T(8,128)(2,1)S(1)} %pad_maximum_fusion.refs_0_), channel_id=1, source_target_pairs={{0,96},{16,112},{32,0},{48,16},{64,32},{80,48},{96,64},{112,80},{1... | collective-permute-start | bytes 1572872 | tf_op jit(solution)/shard_map/ppermute | solution.py:756
  114.8 0.5 collective-permute-start.8
  115.3 7.9 %feed.1 = (f32[64,3072]{1,0:T(8,128)}, bf16[64,3072]{1,0:T(8,128)(2,1)}, bf16[64,3072]{1,0:T(8,128)(2,1)}) custom-call(bf16[16,96,128]{2,1,0:T(8,128)(2,1)} %all-to-all-done.6.spread, bf16[64,3072]{1,0:T(8,128)(2,1)} %get-tuple-element.70.embedded, f32[1,3072]{1,0:T(1,128)} %bitcast.33, bf16[288,3072]{1,0:T(8,128)(2,1)} %pack.1.refs_0_, ...), custom_call_target="tpu_custom_call" | custom-call | flops 20000000000 | bytes 1024 | tf_op jit(solution)/shard_map/feed/pallas_call | solution.py:617
  123.3 0.9 copy-done.16
  124.5 5.2 %feed_rest.1 = bf16[16,4,3072]{2,1,0:T(4,128)(2,1)} custom-call(f32[64,3072]{1,0:T(8,128)} %get-tuple-element.75.so_far, bf16[64,3072]{1,0:T(8,128)(2,1)} %get-tuple-element.76.second, bf16[144,3072]{1,0:T(8,128)(2,1)} %collective-permute-done.5.refs_0_, bf16[144,3072]{1,0:T(8,128)(2,1)} %collective-permute-done.6.refs_1_, bf16[144,3072]{1,0:T(8,128)(2,1)} %copy-done.16, ...), custom_call_target="tpu_custom_call" | custom-call | flops 4000000000 | bytes 1024 | tf_op jit(solution)/shard_map/feed_rest/pallas_call | solution.py:633
  129.7 7.1 %all-to-all-start.7 = ((bf16[16,4,3072]{2,1,0:T(4,128)(2,1)}), bf16[16,4,3072]{2,1,0:T(4,128)(2,1)S(1)}, u32[]{:S(2)}, u32[]{:S(2)}) async-start(bf16[16,4,3072]{2,1,0:T(4,128)(2,1)} %feed_rest.1), calls=%async_computation.7 | async-start | bytes 786432 | tf_op jit(solution)/shard_map/all_to_all | solution.py:839
  136.8 0.5 and_select_fusion.3.turns
  137.3 0.8 copy-done.9
  138.3 2.5 %pick.1 = f32[4,128,256]{2,1,0:T(8,128)} custom-call(s32[4]{0:T(128)} %and_select_fusion.3.turns, s32[4]{0:T(128)} %get-tuple-element.98.rows, bf16[8,128,256]{2,1,0:T(8,128)(2,1)} %copy-done.6, bf16[8,128,256]{2,1,0:T(8,128)(2,1)} %copy-done.9, bf16[8,128,256]{2,1,0:T(8,128)(2,1)} %copy-done.10, bf16[8,128,256]{2,1,0:T(8,128)(2,1)} %collective-permute-done.12.refs_3_), custom_call_target="tpu_custom_call" | custom-call | tf_op jit(solution)/shard_map/pick/pallas_call | solution.py:704
  140.8 0.8 constant_dynamic-slice_fusion
  141.6 5.5 %all-to-all-done.7 = bf16[16,4,3072]{2,1,0:T(4,128)(2,1)S(1)} async-done(((bf16[16,4,3072]{2,1,0:T(4,128)(2,1)}), bf16[16,4,3072]{2,1,0:T(4,128)(2,1)S(1)}, u32[]{:S(2)}, u32[]{:S(2)}) %all-to-all-start.7) | async-done | bytes 393248 | tf_op jit(solution)/shard_map/all_to_all | solution.py:839
  147.3 0.6 add_convert_fusion
  (55 shorter events, 1.3 us)
Async XLA Ops:
  0.6 21.7 %copy-start = (s32[32]{0:T(128)S(1)}, s32[32]{0:T(128)}, u32[]{:S(2)}) copy-start(s32[32]{0:T(128)} %param.30) | copy-start | bytes 388
  4.9 27.5 %all-to-all-start.2 = ((bf16[128,24,128]{2,1,0:T(8,128)(2,1)}), bf16[128,24,128]{2,1,0:T(8,128)(2,1)S(1)}, u32[]{:S(2)}, u32[]{:S(2)}) async-start(bf16[128,24,128]{2,1,0:T(8,128)(2,1)} %get-tuple-element.60), calls=%async_computation.2 | async-start | bytes 1572864 | tf_op jit(solution)/shard_map/all_to_all | solution.py:767
  16.1 6.1 %copy-start.3 = (s32[32]{0:T(128)S(1)}, s32[32]{0:T(128)}, u32[]{:S(2)}) copy-start(s32[32]{0:T(128)} %param.31) | copy-start | bytes 388
  16.1 6.9 %copy-start.4 = (s32[32]{0:T(128)S(1)}, s32[32]{0:T(128)}, u32[]{:S(2)}) copy-start(s32[32]{0:T(128)} %param.33) | copy-start | bytes 388
  16.1 16.3 %copy-start.1 = (s32[4]{0:T(128)S(1)}, s32[4]{0:T(128)}, u32[]{:S(2)}) copy-start(s32[4]{0:T(128)} %get-tuple-element.59.origin) | copy-start | bytes 52
  18.9 48.3 %collective-permute-start = (bf16[288,3072]{1,0:T(8,128)(2,1)}, bf16[288,3072]{1,0:T(8,128)(2,1)S(1)}, u32[]{:S(2)}, u32[]{:S(2)}) collective-permute-start(bf16[288,3072]{1,0:T(8,128)(2,1)} %pack.1.refs_0_), channel_id=1, source_target_pairs={{0,32},{16,48},{32,64},{48,80},{64,96},{80,112},{96,0},{112,16},{1... | collective-permute-start | bytes 5308424 | tf_op jit(solution)/shard_map/ppermute | solution.py:756
  20.0 47.2 %collective-permute-start.1 = (bf16[288,3072]{1,0:T(8,128)(2,1)}, bf16[288,3072]{1,0:T(8,128)(2,1)}, u32[]{:S(2)}, u32[]{:S(2)}) collective-permute-start(bf16[288,3072]{1,0:T(8,128)(2,1)} %pack.1.refs_0_), channel_id=1, source_target_pairs={{0,96},{16,112},{32,0},{48,16},{64,32},{80,48},{96,64},{112,80},{1... | collective-permute-start | bytes 5308424 | tf_op jit(solution)/shard_map/ppermute | solution.py:756
  22.2 45.0 %collective-permute-start.2 = (bf16[288,3072]{1,0:T(8,128)(2,1)}, bf16[288,3072]{1,0:T(8,128)(2,1)}, u32[]{:S(2)}, u32[]{:S(2)}) collective-permute-start(bf16[288,3072]{1,0:T(8,128)(2,1)} %pack.1.refs_0_), channel_id=1, source_target_pairs={{0,16},{16,0},{32,48},{48,32},{64,80},{80,64},{96,112},{112,96},{1... | collective-permute-start | bytes 5308424 | tf_op jit(solution)/shard_map/ppermute | solution.py:761
  32.4 1.4 copy-start.13
  34.5 13.8 %all-to-all-start.3 = ((bf16[16,96,128]{2,1,0:T(8,128)(2,1)}), bf16[16,96,128]{2,1,0:T(8,128)(2,1)S(1)}, u32[]{:S(2)}, u32[]{:S(2)}) async-start(bf16[16,96,128]{2,1,0:T(8,128)(2,1)} %hand.2), calls=%async_computation.3 | async-start | bytes 786432 | tf_op jit(solution)/shard_map/all_to_all | solution.py:771
  48.2 0.7 copy-start.12
  56.2 14.9 %all-to-all-start.4 = ((bf16[16,4,896]{2,1,0:T(4,128)(2,1)}), bf16[16,4,896]{2,1,0:T(4,128)(2,1)S(1)}, u32[]{:S(2)}, u32[]{:S(2)}) async-start(bf16[16,4,896]{2,1,0:T(4,128)(2,1)} %get-tuple-element.64.ready), calls=%async_computation.4 | async-start | bytes 229376 | tf_op jit(solution)/shard_map/all_to_all | solution.py:808
  67.2 1.2 copy-start.7
  71.1 9.2 %copy-start.18 = (s32[32]{0:T(128)S(1)}, s32[32]{0:T(128)}, u32[]{:S(2)}) copy-start(s32[32]{0:T(128)} %param.32) | copy-start | bytes 388
  71.1 12.6 %copy-start.8 = (bf16[288,3072]{1,0:T(8,128)(2,1)S(1)}, bf16[288,3072]{1,0:T(8,128)(2,1)}, u32[]{:S(2)}) copy-start(bf16[288,3072]{1,0:T(8,128)(2,1)} %copy-done.7) | copy-start | bytes 5308420
  71.1 13.1 %copy-start.14 = (bf16[4,1,128,256]{3,2,1,0:T(8,128)(2,1)S(1)}, bf16[4,1,128,256]{3,2,1,0:T(8,128)(2,1)}, u32[]{:S(2)}) copy-start(bf16[4,1,128,256]{3,2,1,0:T(8,128)(2,1)} %get-tuple-element.79) | copy-start | bytes 786436
  71.1 0.6 copy-start.15
  73.8 16.9 %all-to-all-start.5 = ((bf16[16,120,128]{2,1,0:T(8,128)(2,1)}), bf16[16,120,128]{2,1,0:T(8,128)(2,1)S(1)}, u32[]{:S(2)}, u32[]{:S(2)}) async-start(bf16[16,120,128]{2,1,0:T(8,128)(2,1)} %join.1), calls=%async_computation.5 | async-start | bytes 983040 | tf_op jit(solution)/shard_map/all_to_all | solution.py:828
  80.5 22.9 %collective-permute-start.5 = (bf16[144,3072]{1,0:T(8,128)(2,1)}, bf16[144,3072]{1,0:T(8,128)(2,1)}, u32[]{:S(2)}, u32[]{:S(2)}) collective-permute-start(bf16[144,3072]{1,0:T(8,128)(2,1)} %get-tuple-element.67), channel_id=1, source_target_pairs={{0,32},{16,48},{32,64},{48,80},{64,96},{80,112},{96,0},{112,16},{1... | collective-permute-start | bytes 2654216 | tf_op jit(solution)/shard_map/ppermute | solution.py:756
  81.3 29.3 %collective-permute-start.6 = (bf16[144,3072]{1,0:T(8,128)(2,1)}, bf16[144,3072]{1,0:T(8,128)(2,1)}, u32[]{:S(2)}, u32[]{:S(2)}) collective-permute-start(bf16[144,3072]{1,0:T(8,128)(2,1)} %get-tuple-element.68), channel_id=1, source_target_pairs={{0,96},{16,112},{32,0},{48,16},{64,32},{80,48},{96,64},{112,80},{1... | collective-permute-start | bytes 2654216 | tf_op jit(solution)/shard_map/ppermute | solution.py:756
  83.7 31.1 %collective-permute-start.3 = (bf16[288,3072]{1,0:T(8,128)(2,1)S(1)}, bf16[288,3072]{1,0:T(8,128)(2,1)}, u32[]{:S(2)}, u32[]{:S(2)}) collective-permute-start(bf16[288,3072]{1,0:T(8,128)(2,1)S(1)} %copy-done.8), channel_id=1, source_target_pairs={{0,16},{16,0},{32,48},{48,32},{64,80},{80,64},{96,112},{112,96},{1... | collective-permute-start | bytes 5308424 | tf_op jit(solution)/shard_map/ppermute | solution.py:761
  83.7 31.1 %collective-permute-start.4 = (bf16[288,3072]{1,0:T(8,128)(2,1)}, bf16[288,3072]{1,0:T(8,128)(2,1)}, u32[]{:S(2)}, u32[]{:S(2)}) collective-permute-start(bf16[288,3072]{1,0:T(8,128)(2,1)} %collective-permute-done.1.above.refs_3_), channel_id=1, source_target_pairs={{0,16},{16,0},{32,48},{48,32},{64,80},{80,64},{96,112},{112,96},{1... | collective-permute-start | bytes 5308424 | tf_op jit(solution)/shard_map/ppermute | solution.py:761
  84.3 15.0 %collective-permute-start.9 = (bf16[4,128,256]{2,1,0:T(8,128)(2,1)S(1)}, bf16[4,128,256]{2,1,0:T(8,128)(2,1)S(1)}, u32[]{:S(2)}, u32[]{:S(2)}) collective-permute-start(bf16[4,128,256]{2,1,0:T(8,128)(2,1)S(1)} %bitcast.28), channel_id=1, source_target_pairs={{0,16},{16,0},{32,48},{48,32},{64,80},{80,64},{96,112},{112,96},{1... | collective-permute-start | bytes 786440 | tf_op jit(solution)/shard_map/ppermute | solution.py:761
  90.7 0.8 copy-start.11
  93.7 21.6 %all-to-all-start.6 = ((bf16[16,96,128]{2,1,0:T(8,128)(2,1)}), bf16[16,96,128]{2,1,0:T(8,128)(2,1)}, u32[]{:S(2)}, u32[]{:S(2)}) async-start(bf16[16,96,128]{2,1,0:T(8,128)(2,1)} %project.1), calls=%async_computation.6 | async-start | bytes 786432 | tf_op jit(solution)/shard_map/all_to_all | solution.py:836
  99.3 23.9 %copy-start.6 = (bf16[8,128,256]{2,1,0:T(8,128)(2,1)}, bf16[8,128,256]{2,1,0:T(8,128)(2,1)S(1)}, u32[]{:S(2)}) copy-start(bf16[8,128,256]{2,1,0:T(8,128)(2,1)S(1)} %pad_maximum_fusion.refs_0_) | copy-start | bytes 1572868
  99.3 38.0 %collective-permute-start.10 = (bf16[8,128,256]{2,1,0:T(8,128)(2,1)S(1)}, bf16[8,128,256]{2,1,0:T(8,128)(2,1)S(1)}, u32[]{:S(2)}, u32[]{:S(2)}) collective-permute-start(bf16[8,128,256]{2,1,0:T(8,128)(2,1)S(1)} %pad_maximum_fusion.refs_0_), channel_id=1, source_target_pairs={{0,32},{16,48},{32,64},{48,80},{64,96},{80,112},{96,0},{112,16},{1... | collective-permute-start | bytes 1572872 | tf_op jit(solution)/shard_map/ppermute | solution.py:756
  103.4 33.9 %collective-permute-start.11 = (bf16[8,128,256]{2,1,0:T(8,128)(2,1)S(1)}, bf16[8,128,256]{2,1,0:T(8,128)(2,1)S(1)}, u32[]{:S(2)}, u32[]{:S(2)}) collective-permute-start(bf16[8,128,256]{2,1,0:T(8,128)(2,1)S(1)} %pad_maximum_fusion.refs_0_), channel_id=1, source_target_pairs={{0,64},{16,80},{32,96},{48,112},{64,0},{80,16},{96,32},{112,48},{1... | collective-permute-start | bytes 1572872 | tf_op jit(solution)/shard_map/ppermute | solution.py:756
  110.6 26.7 %collective-permute-start.12 = (bf16[8,128,256]{2,1,0:T(8,128)(2,1)S(1)}, bf16[8,128,256]{2,1,0:T(8,128)(2,1)}, u32[]{:S(2)}, u32[]{:S(2)}) collective-permute-start(bf16[8,128,256]{2,1,0:T(8,128)(2,1)S(1)} %pad_maximum_fusion.refs_0_), channel_id=1, source_target_pairs={{0,96},{16,112},{32,0},{48,16},{64,32},{80,48},{96,64},{112,80},{1... | collective-permute-start | bytes 1572872 | tf_op jit(solution)/shard_map/ppermute | solution.py:756
  114.8 8.4 %collective-permute-start.7 = (bf16[144,3072]{1,0:T(8,128)(2,1)}, bf16[144,3072]{1,0:T(8,128)(2,1)S(1)}, u32[]{:S(2)}, u32[]{:S(2)}) collective-permute-start(bf16[144,3072]{1,0:T(8,128)(2,1)} %collective-permute-done.5.refs_0_), channel_id=1, source_target_pairs={{0,16},{16,0},{32,48},{48,32},{64,80},{80,64},{96,112},{112,96},{1... | collective-permute-start | bytes 2654216 | tf_op jit(solution)/shard_map/ppermute | solution.py:761
  114.8 8.4 %collective-permute-start.8 = (bf16[144,3072]{1,0:T(8,128)(2,1)}, bf16[144,3072]{1,0:T(8,128)(2,1)S(1)}, u32[]{:S(2)}, u32[]{:S(2)}) collective-permute-start(bf16[144,3072]{1,0:T(8,128)(2,1)} %collective-permute-done.6.refs_1_), channel_id=1, source_target_pairs={{0,16},{16,0},{32,48},{48,32},{64,80},{80,64},{96,112},{112,96},{1... | collective-permute-start | bytes 2654216 | tf_op jit(solution)/shard_map/ppermute | solution.py:761
  123.2 0.9 copy-start.16
  123.3 1.2 copy-start.17
  129.7 17.4 %all-to-all-start.7 = ((bf16[16,4,3072]{2,1,0:T(4,128)(2,1)}), bf16[16,4,3072]{2,1,0:T(4,128)(2,1)S(1)}, u32[]{:S(2)}, u32[]{:S(2)}) async-start(bf16[16,4,3072]{2,1,0:T(4,128)(2,1)} %feed_rest.1), calls=%async_computation.7 | async-start | bytes 786432 | tf_op jit(solution)/shard_map/all_to_all | solution.py:839
  137.3 0.8 copy-start.9
  137.3 1.0 copy-start.10

commit v8 on v7

--- a/solution.py
+++ b/solution.py
@@ -558,7 +558,8 @@
     return copies
 
 
-def use_units(second, copies, gates, ups, downs, acc, chunk=192):
+def use_units(second, copies, gates, ups, downs, chunk=256):
+    acc = None
     ready = 0
     waiting = list(copies)
     for first in range(0, gates.shape[0], chunk):
@@ -577,26 +578,17 @@
 
 def feed_kernel(spread, embedded, gain, *refs, count, units):
     weights = refs[:count]
-    acc, second, mixed, gates, ups, downs, sems = refs[count:]
+    out, mixed, gates, ups, downs, sems = refs[count:]
     copies = load_units(weights, gates, ups, downs, sems, units)
     tokens = embedded.shape[0]
-    peers = spread.shape[0]
+    peers, own, _ = out.shape
     added = jnp.concatenate([unfold(spread[j].astype(F32), tokens) for j in range(peers)], axis=1)
     rows = (embedded[...].astype(F32) + added).astype(BF)
     mixed[...] = rows
     wide = rows.astype(F32)
     factor = lax.rsqrt(jnp.mean(wide * wide, axis=-1, keepdims=True) + 1e-05)
     rows_norm = (wide * factor * gain[...]).astype(BF)
-    second[...] = rows_norm
-    acc[...] = use_units(rows_norm, copies, gates, ups, downs, None)
-
-
-def rest_kernel(so_far, second, *refs, count, units):
-    weights = refs[:count]
-    out, gates, ups, downs, sems = refs[count:]
-    copies = load_units(weights, gates, ups, downs, sems, units)
-    peers, own, _ = out.shape
-    acc = use_units(second[...], copies, gates, ups, downs, so_far[...])
+    acc = use_units(rows_norm, copies, gates, ups, downs)
     for j in range(peers):
         out[j] = acc[j * own : (j + 1) * own, :].astype(BF)
 
@@ -609,9 +601,10 @@
 
 
 def feed(spread, embedded, gain, weights, units):
+    members = spread.shape[0]
+    tokens, width = embedded.shape
     outs = [
-        jax.ShapeDtypeStruct(embedded.shape, F32),
-        jax.ShapeDtypeStruct(embedded.shape, BF),
+        jax.ShapeDtypeStruct((members, tokens // members, width), BF),
         jax.ShapeDtypeStruct(embedded.shape, BF),
     ]
     return pl.pallas_call(
@@ -627,64 +620,26 @@
     )(spread, embedded, gain, *weights)
 
 
-def feed_rest(acc, second, weights, units, members):
-    tokens, width = acc.shape
-    out = jax.ShapeDtypeStruct((members, tokens // members, width), BF)
-    return pl.pallas_call(
-        functools.partial(rest_kernel, count=len(weights), units=units),
-        grid=(1,),
-        in_specs=whole([acc, second]) + streamed(len(weights)),
-        out_specs=whole([out])[0],
-        out_shape=out,
-        scratch_shapes=unit_scratch(weights, units),
-        compiler_params=PARAMS,
-        cost_estimate=lasting(4),
-        name="feed_rest",
-    )(acc, second, *weights)
-
-
-def pack_kernel(gate, up, down, ready, out):
-    half = gate.shape[0] // 2
-    for h in range(2):
-        for k, part in enumerate((gate, up, down)):
-            at = (3 * h + k) * half
-            out[at : at + half] = part[h * half : (h + 1) * half]
+def pack_kernel(gate, up, down, ready, low, high):
+    half = low.shape[0] // 3
+    for k, part in enumerate((gate, up, down)):
+        low[k * half : (k + 1) * half] = part[:half]
+        high[k * half : (k + 1) * half] = part[half:]
 
 
 def pack(gate, up, down, ready):
     units, width = gate.shape
-    out = jax.ShapeDtypeStruct((3 * units, width), gate.dtype)
+    out = jax.ShapeDtypeStruct((3 * units // 2, width), gate.dtype)
     return pl.pallas_call(
         pack_kernel,
         grid=(1,),
         in_specs=whole([gate, up, down]) + streamed(1),
-        out_specs=whole([out])[0],
-        out_shape=out,
+        out_specs=whole([out, out]),
+        out_shape=[out, out],
         compiler_params=PARAMS,
         cost_estimate=cost(0, 1024),
         name="pack",
     )(gate, up, down, ready)
-
-
-def split_kernel(below, above, beside, ready, low, high):
-    low[...] = below[...]
-    high[...] = above[...]
-
-
-def split(below, above, beside, ready):
-    rows, width = below.shape
-    out = jax.ShapeDtypeStruct((rows // 2, width), below.dtype)
-    block = lambda n: pl.BlockSpec(out.shape, lambda i: (n, 0))
-    return pl.pallas_call(
-        split_kernel,
-        grid=(1,),
-        in_specs=[block(0), block(1)] + streamed(2),
-        out_specs=[block(0), block(0)],
-        out_shape=[out, out],
-        compiler_params=PARAMS,
-        cost_estimate=cost(0, 1024),
-        name="split",
-    )(below, above, beside, ready)
 
 
 def pick_kernel(turns, rows, *refs):
@@ -772,9 +727,11 @@
 
     came, places, origin, most = exchange(jnp.zeros((1,), jnp.int32))
 
-    block = pack(gate_weight.T, up_weight.T, down_weight.T, places)
-    below, above = turn(block, 1), turn(block, -1)
-    arrived = plane(hand(origin, came, members))
+    low, high = pack(gate_weight.T, up_weight.T, down_weight.T, places)
+    near_z = [turn(low, 1), turn(high, -1), turn(high, 1), turn(low, -1)]
+    handed = hand(origin, came, members)
+    weights = [low, high] + near_z
+    arrived = plane(handed)
 
     def more(carry):
         return carry[0][0] < most[0]
@@ -806,10 +763,8 @@
         value_cache,
     )
     parts = lax.all_to_all(payload, "tok", 0, 0, tiled=True)
-    beside = across(block)
-    low, high = split(below, above, beside, payload)
-    far = [turn(low, 1), turn(high, -1)]
-    weights = [block, beside, below, above]
+    later = lax.optimization_barrier((near_z[0], near_z[1], payload))
+    far = [turn(later[0], 1), turn(later[1], -1)]
     blocks, chosen = mamba(
         ints,
         reals,
@@ -823,19 +778,21 @@
         members,
         query_heads * own,
     )
-    blocks, *_ = lax.optimization_barrier((blocks, low, high))
     joint = join(parts, blocks, query_heads, head_size)
     joined = lax.all_to_all(joint, "tok", 0, 0, tiled=True)
-    below, above, chosen, _ = lax.optimization_barrier((below, above, chosen, joint))
-    weights += [across(below), across(above)]
+    *later, chosen, _ = lax.optimization_barrier((*weights, chosen, joint))
+    weights += [across(w) for w in later]
+    chosen = chosen[:, 0]
+    pair = jnp.concatenate([chosen, across(chosen)], axis=0)
+    joined, *_ = lax.optimization_barrier((joined, *far))
     folded = members * own * (width // members) // AUX
     spread = project(joined, attention_out.T, folded, query_heads, head_size)
-    *far, _ = lax.optimization_barrier((*far, spread))
+    first, second, spread, pair, *_ = lax.optimization_barrier((*far, spread, pair, *weights[-6:]))
+    far = [first, second]
+    weights += far + [across(w) for w in far]
+    added = lax.all_to_all(spread, "tok", 0, 0, tiled=True)
     half = gate_weight.shape[1] // 2
-    last = far + [across(w) for w in far]
-    added = lax.all_to_all(spread, "tok", 0, 0, tiled=True)
-    acc, second, mixed = feed(added, embedded, mlp_gain[None], weights, half)
-    mlp_part = feed_rest(acc, second, last, half, members)
+    mlp_part, mixed = feed(added, embedded, mlp_gain[None], weights, half)
     mlp_rows = lax.all_to_all(mlp_part, "tok", 0, 0, tiled=True)
     own_rows = lax.optimization_barrier(lax.dynamic_slice_in_dim(mixed, member * own, own))
     hidden_out = (own_rows.astype(F32) + jnp.sum(mlp_rows.astype(F32), axis=0)).astype(BF)
@@ -843,8 +800,6 @@
     incoming = inverse_of(new_slot)
     local_targets = lax.dynamic_slice_in_dim(incoming, group_index * slots_dev, slots_dev)
     sources = jnp.take(current_slot, local_targets)
-    chosen = chosen[:, 0]
-    pair = jnp.concatenate([chosen, across(chosen)], axis=0)
     held = [pair] + [turn(pair, by) for by in range(1, chips)]
     source_group = sources // slots_dev
     turns = (group_index // cores - source_group // cores) % chips

time: 149 us -> 139 us (0.933)
  Pallas kernels: 44.9 us -> 38.4 us
  starting transfers between devices: 48.3 us -> 45 us
  local copies, waits for them, and re-layouts: 8.38 us -> 6.48 us
    pallas_call x2 -> x0, Pallas kernels: 7.92 us -> none  [the longest x1 5.21 us: feed_rest(): pl.pallas_call(functools.partial(rest_kernel, count=len(weights), units=u...]
    all_to_all x1, waiting for transfers between devices: 0.01 us -> 5.75 us  [local(): added = lax.all_to_all(spread, 'tok', 0, 0, tiled=True)]
    all_to_all x1, waiting for transfers between devices: 5.49 us -> 0.59 us  [local(): mlp_rows = lax.all_to_all(mlp_part, 'tok', 0, 0, tiled=True)]
    all_to_all x1, starting transfers between devices: 7.06 us -> 3.56 us  [local(): mlp_rows = lax.all_to_all(mlp_part, 'tok', 0, 0, tiled=True)]
    unnamed x34 -> x36, local copies, waits for them, and re-layouts: 5.61 us -> 3.72 us
    ppermute x7 -> x9, waiting for transfers between devices: 11.4 us -> 13.3 us  [turn(): lax.ppermute(value, 'req', [(g, (g + by * cores) % groups) for g in range...]
    ppermute x7 -> x9, starting transfers between devices: 11.1 us -> 12.8 us  [turn(): lax.ppermute(value, 'req', [(g, (g + by * cores) % groups) for g in range...]
    all_to_all x1, waiting for transfers between devices: 6.8 us -> 5.25 us  [exchange(): came = lax.all_to_all(sent, ('req', 'tok'), 0, 0, tiled=True)]
  transfers between devices with their start and end apart: 19 -> 24, of which waited for: 7 -> 10; matrix products, arithmetic and copies ran while one was open for 4% -> 4% of each run, Pallas kernels for 26% -> 25%
where the time goes in v8:
time: 139 us; the launch traced here: 137 us
  starting transfers between devices  45 us (32%)
  waiting for transfers between devices  40 us (29%)
  Pallas kernels  38.4 us (28%)
  local copies, waits for them, and re-layouts  6.48 us (5%)
  other arithmetic  3.76 us (3%)
  between operations  2.94 us (2%)
    ppermute x9, waiting for transfers between devices, turn(): lax.ppermute(value, 'req', [(g, (g + by * cores) % groups) for g in range...  13.3 us
    ppermute x9, starting transfers between devices, turn(): lax.ppermute(value, 'req', [(g, (g + by * cores) % groups) for g in range...  12.8 us
    all_to_all x1, starting transfers between devices, exchange(): came = lax.all_to_all(sent, ('req', 'tok'), 0, 0, tiled=True)  11.1 us
    pallas_call x1, Pallas kernels, feed(): pl.pallas_call(functools.partial(feed_kernel, count=len(weights), units=u...  9.13 us
    all_to_all x1, waiting for transfers between devices, plane(): return lax.all_to_all(rows, 'tok', 0, 0, tiled=True)  7.6 us
    pallas_call x1, Pallas kernels, attend(): pl.pallas_call(attend_kernel, grid=(1,), in_specs=scalars(1) + near(1) +...  7.31 us
    pallas_call x1, Pallas kernels, mamba(): pl.pallas_call(mamba_kernel, grid=(1,), in_specs=scalars(2) + whole([norm...  6.7 us
    all_to_all x1, waiting for transfers between devices, local(): joined = lax.all_to_all(joint, 'tok', 0, 0, tiled=True)  6.45 us
  transfers between devices with their start and end apart: 24, of which 10 were waited for; matrix products, arithmetic and copies ran while one was open for 4% of the time, Pallas kernels for 25%

profile of v8, /device:TPU:0, one launch (start us, length us, event | category | flops | bytes accessed | tf_op | source)
XLA Modules:
  0.0 137.3 jit_solution(12749191526246718819)
XLA Ops:
  0.7 4.3 %fetch.2 = (bf16[128,24,128]{2,1,0:T(8,128)(2,1)}, s32[64,128]{1,0:T(8,128)}, s32[4]{0:T(128)}, s32[1]{0:T(128)}) custom-call(s32[1]{0:T(128)} %constant.84.clone.1.turn, s32[1,32]{1,0:T(1,128)} %bitcast.20, s32[16,32]{1,0:T(8,128)} %bitcast.26, bf16[512,3072]{1,0:T(8,128)(2,1)} %table_far.1), custom_call_target="tpu_custom_call" | custom-call | flops 402653184 | bytes 3145728 | tf_op jit(solution)/shard_map/fetch/pallas_call | solution.py:150
  5.0 11.1 %all-to-all-start.2 = ((bf16[128,24,128]{2,1,0:T(8,128)(2,1)}), bf16[128,24,128]{2,1,0:T(8,128)(2,1)S(1)}, u32[]{:S(2)}, u32[]{:S(2)}) async-start(bf16[128,24,128]{2,1,0:T(8,128)(2,1)} %get-tuple-element.70), calls=%async_computation.2 | async-start | bytes 1572864 | tf_op jit(solution)/shard_map/all_to_all | solution.py:722
  16.1 2.8 %pack.1 = (bf16[144,3072]{1,0:T(8,128)(2,1)}, bf16[144,3072]{1,0:T(8,128)(2,1)}) custom-call(bf16[96,3072]{1,0:T(8,128)(2,1)} %bitcast.22, bf16[96,3072]{1,0:T(8,128)(2,1)} %bitcast.23, bf16[96,3072]{1,0:T(8,128)(2,1)} %bitcast.24, s32[64,128]{1,0:T(8,128)} %get-tuple-element.66.ready.places), custom_call_target="tpu_custom_call" | custom-call | bytes 1024 | tf_op jit(solution)/shard_map/pack/pallas_call | solution.py:633
  18.9 2.8 %collective-permute-start.5 = (bf16[144,3072]{1,0:T(8,128)(2,1)}, bf16[144,3072]{1,0:T(8,128)(2,1)}, u32[]{:S(2)}, u32[]{:S(2)}) collective-permute-start(bf16[144,3072]{1,0:T(8,128)(2,1)} %get-tuple-element.81.refs_0_), channel_id=1, source_target_pairs={{0,96},{16,112},{32,0},{48,16},{64,32},{80,48},{96,64},{112,80},{1... | collective-permute-start | bytes 2654216 | tf_op jit(solution)/shard_map/ppermute | solution.py:711
  22.0 3.0 %collective-permute-start.1 = (bf16[144,3072]{1,0:T(8,128)(2,1)}, bf16[144,3072]{1,0:T(8,128)(2,1)}, u32[]{:S(2)}, u32[]{:S(2)}) collective-permute-start(bf16[144,3072]{1,0:T(8,128)(2,1)} %get-tuple-element.82.refs_1_), channel_id=1, source_target_pairs={{0,96},{16,112},{32,0},{48,16},{64,32},{80,48},{96,64},{112,80},{1... | collective-permute-start | bytes 2654216 | tf_op jit(solution)/shard_map/ppermute | solution.py:711
  27.2 5.3 %all-to-all-done.2.came = bf16[128,24,128]{2,1,0:T(8,128)(2,1)S(1)} async-done(((bf16[128,24,128]{2,1,0:T(8,128)(2,1)}), bf16[128,24,128]{2,1,0:T(8,128)(2,1)S(1)}, u32[]{:S(2)}, u32[]{:S(2)}) %all-to-all-start.2) | async-done | bytes 786464 | tf_op jit(solution)/shard_map/all_to_all | solution.py:722
  32.5 1.3 hand.2
  33.8 0.6 while.10
  34.5 3.6 %all-to-all-start.3 = ((bf16[16,96,128]{2,1,0:T(8,128)(2,1)}), bf16[16,96,128]{2,1,0:T(8,128)(2,1)S(1)}, u32[]{:S(2)}, u32[]{:S(2)}) async-start(bf16[16,96,128]{2,1,0:T(8,128)(2,1)} %hand.2), calls=%async_computation.3 | async-start | bytes 786432 | tf_op jit(solution)/shard_map/all_to_all | solution.py:726
  38.1 0.7 pad_maximum_fusion.1.reals
  38.7 0.6 gather_fusion.1
  39.4 0.6 gather_fusion
  40.1 0.6 pad_add_fusion.ints
  40.7 7.6 %all-to-all-done.3.arrived = bf16[16,96,128]{2,1,0:T(8,128)(2,1)S(1)} async-done(((bf16[16,96,128]{2,1,0:T(8,128)(2,1)}), bf16[16,96,128]{2,1,0:T(8,128)(2,1)S(1)}, u32[]{:S(2)}, u32[]{:S(2)}) %all-to-all-start.3) | async-done | bytes 393248 | tf_op jit(solution)/shard_map/all_to_all | solution.py:726
  48.3 0.7 copy-done.12
  49.0 7.3 %attend.1 = (bf16[16,4,896]{2,1,0:T(4,128)(2,1)}, bf16[64,3072]{1,0:T(8,128)(2,1)}, bf16[64,3072]{1,0:T(8,128)(2,1)}) custom-call(s32[9]{0:T(128)} %pad_add_fusion.ints, bf16[16,96,128]{2,1,0:T(8,128)(2,1)} %copy-done.12, s32[64,128]{1,0:T(8,128)} %get-tuple-element.66.ready.places, bf16[64,3072]{1,0:T(8,128)(2,1)S(1)} %get-tuple-element.72.extra, ...), custom_call_target="tpu_custom_call" | custom-call | flops 20000000000 | bytes 1024 | tf_op jit(solution)/shard_map/attend/pallas_call | solution.py:319
  56.3 3.5 %all-to-all-start.4 = ((bf16[16,4,896]{2,1,0:T(4,128)(2,1)}), bf16[16,4,896]{2,1,0:T(4,128)(2,1)S(1)}, u32[]{:S(2)}, u32[]{:S(2)}) async-start(bf16[16,4,896]{2,1,0:T(4,128)(2,1)} %get-tuple-element.73), calls=%async_computation.4 | async-start | bytes 229376 | tf_op jit(solution)/shard_map/all_to_all | solution.py:765
  59.9 5.6 %collective-permute-done.1.refs_3_ = bf16[144,3072]{1,0:T(8,128)(2,1)} collective-permute-done((bf16[144,3072]{1,0:T(8,128)(2,1)}, bf16[144,3072]{1,0:T(8,128)(2,1)}, u32[]{:S(2)}, u32[]{:S(2)}) %collective-permute-start.1) | collective-permute-done | bytes 884768 | tf_op jit(solution)/shard_map/ppermute | solution.py:711
  65.5 2.2 %collective-permute-start.2 = (bf16[144,3072]{1,0:T(8,128)(2,1)}, bf16[144,3072]{1,0:T(8,128)(2,1)}, u32[]{:S(2)}, u32[]{:S(2)}) collective-permute-start(bf16[144,3072]{1,0:T(8,128)(2,1)} %collective-permute-done.refs_2_), channel_id=1, source_target_pairs={{0,32},{16,48},{32,64},{48,80},{64,96},{80,112},{96,0},{112,16},{1... | collective-permute-start | bytes 2654216 | tf_op jit(solution)/shard_map/ppermute | solution.py:711
  67.6 1.1 collective-permute-start.3
  68.7 6.7 %mamba.1 = (bf16[16,120,128]{2,1,0:T(8,128)(2,1)}, bf16[4,1,128,256]{3,2,1,0:T(8,128)(2,1)}) custom-call(s32[9]{0:T(128)} %pad_add_fusion.ints, f32[3]{0:T(128)} %pad_maximum_fusion.1.reals, bf16[64,3072]{1,0:T(8,128)(2,1)} %get-tuple-element.76.normed, bf16[3072,128]{1,0:T(8,128)(2,1)} %input_weight.1, bf16[3072,128]{1,0:T(8,128)(2,1)} %gate_weight.1, ...), custom_call_target="tpu_custom_call" | custom-call | flops 8000000000 | bytes 1024 | tf_op jit(solution)/shard_map/mamba/pallas_call | solution.py:450
  75.4 0.6 copy-done.15
  76.1 2.1 %join.1 = bf16[16,120,128]{2,1,0:T(8,128)(2,1)} custom-call(bf16[16,4,896]{2,1,0:T(4,128)(2,1)} %copy-done.15, bf16[16,120,128]{2,1,0:T(8,128)(2,1)} %get-tuple-element.77.blocks), custom_call_target="tpu_custom_call", output_to_operand_aliasing={{}: (1, {})} | custom-call | flops 20000000000 | bytes 1024 | tf_op jit(solution)/shard_map/join/pallas_call | solution.py:494
  78.3 5.5 %all-to-all-start.5 = ((bf16[16,120,128]{2,1,0:T(8,128)(2,1)}), bf16[16,120,128]{2,1,0:T(8,128)(2,1)S(1)}, u32[]{:S(2)}, u32[]{:S(2)}) async-start(bf16[16,120,128]{2,1,0:T(8,128)(2,1)} %join.1), calls=%async_computation.5 | async-start | bytes 983040 | tf_op jit(solution)/shard_map/all_to_all | solution.py:782
  84.4 1.0 collective-permute-done.6
  85.7 2.8 %collective-permute-done.2.refs_12_ = bf16[144,3072]{1,0:T(8,128)(2,1)} collective-permute-done((bf16[144,3072]{1,0:T(8,128)(2,1)}, bf16[144,3072]{1,0:T(8,128)(2,1)}, u32[]{:S(2)}, u32[]{:S(2)}) %collective-permute-start.2) | collective-permute-done | bytes 884768 | tf_op jit(solution)/shard_map/ppermute | solution.py:711
  88.5 0.7 collective-permute-done.3.refs_13_
  89.2 6.5 %all-to-all-done.5.parts = bf16[16,120,128]{2,1,0:T(8,128)(2,1)S(1)} async-done(((bf16[16,120,128]{2,1,0:T(8,128)(2,1)}), bf16[16,120,128]{2,1,0:T(8,128)(2,1)S(1)}, u32[]{:S(2)}, u32[]{:S(2)}) %all-to-all-start.5) | async-done | bytes 491552 | tf_op jit(solution)/shard_map/all_to_all | solution.py:782
  95.7 0.8 copy-done.10
  96.4 2.3 %project.1 = bf16[16,96,128]{2,1,0:T(8,128)(2,1)} custom-call(bf16[16,120,128]{2,1,0:T(8,128)(2,1)} %copy-done.10, bf16[192,768]{1,0:T(8,128)(2,1)} %bitcast.30), custom_call_target="tpu_custom_call" | custom-call | flops 20000000000 | bytes 1024 | tf_op jit(solution)/shard_map/project/pallas_call | solution.py:530
  98.8 0.5 collective-permute-start.14
  99.4 3.6 %all-to-all-start.6 = ((bf16[16,96,128]{2,1,0:T(8,128)(2,1)}), bf16[16,96,128]{2,1,0:T(8,128)(2,1)S(1)}, u32[]{:S(2)}, u32[]{:S(2)}) async-start(bf16[16,96,128]{2,1,0:T(8,128)(2,1)} %project.1), calls=%async_computation.6 | async-start | bytes 786432 | tf_op jit(solution)/shard_map/all_to_all | solution.py:793
  103.1 0.6 gather_fusion.2
  103.7 0.7 fusion
  104.4 1.0 collective-permute-start.17
  105.4 2.0 %collective-permute-start.16 = (bf16[8,128,256]{2,1,0:T(8,128)(2,1)S(1)}, bf16[8,128,256]{2,1,0:T(8,128)(2,1)S(1)}, u32[]{:S(2)}, u32[]{:S(2)}) collective-permute-start(bf16[8,128,256]{2,1,0:T(8,128)(2,1)S(1)} %pad_maximum_fusion.refs_0_), channel_id=1, source_target_pairs={{0,64},{16,80},{32,96},{48,112},{64,0},{80,16},{96,32},{112,48},{1... | collective-permute-start | bytes 1572872 | tf_op jit(solution)/shard_map/ppermute | solution.py:711
  107.4 0.5 collective-permute-start.15
  107.8 5.7 %all-to-all-done.6.spread = bf16[16,96,128]{2,1,0:T(8,128)(2,1)S(1)} async-done(((bf16[16,96,128]{2,1,0:T(8,128)(2,1)}), bf16[16,96,128]{2,1,0:T(8,128)(2,1)S(1)}, u32[]{:S(2)}, u32[]{:S(2)}) %all-to-all-start.6) | async-done | bytes 393248 | tf_op jit(solution)/shard_map/all_to_all | solution.py:793
  113.6 0.7 copy-done.11
  114.3 9.1 %feed.1 = (bf16[16,4,3072]{2,1,0:T(4,128)(2,1)}, bf16[64,3072]{1,0:T(8,128)(2,1)}) custom-call(bf16[16,96,128]{2,1,0:T(8,128)(2,1)} %copy-done.11, bf16[64,3072]{1,0:T(8,128)(2,1)} %get-tuple-element.88.embedded, f32[1,3072]{1,0:T(1,128)} %bitcast.33, bf16[144,3072]{1,0:T(8,128)(2,1)} %get-tuple-element.81.refs_0_, ...), custom_call_target="tpu_custom_call" | custom-call | flops 20000000000 | bytes 1024 | tf_op jit(solution)/shard_map/feed/pallas_call | solution.py:610
  123.5 3.6 %all-to-all-start.7 = ((bf16[16,4,3072]{2,1,0:T(4,128)(2,1)}), bf16[16,4,3072]{2,1,0:T(4,128)(2,1)S(1)}, u32[]{:S(2)}, u32[]{:S(2)}) async-start(bf16[16,4,3072]{2,1,0:T(4,128)(2,1)} %get-tuple-element.92), calls=%async_computation.7 | async-start | bytes 786432 | tf_op jit(solution)/shard_map/all_to_all | solution.py:796
  127.0 0.5 and_select_fusion.3.turns
  127.6 4.2 %collective-permute-done.15.refs_1_ = bf16[8,128,256]{2,1,0:T(8,128)(2,1)S(1)} collective-permute-done((bf16[8,128,256]{2,1,0:T(8,128)(2,1)S(1)}, bf16[8,128,256]{2,1,0:T(8,128)(2,1)S(1)}, u32[]{:S(2)}, u32[]{:S(2)}) %collective-permute-start.15) | collective-permute-done | bytes 524320 | tf_op jit(solution)/shard_map/ppermute | solution.py:711
  131.8 0.8 copy-done.9
  132.6 2.5 %pick.1 = f32[4,128,256]{2,1,0:T(8,128)} custom-call(s32[4]{0:T(128)} %and_select_fusion.3.turns, s32[4]{0:T(128)} %get-tuple-element.112.rows, bf16[8,128,256]{2,1,0:T(8,128)(2,1)} %copy-done.6, bf16[8,128,256]{2,1,0:T(8,128)(2,1)} %copy-done.9, bf16[8,128,256]{2,1,0:T(8,128)(2,1)} %copy-done.8, bf16[8,128,256]{2,1,0:T(8,128)(2,1)} %copy-done.7), custom_call_target="tpu_custom_call" | custom-call | tf_op jit(solution)/shard_map/pick/pallas_call | solution.py:659
  135.1 0.8 constant_dynamic-slice_fusion
  135.9 0.6 all-to-all-done.7
  136.7 0.6 add_convert_fusion
  (65 shorter events, 2.1 us)
Async XLA Ops:
  0.6 38.1 %copy-start = (s32[32]{0:T(128)S(1)}, s32[32]{0:T(128)}, u32[]{:S(2)}) copy-start(s32[32]{0:T(128)} %param.33) | copy-start | bytes 388
  0.6 26.4 %copy-start.3 = (s32[32]{0:T(128)S(1)}, s32[32]{0:T(128)}, u32[]{:S(2)}) copy-start(s32[32]{0:T(128)} %param.31) | copy-start | bytes 388
  5.0 27.5 %copy-start.1 = (s32[4]{0:T(128)S(1)}, s32[4]{0:T(128)}, u32[]{:S(2)}) copy-start(s32[4]{0:T(128)} %get-tuple-element.69.origin) | copy-start | bytes 52
  5.0 27.5 %all-to-all-start.2 = ((bf16[128,24,128]{2,1,0:T(8,128)(2,1)}), bf16[128,24,128]{2,1,0:T(8,128)(2,1)S(1)}, u32[]{:S(2)}, u32[]{:S(2)}) async-start(bf16[128,24,128]{2,1,0:T(8,128)(2,1)} %get-tuple-element.70), calls=%async_computation.2 | async-start | bytes 1572864 | tf_op jit(solution)/shard_map/all_to_all | solution.py:722
  18.9 59.3 %collective-permute-start.5 = (bf16[144,3072]{1,0:T(8,128)(2,1)}, bf16[144,3072]{1,0:T(8,128)(2,1)}, u32[]{:S(2)}, u32[]{:S(2)}) collective-permute-start(bf16[144,3072]{1,0:T(8,128)(2,1)} %get-tuple-element.81.refs_0_), channel_id=1, source_target_pairs={{0,96},{16,112},{32,0},{48,16},{64,32},{80,48},{96,64},{112,80},{1... | collective-permute-start | bytes 2654216 | tf_op jit(solution)/shard_map/ppermute | solution.py:711
  21.7 38.1 %collective-permute-start = (bf16[144,3072]{1,0:T(8,128)(2,1)}, bf16[144,3072]{1,0:T(8,128)(2,1)}, u32[]{:S(2)}, u32[]{:S(2)}) collective-permute-start(bf16[144,3072]{1,0:T(8,128)(2,1)} %get-tuple-element.81.refs_0_), channel_id=1, source_target_pairs={{0,32},{16,48},{32,64},{48,80},{64,96},{80,112},{96,0},{112,16},{1... | collective-permute-start | bytes 2654216 | tf_op jit(solution)/shard_map/ppermute | solution.py:711
  21.7 56.5 %collective-permute-start.4 = (bf16[144,3072]{1,0:T(8,128)(2,1)}, bf16[144,3072]{1,0:T(8,128)(2,1)}, u32[]{:S(2)}, u32[]{:S(2)}) collective-permute-start(bf16[144,3072]{1,0:T(8,128)(2,1)} %get-tuple-element.82.refs_1_), channel_id=1, source_target_pairs={{0,32},{16,48},{32,64},{48,80},{64,96},{80,112},{96,0},{112,16},{1... | collective-permute-start | bytes 2654216 | tf_op jit(solution)/shard_map/ppermute | solution.py:711
  22.0 43.4 %collective-permute-start.1 = (bf16[144,3072]{1,0:T(8,128)(2,1)}, bf16[144,3072]{1,0:T(8,128)(2,1)}, u32[]{:S(2)}, u32[]{:S(2)}) collective-permute-start(bf16[144,3072]{1,0:T(8,128)(2,1)} %get-tuple-element.82.refs_1_), channel_id=1, source_target_pairs={{0,96},{16,112},{32,0},{48,16},{64,32},{80,48},{96,64},{112,80},{1... | collective-permute-start | bytes 2654216 | tf_op jit(solution)/shard_map/ppermute | solution.py:711
  32.5 1.4 copy-start.13
  33.8 5.5 %copy-start.4 = (s32[32]{0:T(128)S(1)}, s32[32]{0:T(128)}, u32[]{:S(2)}) copy-start(s32[32]{0:T(128)} %param.30) | copy-start | bytes 388
  34.5 13.8 %all-to-all-start.3 = ((bf16[16,96,128]{2,1,0:T(8,128)(2,1)}), bf16[16,96,128]{2,1,0:T(8,128)(2,1)S(1)}, u32[]{:S(2)}, u32[]{:S(2)}) async-start(bf16[16,96,128]{2,1,0:T(8,128)(2,1)} %hand.2), calls=%async_computation.3 | async-start | bytes 786432 | tf_op jit(solution)/shard_map/all_to_all | solution.py:726
  48.3 0.7 copy-start.12
  56.3 19.1 %all-to-all-start.4 = ((bf16[16,4,896]{2,1,0:T(4,128)(2,1)}), bf16[16,4,896]{2,1,0:T(4,128)(2,1)S(1)}, u32[]{:S(2)}, u32[]{:S(2)}) async-start(bf16[16,4,896]{2,1,0:T(4,128)(2,1)} %get-tuple-element.73), calls=%async_computation.4 | async-start | bytes 229376 | tf_op jit(solution)/shard_map/all_to_all | solution.py:765
  65.5 23.0 %collective-permute-start.2 = (bf16[144,3072]{1,0:T(8,128)(2,1)}, bf16[144,3072]{1,0:T(8,128)(2,1)}, u32[]{:S(2)}, u32[]{:S(2)}) collective-permute-start(bf16[144,3072]{1,0:T(8,128)(2,1)} %collective-permute-done.refs_2_), channel_id=1, source_target_pairs={{0,32},{16,48},{32,64},{48,80},{64,96},{80,112},{96,0},{112,16},{1... | collective-permute-start | bytes 2654216 | tf_op jit(solution)/shard_map/ppermute | solution.py:711
  67.6 21.6 %collective-permute-start.3 = (bf16[144,3072]{1,0:T(8,128)(2,1)}, bf16[144,3072]{1,0:T(8,128)(2,1)}, u32[]{:S(2)}, u32[]{:S(2)}) collective-permute-start(bf16[144,3072]{1,0:T(8,128)(2,1)} %collective-permute-done.1.refs_3_), channel_id=1, source_target_pairs={{0,96},{16,112},{32,0},{48,16},{64,32},{80,48},{96,64},{112,80},{1... | collective-permute-start | bytes 2654216 | tf_op jit(solution)/shard_map/ppermute | solution.py:711
  75.4 0.6 copy-start.15
  76.1 2.2 %copy-start.16 = (bf16[144,3072]{1,0:T(8,128)(2,1)S(1)}, bf16[144,3072]{1,0:T(8,128)(2,1)}, u32[]{:S(2)}) copy-start(bf16[144,3072]{1,0:T(8,128)(2,1)} %get-tuple-element.81.refs_0_) | copy-start | bytes 2654212
  76.1 7.8 %copy-start.14 = (bf16[4,1,128,256]{3,2,1,0:T(8,128)(2,1)S(1)}, bf16[4,1,128,256]{3,2,1,0:T(8,128)(2,1)}, u32[]{:S(2)}) copy-start(bf16[4,1,128,256]{3,2,1,0:T(8,128)(2,1)} %get-tuple-element.80) | copy-start | bytes 786436
  76.1 8.0 %copy-start.17 = (bf16[144,3072]{1,0:T(8,128)(2,1)S(1)}, bf16[144,3072]{1,0:T(8,128)(2,1)}, u32[]{:S(2)}) copy-start(bf16[144,3072]{1,0:T(8,128)(2,1)} %get-tuple-element.82.refs_1_) | copy-start | bytes 2654212
  78.2 17.4 %collective-permute-start.7 = (bf16[144,3072]{1,0:T(8,128)(2,1)S(1)}, bf16[144,3072]{1,0:T(8,128)(2,1)}, u32[]{:S(2)}, u32[]{:S(2)}) collective-permute-start(bf16[144,3072]{1,0:T(8,128)(2,1)S(1)} %copy-done.16), channel_id=1, source_target_pairs={{0,16},{16,0},{32,48},{48,32},{64,80},{80,64},{96,112},{112,96},{1... | collective-permute-start | bytes 2654216 | tf_op jit(solution)/shard_map/ppermute | solution.py:716
  78.3 17.3 %all-to-all-start.5 = ((bf16[16,120,128]{2,1,0:T(8,128)(2,1)}), bf16[16,120,128]{2,1,0:T(8,128)(2,1)S(1)}, u32[]{:S(2)}, u32[]{:S(2)}) async-start(bf16[16,120,128]{2,1,0:T(8,128)(2,1)} %join.1), calls=%async_computation.5 | async-start | bytes 983040 | tf_op jit(solution)/shard_map/all_to_all | solution.py:782
  83.8 1.6 %collective-permute-start.6 = (bf16[4,128,256]{2,1,0:T(8,128)(2,1)S(1)}, bf16[4,128,256]{2,1,0:T(8,128)(2,1)S(1)}, u32[]{:S(2)}, u32[]{:S(2)}) collective-permute-start(bf16[4,128,256]{2,1,0:T(8,128)(2,1)S(1)} %bitcast.28), channel_id=1, source_target_pairs={{0,16},{16,0},{32,48},{48,32},{64,80},{80,64},{96,112},{112,96},{1... | collective-permute-start | bytes 786440 | tf_op jit(solution)/shard_map/ppermute | solution.py:716
  84.1 14.6 %collective-permute-start.8 = (bf16[144,3072]{1,0:T(8,128)(2,1)S(1)}, bf16[144,3072]{1,0:T(8,128)(2,1)}, u32[]{:S(2)}, u32[]{:S(2)}) collective-permute-start(bf16[144,3072]{1,0:T(8,128)(2,1)S(1)} %copy-done.17), channel_id=1, source_target_pairs={{0,16},{16,0},{32,48},{48,32},{64,80},{80,64},{96,112},{112,96},{1... | collective-permute-start | bytes 2654216 | tf_op jit(solution)/shard_map/ppermute | solution.py:716
  85.4 13.3 %collective-permute-start.9 = (bf16[144,3072]{1,0:T(8,128)(2,1)}, bf16[144,3072]{1,0:T(8,128)(2,1)}, u32[]{:S(2)}, u32[]{:S(2)}) collective-permute-start(bf16[144,3072]{1,0:T(8,128)(2,1)} %collective-permute-done.refs_2_), channel_id=1, source_target_pairs={{0,16},{16,0},{32,48},{48,32},{64,80},{80,64},{96,112},{112,96},{1... | collective-permute-start | bytes 2654216 | tf_op jit(solution)/shard_map/ppermute | solution.py:716
  85.7 21.7 %copy-start.6 = (bf16[8,128,256]{2,1,0:T(8,128)(2,1)}, bf16[8,128,256]{2,1,0:T(8,128)(2,1)S(1)}, u32[]{:S(2)}) copy-start(bf16[8,128,256]{2,1,0:T(8,128)(2,1)S(1)} %pad_maximum_fusion.refs_0_) | copy-start | bytes 1572868
  88.5 10.2 %collective-permute-start.10 = (bf16[144,3072]{1,0:T(8,128)(2,1)}, bf16[144,3072]{1,0:T(8,128)(2,1)}, u32[]{:S(2)}, u32[]{:S(2)}) collective-permute-start(bf16[144,3072]{1,0:T(8,128)(2,1)} %collective-permute-done.1.refs_3_), channel_id=1, source_target_pairs={{0,16},{16,0},{32,48},{48,32},{64,80},{80,64},{96,112},{112,96},{1... | collective-permute-start | bytes 2654216 | tf_op jit(solution)/shard_map/ppermute | solution.py:716
  89.2 9.5 %collective-permute-start.11 = (bf16[144,3072]{1,0:T(8,128)(2,1)}, bf16[144,3072]{1,0:T(8,128)(2,1)}, u32[]{:S(2)}, u32[]{:S(2)}) collective-permute-start(bf16[144,3072]{1,0:T(8,128)(2,1)} %collective-permute-done.4.refs_4_), channel_id=1, source_target_pairs={{0,16},{16,0},{32,48},{48,32},{64,80},{80,64},{96,112},{112,96},{1... | collective-permute-start | bytes 2654216 | tf_op jit(solution)/shard_map/ppermute | solution.py:716
  95.6 0.8 copy-start.10
  95.6 3.1 %collective-permute-start.12 = (bf16[144,3072]{1,0:T(8,128)(2,1)}, bf16[144,3072]{1,0:T(8,128)(2,1)S(1)}, u32[]{:S(2)}, u32[]{:S(2)}) collective-permute-start(bf16[144,3072]{1,0:T(8,128)(2,1)} %collective-permute-done.5.refs_5_), channel_id=1, source_target_pairs={{0,16},{16,0},{32,48},{48,32},{64,80},{80,64},{96,112},{112,96},{1... | collective-permute-start | bytes 2654216 | tf_op jit(solution)/shard_map/ppermute | solution.py:716
  96.4 2.9 %copy-start.19 = (s32[32]{0:T(128)S(1)}, s32[32]{0:T(128)}, u32[]{:S(2)}) copy-start(s32[32]{0:T(128)} %param.32) | copy-start | bytes 388
  98.7 14.9 %copy-start.18 = (bf16[144,3072]{1,0:T(8,128)(2,1)}, bf16[144,3072]{1,0:T(8,128)(2,1)S(1)}, u32[]{:S(2)}) copy-start(bf16[144,3072]{1,0:T(8,128)(2,1)S(1)} %collective-permute-done.12.refs_11_) | copy-start | bytes 2654212
  98.7 14.9 %collective-permute-start.13 = (bf16[144,3072]{1,0:T(8,128)(2,1)}, bf16[144,3072]{1,0:T(8,128)(2,1)}, u32[]{:S(2)}, u32[]{:S(2)}) collective-permute-start(bf16[144,3072]{1,0:T(8,128)(2,1)} %collective-permute-done.2.refs_12_), channel_id=1, source_target_pairs={{0,16},{16,0},{32,48},{48,32},{64,80},{80,64},{96,112},{112,96},{1... | collective-permute-start | bytes 2654216 | tf_op jit(solution)/shard_map/ppermute | solution.py:716
  98.8 14.8 %collective-permute-start.14 = (bf16[144,3072]{1,0:T(8,128)(2,1)}, bf16[144,3072]{1,0:T(8,128)(2,1)}, u32[]{:S(2)}, u32[]{:S(2)}) collective-permute-start(bf16[144,3072]{1,0:T(8,128)(2,1)} %collective-permute-done.3.refs_13_), channel_id=1, source_target_pairs={{0,16},{16,0},{32,48},{48,32},{64,80},{80,64},{96,112},{112,96},{1... | collective-permute-start | bytes 2654216 | tf_op jit(solution)/shard_map/ppermute | solution.py:716
  99.4 14.2 %all-to-all-start.6 = ((bf16[16,96,128]{2,1,0:T(8,128)(2,1)}), bf16[16,96,128]{2,1,0:T(8,128)(2,1)S(1)}, u32[]{:S(2)}, u32[]{:S(2)}) async-start(bf16[16,96,128]{2,1,0:T(8,128)(2,1)} %project.1), calls=%async_computation.6 | async-start | bytes 786432 | tf_op jit(solution)/shard_map/all_to_all | solution.py:793
  104.4 23.2 %collective-permute-start.17 = (bf16[8,128,256]{2,1,0:T(8,128)(2,1)S(1)}, bf16[8,128,256]{2,1,0:T(8,128)(2,1)S(1)}, u32[]{:S(2)}, u32[]{:S(2)}) collective-permute-start(bf16[8,128,256]{2,1,0:T(8,128)(2,1)S(1)} %pad_maximum_fusion.refs_0_), channel_id=1, source_target_pairs={{0,96},{16,112},{32,0},{48,16},{64,32},{80,48},{96,64},{112,80},{1... | collective-permute-start | bytes 1572872 | tf_op jit(solution)/shard_map/ppermute | solution.py:711
  105.4 22.2 %collective-permute-start.16 = (bf16[8,128,256]{2,1,0:T(8,128)(2,1)S(1)}, bf16[8,128,256]{2,1,0:T(8,128)(2,1)S(1)}, u32[]{:S(2)}, u32[]{:S(2)}) collective-permute-start(bf16[8,128,256]{2,1,0:T(8,128)(2,1)S(1)} %pad_maximum_fusion.refs_0_), channel_id=1, source_target_pairs={{0,64},{16,80},{32,96},{48,112},{64,0},{80,16},{96,32},{112,48},{1... | collective-permute-start | bytes 1572872 | tf_op jit(solution)/shard_map/ppermute | solution.py:711
  107.4 24.4 %collective-permute-start.15 = (bf16[8,128,256]{2,1,0:T(8,128)(2,1)S(1)}, bf16[8,128,256]{2,1,0:T(8,128)(2,1)S(1)}, u32[]{:S(2)}, u32[]{:S(2)}) collective-permute-start(bf16[8,128,256]{2,1,0:T(8,128)(2,1)S(1)} %pad_maximum_fusion.refs_0_), channel_id=1, source_target_pairs={{0,32},{16,48},{32,64},{48,80},{64,96},{80,112},{96,0},{112,16},{1... | collective-permute-start | bytes 1572872 | tf_op jit(solution)/shard_map/ppermute | solution.py:711
  113.6 0.7 copy-start.11
  123.5 13.0 %all-to-all-start.7 = ((bf16[16,4,3072]{2,1,0:T(4,128)(2,1)}), bf16[16,4,3072]{2,1,0:T(4,128)(2,1)S(1)}, u32[]{:S(2)}, u32[]{:S(2)}) async-start(bf16[16,4,3072]{2,1,0:T(4,128)(2,1)} %get-tuple-element.92), calls=%async_computation.7 | async-start | bytes 786432 | tf_op jit(solution)/shard_map/all_to_all | solution.py:796
  127.6 4.2 %copy-start.7 = (bf16[8,128,256]{2,1,0:T(8,128)(2,1)}, bf16[8,128,256]{2,1,0:T(8,128)(2,1)S(1)}, u32[]{:S(2)}) copy-start(bf16[8,128,256]{2,1,0:T(8,128)(2,1)S(1)} %collective-permute-done.17.refs_3_) | copy-start | bytes 1572868
  127.6 4.2 %copy-start.8 = (bf16[8,128,256]{2,1,0:T(8,128)(2,1)}, bf16[8,128,256]{2,1,0:T(8,128)(2,1)S(1)}, u32[]{:S(2)}) copy-start(bf16[8,128,256]{2,1,0:T(8,128)(2,1)S(1)} %collective-permute-done.16.refs_2_) | copy-start | bytes 1572868
  131.8 0.8 copy-start.9

commit v9 on v8

--- a/solution.py
+++ b/solution.py
@@ -11,6 +11,7 @@
 F32 = jnp.float32
 NEG = -1e30
 AUX = 128
+VMEM = 63 << 10
 
 
 def inverse_of(mapping):
@@ -64,7 +65,7 @@
     return [pl.BlockSpec(memory_space=pltpu.SMEM)] * count
 
 
-PARAMS = pltpu.CompilerParams(vmem_limit_bytes=60 << 20)
+PARAMS = pltpu.CompilerParams(vmem_limit_bytes=VMEM << 10)
 SMALL = pltpu.CompilerParams(vmem_limit_bytes=8 << 20)
 
 
@@ -319,7 +320,7 @@
     return pl.pallas_call(
         attend_kernel,
         grid=(1,),
-        in_specs=scalars(1) + near(1) + whole([places, extra, gain]) + streamed(4),
+        in_specs=scalars(1) + whole([arrived, places, extra, gain]) + streamed(4),
         out_specs=whole(outs),
         out_shape=outs,
         scratch_shapes=[pltpu.VMEM(a.shape, a.dtype) for a in far]
@@ -469,15 +470,15 @@
     peers, own, _ = parts.shape
     rows = heads * own
     aux = parts[:, :, heads * size : heads * size + AUX].astype(F32)
+    get = lambda k: aux[:, :, k * heads : (k + 1) * heads]
+    top = get(0) + get(1) + get(2)
+    total = get(3) + get(4)
+    factors = jnp.exp(top - jnp.max(top, axis=0, keepdims=True))
+    factors = factors / jnp.sum(factors * total, axis=0, keepdims=True)
     for h in range(heads):
-        get = lambda k: aux[:, :, k * heads + h : k * heads + h + 1]
-        top = get(0) + get(1) + get(2)
-        total = get(3) + get(4)
-        factor = jnp.exp(top - jnp.max(top, axis=0, keepdims=True))
-        norm = jnp.sum(factor * total, axis=0)
         value = parts[:, :, h * size : (h + 1) * size].astype(F32)
-        summed = jnp.sum(factor * value, axis=0)
-        piece[h * own : (h + 1) * own, :] = (summed / norm).astype(BF)
+        summed = jnp.sum(factors[:, :, h : h + 1] * value, axis=0)
+        piece[h * own : (h + 1) * own, :] = summed.astype(BF)
     first = payload.shape[1] - rows
     copies = [
         pltpu.make_async_copy(piece, payload.at[j, pl.ds(first, rows), :], sem.at[j])
@@ -494,7 +495,7 @@
     return pl.pallas_call(
         functools.partial(join_kernel, heads=heads, size=size),
         grid=(1,),
-        in_specs=near(1) + streamed(1),
+        in_specs=whole([parts]) + streamed(1),
         out_specs=streamed(1)[0],
         out_shape=jax.ShapeDtypeStruct(blocks.shape, BF),
         input_output_aliases={1: 0},
@@ -530,7 +531,7 @@
     return pl.pallas_call(
         functools.partial(project_kernel, heads=heads, size=size),
         grid=(1,),
-        in_specs=near(1) + whole([out_weight]),
+        in_specs=whole([parts, out_weight]),
         out_specs=whole([out])[0],
         out_shape=out,
         compiler_params=PARAMS,
@@ -610,7 +611,7 @@
     return pl.pallas_call(
         functools.partial(feed_kernel, count=len(weights), units=units),
         grid=(1,),
-        in_specs=near(1) + whole([embedded, gain]) + streamed(len(weights)),
+        in_specs=whole([spread, embedded, gain]) + streamed(len(weights)),
         out_specs=whole(outs),
         out_shape=outs,
         scratch_shapes=unit_scratch(weights, units),
@@ -763,8 +764,6 @@
         value_cache,
     )
     parts = lax.all_to_all(payload, "tok", 0, 0, tiled=True)
-    later = lax.optimization_barrier((near_z[0], near_z[1], payload))
-    far = [turn(later[0], 1), turn(later[1], -1)]
     blocks, chosen = mamba(
         ints,
         reals,
@@ -778,6 +777,8 @@
         members,
         query_heads * own,
     )
+    later = lax.optimization_barrier((near_z[0], near_z[1], blocks))
+    far = [turn(later[0], 1), turn(later[1], -1)]
     joint = join(parts, blocks, query_heads, head_size)
     joined = lax.all_to_all(joint, "tok", 0, 0, tiled=True)
     *later, chosen, _ = lax.optimization_barrier((*weights, chosen, joint))

time: 139 us -> 136 us (0.978)
  waiting for transfers between devices: 40 us -> 36.4 us
  starting transfers between devices: 45 us -> 48.5 us
  local copies, waits for them, and re-layouts: 6.48 us -> 4.91 us
    all_to_all x1, waiting for transfers between devices: 6.45 us -> 2.49 us  [local(): joined = lax.all_to_all(joint, 'tok', 0, 0, tiled=True)]
    all_to_all x1, starting transfers between devices: 3.56 us -> 6.13 us  [local(): added = lax.all_to_all(spread, 'tok', 0, 0, tiled=True)]
    unnamed x36 -> x22, local copies, waits for them, and re-layouts: 3.72 us -> 2.16 us
    all_to_all x1, starting transfers between devices: 5.46 us -> 7.03 us  [local(): joined = lax.all_to_all(joint, 'tok', 0, 0, tiled=True)]
where the time goes in v9:
time: 136 us; the launch traced here: 135 us
  starting transfers between devices  48.5 us (36%)
  Pallas kernels  38.3 us (28%)
  waiting for transfers between devices  36.4 us (27%)
  local copies, waits for them, and re-layouts  4.91 us (4%)
  other arithmetic  3.82 us (3%)
  between operations  2.88 us (2%)
    ppermute x9, waiting for transfers between devices, turn(): lax.ppermute(value, 'req', [(g, (g + by * cores) % groups) for g in range...  12.1 us
    ppermute x9, starting transfers between devices, turn(): lax.ppermute(value, 'req', [(g, (g + by * cores) % groups) for g in range...  12 us
    all_to_all x1, starting transfers between devices, exchange(): came = lax.all_to_all(sent, ('req', 'tok'), 0, 0, tiled=True)  11.1 us
    pallas_call x1, Pallas kernels, feed(): pl.pallas_call(functools.partial(feed_kernel, count=len(weights), units=u...  9.13 us
    all_to_all x1, waiting for transfers between devices, plane(): return lax.all_to_all(rows, 'tok', 0, 0, tiled=True)  7.56 us
    pallas_call x1, Pallas kernels, attend(): pl.pallas_call(attend_kernel, grid=(1,), in_specs=scalars(1) + whole([arr...  7.27 us
    all_to_all x1, starting transfers between devices, local(): joined = lax.all_to_all(joint, 'tok', 0, 0, tiled=True)  7.03 us
    pallas_call x1, Pallas kernels, mamba(): pl.pallas_call(mamba_kernel, grid=(1,), in_specs=scalars(2) + whole([norm...  6.71 us
  transfers between devices with their start and end apart: 24, of which 10 were waited for; matrix products, arithmetic and copies ran while one was open for 4% of the time, Pallas kernels for 25%

profile of v9, /device:TPU:0, one launch (start us, length us, event | category | flops | bytes accessed | tf_op | source)
XLA Modules:
  0.0 135.4 jit_solution(9301617866568670958)
XLA Ops:
  0.7 4.3 %fetch.2 = (bf16[128,24,128]{2,1,0:T(8,128)(2,1)}, s32[64,128]{1,0:T(8,128)}, s32[4]{0:T(128)}, s32[1]{0:T(128)}) custom-call(s32[1]{0:T(128)} %constant.84.clone.1.turn, s32[1,32]{1,0:T(1,128)} %bitcast.20, s32[16,32]{1,0:T(8,128)} %bitcast.26, bf16[512,3072]{1,0:T(8,128)(2,1)} %table_far.1), custom_call_target="tpu_custom_call" | custom-call | flops 402653184 | bytes 3145728 | tf_op jit(solution)/shard_map/fetch/pallas_call | solution.py:151
  5.0 11.1 %all-to-all-start.2 = ((bf16[128,24,128]{2,1,0:T(8,128)(2,1)}), bf16[128,24,128]{2,1,0:T(8,128)(2,1)S(1)}, u32[]{:S(2)}, u32[]{:S(2)}) async-start(bf16[128,24,128]{2,1,0:T(8,128)(2,1)} %get-tuple-element.70), calls=%async_computation.2 | async-start | bytes 1572864 | tf_op jit(solution)/shard_map/all_to_all | solution.py:723
  16.1 2.8 %pack.1 = (bf16[144,3072]{1,0:T(8,128)(2,1)}, bf16[144,3072]{1,0:T(8,128)(2,1)}) custom-call(bf16[96,3072]{1,0:T(8,128)(2,1)} %bitcast.22, bf16[96,3072]{1,0:T(8,128)(2,1)} %bitcast.23, bf16[96,3072]{1,0:T(8,128)(2,1)} %bitcast.24, s32[64,128]{1,0:T(8,128)} %get-tuple-element.66.ready.places), custom_call_target="tpu_custom_call" | custom-call | bytes 1024 | tf_op jit(solution)/shard_map/pack/pallas_call | solution.py:634
  18.9 2.8 %collective-permute-start.5 = (bf16[144,3072]{1,0:T(8,128)(2,1)}, bf16[144,3072]{1,0:T(8,128)(2,1)}, u32[]{:S(2)}, u32[]{:S(2)}) collective-permute-start(bf16[144,3072]{1,0:T(8,128)(2,1)} %get-tuple-element.81.refs_0_), channel_id=1, source_target_pairs={{0,96},{16,112},{32,0},{48,16},{64,32},{80,48},{96,64},{112,80},{1... | collective-permute-start | bytes 2654216 | tf_op jit(solution)/shard_map/ppermute | solution.py:712
  21.7 0.3 collective-permute-start.4
  22.0 3.0 %collective-permute-start.1 = (bf16[144,3072]{1,0:T(8,128)(2,1)}, bf16[144,3072]{1,0:T(8,128)(2,1)}, u32[]{:S(2)}, u32[]{:S(2)}) collective-permute-start(bf16[144,3072]{1,0:T(8,128)(2,1)} %get-tuple-element.82.refs_1_), channel_id=1, source_target_pairs={{0,96},{16,112},{32,0},{48,16},{64,32},{80,48},{96,64},{112,80},{1... | collective-permute-start | bytes 2654216 | tf_op jit(solution)/shard_map/ppermute | solution.py:712
  27.2 5.3 %all-to-all-done.2.came = bf16[128,24,128]{2,1,0:T(8,128)(2,1)S(1)} async-done(((bf16[128,24,128]{2,1,0:T(8,128)(2,1)}), bf16[128,24,128]{2,1,0:T(8,128)(2,1)S(1)}, u32[]{:S(2)}, u32[]{:S(2)}) %all-to-all-start.2) | async-done | bytes 786464 | tf_op jit(solution)/shard_map/all_to_all | solution.py:723
  32.5 1.3 hand.2
  33.9 0.6 while.10
  34.4 3.6 %all-to-all-start.3 = ((bf16[16,96,128]{2,1,0:T(8,128)(2,1)}), bf16[16,96,128]{2,1,0:T(8,128)(2,1)S(1)}, u32[]{:S(2)}, u32[]{:S(2)}) async-start(bf16[16,96,128]{2,1,0:T(8,128)(2,1)} %hand.2), calls=%async_computation.3 | async-start | bytes 786432 | tf_op jit(solution)/shard_map/all_to_all | solution.py:727
  38.0 0.6 pad_maximum_fusion.1.reals
  38.6 0.6 gather_fusion.1
  39.2 0.6 gather_fusion
  40.0 0.7 pad_add_fusion.ints
  40.6 7.6 %all-to-all-done.3.arrived = bf16[16,96,128]{2,1,0:T(8,128)(2,1)S(1)} async-done(((bf16[16,96,128]{2,1,0:T(8,128)(2,1)}), bf16[16,96,128]{2,1,0:T(8,128)(2,1)S(1)}, u32[]{:S(2)}, u32[]{:S(2)}) %all-to-all-start.3) | async-done | bytes 393248 | tf_op jit(solution)/shard_map/all_to_all | solution.py:727
  48.2 0.7 copy-done.8
  48.9 7.3 %attend.1 = (bf16[16,4,896]{2,1,0:T(4,128)(2,1)}, bf16[64,3072]{1,0:T(8,128)(2,1)}, bf16[64,3072]{1,0:T(8,128)(2,1)}) custom-call(s32[9]{0:T(128)} %pad_add_fusion.ints, bf16[16,96,128]{2,1,0:T(8,128)(2,1)} %copy-done.8, s32[64,128]{1,0:T(8,128)} %get-tuple-element.66.ready.places, bf16[64,3072]{1,0:T(8,128)(2,1)S(1)} %get-tuple-element.72.extra, ...), custom_call_target="tpu_custom_call" | custom-call | flops 20000000000 | bytes 1024 | tf_op jit(solution)/shard_map/attend/pallas_call | solution.py:320
  56.2 3.7 %all-to-all-start.4 = ((bf16[16,4,896]{2,1,0:T(4,128)(2,1)}), bf16[16,4,896]{2,1,0:T(4,128)(2,1)S(1)}, u32[]{:S(2)}, u32[]{:S(2)}) async-start(bf16[16,4,896]{2,1,0:T(4,128)(2,1)} %get-tuple-element.77), calls=%async_computation.4 | async-start | bytes 229376 | tf_op jit(solution)/shard_map/all_to_all | solution.py:766
  59.9 6.7 %mamba.1 = (bf16[16,120,128]{2,1,0:T(8,128)(2,1)}, bf16[4,1,128,256]{3,2,1,0:T(8,128)(2,1)}) custom-call(s32[9]{0:T(128)} %pad_add_fusion.ints, f32[3]{0:T(128)} %pad_maximum_fusion.1.reals, bf16[64,3072]{1,0:T(8,128)(2,1)} %get-tuple-element.73.normed, bf16[3072,128]{1,0:T(8,128)(2,1)} %input_weight.1, bf16[3072,128]{1,0:T(8,128)(2,1)} %gate_weight.1, ...), custom_call_target="tpu_custom_call" | custom-call | flops 8000000000 | bytes 1024 | tf_op jit(solution)/shard_map/mamba/pallas_call | solution.py:451
  66.7 1.0 collective-permute-start.2
  67.6 2.3 %collective-permute-start.3 = (bf16[144,3072]{1,0:T(8,128)(2,1)}, bf16[144,3072]{1,0:T(8,128)(2,1)}, u32[]{:S(2)}, u32[]{:S(2)}) collective-permute-start(bf16[144,3072]{1,0:T(8,128)(2,1)} %collective-permute-done.1.refs_3_), channel_id=1, source_target_pairs={{0,96},{16,112},{32,0},{48,16},{64,32},{80,48},{96,64},{112,80},{1... | collective-permute-start | bytes 2654216 | tf_op jit(solution)/shard_map/ppermute | solution.py:712
  70.0 0.6 copy-done.11
  70.6 2.0 %join.1 = bf16[16,120,128]{2,1,0:T(8,128)(2,1)} custom-call(bf16[16,4,896]{2,1,0:T(4,128)(2,1)} %copy-done.11, bf16[16,120,128]{2,1,0:T(8,128)(2,1)} %get-tuple-element.74.blocks), custom_call_target="tpu_custom_call", output_to_operand_aliasing={{}: (1, {})} | custom-call | flops 20000000000 | bytes 1024 | tf_op jit(solution)/shard_map/join/pallas_call | solution.py:495
  72.8 7.0 %all-to-all-start.5 = ((bf16[16,120,128]{2,1,0:T(8,128)(2,1)}), bf16[16,120,128]{2,1,0:T(8,128)(2,1)}, u32[]{:S(2)}, u32[]{:S(2)}) async-start(bf16[16,120,128]{2,1,0:T(8,128)(2,1)} %join.1), calls=%async_computation.5 | async-start | bytes 983040 | tf_op jit(solution)/shard_map/all_to_all | solution.py:783
  79.8 0.3 collective-permute-start.6
  80.1 0.3 collective-permute-start.8
  80.4 1.0 collective-permute-done.6
  81.7 6.9 %collective-permute-done.2.refs_12_ = bf16[144,3072]{1,0:T(8,128)(2,1)} collective-permute-done((bf16[144,3072]{1,0:T(8,128)(2,1)}, bf16[144,3072]{1,0:T(8,128)(2,1)}, u32[]{:S(2)}, u32[]{:S(2)}) %collective-permute-start.2) | collective-permute-done | bytes 884768 | tf_op jit(solution)/shard_map/ppermute | solution.py:712
  88.6 0.6 collective-permute-done.3.refs_13_
  89.2 2.5 %all-to-all-done.5.parts = bf16[16,120,128]{2,1,0:T(8,128)(2,1)} async-done(((bf16[16,120,128]{2,1,0:T(8,128)(2,1)}), bf16[16,120,128]{2,1,0:T(8,128)(2,1)}, u32[]{:S(2)}, u32[]{:S(2)}) %all-to-all-start.5) | async-done | bytes 491552 | tf_op jit(solution)/shard_map/all_to_all | solution.py:783
  91.7 2.3 %project.1 = bf16[16,96,128]{2,1,0:T(8,128)(2,1)} custom-call(bf16[16,120,128]{2,1,0:T(8,128)(2,1)} %all-to-all-done.5.parts, bf16[192,768]{1,0:T(8,128)(2,1)} %bitcast.30), custom_call_target="tpu_custom_call" | custom-call | flops 20000000000 | bytes 1024 | tf_op jit(solution)/shard_map/project/pallas_call | solution.py:531
  94.0 0.5 collective-permute-done.12.refs_11_
  94.6 0.4 collective-permute-start.14
  95.1 6.1 %all-to-all-start.6 = ((bf16[16,96,128]{2,1,0:T(8,128)(2,1)}), bf16[16,96,128]{2,1,0:T(8,128)(2,1)S(1)}, u32[]{:S(2)}, u32[]{:S(2)}) async-start(bf16[16,96,128]{2,1,0:T(8,128)(2,1)} %project.1), calls=%async_computation.6 | async-start | bytes 786432 | tf_op jit(solution)/shard_map/all_to_all | solution.py:794
  101.3 0.6 gather_fusion.2
  102.0 0.7 fusion
  102.6 1.7 %collective-permute-start.17 = (bf16[8,128,256]{2,1,0:T(8,128)(2,1)S(1)}, bf16[8,128,256]{2,1,0:T(8,128)(2,1)}, u32[]{:S(2)}, u32[]{:S(2)}) collective-permute-start(bf16[8,128,256]{2,1,0:T(8,128)(2,1)S(1)} %pad_maximum_fusion.refs_0_), channel_id=1, source_target_pairs={{0,96},{16,112},{32,0},{48,16},{64,32},{80,48},{96,64},{112,80},{1... | collective-permute-start | bytes 1572872 | tf_op jit(solution)/shard_map/ppermute | solution.py:712
  104.3 0.9 collective-permute-start.15
  105.2 6.4 %all-to-all-done.6.spread = bf16[16,96,128]{2,1,0:T(8,128)(2,1)S(1)} async-done(((bf16[16,96,128]{2,1,0:T(8,128)(2,1)}), bf16[16,96,128]{2,1,0:T(8,128)(2,1)S(1)}, u32[]{:S(2)}, u32[]{:S(2)}) %all-to-all-start.6) | async-done | bytes 393248 | tf_op jit(solution)/shard_map/all_to_all | solution.py:794
  111.6 0.7 copy-done.7
  112.4 9.1 %feed.1 = (bf16[16,4,3072]{2,1,0:T(4,128)(2,1)}, bf16[64,3072]{1,0:T(8,128)(2,1)}) custom-call(bf16[16,96,128]{2,1,0:T(8,128)(2,1)} %copy-done.7, bf16[64,3072]{1,0:T(8,128)(2,1)} %get-tuple-element.88.embedded, f32[1,3072]{1,0:T(1,128)} %bitcast.33, bf16[144,3072]{1,0:T(8,128)(2,1)} %get-tuple-element.81.refs_0_, ...), custom_call_target="tpu_custom_call" | custom-call | flops 20000000000 | bytes 1024 | tf_op jit(solution)/shard_map/feed/pallas_call | solution.py:611
  121.5 3.6 %all-to-all-start.7 = ((bf16[16,4,3072]{2,1,0:T(4,128)(2,1)}), bf16[16,4,3072]{2,1,0:T(4,128)(2,1)S(1)}, u32[]{:S(2)}, u32[]{:S(2)}) async-start(bf16[16,4,3072]{2,1,0:T(4,128)(2,1)} %get-tuple-element.92), calls=%async_computation.7 | async-start | bytes 786432 | tf_op jit(solution)/shard_map/all_to_all | solution.py:797
  125.1 0.6 and_select_fusion.3.turns
  125.7 4.6 %collective-permute-done.15.refs_1_ = bf16[8,128,256]{2,1,0:T(8,128)(2,1)} collective-permute-done((bf16[8,128,256]{2,1,0:T(8,128)(2,1)S(1)}, bf16[8,128,256]{2,1,0:T(8,128)(2,1)}, u32[]{:S(2)}, u32[]{:S(2)}) %collective-permute-start.15) | collective-permute-done | bytes 524320 | tf_op jit(solution)/shard_map/ppermute | solution.py:712
  130.3 2.5 %pick.1 = f32[4,128,256]{2,1,0:T(8,128)} custom-call(s32[4]{0:T(128)} %and_select_fusion.3.turns, s32[4]{0:T(128)} %get-tuple-element.112.rows, bf16[8,128,256]{2,1,0:T(8,128)(2,1)} %copy-done.6, bf16[8,128,256]{2,1,0:T(8,128)(2,1)} %collective-permute-done.15.refs_1_, bf16[8,128,256]{2,1,0:T(8,128)(2,1)} %collective-permute-done.16.refs_2_, ...), custom_call_target="tpu_custom_call" | custom-call | tf_op jit(solution)/shard_map/pick/pallas_call | solution.py:660
  132.8 0.8 constant_dynamic-slice_fusion
  133.6 1.0 all-to-all-done.7
  134.7 0.6 add_convert_fusion
  (51 shorter events, 1.2 us)
Async XLA Ops:
  0.6 38.0 %copy-start = (s32[32]{0:T(128)S(1)}, s32[32]{0:T(128)}, u32[]{:S(2)}) copy-start(s32[32]{0:T(128)} %param.33) | copy-start | bytes 388
  0.6 26.3 %copy-start.3 = (s32[32]{0:T(128)S(1)}, s32[32]{0:T(128)}, u32[]{:S(2)}) copy-start(s32[32]{0:T(128)} %param.31) | copy-start | bytes 388
  5.0 27.5 %copy-start.1 = (s32[4]{0:T(128)S(1)}, s32[4]{0:T(128)}, u32[]{:S(2)}) copy-start(s32[4]{0:T(128)} %get-tuple-element.69.origin) | copy-start | bytes 52
  5.0 27.5 %all-to-all-start.2 = ((bf16[128,24,128]{2,1,0:T(8,128)(2,1)}), bf16[128,24,128]{2,1,0:T(8,128)(2,1)S(1)}, u32[]{:S(2)}, u32[]{:S(2)}) async-start(bf16[128,24,128]{2,1,0:T(8,128)(2,1)} %get-tuple-element.70), calls=%async_computation.2 | async-start | bytes 1572864 | tf_op jit(solution)/shard_map/all_to_all | solution.py:723
  18.9 53.8 %collective-permute-start.5 = (bf16[144,3072]{1,0:T(8,128)(2,1)}, bf16[144,3072]{1,0:T(8,128)(2,1)}, u32[]{:S(2)}, u32[]{:S(2)}) collective-permute-start(bf16[144,3072]{1,0:T(8,128)(2,1)} %get-tuple-element.81.refs_0_), channel_id=1, source_target_pairs={{0,96},{16,112},{32,0},{48,16},{64,32},{80,48},{96,64},{112,80},{1... | collective-permute-start | bytes 2654216 | tf_op jit(solution)/shard_map/ppermute | solution.py:712
  21.7 44.9 %collective-permute-start = (bf16[144,3072]{1,0:T(8,128)(2,1)}, bf16[144,3072]{1,0:T(8,128)(2,1)}, u32[]{:S(2)}, u32[]{:S(2)}) collective-permute-start(bf16[144,3072]{1,0:T(8,128)(2,1)} %get-tuple-element.81.refs_0_), channel_id=1, source_target_pairs={{0,32},{16,48},{32,64},{48,80},{64,96},{80,112},{96,0},{112,16},{1... | collective-permute-start | bytes 2654216 | tf_op jit(solution)/shard_map/ppermute | solution.py:712
  21.7 50.9 %collective-permute-start.4 = (bf16[144,3072]{1,0:T(8,128)(2,1)}, bf16[144,3072]{1,0:T(8,128)(2,1)}, u32[]{:S(2)}, u32[]{:S(2)}) collective-permute-start(bf16[144,3072]{1,0:T(8,128)(2,1)} %get-tuple-element.82.refs_1_), channel_id=1, source_target_pairs={{0,32},{16,48},{32,64},{48,80},{64,96},{80,112},{96,0},{112,16},{1... | collective-permute-start | bytes 2654216 | tf_op jit(solution)/shard_map/ppermute | solution.py:712
  22.0 44.7 %collective-permute-start.1 = (bf16[144,3072]{1,0:T(8,128)(2,1)}, bf16[144,3072]{1,0:T(8,128)(2,1)}, u32[]{:S(2)}, u32[]{:S(2)}) collective-permute-start(bf16[144,3072]{1,0:T(8,128)(2,1)} %get-tuple-element.82.refs_1_), channel_id=1, source_target_pairs={{0,96},{16,112},{32,0},{48,16},{64,32},{80,48},{96,64},{112,80},{1... | collective-permute-start | bytes 2654216 | tf_op jit(solution)/shard_map/ppermute | solution.py:712
  32.5 1.4 %copy-start.9 = (s32[32,16]{0,1:T(8,128)S(1)}, s32[32,16]{0,1:T(8,128)}, u32[]{:S(2)}) copy-start(s32[32,16]{0,1:T(8,128)} %param.29) | copy-start | bytes 6148
  33.9 5.4 %copy-start.4 = (s32[32]{0:T(128)S(1)}, s32[32]{0:T(128)}, u32[]{:S(2)}) copy-start(s32[32]{0:T(128)} %param.30) | copy-start | bytes 388
  34.4 13.8 %all-to-all-start.3 = ((bf16[16,96,128]{2,1,0:T(8,128)(2,1)}), bf16[16,96,128]{2,1,0:T(8,128)(2,1)S(1)}, u32[]{:S(2)}, u32[]{:S(2)}) async-start(bf16[16,96,128]{2,1,0:T(8,128)(2,1)} %hand.2), calls=%async_computation.3 | async-start | bytes 786432 | tf_op jit(solution)/shard_map/all_to_all | solution.py:727
  48.2 0.7 copy-start.8
  56.2 13.8 %all-to-all-start.4 = ((bf16[16,4,896]{2,1,0:T(4,128)(2,1)}), bf16[16,4,896]{2,1,0:T(4,128)(2,1)S(1)}, u32[]{:S(2)}, u32[]{:S(2)}) async-start(bf16[16,4,896]{2,1,0:T(4,128)(2,1)} %get-tuple-element.77), calls=%async_computation.4 | async-start | bytes 229376 | tf_op jit(solution)/shard_map/all_to_all | solution.py:766
  66.7 13.2 %copy-start.10 = (bf16[4,1,128,256]{3,2,1,0:T(8,128)(2,1)S(1)}, bf16[4,1,128,256]{3,2,1,0:T(8,128)(2,1)}, u32[]{:S(2)}) copy-start(bf16[4,1,128,256]{3,2,1,0:T(8,128)(2,1)} %get-tuple-element.80) | copy-start | bytes 786436
  66.7 21.9 %collective-permute-start.2 = (bf16[144,3072]{1,0:T(8,128)(2,1)}, bf16[144,3072]{1,0:T(8,128)(2,1)}, u32[]{:S(2)}, u32[]{:S(2)}) collective-permute-start(bf16[144,3072]{1,0:T(8,128)(2,1)} %collective-permute-done.refs_2_), channel_id=1, source_target_pairs={{0,32},{16,48},{32,64},{48,80},{64,96},{80,112},{96,0},{112,16},{1... | collective-permute-start | bytes 2654216 | tf_op jit(solution)/shard_map/ppermute | solution.py:712
  67.6 21.6 %collective-permute-start.3 = (bf16[144,3072]{1,0:T(8,128)(2,1)}, bf16[144,3072]{1,0:T(8,128)(2,1)}, u32[]{:S(2)}, u32[]{:S(2)}) collective-permute-start(bf16[144,3072]{1,0:T(8,128)(2,1)} %collective-permute-done.1.refs_3_), channel_id=1, source_target_pairs={{0,96},{16,112},{32,0},{48,16},{64,32},{80,48},{96,64},{112,80},{1... | collective-permute-start | bytes 2654216 | tf_op jit(solution)/shard_map/ppermute | solution.py:712
  70.0 0.6 copy-start.11
  72.7 19.0 %collective-permute-start.7 = (bf16[144,3072]{1,0:T(8,128)(2,1)}, bf16[144,3072]{1,0:T(8,128)(2,1)}, u32[]{:S(2)}, u32[]{:S(2)}) collective-permute-start(bf16[144,3072]{1,0:T(8,128)(2,1)} %get-tuple-element.81.refs_0_), channel_id=1, source_target_pairs={{0,16},{16,0},{32,48},{48,32},{64,80},{80,64},{96,112},{112,96},{1... | collective-permute-start | bytes 2654216 | tf_op jit(solution)/shard_map/ppermute | solution.py:717
  72.8 18.9 %all-to-all-start.5 = ((bf16[16,120,128]{2,1,0:T(8,128)(2,1)}), bf16[16,120,128]{2,1,0:T(8,128)(2,1)}, u32[]{:S(2)}, u32[]{:S(2)}) async-start(bf16[16,120,128]{2,1,0:T(8,128)(2,1)} %join.1), calls=%async_computation.5 | async-start | bytes 983040 | tf_op jit(solution)/shard_map/all_to_all | solution.py:783
  79.8 1.6 %collective-permute-start.6 = (bf16[4,128,256]{2,1,0:T(8,128)(2,1)S(1)}, bf16[4,128,256]{2,1,0:T(8,128)(2,1)S(1)}, u32[]{:S(2)}, u32[]{:S(2)}) collective-permute-start(bf16[4,128,256]{2,1,0:T(8,128)(2,1)S(1)} %bitcast.28), channel_id=1, source_target_pairs={{0,16},{16,0},{32,48},{48,32},{64,80},{80,64},{96,112},{112,96},{1... | collective-permute-start | bytes 786440 | tf_op jit(solution)/shard_map/ppermute | solution.py:717
  80.1 13.9 %collective-permute-start.8 = (bf16[144,3072]{1,0:T(8,128)(2,1)}, bf16[144,3072]{1,0:T(8,128)(2,1)}, u32[]{:S(2)}, u32[]{:S(2)}) collective-permute-start(bf16[144,3072]{1,0:T(8,128)(2,1)} %get-tuple-element.82.refs_1_), channel_id=1, source_target_pairs={{0,16},{16,0},{32,48},{48,32},{64,80},{80,64},{96,112},{112,96},{1... | collective-permute-start | bytes 2654216 | tf_op jit(solution)/shard_map/ppermute | solution.py:717
  81.4 12.5 %collective-permute-start.9 = (bf16[144,3072]{1,0:T(8,128)(2,1)}, bf16[144,3072]{1,0:T(8,128)(2,1)}, u32[]{:S(2)}, u32[]{:S(2)}) collective-permute-start(bf16[144,3072]{1,0:T(8,128)(2,1)} %collective-permute-done.refs_2_), channel_id=1, source_target_pairs={{0,16},{16,0},{32,48},{48,32},{64,80},{80,64},{96,112},{112,96},{1... | collective-permute-start | bytes 2654216 | tf_op jit(solution)/shard_map/ppermute | solution.py:717
  81.7 22.6 %copy-start.6 = (bf16[8,128,256]{2,1,0:T(8,128)(2,1)}, bf16[8,128,256]{2,1,0:T(8,128)(2,1)S(1)}, u32[]{:S(2)}) copy-start(bf16[8,128,256]{2,1,0:T(8,128)(2,1)S(1)} %pad_maximum_fusion.refs_0_) | copy-start | bytes 1572868
  88.6 5.4 %collective-permute-start.10 = (bf16[144,3072]{1,0:T(8,128)(2,1)}, bf16[144,3072]{1,0:T(8,128)(2,1)}, u32[]{:S(2)}, u32[]{:S(2)}) collective-permute-start(bf16[144,3072]{1,0:T(8,128)(2,1)} %collective-permute-done.1.refs_3_), channel_id=1, source_target_pairs={{0,16},{16,0},{32,48},{48,32},{64,80},{80,64},{96,112},{112,96},{1... | collective-permute-start | bytes 2654216 | tf_op jit(solution)/shard_map/ppermute | solution.py:717
  89.2 4.8 %collective-permute-start.11 = (bf16[144,3072]{1,0:T(8,128)(2,1)}, bf16[144,3072]{1,0:T(8,128)(2,1)}, u32[]{:S(2)}, u32[]{:S(2)}) collective-permute-start(bf16[144,3072]{1,0:T(8,128)(2,1)} %collective-permute-done.4.refs_4_), channel_id=1, source_target_pairs={{0,16},{16,0},{32,48},{48,32},{64,80},{80,64},{96,112},{112,96},{1... | collective-permute-start | bytes 2654216 | tf_op jit(solution)/shard_map/ppermute | solution.py:717
  91.7 2.8 %collective-permute-start.12 = (bf16[144,3072]{1,0:T(8,128)(2,1)}, bf16[144,3072]{1,0:T(8,128)(2,1)}, u32[]{:S(2)}, u32[]{:S(2)}) collective-permute-start(bf16[144,3072]{1,0:T(8,128)(2,1)} %collective-permute-done.5.refs_5_), channel_id=1, source_target_pairs={{0,16},{16,0},{32,48},{48,32},{64,80},{80,64},{96,112},{112,96},{1... | collective-permute-start | bytes 2654216 | tf_op jit(solution)/shard_map/ppermute | solution.py:717
  91.7 3.3 %copy-start.12 = (s32[32]{0:T(128)S(1)}, s32[32]{0:T(128)}, u32[]{:S(2)}) copy-start(s32[32]{0:T(128)} %param.32) | copy-start | bytes 388
  94.5 17.2 %collective-permute-start.13 = (bf16[144,3072]{1,0:T(8,128)(2,1)}, bf16[144,3072]{1,0:T(8,128)(2,1)}, u32[]{:S(2)}, u32[]{:S(2)}) collective-permute-start(bf16[144,3072]{1,0:T(8,128)(2,1)} %collective-permute-done.2.refs_12_), channel_id=1, source_target_pairs={{0,16},{16,0},{32,48},{48,32},{64,80},{80,64},{96,112},{112,96},{1... | collective-permute-start | bytes 2654216 | tf_op jit(solution)/shard_map/ppermute | solution.py:717
  94.6 17.0 %collective-permute-start.14 = (bf16[144,3072]{1,0:T(8,128)(2,1)}, bf16[144,3072]{1,0:T(8,128)(2,1)}, u32[]{:S(2)}, u32[]{:S(2)}) collective-permute-start(bf16[144,3072]{1,0:T(8,128)(2,1)} %collective-permute-done.3.refs_13_), channel_id=1, source_target_pairs={{0,16},{16,0},{32,48},{48,32},{64,80},{80,64},{96,112},{112,96},{1... | collective-permute-start | bytes 2654216 | tf_op jit(solution)/shard_map/ppermute | solution.py:717
  95.1 16.5 %all-to-all-start.6 = ((bf16[16,96,128]{2,1,0:T(8,128)(2,1)}), bf16[16,96,128]{2,1,0:T(8,128)(2,1)S(1)}, u32[]{:S(2)}, u32[]{:S(2)}) async-start(bf16[16,96,128]{2,1,0:T(8,128)(2,1)} %project.1), calls=%async_computation.6 | async-start | bytes 786432 | tf_op jit(solution)/shard_map/all_to_all | solution.py:794
  102.6 23.0 %collective-permute-start.17 = (bf16[8,128,256]{2,1,0:T(8,128)(2,1)S(1)}, bf16[8,128,256]{2,1,0:T(8,128)(2,1)}, u32[]{:S(2)}, u32[]{:S(2)}) collective-permute-start(bf16[8,128,256]{2,1,0:T(8,128)(2,1)S(1)} %pad_maximum_fusion.refs_0_), channel_id=1, source_target_pairs={{0,96},{16,112},{32,0},{48,16},{64,32},{80,48},{96,64},{112,80},{1... | collective-permute-start | bytes 1572872 | tf_op jit(solution)/shard_map/ppermute | solution.py:712
  104.3 21.3 %collective-permute-start.16 = (bf16[8,128,256]{2,1,0:T(8,128)(2,1)S(1)}, bf16[8,128,256]{2,1,0:T(8,128)(2,1)}, u32[]{:S(2)}, u32[]{:S(2)}) collective-permute-start(bf16[8,128,256]{2,1,0:T(8,128)(2,1)S(1)} %pad_maximum_fusion.refs_0_), channel_id=1, source_target_pairs={{0,64},{16,80},{32,96},{48,112},{64,0},{80,16},{96,32},{112,48},{1... | collective-permute-start | bytes 1572872 | tf_op jit(solution)/shard_map/ppermute | solution.py:712
  104.3 26.0 %collective-permute-start.15 = (bf16[8,128,256]{2,1,0:T(8,128)(2,1)S(1)}, bf16[8,128,256]{2,1,0:T(8,128)(2,1)}, u32[]{:S(2)}, u32[]{:S(2)}) collective-permute-start(bf16[8,128,256]{2,1,0:T(8,128)(2,1)S(1)} %pad_maximum_fusion.refs_0_), channel_id=1, source_target_pairs={{0,32},{16,48},{32,64},{48,80},{64,96},{80,112},{96,0},{112,16},{1... | collective-permute-start | bytes 1572872 | tf_op jit(solution)/shard_map/ppermute | solution.py:712
  111.6 0.7 copy-start.7
  121.5 13.1 %all-to-all-start.7 = ((bf16[16,4,3072]{2,1,0:T(4,128)(2,1)}), bf16[16,4,3072]{2,1,0:T(4,128)(2,1)S(1)}, u32[]{:S(2)}, u32[]{:S(2)}) async-start(bf16[16,4,3072]{2,1,0:T(4,128)(2,1)} %get-tuple-element.92), calls=%async_computation.7 | async-start | bytes 786432 | tf_op jit(solution)/shard_map/all_to_all | solution.py:797

commit v10 on v9

--- a/solution.py
+++ b/solution.py
@@ -5,6 +5,7 @@
 from jax import lax
 from jax.experimental import pallas as pl
 from jax.experimental.pallas import tpu as pltpu
+from jax.sharding import Mesh
 from jax.sharding import PartitionSpec as P
 
 BF = jnp.bfloat16
@@ -39,6 +40,8 @@
 
 
 HI = lax.Precision.HIGHEST
+REQ = ("z", "core")
+CORES = 2
 
 
 def cost(flops, moved, special=0):
@@ -70,7 +73,7 @@
 
 
 def fetch_kernel(
-    turn, slots_row, ids_cols, table_far, payload, places, origin, most, table, sem, *, groups, members
+    turn, slots_row, ids_cols, table_far, keep, give, places, origin, most, table, sem, *, groups, members
 ):
     load = pltpu.make_async_copy(table_far, table, sem)
     load.start()
@@ -78,7 +81,8 @@
     vocab = table.shape[0]
     count = requests * drafts // groups
     slots = requests // groups
-    group = lax.axis_index("req")
+    core = lax.axis_index("core")
+    group = lax.axis_index("z") * CORES + core
     member = lax.axis_index("tok")
     me = group * members + member
     now = turn[0]
@@ -99,7 +103,9 @@
     own_place = jnp.zeros((count, 1), jnp.int32)
     own_from = [jnp.zeros((1, count), jnp.int32)] * own
     peak = jnp.zeros((1, count), jnp.int32)
-    for g in range(groups):
+    for n in range(groups):
+        chips = groups // CORES
+        g = (n % chips) * CORES + (core if n < chips else 1 - core)
         pick = jnp.where(slots_row[...] == row_slot + g * slots, 1.0, 0.0).astype(BF)
         mixed_ids = dot_nt(pick, ids_hi) * 256.0 + dot_nt(pick, ids_lo)
         id_c = jnp.sum(
@@ -111,14 +117,16 @@
         first_r = jnp.min(jnp.where(same, sub, count), axis=0, keepdims=True)
         owner_c = id_c // vocab
         owner_r = id_r // vocab
-        alike = owner_c == owner_r
+        chip_c = (owner_c // (CORES * members)) * members + owner_c % members
+        chip_r = (owner_r // (CORES * members)) * members + owner_r % members
+        alike = chip_c == chip_r
         before_r = (first_c == sub_c) & alike & (sub < first_r)
-        less_r = (first_c == sub_c) & (owner_c < owner_r)
+        less_r = (first_c == sub_c) & (chip_c < chip_r)
         nth_r = jnp.sum(jnp.where(before_r, 1, 0), axis=0, keepdims=True)
         rank_r = nth_r + jnp.sum(jnp.where(less_r, 1, 0), axis=0, keepdims=True)
         peak = jnp.maximum(peak, nth_r // members + 1)
         before_c = (first_r == lane_r) & alike & (lane < first_c)
-        less_c = (first_r == lane_r) & (owner_r < owner_c)
+        less_c = (first_r == lane_r) & (chip_r < chip_c)
         nth_c = jnp.sum(jnp.where(before_c, 1, 0), axis=1, keepdims=True)
         rank_c = nth_c + jnp.sum(jnp.where(less_c, 1, 0), axis=1, keepdims=True)
         spot = (rank_c % members) * own + rank_c // members
@@ -130,20 +138,24 @@
         hots.append(jnp.where(local_iota == row, 1.0, 0.0))
         for k in range(own):
             here = sent_r & (rank_r == k * members + member) & (group == g)
-            own_from[k] = own_from[k] + jnp.where(here, owner_r + 1, 0)
+            own_from[k] = own_from[k] + jnp.where(here, chip_r + 1, 0)
     places[...] = jnp.broadcast_to(own_place, places.shape)
     for k in range(own):
         origin[k] = jnp.sum(own_from[k]) - 1
     most[0] = jnp.max(peak)
     hot = jnp.concatenate(hots, axis=0).astype(BF)
     load.wait()
-    payload[...] = dot_nn(hot, table[...]).reshape(payload.shape).astype(BF)
+    peers = keep.shape[0]
+    keep[...] = dot_nn(hot[:peers], table[...]).reshape(keep.shape).astype(BF)
+    give[...] = dot_nn(hot[peers:], table[...]).reshape(give.shape).astype(BF)
 
 
 def fetch(turn, slots_row, ids_cols, table, groups, members):
     count = ids_cols.size // groups
+    rows = jax.ShapeDtypeStruct((groups // CORES * members, table.shape[1] // AUX, AUX), BF)
     outs = [
-        jax.ShapeDtypeStruct((groups * members, table.shape[1] // AUX, AUX), BF),
+        rows,
+        rows,
         jax.ShapeDtypeStruct((count, AUX), jnp.int32),
         jax.ShapeDtypeStruct((count // members,), jnp.int32),
         jax.ShapeDtypeStruct((1,), jnp.int32),
@@ -152,7 +164,7 @@
         functools.partial(fetch_kernel, groups=groups, members=members),
         grid=(1,),
         in_specs=scalars(1) + whole([slots_row, ids_cols]) + streamed(1),
-        out_specs=whole(outs[:2]) + scalars(2),
+        out_specs=whole(outs[:3]) + scalars(2),
         out_shape=outs,
         scratch_shapes=[pltpu.VMEM(table.shape, table.dtype), pltpu.SemaphoreType.DMA],
         compiler_params=PARAMS,
@@ -696,8 +708,8 @@
     down_weight,
 ):
     members = lax.axis_size("tok")
-    groups = lax.axis_size("req")
-    group_index = lax.axis_index("req")
+    groups = lax.axis_size(REQ)
+    group_index = lax.axis_index(REQ)
     member = lax.axis_index("tok")
     slots_dev, cache_dev, head_size = key_cache.shape
     draft_len = draft_ids.shape[1]
@@ -705,22 +717,22 @@
     query_heads = query_weight.shape[1] // head_size
     own = slots_dev * draft_len // members
 
-    cores = 2
+    cores = CORES
     chips = groups // cores
 
     def turn(value, by):
         return lax.ppermute(
-            value, "req", [(g, (g + by * cores) % groups) for g in range(groups)]
+            value, REQ, [(g, (g + by * cores) % groups) for g in range(groups)]
         )
 
     def across(value):
-        return lax.ppermute(value, "req", [(g, g ^ 1) for g in range(groups)])
+        return lax.ppermute(value, REQ, [(g, g ^ 1) for g in range(groups)])
 
     def exchange(turn):
-        sent, places, origin, most = fetch(
+        keep, give, places, origin, most = fetch(
             turn, current_slot[None], draft_ids.T, embed_table, groups, members
         )
-        came = lax.all_to_all(sent, ("req", "tok"), 0, 0, tiled=True)
+        came = lax.all_to_all(keep + across(give), ("z", "tok"), 0, 0, tiled=True)
         return came, places, origin, most
 
     def plane(rows):
@@ -811,6 +823,9 @@
 
 
 def solution(mesh):
+    groups, members = mesh.devices.shape
+    devices = mesh.devices.reshape(groups // CORES, CORES, members)
+    mesh = Mesh(devices, ("z", "core", "tok"))
     return jax.shard_map(
         local,
         mesh=mesh,
@@ -820,12 +835,12 @@
             P(),
             P(),
             P(),
-            P(("req", "tok"), None),
-            P(),
-            P(),
-            P(),
-            P("req", "tok", None),
-            P("req", "tok", None),
+            P(("z", "core", "tok"), None),
+            P(),
+            P(),
+            P(),
+            P(REQ, "tok", None),
+            P(REQ, "tok", None),
             P(None, "tok"),
             P(None, "tok"),
             P(None, "tok"),
@@ -834,13 +849,13 @@
             P("tok"),
             P("tok"),
             P("tok"),
-            P("req", "tok", None, None),
+            P(REQ, "tok", None, None),
             P("tok", None),
             P(),
-            P(None, ("req", "tok")),
-            P(None, ("req", "tok")),
-            P(None, ("req", "tok")),
+            P(None, ("z", "core", "tok")),
+            P(None, ("z", "core", "tok")),
+            P(None, ("z", "core", "tok")),
         ),
-        out_specs=(P(("req", "tok"), None), P("req", "tok", None, None)),
+        out_specs=(P(("z", "core", "tok"), None), P(REQ, "tok", None, None)),
         check_vma=False,
     )

time: 136 us -> 137 us (level)
  waiting for transfers between devices: 36.4 us -> 32.9 us
  starting transfers between devices: 48.5 us -> 50.5 us
  other arithmetic: 3.82 us -> 5.64 us
    all_to_all x1, waiting for transfers between devices: 5.28 us -> 1.08 us  [exchange(): came = lax.all_to_all(keep + across(give), ('z', 'tok'), 0, 0, tiled=True)]
    all_to_all x1, starting transfers between devices: 3.57 us -> 5.79 us  [plane(): return lax.all_to_all(rows, 'tok', 0, 0, tiled=True)]
    add x0 -> x1, other arithmetic: none -> 1.85 us  [exchange(): came = lax.all_to_all(keep + across(give), ('z', 'tok'), 0, 0, tiled=True)]
    ppermute x18 -> x19, starting transfers between devices: 13.4 us -> 14 us  [the longest x9 12.1 us: turn(): lax.ppermute(value, REQ, [(g, (g + by * cores) % groups) for g in range(g...]
    ppermute x18 -> x19, waiting for transfers between devices: 13.7 us -> 14.3 us  [the longest x9 10.8 us: turn(): lax.ppermute(value, REQ, [(g, (g + by * cores) % groups) for g in range(g...]
  transfers between devices with their start and end apart: 24 -> 25, of which waited for: 10 -> 11; matrix products, arithmetic and copies ran while one was open for 4% -> 4% of each run, Pallas kernels for 25% -> 25%
where the time goes in v10:
time: 137 us; the launch traced here: 136 us
  starting transfers between devices  50.5 us (37%)
  Pallas kernels  38.9 us (28%)
  waiting for transfers between devices  32.9 us (24%)
  other arithmetic  5.64 us (4%)
  local copies, waits for them, and re-layouts  4.92 us (4%)
  between operations  2.89 us (2%)
    ppermute x9, starting transfers between devices, turn(): lax.ppermute(value, REQ, [(g, (g + by * cores) % groups) for g in range(g...  12.1 us
    all_to_all x1, starting transfers between devices, exchange(): came = lax.all_to_all(keep + across(give), ('z', 'tok'), 0, 0, tiled=True)  11.5 us
    ppermute x9, waiting for transfers between devices, turn(): lax.ppermute(value, REQ, [(g, (g + by * cores) % groups) for g in range(g...  10.8 us
    pallas_call x1, Pallas kernels, feed(): pl.pallas_call(functools.partial(feed_kernel, count=len(weights), units=u...  9.13 us
    pallas_call x1, Pallas kernels, attend(): pl.pallas_call(attend_kernel, grid=(1,), in_specs=scalars(1) + whole([arr...  7.28 us
    all_to_all x1, starting transfers between devices, local(): joined = lax.all_to_all(joint, 'tok', 0, 0, tiled=True)  7.2 us
    all_to_all x1, waiting for transfers between devices, plane(): return lax.all_to_all(rows, 'tok', 0, 0, tiled=True)  6.76 us
    pallas_call x1, Pallas kernels, mamba(): pl.pallas_call(mamba_kernel, grid=(1,), in_specs=scalars(2) + whole([norm...  6.71 us
  transfers between devices with their start and end apart: 25, of which 11 were waited for; matrix products, arithmetic and copies ran while one was open for 4% of the time, Pallas kernels for 25%

profile of v10, /device:TPU:0, one launch (start us, length us, event | category | flops | bytes accessed | tf_op | source)
XLA Modules:
  0.0 136.4 jit_solution(12990750479578294657)
XLA Ops:
  0.7 4.9 %fetch.2 = (bf16[64,24,128]{2,1,0:T(8,128)(2,1)}, bf16[64,24,128]{2,1,0:T(8,128)(2,1)}, s32[64,128]{1,0:T(8,128)}, s32[4]{0:T(128)}, s32[1]{0:T(128)}) custom-call(s32[1]{0:T(128)} %constant.88.clone.1.turn, s32[1,32]{1,0:T(1,128)} %bitcast.20, s32[16,32]{1,0:T(8,128)} %bitcast.26, bf16[512,3072]{1,0:T(8,128)(2,1)} %table_far.1), custom_call_target="tpu_custom_call" | custom-call | flops 402653184 | bytes 3145728 | tf_op jit(solution)/shard_map/fetch/pallas_call | solution.py:163
  5.7 1.9 %collective-permute-done.3 = bf16[64,24,128]{2,1,0:T(8,128)(2,1)S(1)} collective-permute-done((bf16[64,24,128]{2,1,0:T(8,128)(2,1)}, bf16[64,24,128]{2,1,0:T(8,128)(2,1)S(1)}, u32[]{:S(2)}, u32[]{:S(2)}) %collective-permute-start.3) | collective-permute-done | bytes 393248 | tf_op jit(solution)/shard_map/ppermute | solution.py:729
  7.6 1.8 %add.51 = bf16[64,24,128]{2,1,0:T(8,128)(2,1)} add(bf16[64,24,128]{2,1,0:T(8,128)(2,1)} %get-tuple-element.72, bf16[64,24,128]{2,1,0:T(8,128)(2,1)S(1)} %collective-permute-done.3) | non-fusion elementwise | flops 196608 | bytes 1179648 | tf_op jit(solution)/shard_map/add | solution.py:735
  9.4 11.5 %all-to-all-start.2 = ((bf16[64,24,128]{2,1,0:T(8,128)(2,1)}), bf16[64,24,128]{2,1,0:T(8,128)(2,1)S(1)}, u32[]{:S(2)}, u32[]{:S(2)}) async-start(bf16[64,24,128]{2,1,0:T(8,128)(2,1)} %add.51), calls=%async_computation.2 | async-start | bytes 786432 | tf_op jit(solution)/shard_map/all_to_all | solution.py:735
  20.9 2.8 %pack.1 = (bf16[144,3072]{1,0:T(8,128)(2,1)}, bf16[144,3072]{1,0:T(8,128)(2,1)}) custom-call(bf16[96,3072]{1,0:T(8,128)(2,1)} %bitcast.22, bf16[96,3072]{1,0:T(8,128)(2,1)} %bitcast.23, bf16[96,3072]{1,0:T(8,128)(2,1)} %bitcast.24, s32[64,128]{1,0:T(8,128)} %get-tuple-element.68.ready.places), custom_call_target="tpu_custom_call" | custom-call | bytes 1024 | tf_op jit(solution)/shard_map/pack/pallas_call | solution.py:646
  23.7 3.0 %collective-permute-start.7 = (bf16[144,3072]{1,0:T(8,128)(2,1)}, bf16[144,3072]{1,0:T(8,128)(2,1)}, u32[]{:S(2)}, u32[]{:S(2)}) collective-permute-start(bf16[144,3072]{1,0:T(8,128)(2,1)} %get-tuple-element.84.refs_0_), channel_id=1, source_target_pairs={{0,96},{16,112},{32,0},{48,16},{64,32},{80,48},{96,64},{112,80},{1... | collective-permute-start | bytes 2654216 | tf_op jit(solution)/shard_map/ppermute | solution.py:724
  26.7 0.6 collective-permute-start.6
  27.3 2.7 %collective-permute-start.2 = (bf16[144,3072]{1,0:T(8,128)(2,1)}, bf16[144,3072]{1,0:T(8,128)(2,1)}, u32[]{:S(2)}, u32[]{:S(2)}) collective-permute-start(bf16[144,3072]{1,0:T(8,128)(2,1)} %get-tuple-element.85.refs_1_), channel_id=1, source_target_pairs={{0,96},{16,112},{32,0},{48,16},{64,32},{80,48},{96,64},{112,80},{1... | collective-permute-start | bytes 2654216 | tf_op jit(solution)/shard_map/ppermute | solution.py:724
  32.1 1.1 all-to-all-done.2.came
  33.2 1.3 hand.2
  34.6 0.7 while.10
  35.3 5.8 %all-to-all-start.3 = ((bf16[16,96,128]{2,1,0:T(8,128)(2,1)}), bf16[16,96,128]{2,1,0:T(8,128)(2,1)S(1)}, u32[]{:S(2)}, u32[]{:S(2)}) async-start(bf16[16,96,128]{2,1,0:T(8,128)(2,1)} %hand.2), calls=%async_computation.3 | async-start | bytes 786432 | tf_op jit(solution)/shard_map/all_to_all | solution.py:739
  41.1 0.6 pad_maximum_fusion.1.reals
  41.7 0.6 gather_fusion.1
  42.4 0.6 gather_fusion
  43.1 0.6 pad_add_fusion.ints
  43.7 6.8 %all-to-all-done.3.arrived = bf16[16,96,128]{2,1,0:T(8,128)(2,1)S(1)} async-done(((bf16[16,96,128]{2,1,0:T(8,128)(2,1)}), bf16[16,96,128]{2,1,0:T(8,128)(2,1)S(1)}, u32[]{:S(2)}, u32[]{:S(2)}) %all-to-all-start.3) | async-done | bytes 393248 | tf_op jit(solution)/shard_map/all_to_all | solution.py:739
  50.5 0.7 copy-done.8
  51.2 7.3 %attend.1 = (bf16[16,4,896]{2,1,0:T(4,128)(2,1)}, bf16[64,3072]{1,0:T(8,128)(2,1)}, bf16[64,3072]{1,0:T(8,128)(2,1)}) custom-call(s32[9]{0:T(128)} %pad_add_fusion.ints, bf16[16,96,128]{2,1,0:T(8,128)(2,1)} %copy-done.8, s32[64,128]{1,0:T(8,128)} %get-tuple-element.68.ready.places, bf16[64,3072]{1,0:T(8,128)(2,1)S(1)} %get-tuple-element.75.extra, ...), custom_call_target="tpu_custom_call" | custom-call | flops 20000000000 | bytes 1024 | tf_op jit(solution)/shard_map/attend/pallas_call | solution.py:332
  58.5 3.5 %all-to-all-start.4 = ((bf16[16,4,896]{2,1,0:T(4,128)(2,1)}), bf16[16,4,896]{2,1,0:T(4,128)(2,1)S(1)}, u32[]{:S(2)}, u32[]{:S(2)}) async-start(bf16[16,4,896]{2,1,0:T(4,128)(2,1)} %get-tuple-element.80), calls=%async_computation.4 | async-start | bytes 229376 | tf_op jit(solution)/shard_map/all_to_all | solution.py:778
  62.1 6.7 %mamba.1 = (bf16[16,120,128]{2,1,0:T(8,128)(2,1)}, bf16[4,1,128,256]{3,2,1,0:T(8,128)(2,1)}) custom-call(s32[9]{0:T(128)} %pad_add_fusion.ints, f32[3]{0:T(128)} %pad_maximum_fusion.1.reals, bf16[64,3072]{1,0:T(8,128)(2,1)} %get-tuple-element.76.normed, bf16[3072,128]{1,0:T(8,128)(2,1)} %input_weight.1, bf16[3072,128]{1,0:T(8,128)(2,1)} %gate_weight.1, ...), custom_call_target="tpu_custom_call" | custom-call | flops 8000000000 | bytes 1024 | tf_op jit(solution)/shard_map/mamba/pallas_call | solution.py:463
  68.9 3.2 %collective-permute-start.5 = (bf16[144,3072]{1,0:T(8,128)(2,1)}, bf16[144,3072]{1,0:T(8,128)(2,1)}, u32[]{:S(2)}, u32[]{:S(2)}) collective-permute-start(bf16[144,3072]{1,0:T(8,128)(2,1)} %collective-permute-done.2.refs_3_), channel_id=1, source_target_pairs={{0,96},{16,112},{32,0},{48,16},{64,32},{80,48},{96,64},{112,80},{1... | collective-permute-start | bytes 2654216 | tf_op jit(solution)/shard_map/ppermute | solution.py:724
  72.1 0.6 copy-done.11
  72.8 2.0 %join.1 = bf16[16,120,128]{2,1,0:T(8,128)(2,1)} custom-call(bf16[16,4,896]{2,1,0:T(4,128)(2,1)} %copy-done.11, bf16[16,120,128]{2,1,0:T(8,128)(2,1)} %get-tuple-element.77.blocks), custom_call_target="tpu_custom_call", output_to_operand_aliasing={{}: (1, {})} | custom-call | flops 20000000000 | bytes 1024 | tf_op jit(solution)/shard_map/join/pallas_call | solution.py:507
  74.9 7.2 %all-to-all-start.5 = ((bf16[16,120,128]{2,1,0:T(8,128)(2,1)}), bf16[16,120,128]{2,1,0:T(8,128)(2,1)}, u32[]{:S(2)}, u32[]{:S(2)}) async-start(bf16[16,120,128]{2,1,0:T(8,128)(2,1)} %join.1), calls=%async_computation.5 | async-start | bytes 983040 | tf_op jit(solution)/shard_map/all_to_all | solution.py:795
  82.4 0.3 collective-permute-start.10
  82.7 1.0 collective-permute-done.8
  84.0 6.1 %collective-permute-done.4.refs_12_ = bf16[144,3072]{1,0:T(8,128)(2,1)} collective-permute-done((bf16[144,3072]{1,0:T(8,128)(2,1)}, bf16[144,3072]{1,0:T(8,128)(2,1)}, u32[]{:S(2)}, u32[]{:S(2)}) %collective-permute-start.4) | collective-permute-done | bytes 884768 | tf_op jit(solution)/shard_map/ppermute | solution.py:724
  90.2 0.4 collective-permute-start.13
  90.6 3.4 %all-to-all-done.5.parts = bf16[16,120,128]{2,1,0:T(8,128)(2,1)} async-done(((bf16[16,120,128]{2,1,0:T(8,128)(2,1)}), bf16[16,120,128]{2,1,0:T(8,128)(2,1)}, u32[]{:S(2)}, u32[]{:S(2)}) %all-to-all-start.5) | async-done | bytes 491552 | tf_op jit(solution)/shard_map/all_to_all | solution.py:795
  94.0 2.3 %project.1 = bf16[16,96,128]{2,1,0:T(8,128)(2,1)} custom-call(bf16[16,120,128]{2,1,0:T(8,128)(2,1)} %all-to-all-done.5.parts, bf16[192,768]{1,0:T(8,128)(2,1)} %bitcast.30), custom_call_target="tpu_custom_call" | custom-call | flops 20000000000 | bytes 1024 | tf_op jit(solution)/shard_map/project/pallas_call | solution.py:543
  96.3 0.5 collective-permute-done.14.refs_11_
  96.9 0.4 collective-permute-start.16
  97.4 4.9 %all-to-all-start.6 = ((bf16[16,96,128]{2,1,0:T(8,128)(2,1)}), bf16[16,96,128]{2,1,0:T(8,128)(2,1)S(1)}, u32[]{:S(2)}, u32[]{:S(2)}) async-start(bf16[16,96,128]{2,1,0:T(8,128)(2,1)} %project.1), calls=%async_computation.6 | async-start | bytes 786432 | tf_op jit(solution)/shard_map/all_to_all | solution.py:806
  102.4 0.6 gather_fusion.2
  103.0 0.7 fusion
  103.7 1.7 %collective-permute-start.19 = (bf16[8,128,256]{2,1,0:T(8,128)(2,1)S(1)}, bf16[8,128,256]{2,1,0:T(8,128)(2,1)}, u32[]{:S(2)}, u32[]{:S(2)}) collective-permute-start(bf16[8,128,256]{2,1,0:T(8,128)(2,1)S(1)} %pad_maximum_fusion.refs_0_), channel_id=1, source_target_pairs={{0,96},{16,112},{32,0},{48,16},{64,32},{80,48},{96,64},{112,80},{1... | collective-permute-start | bytes 1572872 | tf_op jit(solution)/shard_map/ppermute | solution.py:724
  105.4 0.9 collective-permute-start.17
  106.2 6.4 %all-to-all-done.6.spread = bf16[16,96,128]{2,1,0:T(8,128)(2,1)S(1)} async-done(((bf16[16,96,128]{2,1,0:T(8,128)(2,1)}), bf16[16,96,128]{2,1,0:T(8,128)(2,1)S(1)}, u32[]{:S(2)}, u32[]{:S(2)}) %all-to-all-start.6) | async-done | bytes 393248 | tf_op jit(solution)/shard_map/all_to_all | solution.py:806
  112.7 0.7 copy-done.7
  113.4 9.1 %feed.1 = (bf16[16,4,3072]{2,1,0:T(4,128)(2,1)}, bf16[64,3072]{1,0:T(8,128)(2,1)}) custom-call(bf16[16,96,128]{2,1,0:T(8,128)(2,1)} %copy-done.7, bf16[64,3072]{1,0:T(8,128)(2,1)} %get-tuple-element.91.embedded, f32[1,3072]{1,0:T(1,128)} %bitcast.33, bf16[144,3072]{1,0:T(8,128)(2,1)} %get-tuple-element.84.refs_0_, ...), custom_call_target="tpu_custom_call" | custom-call | flops 20000000000 | bytes 1024 | tf_op jit(solution)/shard_map/feed/pallas_call | solution.py:623
  122.6 3.6 %all-to-all-start.7 = ((bf16[16,4,3072]{2,1,0:T(4,128)(2,1)}), bf16[16,4,3072]{2,1,0:T(4,128)(2,1)S(1)}, u32[]{:S(2)}, u32[]{:S(2)}) async-start(bf16[16,4,3072]{2,1,0:T(4,128)(2,1)} %get-tuple-element.95), calls=%async_computation.7 | async-start | bytes 786432 | tf_op jit(solution)/shard_map/all_to_all | solution.py:809
  126.1 0.5 and_select_fusion.3.turns
  126.7 4.7 %collective-permute-done.17.refs_1_ = bf16[8,128,256]{2,1,0:T(8,128)(2,1)} collective-permute-done((bf16[8,128,256]{2,1,0:T(8,128)(2,1)S(1)}, bf16[8,128,256]{2,1,0:T(8,128)(2,1)}, u32[]{:S(2)}, u32[]{:S(2)}) %collective-permute-start.17) | collective-permute-done | bytes 524320 | tf_op jit(solution)/shard_map/ppermute | solution.py:724
  131.3 2.5 %pick.1 = f32[4,128,256]{2,1,0:T(8,128)} custom-call(s32[4]{0:T(128)} %and_select_fusion.3.turns, s32[4]{0:T(128)} %get-tuple-element.115.rows, bf16[8,128,256]{2,1,0:T(8,128)(2,1)} %copy-done.6, bf16[8,128,256]{2,1,0:T(8,128)(2,1)} %collective-permute-done.17.refs_1_, bf16[8,128,256]{2,1,0:T(8,128)(2,1)} %collective-permute-done.18.refs_2_, ...), custom_call_target="tpu_custom_call" | custom-call | tf_op jit(solution)/shard_map/pick/pallas_call | solution.py:672
  133.8 0.8 constant_dynamic-slice_fusion
  134.7 1.0 all-to-all-done.7
  135.8 0.6 add_convert_fusion
  (54 shorter events, 1.8 us)
Async XLA Ops:
  0.6 41.1 %copy-start = (s32[32]{0:T(128)S(1)}, s32[32]{0:T(128)}, u32[]{:S(2)}) copy-start(s32[32]{0:T(128)} %param.33) | copy-start | bytes 388
  0.6 31.3 %copy-start.3 = (s32[32]{0:T(128)S(1)}, s32[32]{0:T(128)}, u32[]{:S(2)}) copy-start(s32[32]{0:T(128)} %param.31) | copy-start | bytes 388
  5.6 27.7 %copy-start.1 = (s32[4]{0:T(128)S(1)}, s32[4]{0:T(128)}, u32[]{:S(2)}) copy-start(s32[4]{0:T(128)} %get-tuple-element.71.origin) | copy-start | bytes 52
  5.6 2.0 %collective-permute-start.3 = (bf16[64,24,128]{2,1,0:T(8,128)(2,1)}, bf16[64,24,128]{2,1,0:T(8,128)(2,1)S(1)}, u32[]{:S(2)}, u32[]{:S(2)}) collective-permute-start(bf16[64,24,128]{2,1,0:T(8,128)(2,1)} %get-tuple-element.73), channel_id=1, source_target_pairs={{0,16},{16,0},{32,48},{48,32},{64,80},{80,64},{96,112},{112,96},{1... | collective-permute-start | bytes 1179656 | tf_op jit(solution)/shard_map/ppermute | solution.py:729
  9.4 23.8 %all-to-all-start.2 = ((bf16[64,24,128]{2,1,0:T(8,128)(2,1)}), bf16[64,24,128]{2,1,0:T(8,128)(2,1)S(1)}, u32[]{:S(2)}, u32[]{:S(2)}) async-start(bf16[64,24,128]{2,1,0:T(8,128)(2,1)} %add.51), calls=%async_computation.2 | async-start | bytes 786432 | tf_op jit(solution)/shard_map/all_to_all | solution.py:735
  23.7 51.1 %collective-permute-start.7 = (bf16[144,3072]{1,0:T(8,128)(2,1)}, bf16[144,3072]{1,0:T(8,128)(2,1)}, u32[]{:S(2)}, u32[]{:S(2)}) collective-permute-start(bf16[144,3072]{1,0:T(8,128)(2,1)} %get-tuple-element.84.refs_0_), channel_id=1, source_target_pairs={{0,96},{16,112},{32,0},{48,16},{64,32},{80,48},{96,64},{112,80},{1... | collective-permute-start | bytes 2654216 | tf_op jit(solution)/shard_map/ppermute | solution.py:724
  26.7 42.1 %collective-permute-start.1 = (bf16[144,3072]{1,0:T(8,128)(2,1)}, bf16[144,3072]{1,0:T(8,128)(2,1)}, u32[]{:S(2)}, u32[]{:S(2)}) collective-permute-start(bf16[144,3072]{1,0:T(8,128)(2,1)} %get-tuple-element.84.refs_0_), channel_id=1, source_target_pairs={{0,32},{16,48},{32,64},{48,80},{64,96},{80,112},{96,0},{112,16},{1... | collective-permute-start | bytes 2654216 | tf_op jit(solution)/shard_map/ppermute | solution.py:724
  26.7 48.1 %collective-permute-start.6 = (bf16[144,3072]{1,0:T(8,128)(2,1)}, bf16[144,3072]{1,0:T(8,128)(2,1)}, u32[]{:S(2)}, u32[]{:S(2)}) collective-permute-start(bf16[144,3072]{1,0:T(8,128)(2,1)} %get-tuple-element.85.refs_1_), channel_id=1, source_target_pairs={{0,32},{16,48},{32,64},{48,80},{64,96},{80,112},{96,0},{112,16},{1... | collective-permute-start | bytes 2654216 | tf_op jit(solution)/shard_map/ppermute | solution.py:724
  27.3 41.5 %collective-permute-start.2 = (bf16[144,3072]{1,0:T(8,128)(2,1)}, bf16[144,3072]{1,0:T(8,128)(2,1)}, u32[]{:S(2)}, u32[]{:S(2)}) collective-permute-start(bf16[144,3072]{1,0:T(8,128)(2,1)} %get-tuple-element.85.refs_1_), channel_id=1, source_target_pairs={{0,96},{16,112},{32,0},{48,16},{64,32},{80,48},{96,64},{112,80},{1... | collective-permute-start | bytes 2654216 | tf_op jit(solution)/shard_map/ppermute | solution.py:724
  33.2 1.4 %copy-start.9 = (s32[32,16]{0,1:T(8,128)S(1)}, s32[32,16]{0,1:T(8,128)}, u32[]{:S(2)}) copy-start(s32[32,16]{0,1:T(8,128)} %param.29) | copy-start | bytes 6148
  34.6 7.8 %copy-start.4 = (s32[32]{0:T(128)S(1)}, s32[32]{0:T(128)}, u32[]{:S(2)}) copy-start(s32[32]{0:T(128)} %param.30) | copy-start | bytes 388
  35.3 15.2 %all-to-all-start.3 = ((bf16[16,96,128]{2,1,0:T(8,128)(2,1)}), bf16[16,96,128]{2,1,0:T(8,128)(2,1)S(1)}, u32[]{:S(2)}, u32[]{:S(2)}) async-start(bf16[16,96,128]{2,1,0:T(8,128)(2,1)} %hand.2), calls=%async_computation.3 | async-start | bytes 786432 | tf_op jit(solution)/shard_map/all_to_all | solution.py:739
  50.5 0.7 copy-start.8
  58.5 13.6 %all-to-all-start.4 = ((bf16[16,4,896]{2,1,0:T(4,128)(2,1)}), bf16[16,4,896]{2,1,0:T(4,128)(2,1)S(1)}, u32[]{:S(2)}, u32[]{:S(2)}) async-start(bf16[16,4,896]{2,1,0:T(4,128)(2,1)} %get-tuple-element.80), calls=%async_computation.4 | async-start | bytes 229376 | tf_op jit(solution)/shard_map/all_to_all | solution.py:778
  68.8 13.4 %copy-start.10 = (bf16[4,1,128,256]{3,2,1,0:T(8,128)(2,1)S(1)}, bf16[4,1,128,256]{3,2,1,0:T(8,128)(2,1)}, u32[]{:S(2)}) copy-start(bf16[4,1,128,256]{3,2,1,0:T(8,128)(2,1)} %get-tuple-element.83) | copy-start | bytes 786436
  68.8 21.3 %collective-permute-start.4 = (bf16[144,3072]{1,0:T(8,128)(2,1)}, bf16[144,3072]{1,0:T(8,128)(2,1)}, u32[]{:S(2)}, u32[]{:S(2)}) collective-permute-start(bf16[144,3072]{1,0:T(8,128)(2,1)} %collective-permute-done.1.refs_2_), channel_id=1, source_target_pairs={{0,32},{16,48},{32,64},{48,80},{64,96},{80,112},{96,0},{112,16},{1... | collective-permute-start | bytes 2654216 | tf_op jit(solution)/shard_map/ppermute | solution.py:724
  68.9 21.3 %collective-permute-start.5 = (bf16[144,3072]{1,0:T(8,128)(2,1)}, bf16[144,3072]{1,0:T(8,128)(2,1)}, u32[]{:S(2)}, u32[]{:S(2)}) collective-permute-start(bf16[144,3072]{1,0:T(8,128)(2,1)} %collective-permute-done.2.refs_3_), channel_id=1, source_target_pairs={{0,96},{16,112},{32,0},{48,16},{64,32},{80,48},{96,64},{112,80},{1... | collective-permute-start | bytes 2654216 | tf_op jit(solution)/shard_map/ppermute | solution.py:724
  72.1 0.6 copy-start.11
  74.8 19.2 %collective-permute-start.9 = (bf16[144,3072]{1,0:T(8,128)(2,1)}, bf16[144,3072]{1,0:T(8,128)(2,1)}, u32[]{:S(2)}, u32[]{:S(2)}) collective-permute-start(bf16[144,3072]{1,0:T(8,128)(2,1)} %get-tuple-element.84.refs_0_), channel_id=1, source_target_pairs={{0,16},{16,0},{32,48},{48,32},{64,80},{80,64},{96,112},{112,96},{1... | collective-permute-start | bytes 2654216 | tf_op jit(solution)/shard_map/ppermute | solution.py:729
  74.9 19.1 %all-to-all-start.5 = ((bf16[16,120,128]{2,1,0:T(8,128)(2,1)}), bf16[16,120,128]{2,1,0:T(8,128)(2,1)}, u32[]{:S(2)}, u32[]{:S(2)}) async-start(bf16[16,120,128]{2,1,0:T(8,128)(2,1)} %join.1), calls=%async_computation.5 | async-start | bytes 983040 | tf_op jit(solution)/shard_map/all_to_all | solution.py:795
  82.1 1.6 %collective-permute-start.8 = (bf16[4,128,256]{2,1,0:T(8,128)(2,1)S(1)}, bf16[4,128,256]{2,1,0:T(8,128)(2,1)S(1)}, u32[]{:S(2)}, u32[]{:S(2)}) collective-permute-start(bf16[4,128,256]{2,1,0:T(8,128)(2,1)S(1)} %bitcast.28), channel_id=1, source_target_pairs={{0,16},{16,0},{32,48},{48,32},{64,80},{80,64},{96,112},{112,96},{1... | collective-permute-start | bytes 786440 | tf_op jit(solution)/shard_map/ppermute | solution.py:729
  82.4 13.9 %collective-permute-start.10 = (bf16[144,3072]{1,0:T(8,128)(2,1)}, bf16[144,3072]{1,0:T(8,128)(2,1)}, u32[]{:S(2)}, u32[]{:S(2)}) collective-permute-start(bf16[144,3072]{1,0:T(8,128)(2,1)} %get-tuple-element.85.refs_1_), channel_id=1, source_target_pairs={{0,16},{16,0},{32,48},{48,32},{64,80},{80,64},{96,112},{112,96},{1... | collective-permute-start | bytes 2654216 | tf_op jit(solution)/shard_map/ppermute | solution.py:729
  83.7 12.5 %collective-permute-start.11 = (bf16[144,3072]{1,0:T(8,128)(2,1)}, bf16[144,3072]{1,0:T(8,128)(2,1)}, u32[]{:S(2)}, u32[]{:S(2)}) collective-permute-start(bf16[144,3072]{1,0:T(8,128)(2,1)} %collective-permute-done.1.refs_2_), channel_id=1, source_target_pairs={{0,16},{16,0},{32,48},{48,32},{64,80},{80,64},{96,112},{112,96},{1... | collective-permute-start | bytes 2654216 | tf_op jit(solution)/shard_map/ppermute | solution.py:729
  84.0 21.4 %copy-start.6 = (bf16[8,128,256]{2,1,0:T(8,128)(2,1)}, bf16[8,128,256]{2,1,0:T(8,128)(2,1)S(1)}, u32[]{:S(2)}) copy-start(bf16[8,128,256]{2,1,0:T(8,128)(2,1)S(1)} %pad_maximum_fusion.refs_0_) | copy-start | bytes 1572868
  90.1 6.2 %collective-permute-start.12 = (bf16[144,3072]{1,0:T(8,128)(2,1)}, bf16[144,3072]{1,0:T(8,128)(2,1)}, u32[]{:S(2)}, u32[]{:S(2)}) collective-permute-start(bf16[144,3072]{1,0:T(8,128)(2,1)} %collective-permute-done.2.refs_3_), channel_id=1, source_target_pairs={{0,16},{16,0},{32,48},{48,32},{64,80},{80,64},{96,112},{112,96},{1... | collective-permute-start | bytes 2654216 | tf_op jit(solution)/shard_map/ppermute | solution.py:729
  90.2 6.1 %collective-permute-start.13 = (bf16[144,3072]{1,0:T(8,128)(2,1)}, bf16[144,3072]{1,0:T(8,128)(2,1)}, u32[]{:S(2)}, u32[]{:S(2)}) collective-permute-start(bf16[144,3072]{1,0:T(8,128)(2,1)} %collective-permute-done.6.refs_4_), channel_id=1, source_target_pairs={{0,16},{16,0},{32,48},{48,32},{64,80},{80,64},{96,112},{112,96},{1... | collective-permute-start | bytes 2654216 | tf_op jit(solution)/shard_map/ppermute | solution.py:729
  94.0 2.8 %collective-permute-start.14 = (bf16[144,3072]{1,0:T(8,128)(2,1)}, bf16[144,3072]{1,0:T(8,128)(2,1)}, u32[]{:S(2)}, u32[]{:S(2)}) collective-permute-start(bf16[144,3072]{1,0:T(8,128)(2,1)} %collective-permute-done.7.refs_5_), channel_id=1, source_target_pairs={{0,16},{16,0},{32,48},{48,32},{64,80},{80,64},{96,112},{112,96},{1... | collective-permute-start | bytes 2654216 | tf_op jit(solution)/shard_map/ppermute | solution.py:729
  94.0 3.3 %copy-start.12 = (s32[32]{0:T(128)S(1)}, s32[32]{0:T(128)}, u32[]{:S(2)}) copy-start(s32[32]{0:T(128)} %param.32) | copy-start | bytes 388
  96.8 15.9 %collective-permute-start.15 = (bf16[144,3072]{1,0:T(8,128)(2,1)}, bf16[144,3072]{1,0:T(8,128)(2,1)}, u32[]{:S(2)}, u32[]{:S(2)}) collective-permute-start(bf16[144,3072]{1,0:T(8,128)(2,1)} %collective-permute-done.4.refs_12_), channel_id=1, source_target_pairs={{0,16},{16,0},{32,48},{48,32},{64,80},{80,64},{96,112},{112,96},{1... | collective-permute-start | bytes 2654216 | tf_op jit(solution)/shard_map/ppermute | solution.py:729
  96.9 15.8 %collective-permute-start.16 = (bf16[144,3072]{1,0:T(8,128)(2,1)}, bf16[144,3072]{1,0:T(8,128)(2,1)}, u32[]{:S(2)}, u32[]{:S(2)}) collective-permute-start(bf16[144,3072]{1,0:T(8,128)(2,1)} %collective-permute-done.5.refs_13_), channel_id=1, source_target_pairs={{0,16},{16,0},{32,48},{48,32},{64,80},{80,64},{96,112},{112,96},{1... | collective-permute-start | bytes 2654216 | tf_op jit(solution)/shard_map/ppermute | solution.py:729
  97.4 15.3 %all-to-all-start.6 = ((bf16[16,96,128]{2,1,0:T(8,128)(2,1)}), bf16[16,96,128]{2,1,0:T(8,128)(2,1)S(1)}, u32[]{:S(2)}, u32[]{:S(2)}) async-start(bf16[16,96,128]{2,1,0:T(8,128)(2,1)} %project.1), calls=%async_computation.6 | async-start | bytes 786432 | tf_op jit(solution)/shard_map/all_to_all | solution.py:806
  103.7 23.0 %collective-permute-start.19 = (bf16[8,128,256]{2,1,0:T(8,128)(2,1)S(1)}, bf16[8,128,256]{2,1,0:T(8,128)(2,1)}, u32[]{:S(2)}, u32[]{:S(2)}) collective-permute-start(bf16[8,128,256]{2,1,0:T(8,128)(2,1)S(1)} %pad_maximum_fusion.refs_0_), channel_id=1, source_target_pairs={{0,96},{16,112},{32,0},{48,16},{64,32},{80,48},{96,64},{112,80},{1... | collective-permute-start | bytes 1572872 | tf_op jit(solution)/shard_map/ppermute | solution.py:724
  105.4 21.3 %collective-permute-start.18 = (bf16[8,128,256]{2,1,0:T(8,128)(2,1)S(1)}, bf16[8,128,256]{2,1,0:T(8,128)(2,1)}, u32[]{:S(2)}, u32[]{:S(2)}) collective-permute-start(bf16[8,128,256]{2,1,0:T(8,128)(2,1)S(1)} %pad_maximum_fusion.refs_0_), channel_id=1, source_target_pairs={{0,64},{16,80},{32,96},{48,112},{64,0},{80,16},{96,32},{112,48},{1... | collective-permute-start | bytes 1572872 | tf_op jit(solution)/shard_map/ppermute | solution.py:724
  105.4 26.0 %collective-permute-start.17 = (bf16[8,128,256]{2,1,0:T(8,128)(2,1)S(1)}, bf16[8,128,256]{2,1,0:T(8,128)(2,1)}, u32[]{:S(2)}, u32[]{:S(2)}) collective-permute-start(bf16[8,128,256]{2,1,0:T(8,128)(2,1)S(1)} %pad_maximum_fusion.refs_0_), channel_id=1, source_target_pairs={{0,32},{16,48},{32,64},{48,80},{64,96},{80,112},{96,0},{112,16},{1... | collective-permute-start | bytes 1572872 | tf_op jit(solution)/shard_map/ppermute | solution.py:724
  112.7 0.7 copy-start.7
  122.6 13.1 %all-to-all-start.7 = ((bf16[16,4,3072]{2,1,0:T(4,128)(2,1)}), bf16[16,4,3072]{2,1,0:T(4,128)(2,1)S(1)}, u32[]{:S(2)}, u32[]{:S(2)}) async-start(bf16[16,4,3072]{2,1,0:T(4,128)(2,1)} %get-tuple-element.95), calls=%async_computation.7 | async-start | bytes 786432 | tf_op jit(solution)/shard_map/all_to_all | solution.py:809

commit v11 on v10

--- a/solution.py
+++ b/solution.py
@@ -741,8 +741,10 @@
     came, places, origin, most = exchange(jnp.zeros((1,), jnp.int32))
 
     low, high = pack(gate_weight.T, up_weight.T, down_weight.T, places)
-    near_z = [turn(low, 1), turn(high, -1), turn(high, 1), turn(low, -1)]
+    near_z = [turn(low, 1), turn(high, -1)]
     handed = hand(origin, came, members)
+    later = lax.optimization_barrier((low, high, handed))
+    near_z += [turn(later[1], 1), turn(later[0], -1)]
     weights = [low, high] + near_z
     arrived = plane(handed)
 
@@ -776,6 +778,8 @@
         value_cache,
     )
     parts = lax.all_to_all(payload, "tok", 0, 0, tiled=True)
+    later = lax.optimization_barrier((near_z[0], near_z[1], payload))
+    far = [turn(later[0], 1), turn(later[1], -1)]
     blocks, chosen = mamba(
         ints,
         reals,
@@ -789,8 +793,6 @@
         members,
         query_heads * own,
     )
-    later = lax.optimization_barrier((near_z[0], near_z[1], blocks))
-    far = [turn(later[0], 1), turn(later[1], -1)]
     joint = join(parts, blocks, query_heads, head_size)
     joined = lax.all_to_all(joint, "tok", 0, 0, tiled=True)
     *later, chosen, _ = lax.optimization_barrier((*weights, chosen, joint))

time: 137 us -> 134 us (0.978)
  starting transfers between devices: 50.5 us -> 46.9 us
    all_to_all x1, waiting for transfers between devices: 6.76 us -> 3.5 us  [plane(): return lax.all_to_all(rows, 'tok', 0, 0, tiled=True)]
    all_to_all x1, waiting for transfers between devices: 1.08 us -> 4.1 us  [exchange(): came = lax.all_to_all(keep + across(give), ('z', 'tok'), 0, 0, tiled=True)]
    all_to_all x1, starting transfers between devices: 5.79 us -> 3.57 us  [plane(): return lax.all_to_all(rows, 'tok', 0, 0, tiled=True)]
    ppermute x9, waiting for transfers between devices: 10.8 us -> 9.3 us  [turn(): lax.ppermute(value, REQ, [(g, (g + by * cores) % groups) for g in range(g...]
  transfers between devices with their start and end apart: 25 -> 25, of which waited for: 11 -> 10; matrix products, arithmetic and copies ran while one was open for 4% -> 4% of each run, Pallas kernels for 25% -> 26%
where the time goes in v11:
time: 134 us; the launch traced here: 133 us
  starting transfers between devices  46.9 us (35%)
  Pallas kernels  38.9 us (29%)
  waiting for transfers between devices  33.4 us (25%)
  other arithmetic  5.63 us (4%)
  local copies, waits for them, and re-layouts  4.92 us (4%)
  between operations  2.9 us (2%)
    ppermute x9, starting transfers between devices, turn(): lax.ppermute(value, REQ, [(g, (g + by * cores) % groups) for g in range(g...  11.8 us
    all_to_all x1, starting transfers between devices, exchange(): came = lax.all_to_all(keep + across(give), ('z', 'tok'), 0, 0, tiled=True)  11.5 us
    ppermute x9, waiting for transfers between devices, turn(): lax.ppermute(value, REQ, [(g, (g + by * cores) % groups) for g in range(g...  9.3 us
    pallas_call x1, Pallas kernels, feed(): pl.pallas_call(functools.partial(feed_kernel, count=len(weights), units=u...  9.13 us
    pallas_call x1, Pallas kernels, attend(): pl.pallas_call(attend_kernel, grid=(1,), in_specs=scalars(1) + whole([arr...  7.28 us
    all_to_all x1, starting transfers between devices, local(): joined = lax.all_to_all(joint, 'tok', 0, 0, tiled=True)  7.27 us
    all_to_all x1, waiting for transfers between devices, local(): added = lax.all_to_all(spread, 'tok', 0, 0, tiled=True)  7.19 us
    pallas_call x1, Pallas kernels, mamba(): pl.pallas_call(mamba_kernel, grid=(1,), in_specs=scalars(2) + whole([norm...  6.7 us
  transfers between devices with their start and end apart: 25, of which 10 were waited for; matrix products, arithmetic and copies ran while one was open for 4% of the time, Pallas kernels for 26%

profile of v11, /device:TPU:0, one launch (start us, length us, event | category | flops | bytes accessed | tf_op | source)
XLA Modules:
  0.0 133.4 jit_solution(7693063316233639056)
XLA Ops:
  0.7 4.9 %fetch.2 = (bf16[64,24,128]{2,1,0:T(8,128)(2,1)}, bf16[64,24,128]{2,1,0:T(8,128)(2,1)}, s32[64,128]{1,0:T(8,128)}, s32[4]{0:T(128)}, s32[1]{0:T(128)}) custom-call(s32[1]{0:T(128)} %constant.88.clone.1.turn, s32[1,32]{1,0:T(1,128)} %bitcast.20, s32[16,32]{1,0:T(8,128)} %bitcast.26, bf16[512,3072]{1,0:T(8,128)(2,1)} %table_far.1), custom_call_target="tpu_custom_call" | custom-call | flops 402653184 | bytes 3145728 | tf_op jit(solution)/shard_map/fetch/pallas_call | solution.py:163
  5.7 1.9 %collective-permute-done.3 = bf16[64,24,128]{2,1,0:T(8,128)(2,1)S(1)} collective-permute-done((bf16[64,24,128]{2,1,0:T(8,128)(2,1)}, bf16[64,24,128]{2,1,0:T(8,128)(2,1)S(1)}, u32[]{:S(2)}, u32[]{:S(2)}) %collective-permute-start.3) | collective-permute-done | bytes 393248 | tf_op jit(solution)/shard_map/ppermute | solution.py:729
  7.6 1.8 %add.51 = bf16[64,24,128]{2,1,0:T(8,128)(2,1)} add(bf16[64,24,128]{2,1,0:T(8,128)(2,1)} %get-tuple-element.74, bf16[64,24,128]{2,1,0:T(8,128)(2,1)S(1)} %collective-permute-done.3) | non-fusion elementwise | flops 196608 | bytes 1179648 | tf_op jit(solution)/shard_map/add | solution.py:735
  9.4 11.5 %all-to-all-start.2 = ((bf16[64,24,128]{2,1,0:T(8,128)(2,1)}), bf16[64,24,128]{2,1,0:T(8,128)(2,1)S(1)}, u32[]{:S(2)}, u32[]{:S(2)}) async-start(bf16[64,24,128]{2,1,0:T(8,128)(2,1)} %add.51), calls=%async_computation.2 | async-start | bytes 786432 | tf_op jit(solution)/shard_map/all_to_all | solution.py:735
  20.9 2.8 %pack.1 = (bf16[144,3072]{1,0:T(8,128)(2,1)}, bf16[144,3072]{1,0:T(8,128)(2,1)}) custom-call(bf16[96,3072]{1,0:T(8,128)(2,1)} %bitcast.22, bf16[96,3072]{1,0:T(8,128)(2,1)} %bitcast.23, bf16[96,3072]{1,0:T(8,128)(2,1)} %bitcast.24, s32[64,128]{1,0:T(8,128)} %get-tuple-element.70.ready.places), custom_call_target="tpu_custom_call" | custom-call | bytes 1024 | tf_op jit(solution)/shard_map/pack/pallas_call | solution.py:646
  23.7 1.6 %collective-permute-start.1 = (bf16[144,3072]{1,0:T(8,128)(2,1)}, bf16[144,3072]{1,0:T(8,128)(2,1)}, u32[]{:S(2)}, u32[]{:S(2)}) collective-permute-start(bf16[144,3072]{1,0:T(8,128)(2,1)} %get-tuple-element.88.refs_0_), channel_id=1, source_target_pairs={{0,32},{16,48},{32,64},{48,80},{64,96},{80,112},{96,0},{112,16},{1... | collective-permute-start | bytes 2654216 | tf_op jit(solution)/shard_map/ppermute | solution.py:724
  25.3 1.7 %collective-permute-start.2 = (bf16[144,3072]{1,0:T(8,128)(2,1)}, bf16[144,3072]{1,0:T(8,128)(2,1)}, u32[]{:S(2)}, u32[]{:S(2)}) collective-permute-start(bf16[144,3072]{1,0:T(8,128)(2,1)} %get-tuple-element.89.refs_1_), channel_id=1, source_target_pairs={{0,96},{16,112},{32,0},{48,16},{64,32},{80,48},{96,64},{112,80},{1... | collective-permute-start | bytes 2654216 | tf_op jit(solution)/shard_map/ppermute | solution.py:724
  29.1 4.1 %all-to-all-done.2.came = bf16[64,24,128]{2,1,0:T(8,128)(2,1)S(1)} async-done(((bf16[64,24,128]{2,1,0:T(8,128)(2,1)}), bf16[64,24,128]{2,1,0:T(8,128)(2,1)S(1)}, u32[]{:S(2)}, u32[]{:S(2)}) %all-to-all-start.2) | async-done | bytes 393248 | tf_op jit(solution)/shard_map/all_to_all | solution.py:735
  33.2 1.3 hand.2
  34.6 0.7 while.10
  35.3 3.6 %all-to-all-start.3 = ((bf16[16,96,128]{2,1,0:T(8,128)(2,1)}), bf16[16,96,128]{2,1,0:T(8,128)(2,1)S(1)}, u32[]{:S(2)}, u32[]{:S(2)}) async-start(bf16[16,96,128]{2,1,0:T(8,128)(2,1)} %hand.2), calls=%async_computation.3 | async-start | bytes 786432 | tf_op jit(solution)/shard_map/all_to_all | solution.py:739
  38.9 0.6 pad_maximum_fusion.1.reals
  39.5 0.6 gather_fusion.1
  40.1 0.6 gather_fusion
  40.8 0.7 pad_add_fusion.ints
  41.5 0.6 collective-permute-start.6
  42.1 2.6 %collective-permute-start.7 = (bf16[144,3072]{1,0:T(8,128)(2,1)}, bf16[144,3072]{1,0:T(8,128)(2,1)}, u32[]{:S(2)}, u32[]{:S(2)}) collective-permute-start(bf16[144,3072]{1,0:T(8,128)(2,1)} %get-tuple-element.88.refs_0_), channel_id=1, source_target_pairs={{0,96},{16,112},{32,0},{48,16},{64,32},{80,48},{96,64},{112,80},{1... | collective-permute-start | bytes 2654216 | tf_op jit(solution)/shard_map/ppermute | solution.py:724
  44.7 3.5 %all-to-all-done.3.arrived = bf16[16,96,128]{2,1,0:T(8,128)(2,1)S(1)} async-done(((bf16[16,96,128]{2,1,0:T(8,128)(2,1)}), bf16[16,96,128]{2,1,0:T(8,128)(2,1)S(1)}, u32[]{:S(2)}, u32[]{:S(2)}) %all-to-all-start.3) | async-done | bytes 393248 | tf_op jit(solution)/shard_map/all_to_all | solution.py:739
  48.2 0.7 copy-done.8
  49.0 7.3 %attend.1 = (bf16[16,4,896]{2,1,0:T(4,128)(2,1)}, bf16[64,3072]{1,0:T(8,128)(2,1)}, bf16[64,3072]{1,0:T(8,128)(2,1)}) custom-call(s32[9]{0:T(128)} %pad_add_fusion.ints, bf16[16,96,128]{2,1,0:T(8,128)(2,1)} %copy-done.8, s32[64,128]{1,0:T(8,128)} %get-tuple-element.70.ready.places, bf16[64,3072]{1,0:T(8,128)(2,1)S(1)} %get-tuple-element.77.extra, ...), custom_call_target="tpu_custom_call" | custom-call | flops 20000000000 | bytes 1024 | tf_op jit(solution)/shard_map/attend/pallas_call | solution.py:332
  56.3 3.7 %all-to-all-start.4 = ((bf16[16,4,896]{2,1,0:T(4,128)(2,1)}), bf16[16,4,896]{2,1,0:T(4,128)(2,1)S(1)}, u32[]{:S(2)}, u32[]{:S(2)}) async-start(bf16[16,4,896]{2,1,0:T(4,128)(2,1)} %get-tuple-element.78), calls=%async_computation.4 | async-start | bytes 229376 | tf_op jit(solution)/shard_map/all_to_all | solution.py:780
  60.0 0.6 collective-permute-start.4
  60.5 2.7 %collective-permute-start.5 = (bf16[144,3072]{1,0:T(8,128)(2,1)}, bf16[144,3072]{1,0:T(8,128)(2,1)}, u32[]{:S(2)}, u32[]{:S(2)}) collective-permute-start(bf16[144,3072]{1,0:T(8,128)(2,1)} %collective-permute-done.2.refs_3_), channel_id=1, source_target_pairs={{0,96},{16,112},{32,0},{48,16},{64,32},{80,48},{96,64},{112,80},{1... | collective-permute-start | bytes 2654216 | tf_op jit(solution)/shard_map/ppermute | solution.py:724
  63.3 6.7 %mamba.1 = (bf16[16,120,128]{2,1,0:T(8,128)(2,1)}, bf16[4,1,128,256]{3,2,1,0:T(8,128)(2,1)}) custom-call(s32[9]{0:T(128)} %pad_add_fusion.ints, f32[3]{0:T(128)} %pad_maximum_fusion.1.reals, bf16[64,3072]{1,0:T(8,128)(2,1)} %get-tuple-element.81.normed, bf16[3072,128]{1,0:T(8,128)(2,1)} %input_weight.1, bf16[3072,128]{1,0:T(8,128)(2,1)} %gate_weight.1, ...), custom_call_target="tpu_custom_call" | custom-call | flops 8000000000 | bytes 1024 | tf_op jit(solution)/shard_map/mamba/pallas_call | solution.py:463
  70.0 0.6 copy-done.11
  70.6 2.1 %join.1 = bf16[16,120,128]{2,1,0:T(8,128)(2,1)} custom-call(bf16[16,4,896]{2,1,0:T(4,128)(2,1)} %copy-done.11, bf16[16,120,128]{2,1,0:T(8,128)(2,1)} %get-tuple-element.82.blocks), custom_call_target="tpu_custom_call", output_to_operand_aliasing={{}: (1, {})} | custom-call | flops 20000000000 | bytes 1024 | tf_op jit(solution)/shard_map/join/pallas_call | solution.py:507
  72.8 7.3 %all-to-all-start.5 = ((bf16[16,120,128]{2,1,0:T(8,128)(2,1)}), bf16[16,120,128]{2,1,0:T(8,128)(2,1)}, u32[]{:S(2)}, u32[]{:S(2)}) async-start(bf16[16,120,128]{2,1,0:T(8,128)(2,1)} %join.1), calls=%async_computation.5 | async-start | bytes 983040 | tf_op jit(solution)/shard_map/all_to_all | solution.py:797
  80.7 1.0 collective-permute-done.8
  82.0 5.7 %collective-permute-done.4.refs_12_ = bf16[144,3072]{1,0:T(8,128)(2,1)} collective-permute-done((bf16[144,3072]{1,0:T(8,128)(2,1)}, bf16[144,3072]{1,0:T(8,128)(2,1)}, u32[]{:S(2)}, u32[]{:S(2)}) %collective-permute-start.4) | collective-permute-done | bytes 884768 | tf_op jit(solution)/shard_map/ppermute | solution.py:724
  87.7 0.5 collective-permute-start.13
  88.2 3.8 %all-to-all-done.5.parts = bf16[16,120,128]{2,1,0:T(8,128)(2,1)} async-done(((bf16[16,120,128]{2,1,0:T(8,128)(2,1)}), bf16[16,120,128]{2,1,0:T(8,128)(2,1)}, u32[]{:S(2)}, u32[]{:S(2)}) %all-to-all-start.5) | async-done | bytes 491552 | tf_op jit(solution)/shard_map/all_to_all | solution.py:797
  92.0 2.3 %project.1 = bf16[16,96,128]{2,1,0:T(8,128)(2,1)} custom-call(bf16[16,120,128]{2,1,0:T(8,128)(2,1)} %all-to-all-done.5.parts, bf16[192,768]{1,0:T(8,128)(2,1)} %bitcast.30), custom_call_target="tpu_custom_call" | custom-call | flops 20000000000 | bytes 1024 | tf_op jit(solution)/shard_map/project/pallas_call | solution.py:543
  94.3 0.5 collective-permute-done.14.refs_11_
  95.4 3.6 %all-to-all-start.6 = ((bf16[16,96,128]{2,1,0:T(8,128)(2,1)}), bf16[16,96,128]{2,1,0:T(8,128)(2,1)S(1)}, u32[]{:S(2)}, u32[]{:S(2)}) async-start(bf16[16,96,128]{2,1,0:T(8,128)(2,1)} %project.1), calls=%async_computation.6 | async-start | bytes 786432 | tf_op jit(solution)/shard_map/all_to_all | solution.py:808
  99.1 0.6 gather_fusion.2
  99.7 0.7 fusion
  100.7 0.9 collective-permute-start.18
  101.7 0.7 collective-permute-start.17
  102.4 7.2 %all-to-all-done.6.spread = bf16[16,96,128]{2,1,0:T(8,128)(2,1)S(1)} async-done(((bf16[16,96,128]{2,1,0:T(8,128)(2,1)}), bf16[16,96,128]{2,1,0:T(8,128)(2,1)S(1)}, u32[]{:S(2)}, u32[]{:S(2)}) %all-to-all-start.6) | async-done | bytes 393248 | tf_op jit(solution)/shard_map/all_to_all | solution.py:808
  109.6 0.7 copy-done.7
  110.4 9.1 %feed.1 = (bf16[16,4,3072]{2,1,0:T(4,128)(2,1)}, bf16[64,3072]{1,0:T(8,128)(2,1)}) custom-call(bf16[16,96,128]{2,1,0:T(8,128)(2,1)} %copy-done.7, bf16[64,3072]{1,0:T(8,128)(2,1)} %get-tuple-element.95.embedded, f32[1,3072]{1,0:T(1,128)} %bitcast.33, bf16[144,3072]{1,0:T(8,128)(2,1)} %get-tuple-element.88.refs_0_, ...), custom_call_target="tpu_custom_call" | custom-call | flops 20000000000 | bytes 1024 | tf_op jit(solution)/shard_map/feed/pallas_call | solution.py:623
  119.5 3.6 %all-to-all-start.7 = ((bf16[16,4,3072]{2,1,0:T(4,128)(2,1)}), bf16[16,4,3072]{2,1,0:T(4,128)(2,1)S(1)}, u32[]{:S(2)}, u32[]{:S(2)}) async-start(bf16[16,4,3072]{2,1,0:T(4,128)(2,1)} %get-tuple-element.99), calls=%async_computation.7 | async-start | bytes 786432 | tf_op jit(solution)/shard_map/all_to_all | solution.py:811
  123.1 0.5 and_select_fusion.3.turns
  123.6 3.6 %collective-permute-done.17.refs_1_ = bf16[8,128,256]{2,1,0:T(8,128)(2,1)} collective-permute-done((bf16[8,128,256]{2,1,0:T(8,128)(2,1)S(1)}, bf16[8,128,256]{2,1,0:T(8,128)(2,1)}, u32[]{:S(2)}, u32[]{:S(2)}) %collective-permute-start.17) | collective-permute-done | bytes 524320 | tf_op jit(solution)/shard_map/ppermute | solution.py:724
  127.2 2.5 %pick.1 = f32[4,128,256]{2,1,0:T(8,128)} custom-call(s32[4]{0:T(128)} %and_select_fusion.3.turns, s32[4]{0:T(128)} %get-tuple-element.119.rows, bf16[8,128,256]{2,1,0:T(8,128)(2,1)} %copy-done.6, bf16[8,128,256]{2,1,0:T(8,128)(2,1)} %collective-permute-done.17.refs_1_, bf16[8,128,256]{2,1,0:T(8,128)(2,1)} %collective-permute-done.18.refs_2_, ...), custom_call_target="tpu_custom_call" | custom-call | tf_op jit(solution)/shard_map/pick/pallas_call | solution.py:672
  129.7 0.8 constant_dynamic-slice_fusion
  130.5 2.1 %all-to-all-done.7 = bf16[16,4,3072]{2,1,0:T(4,128)(2,1)S(1)} async-done(((bf16[16,4,3072]{2,1,0:T(4,128)(2,1)}), bf16[16,4,3072]{2,1,0:T(4,128)(2,1)S(1)}, u32[]{:S(2)}, u32[]{:S(2)}) %all-to-all-start.7) | async-done | bytes 393248 | tf_op jit(solution)/shard_map/all_to_all | solution.py:811
  132.7 0.6 add_convert_fusion
  (54 shorter events, 2.7 us)
Async XLA Ops:
  0.6 38.8 %copy-start = (s32[32]{0:T(128)S(1)}, s32[32]{0:T(128)}, u32[]{:S(2)}) copy-start(s32[32]{0:T(128)} %param.33) | copy-start | bytes 388
  0.6 28.3 %copy-start.3 = (s32[32]{0:T(128)S(1)}, s32[32]{0:T(128)}, u32[]{:S(2)}) copy-start(s32[32]{0:T(128)} %param.31) | copy-start | bytes 388
  5.6 27.7 %copy-start.1 = (s32[4]{0:T(128)S(1)}, s32[4]{0:T(128)}, u32[]{:S(2)}) copy-start(s32[4]{0:T(128)} %get-tuple-element.73.origin) | copy-start | bytes 52
  5.6 2.0 %collective-permute-start.3 = (bf16[64,24,128]{2,1,0:T(8,128)(2,1)}, bf16[64,24,128]{2,1,0:T(8,128)(2,1)S(1)}, u32[]{:S(2)}, u32[]{:S(2)}) collective-permute-start(bf16[64,24,128]{2,1,0:T(8,128)(2,1)} %get-tuple-element.75), channel_id=1, source_target_pairs={{0,16},{16,0},{32,48},{48,32},{64,80},{80,64},{96,112},{112,96},{1... | collective-permute-start | bytes 1179656 | tf_op jit(solution)/shard_map/ppermute | solution.py:729
  9.4 23.8 %all-to-all-start.2 = ((bf16[64,24,128]{2,1,0:T(8,128)(2,1)}), bf16[64,24,128]{2,1,0:T(8,128)(2,1)S(1)}, u32[]{:S(2)}, u32[]{:S(2)}) async-start(bf16[64,24,128]{2,1,0:T(8,128)(2,1)} %add.51), calls=%async_computation.2 | async-start | bytes 786432 | tf_op jit(solution)/shard_map/all_to_all | solution.py:735
  23.7 36.3 %collective-permute-start.1 = (bf16[144,3072]{1,0:T(8,128)(2,1)}, bf16[144,3072]{1,0:T(8,128)(2,1)}, u32[]{:S(2)}, u32[]{:S(2)}) collective-permute-start(bf16[144,3072]{1,0:T(8,128)(2,1)} %get-tuple-element.88.refs_0_), channel_id=1, source_target_pairs={{0,32},{16,48},{32,64},{48,80},{64,96},{80,112},{96,0},{112,16},{1... | collective-permute-start | bytes 2654216 | tf_op jit(solution)/shard_map/ppermute | solution.py:724
  25.3 34.7 %collective-permute-start.2 = (bf16[144,3072]{1,0:T(8,128)(2,1)}, bf16[144,3072]{1,0:T(8,128)(2,1)}, u32[]{:S(2)}, u32[]{:S(2)}) collective-permute-start(bf16[144,3072]{1,0:T(8,128)(2,1)} %get-tuple-element.89.refs_1_), channel_id=1, source_target_pairs={{0,96},{16,112},{32,0},{48,16},{64,32},{80,48},{96,64},{112,80},{1... | collective-permute-start | bytes 2654216 | tf_op jit(solution)/shard_map/ppermute | solution.py:724
  33.2 1.4 %copy-start.9 = (s32[32,16]{0,1:T(8,128)S(1)}, s32[32,16]{0,1:T(8,128)}, u32[]{:S(2)}) copy-start(s32[32,16]{0,1:T(8,128)} %param.29) | copy-start | bytes 6148
  34.6 5.5 %copy-start.4 = (s32[32]{0:T(128)S(1)}, s32[32]{0:T(128)}, u32[]{:S(2)}) copy-start(s32[32]{0:T(128)} %param.30) | copy-start | bytes 388
  35.3 12.9 %all-to-all-start.3 = ((bf16[16,96,128]{2,1,0:T(8,128)(2,1)}), bf16[16,96,128]{2,1,0:T(8,128)(2,1)S(1)}, u32[]{:S(2)}, u32[]{:S(2)}) async-start(bf16[16,96,128]{2,1,0:T(8,128)(2,1)} %hand.2), calls=%async_computation.3 | async-start | bytes 786432 | tf_op jit(solution)/shard_map/all_to_all | solution.py:739
  41.5 31.2 %collective-permute-start.6 = (bf16[144,3072]{1,0:T(8,128)(2,1)}, bf16[144,3072]{1,0:T(8,128)(2,1)}, u32[]{:S(2)}, u32[]{:S(2)}) collective-permute-start(bf16[144,3072]{1,0:T(8,128)(2,1)} %get-tuple-element.89.refs_1_), channel_id=1, source_target_pairs={{0,32},{16,48},{32,64},{48,80},{64,96},{80,112},{96,0},{112,16},{1... | collective-permute-start | bytes 2654216 | tf_op jit(solution)/shard_map/ppermute | solution.py:724
  42.1 30.6 %collective-permute-start.7 = (bf16[144,3072]{1,0:T(8,128)(2,1)}, bf16[144,3072]{1,0:T(8,128)(2,1)}, u32[]{:S(2)}, u32[]{:S(2)}) collective-permute-start(bf16[144,3072]{1,0:T(8,128)(2,1)} %get-tuple-element.88.refs_0_), channel_id=1, source_target_pairs={{0,96},{16,112},{32,0},{48,16},{64,32},{80,48},{96,64},{112,80},{1... | collective-permute-start | bytes 2654216 | tf_op jit(solution)/shard_map/ppermute | solution.py:724
  48.2 0.7 copy-start.8
  56.3 13.7 %all-to-all-start.4 = ((bf16[16,4,896]{2,1,0:T(4,128)(2,1)}), bf16[16,4,896]{2,1,0:T(4,128)(2,1)S(1)}, u32[]{:S(2)}, u32[]{:S(2)}) async-start(bf16[16,4,896]{2,1,0:T(4,128)(2,1)} %get-tuple-element.78), calls=%async_computation.4 | async-start | bytes 229376 | tf_op jit(solution)/shard_map/all_to_all | solution.py:780
  60.0 27.7 %collective-permute-start.4 = (bf16[144,3072]{1,0:T(8,128)(2,1)}, bf16[144,3072]{1,0:T(8,128)(2,1)}, u32[]{:S(2)}, u32[]{:S(2)}) collective-permute-start(bf16[144,3072]{1,0:T(8,128)(2,1)} %collective-permute-done.1.refs_2_), channel_id=1, source_target_pairs={{0,32},{16,48},{32,64},{48,80},{64,96},{80,112},{96,0},{112,16},{1... | collective-permute-start | bytes 2654216 | tf_op jit(solution)/shard_map/ppermute | solution.py:724
  60.5 27.2 %collective-permute-start.5 = (bf16[144,3072]{1,0:T(8,128)(2,1)}, bf16[144,3072]{1,0:T(8,128)(2,1)}, u32[]{:S(2)}, u32[]{:S(2)}) collective-permute-start(bf16[144,3072]{1,0:T(8,128)(2,1)} %collective-permute-done.2.refs_3_), channel_id=1, source_target_pairs={{0,96},{16,112},{32,0},{48,16},{64,32},{80,48},{96,64},{112,80},{1... | collective-permute-start | bytes 2654216 | tf_op jit(solution)/shard_map/ppermute | solution.py:724
  70.0 0.6 copy-start.11
  70.6 9.5 %copy-start.10 = (bf16[4,1,128,256]{3,2,1,0:T(8,128)(2,1)S(1)}, bf16[4,1,128,256]{3,2,1,0:T(8,128)(2,1)}, u32[]{:S(2)}) copy-start(bf16[4,1,128,256]{3,2,1,0:T(8,128)(2,1)} %get-tuple-element.87) | copy-start | bytes 786436
  72.7 19.3 %collective-permute-start.9 = (bf16[144,3072]{1,0:T(8,128)(2,1)}, bf16[144,3072]{1,0:T(8,128)(2,1)}, u32[]{:S(2)}, u32[]{:S(2)}) collective-permute-start(bf16[144,3072]{1,0:T(8,128)(2,1)} %get-tuple-element.88.refs_0_), channel_id=1, source_target_pairs={{0,16},{16,0},{32,48},{48,32},{64,80},{80,64},{96,112},{112,96},{1... | collective-permute-start | bytes 2654216 | tf_op jit(solution)/shard_map/ppermute | solution.py:729
  72.8 19.2 %all-to-all-start.5 = ((bf16[16,120,128]{2,1,0:T(8,128)(2,1)}), bf16[16,120,128]{2,1,0:T(8,128)(2,1)}, u32[]{:S(2)}, u32[]{:S(2)}) async-start(bf16[16,120,128]{2,1,0:T(8,128)(2,1)} %join.1), calls=%async_computation.5 | async-start | bytes 983040 | tf_op jit(solution)/shard_map/all_to_all | solution.py:797
  80.1 1.6 %collective-permute-start.8 = (bf16[4,128,256]{2,1,0:T(8,128)(2,1)S(1)}, bf16[4,128,256]{2,1,0:T(8,128)(2,1)S(1)}, u32[]{:S(2)}, u32[]{:S(2)}) collective-permute-start(bf16[4,128,256]{2,1,0:T(8,128)(2,1)S(1)} %bitcast.28), channel_id=1, source_target_pairs={{0,16},{16,0},{32,48},{48,32},{64,80},{80,64},{96,112},{112,96},{1... | collective-permute-start | bytes 786440 | tf_op jit(solution)/shard_map/ppermute | solution.py:729
  80.4 13.9 %collective-permute-start.10 = (bf16[144,3072]{1,0:T(8,128)(2,1)}, bf16[144,3072]{1,0:T(8,128)(2,1)}, u32[]{:S(2)}, u32[]{:S(2)}) collective-permute-start(bf16[144,3072]{1,0:T(8,128)(2,1)} %get-tuple-element.89.refs_1_), channel_id=1, source_target_pairs={{0,16},{16,0},{32,48},{48,32},{64,80},{80,64},{96,112},{112,96},{1... | collective-permute-start | bytes 2654216 | tf_op jit(solution)/shard_map/ppermute | solution.py:729
  81.7 12.5 %collective-permute-start.11 = (bf16[144,3072]{1,0:T(8,128)(2,1)}, bf16[144,3072]{1,0:T(8,128)(2,1)}, u32[]{:S(2)}, u32[]{:S(2)}) collective-permute-start(bf16[144,3072]{1,0:T(8,128)(2,1)} %collective-permute-done.1.refs_2_), channel_id=1, source_target_pairs={{0,16},{16,0},{32,48},{48,32},{64,80},{80,64},{96,112},{112,96},{1... | collective-permute-start | bytes 2654216 | tf_op jit(solution)/shard_map/ppermute | solution.py:729
  82.0 19.7 %copy-start.6 = (bf16[8,128,256]{2,1,0:T(8,128)(2,1)}, bf16[8,128,256]{2,1,0:T(8,128)(2,1)S(1)}, u32[]{:S(2)}) copy-start(bf16[8,128,256]{2,1,0:T(8,128)(2,1)S(1)} %pad_maximum_fusion.refs_0_) | copy-start | bytes 1572868
  87.7 6.6 %collective-permute-start.12 = (bf16[144,3072]{1,0:T(8,128)(2,1)}, bf16[144,3072]{1,0:T(8,128)(2,1)}, u32[]{:S(2)}, u32[]{:S(2)}) collective-permute-start(bf16[144,3072]{1,0:T(8,128)(2,1)} %collective-permute-done.2.refs_3_), channel_id=1, source_target_pairs={{0,16},{16,0},{32,48},{48,32},{64,80},{80,64},{96,112},{112,96},{1... | collective-permute-start | bytes 2654216 | tf_op jit(solution)/shard_map/ppermute | solution.py:729
  87.7 6.6 %collective-permute-start.13 = (bf16[144,3072]{1,0:T(8,128)(2,1)}, bf16[144,3072]{1,0:T(8,128)(2,1)}, u32[]{:S(2)}, u32[]{:S(2)}) collective-permute-start(bf16[144,3072]{1,0:T(8,128)(2,1)} %collective-permute-done.6.refs_4_), channel_id=1, source_target_pairs={{0,16},{16,0},{32,48},{48,32},{64,80},{80,64},{96,112},{112,96},{1... | collective-permute-start | bytes 2654216 | tf_op jit(solution)/shard_map/ppermute | solution.py:729
  92.0 2.8 %collective-permute-start.14 = (bf16[144,3072]{1,0:T(8,128)(2,1)}, bf16[144,3072]{1,0:T(8,128)(2,1)}, u32[]{:S(2)}, u32[]{:S(2)}) collective-permute-start(bf16[144,3072]{1,0:T(8,128)(2,1)} %collective-permute-done.7.refs_5_), channel_id=1, source_target_pairs={{0,16},{16,0},{32,48},{48,32},{64,80},{80,64},{96,112},{112,96},{1... | collective-permute-start | bytes 2654216 | tf_op jit(solution)/shard_map/ppermute | solution.py:729
  92.0 3.3 %copy-start.12 = (s32[32]{0:T(128)S(1)}, s32[32]{0:T(128)}, u32[]{:S(2)}) copy-start(s32[32]{0:T(128)} %param.32) | copy-start | bytes 388
  94.8 14.8 %collective-permute-start.15 = (bf16[144,3072]{1,0:T(8,128)(2,1)}, bf16[144,3072]{1,0:T(8,128)(2,1)}, u32[]{:S(2)}, u32[]{:S(2)}) collective-permute-start(bf16[144,3072]{1,0:T(8,128)(2,1)} %collective-permute-done.4.refs_12_), channel_id=1, source_target_pairs={{0,16},{16,0},{32,48},{48,32},{64,80},{80,64},{96,112},{112,96},{1... | collective-permute-start | bytes 2654216 | tf_op jit(solution)/shard_map/ppermute | solution.py:729
  94.9 14.7 %collective-permute-start.16 = (bf16[144,3072]{1,0:T(8,128)(2,1)}, bf16[144,3072]{1,0:T(8,128)(2,1)}, u32[]{:S(2)}, u32[]{:S(2)}) collective-permute-start(bf16[144,3072]{1,0:T(8,128)(2,1)} %collective-permute-done.5.refs_13_), channel_id=1, source_target_pairs={{0,16},{16,0},{32,48},{48,32},{64,80},{80,64},{96,112},{112,96},{1... | collective-permute-start | bytes 2654216 | tf_op jit(solution)/shard_map/ppermute | solution.py:729
  95.4 14.2 %all-to-all-start.6 = ((bf16[16,96,128]{2,1,0:T(8,128)(2,1)}), bf16[16,96,128]{2,1,0:T(8,128)(2,1)S(1)}, u32[]{:S(2)}, u32[]{:S(2)}) async-start(bf16[16,96,128]{2,1,0:T(8,128)(2,1)} %project.1), calls=%async_computation.6 | async-start | bytes 786432 | tf_op jit(solution)/shard_map/all_to_all | solution.py:808
  100.4 23.2 %collective-permute-start.19 = (bf16[8,128,256]{2,1,0:T(8,128)(2,1)S(1)}, bf16[8,128,256]{2,1,0:T(8,128)(2,1)}, u32[]{:S(2)}, u32[]{:S(2)}) collective-permute-start(bf16[8,128,256]{2,1,0:T(8,128)(2,1)S(1)} %pad_maximum_fusion.refs_0_), channel_id=1, source_target_pairs={{0,96},{16,112},{32,0},{48,16},{64,32},{80,48},{96,64},{112,80},{1... | collective-permute-start | bytes 1572872 | tf_op jit(solution)/shard_map/ppermute | solution.py:724
  100.7 22.9 %collective-permute-start.18 = (bf16[8,128,256]{2,1,0:T(8,128)(2,1)S(1)}, bf16[8,128,256]{2,1,0:T(8,128)(2,1)}, u32[]{:S(2)}, u32[]{:S(2)}) collective-permute-start(bf16[8,128,256]{2,1,0:T(8,128)(2,1)S(1)} %pad_maximum_fusion.refs_0_), channel_id=1, source_target_pairs={{0,64},{16,80},{32,96},{48,112},{64,0},{80,16},{96,32},{112,48},{1... | collective-permute-start | bytes 1572872 | tf_op jit(solution)/shard_map/ppermute | solution.py:724
  101.7 25.5 %collective-permute-start.17 = (bf16[8,128,256]{2,1,0:T(8,128)(2,1)S(1)}, bf16[8,128,256]{2,1,0:T(8,128)(2,1)}, u32[]{:S(2)}, u32[]{:S(2)}) collective-permute-start(bf16[8,128,256]{2,1,0:T(8,128)(2,1)S(1)} %pad_maximum_fusion.refs_0_), channel_id=1, source_target_pairs={{0,32},{16,48},{32,64},{48,80},{64,96},{80,112},{96,0},{112,16},{1... | collective-permute-start | bytes 1572872 | tf_op jit(solution)/shard_map/ppermute | solution.py:724
  109.6 0.7 copy-start.7
  119.5 13.1 %all-to-all-start.7 = ((bf16[16,4,3072]{2,1,0:T(4,128)(2,1)}), bf16[16,4,3072]{2,1,0:T(4,128)(2,1)S(1)}, u32[]{:S(2)}, u32[]{:S(2)}) async-start(bf16[16,4,3072]{2,1,0:T(4,128)(2,1)} %get-tuple-element.99), calls=%async_computation.7 | async-start | bytes 786432 | tf_op jit(solution)/shard_map/all_to_all | solution.py:811

commit v12 on v9

--- a/solution.py
+++ b/solution.py
@@ -729,8 +729,10 @@
     came, places, origin, most = exchange(jnp.zeros((1,), jnp.int32))
 
     low, high = pack(gate_weight.T, up_weight.T, down_weight.T, places)
-    near_z = [turn(low, 1), turn(high, -1), turn(high, 1), turn(low, -1)]
+    near_z = [turn(low, 1), turn(high, -1)]
     handed = hand(origin, came, members)
+    later = lax.optimization_barrier((low, high, handed))
+    near_z += [turn(later[1], 1), turn(later[0], -1)]
     weights = [low, high] + near_z
     arrived = plane(handed)
 
@@ -764,6 +766,8 @@
         value_cache,
     )
     parts = lax.all_to_all(payload, "tok", 0, 0, tiled=True)
+    later = lax.optimization_barrier((near_z[0], near_z[1], payload))
+    far = [turn(later[0], 1), turn(later[1], -1)]
     blocks, chosen = mamba(
         ints,
         reals,
@@ -777,8 +781,6 @@
         members,
         query_heads * own,
     )
-    later = lax.optimization_barrier((near_z[0], near_z[1], blocks))
-    far = [turn(later[0], 1), turn(later[1], -1)]
     joint = join(parts, blocks, query_heads, head_size)
     joined = lax.all_to_all(joint, "tok", 0, 0, tiled=True)
     *later, chosen, _ = lax.optimization_barrier((*weights, chosen, joint))

time: 136 us -> 134 us (0.985)
  starting transfers between devices: 48.5 us -> 46.5 us
    ppermute x9, waiting for transfers between devices: 12.1 us -> 7.84 us  [turn(): lax.ppermute(value, 'req', [(g, (g + by * cores) % groups) for g in range...]
    all_to_all x1, waiting for transfers between devices: 7.56 us -> 4.25 us  [plane(): return lax.all_to_all(rows, 'tok', 0, 0, tiled=True)]
    all_to_all x1, waiting for transfers between devices: 5.28 us -> 8.14 us  [exchange(): came = lax.all_to_all(sent, ('req', 'tok'), 0, 0, tiled=True)]
    all_to_all x1, waiting for transfers between devices: 2.49 us -> 5.2 us  [local(): joined = lax.all_to_all(joint, 'tok', 0, 0, tiled=True)]
    all_to_all x1, starting transfers between devices: 6.13 us -> 3.56 us  [local(): added = lax.all_to_all(spread, 'tok', 0, 0, tiled=True)]
  transfers between devices with their start and end apart: 24 -> 24, of which waited for: 10 -> 9; matrix products, arithmetic and copies ran while one was open for 4% -> 4% of each run, Pallas kernels for 25% -> 26%
where the time goes in v12:
time: 134 us; the launch traced here: 133 us
  starting transfers between devices  46.5 us (35%)
  Pallas kernels  38.3 us (29%)
  waiting for transfers between devices  36.2 us (27%)
  local copies, waits for them, and re-layouts  4.91 us (4%)
  other arithmetic  3.89 us (3%)
  between operations  2.89 us (2%)
    ppermute x9, starting transfers between devices, turn(): lax.ppermute(value, 'req', [(g, (g + by * cores) % groups) for g in range...  12 us
    all_to_all x1, starting transfers between devices, exchange(): came = lax.all_to_all(sent, ('req', 'tok'), 0, 0, tiled=True)  11.1 us
    pallas_call x1, Pallas kernels, feed(): pl.pallas_call(functools.partial(feed_kernel, count=len(weights), units=u...  9.12 us
    all_to_all x1, waiting for transfers between devices, exchange(): came = lax.all_to_all(sent, ('req', 'tok'), 0, 0, tiled=True)  8.14 us
    ppermute x9, waiting for transfers between devices, turn(): lax.ppermute(value, 'req', [(g, (g + by * cores) % groups) for g in range...  7.84 us
    pallas_call x1, Pallas kernels, attend(): pl.pallas_call(attend_kernel, grid=(1,), in_specs=scalars(1) + whole([arr...  7.27 us
    all_to_all x1, starting transfers between devices, local(): joined = lax.all_to_all(joint, 'tok', 0, 0, tiled=True)  7.21 us
    all_to_all x1, waiting for transfers between devices, local(): added = lax.all_to_all(spread, 'tok', 0, 0, tiled=True)  7.2 us
  transfers between devices with their start and end apart: 24, of which 9 were waited for; matrix products, arithmetic and copies ran while one was open for 4% of the time, Pallas kernels for 26%

profile of v12, /device:TPU:0, one launch (start us, length us, event | category | flops | bytes accessed | tf_op | source)
XLA Modules:
  0.0 133.3 jit_solution(756981462052273083)
XLA Ops:
  0.7 4.3 %fetch.2 = (bf16[128,24,128]{2,1,0:T(8,128)(2,1)}, s32[64,128]{1,0:T(8,128)}, s32[4]{0:T(128)}, s32[1]{0:T(128)}) custom-call(s32[1]{0:T(128)} %constant.84.clone.1.turn, s32[1,32]{1,0:T(1,128)} %bitcast.20, s32[16,32]{1,0:T(8,128)} %bitcast.26, bf16[512,3072]{1,0:T(8,128)(2,1)} %table_far.1), custom_call_target="tpu_custom_call" | custom-call | flops 402653184 | bytes 3145728 | tf_op jit(solution)/shard_map/fetch/pallas_call | solution.py:151
  5.0 11.1 %all-to-all-start.2 = ((bf16[128,24,128]{2,1,0:T(8,128)(2,1)}), bf16[128,24,128]{2,1,0:T(8,128)(2,1)S(1)}, u32[]{:S(2)}, u32[]{:S(2)}) async-start(bf16[128,24,128]{2,1,0:T(8,128)(2,1)} %get-tuple-element.72), calls=%async_computation.2 | async-start | bytes 1572864 | tf_op jit(solution)/shard_map/all_to_all | solution.py:723
  16.1 2.8 %pack.1 = (bf16[144,3072]{1,0:T(8,128)(2,1)}, bf16[144,3072]{1,0:T(8,128)(2,1)}) custom-call(bf16[96,3072]{1,0:T(8,128)(2,1)} %bitcast.22, bf16[96,3072]{1,0:T(8,128)(2,1)} %bitcast.23, bf16[96,3072]{1,0:T(8,128)(2,1)} %bitcast.24, s32[64,128]{1,0:T(8,128)} %get-tuple-element.68.ready.places), custom_call_target="tpu_custom_call" | custom-call | bytes 1024 | tf_op jit(solution)/shard_map/pack/pallas_call | solution.py:634
  18.9 1.1 collective-permute-start
  20.0 2.2 %collective-permute-start.1 = (bf16[144,3072]{1,0:T(8,128)(2,1)}, bf16[144,3072]{1,0:T(8,128)(2,1)}, u32[]{:S(2)}, u32[]{:S(2)}) collective-permute-start(bf16[144,3072]{1,0:T(8,128)(2,1)} %get-tuple-element.86.refs_1_), channel_id=1, source_target_pairs={{0,96},{16,112},{32,0},{48,16},{64,32},{80,48},{96,64},{112,80},{1... | collective-permute-start | bytes 2654216 | tf_op jit(solution)/shard_map/ppermute | solution.py:712
  24.3 8.1 %all-to-all-done.2.came = bf16[128,24,128]{2,1,0:T(8,128)(2,1)S(1)} async-done(((bf16[128,24,128]{2,1,0:T(8,128)(2,1)}), bf16[128,24,128]{2,1,0:T(8,128)(2,1)S(1)}, u32[]{:S(2)}, u32[]{:S(2)}) %all-to-all-start.2) | async-done | bytes 786464 | tf_op jit(solution)/shard_map/all_to_all | solution.py:723
  32.5 1.3 hand.2
  33.8 0.6 while.10
  34.5 3.6 %all-to-all-start.3 = ((bf16[16,96,128]{2,1,0:T(8,128)(2,1)}), bf16[16,96,128]{2,1,0:T(8,128)(2,1)S(1)}, u32[]{:S(2)}, u32[]{:S(2)}) async-start(bf16[16,96,128]{2,1,0:T(8,128)(2,1)} %hand.2), calls=%async_computation.3 | async-start | bytes 786432 | tf_op jit(solution)/shard_map/all_to_all | solution.py:727
  38.1 0.7 pad_maximum_fusion.1.reals
  38.7 0.6 gather_fusion.1
  39.4 0.6 gather_fusion
  40.1 0.7 pad_add_fusion.ints
  40.8 0.8 collective-permute-start.4
  41.6 2.4 %collective-permute-start.5 = (bf16[144,3072]{1,0:T(8,128)(2,1)}, bf16[144,3072]{1,0:T(8,128)(2,1)}, u32[]{:S(2)}, u32[]{:S(2)}) collective-permute-start(bf16[144,3072]{1,0:T(8,128)(2,1)} %get-tuple-element.85.refs_0_), channel_id=1, source_target_pairs={{0,96},{16,112},{32,0},{48,16},{64,32},{80,48},{96,64},{112,80},{1... | collective-permute-start | bytes 2654216 | tf_op jit(solution)/shard_map/ppermute | solution.py:712
  44.0 4.3 %all-to-all-done.3.arrived = bf16[16,96,128]{2,1,0:T(8,128)(2,1)S(1)} async-done(((bf16[16,96,128]{2,1,0:T(8,128)(2,1)}), bf16[16,96,128]{2,1,0:T(8,128)(2,1)S(1)}, u32[]{:S(2)}, u32[]{:S(2)}) %all-to-all-start.3) | async-done | bytes 393248 | tf_op jit(solution)/shard_map/all_to_all | solution.py:727
  48.3 0.7 copy-done.8
  49.0 7.3 %attend.1 = (bf16[16,4,896]{2,1,0:T(4,128)(2,1)}, bf16[64,3072]{1,0:T(8,128)(2,1)}, bf16[64,3072]{1,0:T(8,128)(2,1)}) custom-call(s32[9]{0:T(128)} %pad_add_fusion.ints, bf16[16,96,128]{2,1,0:T(8,128)(2,1)} %copy-done.8, s32[64,128]{1,0:T(8,128)} %get-tuple-element.68.ready.places, bf16[64,3072]{1,0:T(8,128)(2,1)S(1)} %get-tuple-element.74.extra, ...), custom_call_target="tpu_custom_call" | custom-call | flops 20000000000 | bytes 1024 | tf_op jit(solution)/shard_map/attend/pallas_call | solution.py:320
  56.3 3.5 %all-to-all-start.4 = ((bf16[16,4,896]{2,1,0:T(4,128)(2,1)}), bf16[16,4,896]{2,1,0:T(4,128)(2,1)S(1)}, u32[]{:S(2)}, u32[]{:S(2)}) async-start(bf16[16,4,896]{2,1,0:T(4,128)(2,1)} %get-tuple-element.75), calls=%async_computation.4 | async-start | bytes 229376 | tf_op jit(solution)/shard_map/all_to_all | solution.py:768
  59.8 1.1 collective-permute-start.2
  60.9 2.4 %collective-permute-start.3 = (bf16[144,3072]{1,0:T(8,128)(2,1)}, bf16[144,3072]{1,0:T(8,128)(2,1)}, u32[]{:S(2)}, u32[]{:S(2)}) collective-permute-start(bf16[144,3072]{1,0:T(8,128)(2,1)} %collective-permute-done.1.refs_3_), channel_id=1, source_target_pairs={{0,96},{16,112},{32,0},{48,16},{64,32},{80,48},{96,64},{112,80},{1... | collective-permute-start | bytes 2654216 | tf_op jit(solution)/shard_map/ppermute | solution.py:712
  63.3 6.7 %mamba.1 = (bf16[16,120,128]{2,1,0:T(8,128)(2,1)}, bf16[4,1,128,256]{3,2,1,0:T(8,128)(2,1)}) custom-call(s32[9]{0:T(128)} %pad_add_fusion.ints, f32[3]{0:T(128)} %pad_maximum_fusion.1.reals, bf16[64,3072]{1,0:T(8,128)(2,1)} %get-tuple-element.78.normed, bf16[3072,128]{1,0:T(8,128)(2,1)} %input_weight.1, bf16[3072,128]{1,0:T(8,128)(2,1)} %gate_weight.1, ...), custom_call_target="tpu_custom_call" | custom-call | flops 8000000000 | bytes 1024 | tf_op jit(solution)/shard_map/mamba/pallas_call | solution.py:451
  70.0 0.6 copy-done.11
  70.7 2.1 %join.1 = bf16[16,120,128]{2,1,0:T(8,128)(2,1)} custom-call(bf16[16,4,896]{2,1,0:T(4,128)(2,1)} %copy-done.11, bf16[16,120,128]{2,1,0:T(8,128)(2,1)} %get-tuple-element.79.blocks), custom_call_target="tpu_custom_call", output_to_operand_aliasing={{}: (1, {})} | custom-call | flops 20000000000 | bytes 1024 | tf_op jit(solution)/shard_map/join/pallas_call | solution.py:495
  72.9 7.2 %all-to-all-start.5 = ((bf16[16,120,128]{2,1,0:T(8,128)(2,1)}), bf16[16,120,128]{2,1,0:T(8,128)(2,1)}, u32[]{:S(2)}, u32[]{:S(2)}) async-start(bf16[16,120,128]{2,1,0:T(8,128)(2,1)} %join.1), calls=%async_computation.5 | async-start | bytes 983040 | tf_op jit(solution)/shard_map/all_to_all | solution.py:785
  80.4 0.3 collective-permute-start.8
  80.7 1.0 collective-permute-done.6
  82.0 4.3 %collective-permute-done.2.refs_12_ = bf16[144,3072]{1,0:T(8,128)(2,1)} collective-permute-done((bf16[144,3072]{1,0:T(8,128)(2,1)}, bf16[144,3072]{1,0:T(8,128)(2,1)}, u32[]{:S(2)}, u32[]{:S(2)}) %collective-permute-start.2) | collective-permute-done | bytes 884768 | tf_op jit(solution)/shard_map/ppermute | solution.py:712
  86.3 0.5 collective-permute-start.11
  86.8 5.2 %all-to-all-done.5.parts = bf16[16,120,128]{2,1,0:T(8,128)(2,1)} async-done(((bf16[16,120,128]{2,1,0:T(8,128)(2,1)}), bf16[16,120,128]{2,1,0:T(8,128)(2,1)}, u32[]{:S(2)}, u32[]{:S(2)}) %all-to-all-start.5) | async-done | bytes 491552 | tf_op jit(solution)/shard_map/all_to_all | solution.py:785
  92.0 2.3 %project.1 = bf16[16,96,128]{2,1,0:T(8,128)(2,1)} custom-call(bf16[16,120,128]{2,1,0:T(8,128)(2,1)} %all-to-all-done.5.parts, bf16[192,768]{1,0:T(8,128)(2,1)} %bitcast.30), custom_call_target="tpu_custom_call" | custom-call | flops 20000000000 | bytes 1024 | tf_op jit(solution)/shard_map/project/pallas_call | solution.py:531
  94.3 0.5 collective-permute-done.12.refs_11_
  94.9 0.4 collective-permute-start.14
  95.4 3.6 %all-to-all-start.6 = ((bf16[16,96,128]{2,1,0:T(8,128)(2,1)}), bf16[16,96,128]{2,1,0:T(8,128)(2,1)S(1)}, u32[]{:S(2)}, u32[]{:S(2)}) async-start(bf16[16,96,128]{2,1,0:T(8,128)(2,1)} %project.1), calls=%async_computation.6 | async-start | bytes 786432 | tf_op jit(solution)/shard_map/all_to_all | solution.py:796
  99.0 0.6 gather_fusion.2
  99.7 0.7 fusion
  100.3 1.7 %collective-permute-start.16 = (bf16[8,128,256]{2,1,0:T(8,128)(2,1)S(1)}, bf16[8,128,256]{2,1,0:T(8,128)(2,1)}, u32[]{:S(2)}, u32[]{:S(2)}) collective-permute-start(bf16[8,128,256]{2,1,0:T(8,128)(2,1)S(1)} %pad_maximum_fusion.refs_0_), channel_id=1, source_target_pairs={{0,64},{16,80},{32,96},{48,112},{64,0},{80,16},{96,32},{112,48},{1... | collective-permute-start | bytes 1572872 | tf_op jit(solution)/shard_map/ppermute | solution.py:712
  102.0 0.3 collective-permute-start.15
  102.4 7.2 %all-to-all-done.6.spread = bf16[16,96,128]{2,1,0:T(8,128)(2,1)S(1)} async-done(((bf16[16,96,128]{2,1,0:T(8,128)(2,1)}), bf16[16,96,128]{2,1,0:T(8,128)(2,1)S(1)}, u32[]{:S(2)}, u32[]{:S(2)}) %all-to-all-start.6) | async-done | bytes 393248 | tf_op jit(solution)/shard_map/all_to_all | solution.py:796
  109.6 0.7 copy-done.7
  110.3 9.1 %feed.1 = (bf16[16,4,3072]{2,1,0:T(4,128)(2,1)}, bf16[64,3072]{1,0:T(8,128)(2,1)}) custom-call(bf16[16,96,128]{2,1,0:T(8,128)(2,1)} %copy-done.7, bf16[64,3072]{1,0:T(8,128)(2,1)} %get-tuple-element.92.embedded, f32[1,3072]{1,0:T(1,128)} %bitcast.33, bf16[144,3072]{1,0:T(8,128)(2,1)} %get-tuple-element.85.refs_0_, ...), custom_call_target="tpu_custom_call" | custom-call | flops 20000000000 | bytes 1024 | tf_op jit(solution)/shard_map/feed/pallas_call | solution.py:611
  119.4 3.6 %all-to-all-start.7 = ((bf16[16,4,3072]{2,1,0:T(4,128)(2,1)}), bf16[16,4,3072]{2,1,0:T(4,128)(2,1)S(1)}, u32[]{:S(2)}, u32[]{:S(2)}) async-start(bf16[16,4,3072]{2,1,0:T(4,128)(2,1)} %get-tuple-element.96), calls=%async_computation.7 | async-start | bytes 786432 | tf_op jit(solution)/shard_map/all_to_all | solution.py:799
  123.0 0.6 and_select_fusion.3.turns
  123.6 3.5 %collective-permute-done.15.refs_1_ = bf16[8,128,256]{2,1,0:T(8,128)(2,1)} collective-permute-done((bf16[8,128,256]{2,1,0:T(8,128)(2,1)S(1)}, bf16[8,128,256]{2,1,0:T(8,128)(2,1)}, u32[]{:S(2)}, u32[]{:S(2)}) %collective-permute-start.15) | collective-permute-done | bytes 524320 | tf_op jit(solution)/shard_map/ppermute | solution.py:712
  127.2 2.5 %pick.1 = f32[4,128,256]{2,1,0:T(8,128)} custom-call(s32[4]{0:T(128)} %and_select_fusion.3.turns, s32[4]{0:T(128)} %get-tuple-element.116.rows, bf16[8,128,256]{2,1,0:T(8,128)(2,1)} %copy-done.6, bf16[8,128,256]{2,1,0:T(8,128)(2,1)} %collective-permute-done.15.refs_1_, bf16[8,128,256]{2,1,0:T(8,128)(2,1)} %collective-permute-done.16.refs_2_, ...), custom_call_target="tpu_custom_call" | custom-call | tf_op jit(solution)/shard_map/pick/pallas_call | solution.py:660
  129.6 0.8 constant_dynamic-slice_fusion
  130.5 2.1 %all-to-all-done.7 = bf16[16,4,3072]{2,1,0:T(4,128)(2,1)S(1)} async-done(((bf16[16,4,3072]{2,1,0:T(4,128)(2,1)}), bf16[16,4,3072]{2,1,0:T(4,128)(2,1)S(1)}, u32[]{:S(2)}, u32[]{:S(2)}) %all-to-all-start.7) | async-done | bytes 393248 | tf_op jit(solution)/shard_map/all_to_all | solution.py:799
  132.7 0.6 add_convert_fusion
  (51 shorter events, 1.5 us)
Async XLA Ops:
  0.6 38.1 %copy-start = (s32[32]{0:T(128)S(1)}, s32[32]{0:T(128)}, u32[]{:S(2)}) copy-start(s32[32]{0:T(128)} %param.33) | copy-start | bytes 388
  0.6 23.5 %copy-start.3 = (s32[32]{0:T(128)S(1)}, s32[32]{0:T(128)}, u32[]{:S(2)}) copy-start(s32[32]{0:T(128)} %param.31) | copy-start | bytes 388
  5.0 27.5 %copy-start.1 = (s32[4]{0:T(128)S(1)}, s32[4]{0:T(128)}, u32[]{:S(2)}) copy-start(s32[4]{0:T(128)} %get-tuple-element.71.origin) | copy-start | bytes 52
  5.0 27.5 %all-to-all-start.2 = ((bf16[128,24,128]{2,1,0:T(8,128)(2,1)}), bf16[128,24,128]{2,1,0:T(8,128)(2,1)S(1)}, u32[]{:S(2)}, u32[]{:S(2)}) async-start(bf16[128,24,128]{2,1,0:T(8,128)(2,1)} %get-tuple-element.72), calls=%async_computation.2 | async-start | bytes 1572864 | tf_op jit(solution)/shard_map/all_to_all | solution.py:723
  18.9 40.9 %collective-permute-start = (bf16[144,3072]{1,0:T(8,128)(2,1)}, bf16[144,3072]{1,0:T(8,128)(2,1)}, u32[]{:S(2)}, u32[]{:S(2)}) collective-permute-start(bf16[144,3072]{1,0:T(8,128)(2,1)} %get-tuple-element.85.refs_0_), channel_id=1, source_target_pairs={{0,32},{16,48},{32,64},{48,80},{64,96},{80,112},{96,0},{112,16},{1... | collective-permute-start | bytes 2654216 | tf_op jit(solution)/shard_map/ppermute | solution.py:712
  20.0 39.9 %collective-permute-start.1 = (bf16[144,3072]{1,0:T(8,128)(2,1)}, bf16[144,3072]{1,0:T(8,128)(2,1)}, u32[]{:S(2)}, u32[]{:S(2)}) collective-permute-start(bf16[144,3072]{1,0:T(8,128)(2,1)} %get-tuple-element.86.refs_1_), channel_id=1, source_target_pairs={{0,96},{16,112},{32,0},{48,16},{64,32},{80,48},{96,64},{112,80},{1... | collective-permute-start | bytes 2654216 | tf_op jit(solution)/shard_map/ppermute | solution.py:712
  32.5 1.4 %copy-start.9 = (s32[32,16]{0,1:T(8,128)S(1)}, s32[32,16]{0,1:T(8,128)}, u32[]{:S(2)}) copy-start(s32[32,16]{0,1:T(8,128)} %param.29) | copy-start | bytes 6148
  33.8 5.5 %copy-start.4 = (s32[32]{0:T(128)S(1)}, s32[32]{0:T(128)}, u32[]{:S(2)}) copy-start(s32[32]{0:T(128)} %param.30) | copy-start | bytes 388
  34.5 13.8 %all-to-all-start.3 = ((bf16[16,96,128]{2,1,0:T(8,128)(2,1)}), bf16[16,96,128]{2,1,0:T(8,128)(2,1)S(1)}, u32[]{:S(2)}, u32[]{:S(2)}) async-start(bf16[16,96,128]{2,1,0:T(8,128)(2,1)} %hand.2), calls=%async_computation.3 | async-start | bytes 786432 | tf_op jit(solution)/shard_map/all_to_all | solution.py:727
  40.8 32.0 %collective-permute-start.4 = (bf16[144,3072]{1,0:T(8,128)(2,1)}, bf16[144,3072]{1,0:T(8,128)(2,1)}, u32[]{:S(2)}, u32[]{:S(2)}) collective-permute-start(bf16[144,3072]{1,0:T(8,128)(2,1)} %get-tuple-element.86.refs_1_), channel_id=1, source_target_pairs={{0,32},{16,48},{32,64},{48,80},{64,96},{80,112},{96,0},{112,16},{1... | collective-permute-start | bytes 2654216 | tf_op jit(solution)/shard_map/ppermute | solution.py:712
  41.6 31.2 %collective-permute-start.5 = (bf16[144,3072]{1,0:T(8,128)(2,1)}, bf16[144,3072]{1,0:T(8,128)(2,1)}, u32[]{:S(2)}, u32[]{:S(2)}) collective-permute-start(bf16[144,3072]{1,0:T(8,128)(2,1)} %get-tuple-element.85.refs_0_), channel_id=1, source_target_pairs={{0,96},{16,112},{32,0},{48,16},{64,32},{80,48},{96,64},{112,80},{1... | collective-permute-start | bytes 2654216 | tf_op jit(solution)/shard_map/ppermute | solution.py:712
  48.2 0.7 copy-start.8
  56.3 13.7 %all-to-all-start.4 = ((bf16[16,4,896]{2,1,0:T(4,128)(2,1)}), bf16[16,4,896]{2,1,0:T(4,128)(2,1)S(1)}, u32[]{:S(2)}, u32[]{:S(2)}) async-start(bf16[16,4,896]{2,1,0:T(4,128)(2,1)} %get-tuple-element.75), calls=%async_computation.4 | async-start | bytes 229376 | tf_op jit(solution)/shard_map/all_to_all | solution.py:768
  59.8 26.4 %collective-permute-start.2 = (bf16[144,3072]{1,0:T(8,128)(2,1)}, bf16[144,3072]{1,0:T(8,128)(2,1)}, u32[]{:S(2)}, u32[]{:S(2)}) collective-permute-start(bf16[144,3072]{1,0:T(8,128)(2,1)} %collective-permute-done.refs_2_), channel_id=1, source_target_pairs={{0,32},{16,48},{32,64},{48,80},{64,96},{80,112},{96,0},{112,16},{1... | collective-permute-start | bytes 2654216 | tf_op jit(solution)/shard_map/ppermute | solution.py:712
  60.9 25.4 %collective-permute-start.3 = (bf16[144,3072]{1,0:T(8,128)(2,1)}, bf16[144,3072]{1,0:T(8,128)(2,1)}, u32[]{:S(2)}, u32[]{:S(2)}) collective-permute-start(bf16[144,3072]{1,0:T(8,128)(2,1)} %collective-permute-done.1.refs_3_), channel_id=1, source_target_pairs={{0,96},{16,112},{32,0},{48,16},{64,32},{80,48},{96,64},{112,80},{1... | collective-permute-start | bytes 2654216 | tf_op jit(solution)/shard_map/ppermute | solution.py:712
  70.0 0.6 copy-start.11
  70.7 9.4 %copy-start.10 = (bf16[4,1,128,256]{3,2,1,0:T(8,128)(2,1)S(1)}, bf16[4,1,128,256]{3,2,1,0:T(8,128)(2,1)}, u32[]{:S(2)}) copy-start(bf16[4,1,128,256]{3,2,1,0:T(8,128)(2,1)} %get-tuple-element.84) | copy-start | bytes 786436
  72.8 19.2 %collective-permute-start.7 = (bf16[144,3072]{1,0:T(8,128)(2,1)}, bf16[144,3072]{1,0:T(8,128)(2,1)}, u32[]{:S(2)}, u32[]{:S(2)}) collective-permute-start(bf16[144,3072]{1,0:T(8,128)(2,1)} %get-tuple-element.85.refs_0_), channel_id=1, source_target_pairs={{0,16},{16,0},{32,48},{48,32},{64,80},{80,64},{96,112},{112,96},{1... | collective-permute-start | bytes 2654216 | tf_op jit(solution)/shard_map/ppermute | solution.py:717
  72.9 19.1 %all-to-all-start.5 = ((bf16[16,120,128]{2,1,0:T(8,128)(2,1)}), bf16[16,120,128]{2,1,0:T(8,128)(2,1)}, u32[]{:S(2)}, u32[]{:S(2)}) async-start(bf16[16,120,128]{2,1,0:T(8,128)(2,1)} %join.1), calls=%async_computation.5 | async-start | bytes 983040 | tf_op jit(solution)/shard_map/all_to_all | solution.py:785
  80.1 1.6 %collective-permute-start.6 = (bf16[4,128,256]{2,1,0:T(8,128)(2,1)S(1)}, bf16[4,128,256]{2,1,0:T(8,128)(2,1)S(1)}, u32[]{:S(2)}, u32[]{:S(2)}) collective-permute-start(bf16[4,128,256]{2,1,0:T(8,128)(2,1)S(1)} %bitcast.28), channel_id=1, source_target_pairs={{0,16},{16,0},{32,48},{48,32},{64,80},{80,64},{96,112},{112,96},{1... | collective-permute-start | bytes 786440 | tf_op jit(solution)/shard_map/ppermute | solution.py:717
  80.4 13.9 %collective-permute-start.8 = (bf16[144,3072]{1,0:T(8,128)(2,1)}, bf16[144,3072]{1,0:T(8,128)(2,1)}, u32[]{:S(2)}, u32[]{:S(2)}) collective-permute-start(bf16[144,3072]{1,0:T(8,128)(2,1)} %get-tuple-element.86.refs_1_), channel_id=1, source_target_pairs={{0,16},{16,0},{32,48},{48,32},{64,80},{80,64},{96,112},{112,96},{1... | collective-permute-start | bytes 2654216 | tf_op jit(solution)/shard_map/ppermute | solution.py:717
  81.7 12.5 %collective-permute-start.9 = (bf16[144,3072]{1,0:T(8,128)(2,1)}, bf16[144,3072]{1,0:T(8,128)(2,1)}, u32[]{:S(2)}, u32[]{:S(2)}) collective-permute-start(bf16[144,3072]{1,0:T(8,128)(2,1)} %collective-permute-done.refs_2_), channel_id=1, source_target_pairs={{0,16},{16,0},{32,48},{48,32},{64,80},{80,64},{96,112},{112,96},{1... | collective-permute-start | bytes 2654216 | tf_op jit(solution)/shard_map/ppermute | solution.py:717
  82.0 20.1 %copy-start.6 = (bf16[8,128,256]{2,1,0:T(8,128)(2,1)}, bf16[8,128,256]{2,1,0:T(8,128)(2,1)S(1)}, u32[]{:S(2)}) copy-start(bf16[8,128,256]{2,1,0:T(8,128)(2,1)S(1)} %pad_maximum_fusion.refs_0_) | copy-start | bytes 1572868
  86.3 8.0 %collective-permute-start.10 = (bf16[144,3072]{1,0:T(8,128)(2,1)}, bf16[144,3072]{1,0:T(8,128)(2,1)}, u32[]{:S(2)}, u32[]{:S(2)}) collective-permute-start(bf16[144,3072]{1,0:T(8,128)(2,1)} %collective-permute-done.1.refs_3_), channel_id=1, source_target_pairs={{0,16},{16,0},{32,48},{48,32},{64,80},{80,64},{96,112},{112,96},{1... | collective-permute-start | bytes 2654216 | tf_op jit(solution)/shard_map/ppermute | solution.py:717
  86.3 8.0 %collective-permute-start.11 = (bf16[144,3072]{1,0:T(8,128)(2,1)}, bf16[144,3072]{1,0:T(8,128)(2,1)}, u32[]{:S(2)}, u32[]{:S(2)}) collective-permute-start(bf16[144,3072]{1,0:T(8,128)(2,1)} %collective-permute-done.4.refs_4_), channel_id=1, source_target_pairs={{0,16},{16,0},{32,48},{48,32},{64,80},{80,64},{96,112},{112,96},{1... | collective-permute-start | bytes 2654216 | tf_op jit(solution)/shard_map/ppermute | solution.py:717
  92.0 2.8 %collective-permute-start.12 = (bf16[144,3072]{1,0:T(8,128)(2,1)}, bf16[144,3072]{1,0:T(8,128)(2,1)}, u32[]{:S(2)}, u32[]{:S(2)}) collective-permute-start(bf16[144,3072]{1,0:T(8,128)(2,1)} %collective-permute-done.5.refs_5_), channel_id=1, source_target_pairs={{0,16},{16,0},{32,48},{48,32},{64,80},{80,64},{96,112},{112,96},{1... | collective-permute-start | bytes 2654216 | tf_op jit(solution)/shard_map/ppermute | solution.py:717
  92.0 3.3 %copy-start.12 = (s32[32]{0:T(128)S(1)}, s32[32]{0:T(128)}, u32[]{:S(2)}) copy-start(s32[32]{0:T(128)} %param.32) | copy-start | bytes 388
  94.7 14.8 %collective-permute-start.13 = (bf16[144,3072]{1,0:T(8,128)(2,1)}, bf16[144,3072]{1,0:T(8,128)(2,1)}, u32[]{:S(2)}, u32[]{:S(2)}) collective-permute-start(bf16[144,3072]{1,0:T(8,128)(2,1)} %collective-permute-done.2.refs_12_), channel_id=1, source_target_pairs={{0,16},{16,0},{32,48},{48,32},{64,80},{80,64},{96,112},{112,96},{1... | collective-permute-start | bytes 2654216 | tf_op jit(solution)/shard_map/ppermute | solution.py:717
  94.9 14.7 %collective-permute-start.14 = (bf16[144,3072]{1,0:T(8,128)(2,1)}, bf16[144,3072]{1,0:T(8,128)(2,1)}, u32[]{:S(2)}, u32[]{:S(2)}) collective-permute-start(bf16[144,3072]{1,0:T(8,128)(2,1)} %collective-permute-done.3.refs_13_), channel_id=1, source_target_pairs={{0,16},{16,0},{32,48},{48,32},{64,80},{80,64},{96,112},{112,96},{1... | collective-permute-start | bytes 2654216 | tf_op jit(solution)/shard_map/ppermute | solution.py:717
  95.4 14.2 %all-to-all-start.6 = ((bf16[16,96,128]{2,1,0:T(8,128)(2,1)}), bf16[16,96,128]{2,1,0:T(8,128)(2,1)S(1)}, u32[]{:S(2)}, u32[]{:S(2)}) async-start(bf16[16,96,128]{2,1,0:T(8,128)(2,1)} %project.1), calls=%async_computation.6 | async-start | bytes 786432 | tf_op jit(solution)/shard_map/all_to_all | solution.py:796
  100.3 23.3 %collective-permute-start.17 = (bf16[8,128,256]{2,1,0:T(8,128)(2,1)S(1)}, bf16[8,128,256]{2,1,0:T(8,128)(2,1)}, u32[]{:S(2)}, u32[]{:S(2)}) collective-permute-start(bf16[8,128,256]{2,1,0:T(8,128)(2,1)S(1)} %pad_maximum_fusion.refs_0_), channel_id=1, source_target_pairs={{0,96},{16,112},{32,0},{48,16},{64,32},{80,48},{96,64},{112,80},{1... | collective-permute-start | bytes 1572872 | tf_op jit(solution)/shard_map/ppermute | solution.py:712
  100.3 23.3 %collective-permute-start.16 = (bf16[8,128,256]{2,1,0:T(8,128)(2,1)S(1)}, bf16[8,128,256]{2,1,0:T(8,128)(2,1)}, u32[]{:S(2)}, u32[]{:S(2)}) collective-permute-start(bf16[8,128,256]{2,1,0:T(8,128)(2,1)S(1)} %pad_maximum_fusion.refs_0_), channel_id=1, source_target_pairs={{0,64},{16,80},{32,96},{48,112},{64,0},{80,16},{96,32},{112,48},{1... | collective-permute-start | bytes 1572872 | tf_op jit(solution)/shard_map/ppermute | solution.py:712
  102.0 25.1 %collective-permute-start.15 = (bf16[8,128,256]{2,1,0:T(8,128)(2,1)S(1)}, bf16[8,128,256]{2,1,0:T(8,128)(2,1)}, u32[]{:S(2)}, u32[]{:S(2)}) collective-permute-start(bf16[8,128,256]{2,1,0:T(8,128)(2,1)S(1)} %pad_maximum_fusion.refs_0_), channel_id=1, source_target_pairs={{0,32},{16,48},{32,64},{48,80},{64,96},{80,112},{96,0},{112,16},{1... | collective-permute-start | bytes 1572872 | tf_op jit(solution)/shard_map/ppermute | solution.py:712
  109.6 0.7 copy-start.7
  119.4 13.1 %all-to-all-start.7 = ((bf16[16,4,3072]{2,1,0:T(4,128)(2,1)}), bf16[16,4,3072]{2,1,0:T(4,128)(2,1)S(1)}, u32[]{:S(2)}, u32[]{:S(2)}) async-start(bf16[16,4,3072]{2,1,0:T(4,128)(2,1)} %get-tuple-element.96), calls=%async_computation.7 | async-start | bytes 786432 | tf_op jit(solution)/shard_map/all_to_all | solution.py:799
